TPU v7x, 32 devices: a whole 2x2x4 slice. The times are simulated.
32 devices in a mesh: rows: 8 (over z, y), blk: 4 (over x, core).
Axes of the slice: x: 2, y: 2, z: 4, core: 2. Of those that a mesh axis runs over, the one named last changes fastest.
Arguments:
- tokens: bfloat16 [8, 2048, 768], P('rows', 'blk'), may hold values from -6 to 6
- seg_ids: int32 [8, 2048], P('rows', 'blk'), may hold values from 0 to 3, never falling along the last dimension, each value on 1 to 1024 neighbouring positions
- valid_len: int32 [8], P('rows'), may hold values from 1792 to 2048, as said below
- ln1_gain: float32 [768], replicated, may hold values from 0.5 to 1.5
- ln1_bias: float32 [768], replicated, may hold values from -3 to 3
- w_qkv: bfloat16 [768, 2304], replicated, may hold values from -0.21875 to 0.21875
- b_qkv: float32 [2304], replicated, may hold values from -3 to 3
- w_out: bfloat16 [768, 768], replicated, may hold values from -3.5 to 3.5
- b_out: float32 [768], replicated, may hold values from -2 to 2
- ln2_gain: float32 [768], replicated, may hold values from 0.5 to 1.5
- ln2_bias: float32 [768], replicated, may hold values from -3 to 3
- w_up: bfloat16 [768, 3072], replicated, may hold values from -0.21875 to 0.21875
- b_up: float32 [3072], replicated, may hold values from -3 to 3
- w_down: bfloat16 [3072, 768], replicated, may hold values from -0.109375 to 0.109375
- b_down: float32 [768], replicated, may hold values from -2 to 2
- cotangent: bfloat16 [8, 2048, 768], P('rows', 'blk'), may hold values from -6 to 6
Outputs:
- out: bfloat16 [8, 2048, 768], P('rows', 'blk')
- grad_tokens: bfloat16 [8, 2048, 768], P('rows', 'blk')
- grad_w_qkv: float32 [768, 2304], P('rows', 'blk')
- grad_w_out: float32 [768, 768], P('rows', 'blk')
- grad_w_up: float32 [768, 3072], P('rows', 'blk')
- grad_w_down: float32 [3072, 768], P('rows', 'blk')
- grad_b_qkv: float32 [2304], replicated
- grad_b_out: float32 [768], replicated
- grad_b_up: float32 [3072], replicated
- grad_b_down: float32 [768], replicated
- grad_ln1_gain: float32 [768], replicated
- grad_ln1_bias: float32 [768], replicated
- grad_ln2_gain: float32 [768], replicated
- grad_ln2_bias: float32 [768], replicated
Inputs may be any that keep to these rules, and one draw needn't show every extreme that they name: `seg_ids`: segment numbers never fall along a row; a segment holds at most half of the row's 2048 positions, and one holds exactly that many. `valid_len`: some row is full and some row has the fewest valid positions.
All inputs are finite; a program needn't handle non-finite values.
Results may differ from a plain program's by a relative error of at most 0.013.
Values may be sent and summed in bfloat16 or wider, within the bound.
No kernel may reach another device: no remote copies, remote signals or barrier semaphores. Data moves between devices by JAX's collectives and lax.ppermute only.
A program may use at most 128 MiB of HBM per device.

v0:
```python
from functools import partial

import jax
import jax.numpy as jnp
from jax import lax
from jax.sharding import PartitionSpec as P

D = 768
HEADS = 12
HDIM = 64
ROT = 16


EPS = 1e-05
MASKED = -1e30


def layer_norm(value, gain, shift):
    center = value - jnp.mean(value, axis=-1, keepdims=True)
    spread = jnp.mean(center * center, axis=-1, keepdims=True)
    return center * lax.rsqrt(spread + EPS) * gain + shift


def angle_table(positions):
    inverse = jnp.exp(-jnp.log(10000.0) * (2.0 * jnp.arange(ROT // 2, dtype=jnp.float32) / ROT))
    return positions.astype(jnp.float32)[:, None] * inverse[None, :]


def rotate(tensor, angles):
    half_rot = ROT // 2
    former = tensor[..., :half_rot]
    latter = tensor[..., half_rot:ROT]
    cos_table = jnp.cos(angles)[:, None, :]
    sin_table = jnp.sin(angles)[:, None, :]
    return jnp.concatenate(
        [
            former * cos_table - latter * sin_table,
            latter * cos_table + former * sin_table,
            tensor[..., ROT:],
        ],
        axis=-1,
    )


def contract_rows(left, right):
    return lax.dot_general(
        left, right, (((0,), (0,)), ((), ())), preferred_element_type=jnp.float32
    )


def times_transpose(left, right):
    return lax.dot_general(
        left, right, (((1,), (1,)), ((), ())), preferred_element_type=jnp.float32
    )


def keep_state(state):
    return state


def local(
    tokens,
    seg_ids,
    valid_len,
    ln1_gain,
    ln1_bias,
    w_qkv,
    b_qkv,
    w_out,
    b_out,
    ln2_gain,
    ln2_bias,
    w_up,
    b_up,
    w_down,
    b_down,
    cotangent,
):
    num_blocks = lax.axis_size("blk")
    block_id = lax.axis_index("blk")
    seq_len = tokens.shape[1]
    total_len = seq_len * num_blocks
    scale = HDIM ** (-0.5)
    inputs = tokens[0].astype(jnp.float32)
    positions = block_id * seq_len + jnp.arange(seq_len, dtype=jnp.int32)
    own_tag = jnp.where(positions < valid_len[0], seg_ids[0], -1)
    query_tag = own_tag.astype(jnp.float32)
    angles = angle_table(positions)
    attn_norm, attn_norm_back = jax.vjp(layer_norm, inputs, ln1_gain, ln1_bias)
    attn_in = attn_norm.astype(jnp.bfloat16)
    joined = jnp.dot(attn_in, w_qkv, preferred_element_type=jnp.float32) + b_qkv

    def split_heads(joined_rows):
        query = rotate(joined_rows[:, :D].reshape(seq_len, HEADS, HDIM), angles)
        keys = rotate(joined_rows[:, D : 2 * D].reshape(seq_len, HEADS, HDIM), angles)
        return (query, keys, joined_rows[:, 2 * D :])

    (query, keys, values), heads_back = jax.vjp(split_heads, joined)
    query_low = query.astype(jnp.bfloat16)
    key_low = keys.astype(jnp.bfloat16).reshape(seq_len, D)
    value_low = values.astype(jnp.bfloat16)
    tag_low = own_tag.astype(jnp.bfloat16)
    all_keys, all_values, all_tags = (
        lax.all_gather(key_low, "blk", axis=0, tiled=True),
        lax.all_gather(value_low, "blk", axis=0, tiled=True),
        lax.all_gather(tag_low, "blk", axis=0, tiled=True),
    )
    key_blocks = all_keys.reshape(num_blocks, seq_len, HEADS, HDIM)
    value_blocks = all_values.reshape(num_blocks, seq_len, HEADS, HDIM)
    tag_blocks = all_tags.reshape(num_blocks, seq_len)

    def block_scores(key_block, tag_block, index):
        scores = (
            jnp.einsum("qhd,khd->hqk", query_low, key_block, preferred_element_type=jnp.float32)
            * scale
        )
        key_pos = index * seq_len + jnp.arange(seq_len, dtype=jnp.int32)
        key_tag = tag_block.astype(jnp.float32)
        earlier = key_pos[None, :] < positions[:, None]
        allowed = (key_pos[None, :] == positions[:, None]) | earlier & (
            key_tag[None, :] == query_tag[:, None]
        ) & (query_tag[:, None] >= 0.0)
        return jnp.where(allowed[None], scores, MASKED)

    def stats_step(index, carry):

        def stats_visit(state):
            row_max, row_sum = state
            masked = block_scores(key_blocks[index], tag_blocks[index], index)
            new_max = jnp.maximum(row_max, jnp.max(masked, axis=-1))
            new_sum = row_sum * jnp.exp(row_max - new_max) + jnp.sum(
                jnp.exp(masked - new_max[..., None]), axis=-1
            )
            return (new_max, new_sum)

        return lax.cond(index <= block_id, stats_visit, keep_state, carry)

    start_stats = (
        jnp.full((HEADS, seq_len), MASKED, jnp.float32),
        jnp.zeros((HEADS, seq_len), jnp.float32),
    )
    row_max, row_sum = lax.fori_loop(0, num_blocks, stats_step, start_stats)

    def output_step(index, total):

        def output_visit(state):
            masked = block_scores(key_blocks[index], tag_blocks[index], index)
            probs_low = (jnp.exp(masked - row_max[..., None]) / row_sum[..., None]).astype(
                jnp.bfloat16
            )
            return state + jnp.einsum(
                "hqk,khd->qhd", probs_low, value_blocks[index], preferred_element_type=jnp.float32
            )

        return lax.cond(index <= block_id, output_visit, keep_state, total)

    attn_heads = lax.fori_loop(
        0, num_blocks, output_step, jnp.zeros((seq_len, HEADS, HDIM), jnp.float32)
    )
    attn_low = attn_heads.reshape(seq_len, D).astype(jnp.bfloat16)
    attn = jnp.dot(attn_low, w_out, preferred_element_type=jnp.float32) + b_out
    mlp_norm, mlp_norm_back = jax.vjp(layer_norm, inputs, ln2_gain, ln2_bias)
    mlp_in = mlp_norm.astype(jnp.bfloat16)
    hidden = jnp.dot(mlp_in, w_up, preferred_element_type=jnp.float32) + b_up
    act, gelu_back = jax.vjp(partial(jax.nn.gelu, approximate=False), hidden)
    act_low = act.astype(jnp.bfloat16)
    mlp = jnp.dot(act_low, w_down, preferred_element_type=jnp.float32) + b_down
    result = (inputs + attn + mlp).astype(jnp.bfloat16)[None]
    upstream = cotangent[0]
    upstream_wide = upstream.astype(jnp.float32)
    grad_w_out = contract_rows(attn_low, upstream)
    grad_b_out = jnp.sum(upstream_wide, axis=0)
    grad_w_down = contract_rows(act_low, upstream)
    grad_act = times_transpose(upstream, w_down)
    (grad_hidden,) = gelu_back(grad_act)
    grad_hidden_low = grad_hidden.astype(jnp.bfloat16)
    grad_w_up = contract_rows(mlp_in, grad_hidden_low)
    grad_b_up = jnp.sum(grad_hidden_low.astype(jnp.float32), axis=0)
    grad_mlp_norm = times_transpose(grad_hidden_low, w_up)
    grad_from_mlp, grad_ln2_gain, grad_ln2_bias = mlp_norm_back(grad_mlp_norm)
    grad_vec = times_transpose(upstream, w_out).astype(jnp.bfloat16).reshape(seq_len, HEADS, HDIM)
    delta = jnp.sum(grad_vec.astype(jnp.float32) * attn_heads, axis=-1).T
    again_keys, again_values, again_tags = (
        lax.all_gather(key_low, "blk", axis=0, tiled=True),
        lax.all_gather(value_low, "blk", axis=0, tiled=True),
        lax.all_gather(tag_low, "blk", axis=0, tiled=True),
    )
    back_keys = again_keys.reshape(num_blocks, seq_len, HEADS, HDIM)
    back_values = again_values.reshape(num_blocks, seq_len, HEADS, HDIM)
    back_tags = again_tags.reshape(num_blocks, seq_len)

    def grad_step(index, carry):

        def grad_visit(state):
            grad_query, key_terms = state
            key_block = back_keys[index]
            value_block = back_values[index]
            masked = block_scores(key_block, back_tags[index], index)
            probs = jnp.exp(masked - row_max[..., None]) / row_sum[..., None]
            grad_probs = jnp.einsum(
                "qhd,khd->hqk", grad_vec, value_block, preferred_element_type=jnp.float32
            )
            grad_scores = (probs * (grad_probs - delta[..., None])).astype(jnp.bfloat16)
            grad_query = grad_query + scale * jnp.einsum(
                "hqk,khd->qhd", grad_scores, key_block, preferred_element_type=jnp.float32
            )
            grad_key = scale * jnp.einsum(
                "hqk,qhd->khd", grad_scores, query_low, preferred_element_type=jnp.float32
            )
            grad_value = jnp.einsum(
                "hqk,qhd->khd",
                probs.astype(jnp.bfloat16),
                grad_vec,
                preferred_element_type=jnp.float32,
            )
            term = jnp.concatenate(
                [grad_key.reshape(seq_len, D), grad_value.reshape(seq_len, D)], axis=1
            )
            return (grad_query, lax.dynamic_update_index_in_dim(key_terms, term, index, 0))

        return lax.cond(index <= block_id, grad_visit, keep_state, carry)

    start_grads = (
        jnp.zeros((seq_len, HEADS, HDIM), jnp.float32),
        jnp.zeros((num_blocks, seq_len, 2 * D), jnp.float32),
    )
    grad_query, key_terms = lax.fori_loop(0, num_blocks, grad_step, start_grads)
    own_terms = lax.psum_scatter(
        key_terms.reshape(total_len, 2 * D).astype(jnp.bfloat16),
        "blk",
        scatter_dimension=0,
        tiled=True,
    ).astype(jnp.float32)
    grad_keys = own_terms[:, :D].reshape(seq_len, HEADS, HDIM)
    grad_values = own_terms[:, D:]
    (grad_joined,) = heads_back((grad_query, grad_keys, grad_values))
    grad_joined_low = grad_joined.astype(jnp.bfloat16)
    grad_w_qkv = contract_rows(attn_in, grad_joined_low)
    grad_b_qkv = jnp.sum(grad_joined_low.astype(jnp.float32), axis=0)
    grad_attn_norm = times_transpose(grad_joined_low, w_qkv)
    grad_from_attn, grad_ln1_gain, grad_ln1_bias = attn_norm_back(grad_attn_norm)
    grad_tokens = (upstream_wide + grad_from_attn + grad_from_mlp).astype(jnp.bfloat16)[None]
    weight_grads = (grad_w_qkv, grad_w_out, grad_w_up, grad_w_down)
    summed = (
        lax.psum_scatter(weight_grads[0], "rows", scatter_dimension=0, tiled=True),
        lax.psum_scatter(weight_grads[1], "rows", scatter_dimension=0, tiled=True),
        lax.psum_scatter(weight_grads[2], "rows", scatter_dimension=0, tiled=True),
        lax.psum_scatter(weight_grads[3], "rows", scatter_dimension=0, tiled=True),
    )
    summed = (
        lax.psum_scatter(
            summed[0].astype(jnp.bfloat16), "blk", scatter_dimension=1, tiled=True
        ).astype(jnp.float32),
        lax.psum_scatter(
            summed[1].astype(jnp.bfloat16), "blk", scatter_dimension=1, tiled=True
        ).astype(jnp.float32),
        lax.psum_scatter(
            summed[2].astype(jnp.bfloat16), "blk", scatter_dimension=1, tiled=True
        ).astype(jnp.float32),
        lax.psum_scatter(
            summed[3].astype(jnp.bfloat16), "blk", scatter_dimension=1, tiled=True
        ).astype(jnp.float32),
    )
    small = lax.psum(
        (
            grad_b_qkv,
            grad_b_out,
            grad_b_up,
            grad_ln1_gain,
            grad_ln1_bias,
            grad_ln2_gain,
            grad_ln2_bias,
        ),
        ("rows", "blk"),
    )
    return (
        result,
        grad_tokens,
        summed[0],
        summed[1],
        summed[2],
        summed[3],
        small[0],
        small[1],
        small[2],
        small[1],
        small[3],
        small[4],
        small[5],
        small[6],
    )


def solution(mesh):
    in_specs = (
        P("rows", "blk", None),
        P("rows", "blk"),
        P("rows"),
        P(),
        P(),
        P(),
        P(),
        P(),
        P(),
        P(),
        P(),
        P(),
        P(),
        P(),
        P(),
        P("rows", "blk", None),
    )
    out_specs = (
        P("rows", "blk", None),
        P("rows", "blk", None),
        P("rows", "blk"),
        P("rows", "blk"),
        P("rows", "blk"),
        P("rows", "blk"),
        P(),
        P(),
        P(),
        P(),
        P(),
        P(),
        P(),
        P(),
    )
    return jax.shard_map(local, mesh=mesh, in_specs=in_specs, out_specs=out_specs, check_vma=False)
```

profile of v0, /device:TPU:0, one launch (start us, length us, event | category | flops | bytes accessed | tf_op | source)
XLA Modules:
  0.0 936.4 jit_solution(7566286224300068631)
XLA Ops:
  37.2 6.8 all-gather
  51.6 4.7 copy.87
  56.3 6.4 reshape.484
  67.0 12.5 %all-gather.6.cloned.1.call-done = bf16[2048,768]{0,1:T(8,128)(2,1)} async-done(((bf16[512,768]{0,1:T(8,128)(2,1)}), bf16[2048,768]{0,1:T(8,128)(2,1)}) %all-gather.6.cloned.1.call-update) | async-done | bytes 3145744 | tf_op jit(solution)/shard_map/all_gather | solution.py:104
  79.5 6.2 reshape.487
  91.2 9.6 %while.49 = (s32[]{:T(128)}, f32[12,512]{1,0:T(8,128)}, f32[12,512]{1,0:T(8,128)}, s32[]{:T(128)}, bf16[4,512]{1,0:T(4,128)(2,1)S(1)}, /*index=5*/f32[512]{0:T(5...) while((s32[]{:T(128)}, f32[12,512]{1,0:T(8,128)}, ...), condition=%wide.region_7.8_spmd.clone, body=%wide.region_2.7_spmd.clone.sunk | while | flops 426260480 | bytes 29014368 | solution.py:142
  91.2 9.6 %conditional.9 = ((f32[12,512]{1,0:T(8,128)}, f32[12,512]{1,0:T(8,128)})) conditional(s32[]{:T(128)} %convert_element_type.302, (f32[12,512]{1,0:T(8,128)}, f32[12,512]{1,0:T(8,128)}) %tuple.167, (s32[]{:T(128)}, s32[]{:T(128)}, bf16[4,512]{1,0:T(4,128)(2,1)S(1)}, f32[512]{0:T(512)S(1)}, bf16[4,512,12,64]{1,3,2,0:T(8,128)(2,1)}, ...), branch_computations={%region_3.3_spmd, %region_4.6_spmd} | conditional | flops 426260480 | bytes 29012110 | solution.py:136
  102.1 9.4 while.50
  102.3 9.1 conditional.10
  103.5 7.9 bitcast_add_fusion
  122.4 29.8 %while.51 = (s32[]{:T(128)}, f32[512,12,64]{0,2,1:T(8,128)}, bf16[4,512,1536]{1,2,0:T(8,128)(2,1)}, s32[]{:T(128)}, bf16[4,512,12,64]{1,3,2,0:T(8,128)(2,1)}, /*...) while((s32[]{:T(128)}, f32[512,12,64]{0,2,1:T(8,128)}, ...), condition=%wide.region_16.17_spmd.clone, body=%wide.region_13.0_spmd.clone.sunk | while | flops 2044725248 | bytes 89602584 | solution.py:227
  122.6 29.5 %conditional.11 = ((f32[512,12,64]{0,2,1:T(8,128)}, bf16[4,512,1536]{1,2,0:T(8,128)(2,1)})) conditional(s32[]{:T(128)} %convert_element_type.304, (f32[512,12,64]{0,2,1:T(8,128)}, bf16[4,512,1536]{1,2,0:T(8,128)(2,1)}) %tuple.172, (s32[]{:T(128)}, bf16[4,512,12,64]{1,3,2,0:T(8,128)(2,1)}, s32[]{:T(128)}, bf16[4,512]{1,0:T(4,128)(2,1)S(1)}, ...), branch_computations={%region_14.14_spmd, %region_15.15_spmd} | conditional | flops 2044725248 | bytes 89600248 | solution.py:221
  123.1 9.9 %fusion.34 = f32[12,512,512]{1,2,0:T(8,128)} fusion(f32[12,512]{1,0:T(8,128)} %get-tuple-element.663, f32[12,512]{1,0:T(8,128)} %get-tuple-element.662, pred[512,512]{0,1:T(8,128)(4,1)S(1)} %and_or_fusion.2, bf16[512,12,64]{0,2,1:T(8,128)(2,1)} %get-tuple-element.661, bf16[4,512,12,64]{1,3,2,0:T(8,128)(2,1)} %get-tuple-element.656, s32[]{:T(128)S(6)} %select_n.27), kind=kOutput, calls=%fused_computation.41 | convolution fusion | flops 415236096 | bytes 14483460 | tf_op jit(solution)/shard_map/while/body/eval_jaxpr/cond/branch_1_fun/qhd,khd->hqk/dot_general | solution.py:114
  133.0 6.6 fusion.35
  139.6 6.8 fusion.31
  152.2 8.7 copy.96
  161.6 20.6 %multiply_convert_fusion = (bf16[512,3072]{1,0:T(8,128)(2,1)S(1)}, f32[512,3072]{1,0:T(8,128)}, f32[512,3072]{1,0:T(8,128)}) fusion(f32[3072]{0:T(1024)} %param.40, bf16[768,3072]{1,0:T(8,128)(2,1)} %param.39, bf16[1,512,768]{2,1,0:T(8,128)(2,1)} %param.28, f32[768]{0:T(1024)S(1)} %copy-done.27, f32[768]{0:T(1024)S(1)} %copy-done.20, ...), kind=kOutput, calls=%fused_computation.66 | convolution fusion | flops 2522087424 | bytes 21256192 | tf_op jit(solution)/shard_map/dot_general | solution.py:164
  183.8 5.1 fusion.80
  189.5 11.5 %convert_reduce_fusion = (f32[3072]{0:T(1024)}, bf16[512,3072]{1,0:T(8,128)(2,1)S(1)}) fusion(f32[512,3072]{1,0:T(8,128)} %get-tuple-element.1070, bf16[3072,768]{1,0:T(8,128)(2,1)} %param.41, bf16[1,512,768]{2,1,0:T(8,128)(2,1)} %param.43, f32[512,3072]{1,0:T(8,128)} %get-tuple-element.1107, f32[3072]{0:T(1024)} %param.40), kind=kOutput, calls=%fused_computation.64 | convolution fusion | flops 2442654720 | bytes 21258240 | tf_op jit(solution)/shard_map/dot_general | solution.py:52
  202.7 5.5 fusion.95
  210.7 32.0 %reduce-scatter.20.cloned.1.call-done = f32[96,768]{1,0:T(8,128)} async-done(((f32[768,768]{1,0:T(8,128)}), f32[96,768]{1,0:T(8,128)}) %reduce-scatter.20.cloned.1.call-update) | async-done | bytes 294928 | tf_op jit(solution)/shard_map/reduce_scatter | solution.py:246
  246.2 117.8 %reduce-scatter.16.cloned.1.call-done = bf16[512,1536]{1,0:T(8,128)(2,1)} async-done(((bf16[2048,1536]{1,0:T(8,128)(2,1)}), bf16[512,1536]{1,0:T(8,128)(2,1)}) %reduce-scatter.16.cloned.1.call-update) | async-done | bytes 1572880 | tf_op jit(solution)/shard_map/reduce_scatter | solution.py:228
  386.3 5.2 fusion.99
  391.5 139.7 %reduce-scatter.26.cloned.1.call-done = f32[384,768]{1,0:T(8,128)} async-done(((f32[3072,768]{1,0:T(8,128)}), f32[384,768]{1,0:T(8,128)}) %reduce-scatter.26.cloned.1.call-update) | async-done | bytes 1179664 | tf_op jit(solution)/shard_map/reduce_scatter | solution.py:248
  535.7 7.3 fusion.110
  543.0 6.1 fusion.109
  549.1 148.5 %reduce-scatter.22.cloned.1.call-done = f32[96,3072]{1,0:T(8,128)} async-done(((f32[768,3072]{1,0:T(8,128)}), f32[96,3072]{1,0:T(8,128)}) %reduce-scatter.22.cloned.1.call-update) | async-done | bytes 1179664 | tf_op jit(solution)/shard_map/reduce_scatter | solution.py:247
  703.8 15.8 %reduce-scatter.30.cloned.1.call-done = bf16[192,96]{1,0:T(8,128)(2,1)} async-done(((bf16[768,96]{1,0:T(8,128)(2,1)}), bf16[192,96]{1,0:T(8,128)(2,1)}) %reduce-scatter.30.cloned.1.call-update) | async-done | bytes 36880
  722.6 6.3 fusion.105
  729.5 123.3 %reduce-scatter.18.cloned.1.call-done = f32[96,2304]{1,0:T(8,128)} async-done(((f32[768,2304]{1,0:T(8,128)}), f32[96,2304]{1,0:T(8,128)}) %reduce-scatter.18.cloned.1.call-update) | async-done | bytes 884752 | tf_op jit(solution)/shard_map/reduce_scatter | solution.py:245
  864.2 41.3 %all-reduce.9 = (f32[2304]{0:T(1024)}, f32[768]{0:T(1024)S(1)}, f32[3072]{0:T(1024)}, f32[768]{0:T(1024)}, f32[768]{0:T(1024)}, /*index=5*/f32[768]{0:T(1024)}, f32[768]{0:T(1024)}) all-reduce(f32[2304]{0:T(1024)} %get-tuple-element.1067, f32[768]{0:T(1024)} %get-tuple-element.1095, ...), channel_id=1, replica_groups=mesh['rows'=8,'blk'=4] {'rows','blk'}, use_global_device_ids=true, to_apply=%region_31.32 | all-reduce | flops 9216 | bytes 73728 | tf_op jit(solution)/shard_map/psum | solution.py:264
  910.6 15.1 %reduce-scatter.28.cloned.1.call-done = bf16[576,96]{1,0:T(8,128)(2,1)} async-done(((bf16[2304,96]{1,0:T(8,128)(2,1)}), bf16[576,96]{1,0:T(8,128)(2,1)}) %reduce-scatter.28.cloned.1.call-update) | async-done | bytes 110608
  (201 shorter events, 143.1 us)
Async XLA Ops:
  7.2 3.6 copy-start
  7.2 44.4 %all-gather.4.cloned.1.call-start = ((), (), s32[]{:S(2)}) async-start(), calls=%async_computation.9 | async-start | bytes 3932160 | tf_op jit(solution)/shard_map/all_gather | solution.py:105
  8.7 5.4 copy-start.21
  17.4 62.1 %all-gather.6.cloned.1.call-start = ((), (), s32[]{:S(2)}) async-start(), calls=%async_computation.10 | async-start | bytes 3932160 | tf_op jit(solution)/shard_map/all_gather | solution.py:104
  27.2 9.9 %copy-start.33 = (s32[1,512]{1,0:T(1,128)S(1)}, s32[1,512]{1,0:T(1,128)}, u32[]{:S(2)}) copy-start(s32[1,512]{1,0:T(1,128)} %param.29) | copy-start | bytes 6148
  34.3 208.4 %reduce-scatter.20.cloned.1.call-start = ((), (), s32[]{:S(2)}) async-start(), calls=%async_computation.13 | async-start | bytes 2654208 | tf_op jit(solution)/shard_map/reduce_scatter | solution.py:246
  91.6 3.6 copy-start.4
  91.6 3.6 copy-start.12
  111.5 4.1 copy-start.16
  117.9 246.0 %reduce-scatter.16.cloned.1.call-start = ((), (), s32[]{:S(2)}) async-start(), calls=%async_computation.11 | async-start | bytes 7864320 | tf_op jit(solution)/shard_map/reduce_scatter | solution.py:228
  123.1 9.9 %copy-start.1 = (bf16[512,12,64]{0,2,1:T(8,128)(2,1)S(1)}, bf16[512,12,64]{0,2,1:T(8,128)(2,1)}, u32[]{:S(2)}) copy-start(bf16[512,12,64]{0,2,1:T(8,128)(2,1)} %get-tuple-element.665) | copy-start | bytes 2359300 | tf_op jit(solution)/shard_map/while/body/eval_jaxpr/cond
  133.0 6.6 copy-start.19
  139.6 6.8 copy-start.2
  160.9 370.2 %reduce-scatter.26.cloned.1.call-start = ((), (), s32[]{:S(2)}) async-start(), calls=%async_computation.16 | async-start | bytes 10616832 | tf_op jit(solution)/shard_map/reduce_scatter | solution.py:248
  161.6 22.3 %copy-start.17 = (bf16[1,512,768]{2,1,0:T(8,128)(2,1)S(1)}, bf16[1,512,768]{2,1,0:T(8,128)(2,1)}, u32[]{:S(2)}) copy-start(bf16[1,512,768]{2,1,0:T(8,128)(2,1)} %param.43) | copy-start | bytes 2359300
  189.0 508.6 %reduce-scatter.22.cloned.1.call-start = ((), (), s32[]{:S(2)}) async-start(), calls=%async_computation.14 | async-start | bytes 10616832 | tf_op jit(solution)/shard_map/reduce_scatter | solution.py:247
  189.5 13.2 %copy-start.6 = (bf16[1,512,768]{2,1,0:T(8,128)(2,1)S(1)}, bf16[1,512,768]{2,1,0:T(8,128)(2,1)}, u32[]{:S(2)}) copy-start(bf16[1,512,768]{2,1,0:T(8,128)(2,1)} %param.28) | copy-start | bytes 2359300
  208.3 511.4 %reduce-scatter.30.cloned.1.call-start = ((), (), s32[]{:S(2)}) async-start(), calls=%async_computation.18 | async-start | bytes 245760
  246.1 606.7 %reduce-scatter.18.cloned.1.call-start = ((), (), s32[]{:S(2)}) async-start(), calls=%async_computation.12 | async-start | bytes 7962624 | tf_op jit(solution)/shard_map/reduce_scatter | solution.py:245
  381.4 4.9 copy-start.7
  381.4 4.9 copy-start.31
  381.4 4.9 copy-start.34
  391.4 514.0 %reduce-scatter.32.cloned.1.call-start = ((), (), s32[]{:S(2)}) async-start(), calls=%async_computation.19 | async-start | bytes 737280
  535.4 373.5 %reduce-scatter.24.cloned.1.call-start = ((), (), s32[]{:S(2)}) async-start(), calls=%async_computation.15 | async-start | bytes 737280 | tf_op jit(solution)/shard_map/reduce_scatter | solution.py:257
  535.7 7.3 copy-start.36
  699.8 226.0 %reduce-scatter.28.cloned.1.call-start = ((), (), s32[]{:S(2)}) async-start(), calls=%async_computation.17 | async-start | bytes 737280
  722.6 6.3 copy-start.30
  856.9 3.7 copy-start.8
  856.9 3.7 copy-start.9
  856.9 3.7 copy-start.10
  856.9 3.7 copy-start.28
  905.5 24.2 %copy-start.32 = (f32[768]{0:T(1024)}, f32[768]{0:T(1024)S(1)}, u32[]{:S(2)}) copy-start(f32[768]{0:T(1024)S(1)} %get-tuple-element.1470) | copy-start | bytes 9220
  (16 other events, 25.0 us)
Sparse Core Ops, SparseCore 0:
  17.5 31.2 all-gather.3
  50.9 28.5 all-gather.5
  118.0 124.6 reduce-scatter.19
  245.1 118.7 reduce-scatter.15
  367.8 163.3 reduce-scatter.25
  535.0 162.5 reduce-scatter.21
  700.7 18.8 reduce-scatter.29
  723.8 129.0 reduce-scatter.17
  855.3 21.2 reduce-scatter.31
  879.0 22.1 reduce-scatter.23
  903.7 22.0 reduce-scatter.27
where the time goes:
time: 943 us; the launch traced here: 936 us
  waiting for transfers between devices  605 us (64%)
  matrix products  119 us (13%)
  local copies, waits for them, and re-layouts  99 us (10%)
  blocking collectives  48.1 us (5%)
  other arithmetic  48 us (5%)
  between operations  15 us (2%)
    reduce_scatter x1, waiting for transfers between devices, local(): lax.psum_scatter(weight_grads[2], 'rows', scatter_dimension=0, tiled=True)  149 us
    reduce_scatter x1, waiting for transfers between devices, local(): lax.psum_scatter(weight_grads[3], 'rows', scatter_dimension=0, tiled=True)  140 us
    reduce_scatter x1, waiting for transfers between devices, local(): lax.psum_scatter(weight_grads[0], 'rows', scatter_dimension=0, tiled=True)  123 us
    reduce_scatter x1, waiting for transfers between devices, local(): lax.psum_scatter(key_terms.reshape(total_len, 2 * D).astype(jnp.bfloat16)...  118 us
    psum x1, blocking collectives, local(): lax.psum((grad_b_qkv, grad_b_out, grad_b_up, grad_ln1_gain, grad_ln1_bias...  41.3 us
    reduce_scatter x1, waiting for transfers between devices, local(): lax.psum_scatter(weight_grads[1], 'rows', scatter_dimension=0, tiled=True)  32 us
    unnamed x72, local copies, waits for them, and re-layouts  31.5 us
    unnamed x14, waiting for transfers between devices  31.1 us
  transfers between devices with their start and end apart: 11, of which 8 were waited for; matrix products, arithmetic and copies ran while one was open for 22% of the time, Pallas kernels for 0%

commit v1 on v0

v1 whole, which is shorter than its diff:
```python
import math
from functools import partial

import jax
import jax.numpy as jnp
import numpy as np
from jax import lax
from jax.experimental import pallas as pl
from jax.experimental.pallas import tpu as pltpu
from jax.sharding import PartitionSpec as P

D = 768
HEADS = 12
HDIM = 64
ROT = 16
FF = 3072
EPS = 1e-05
MASKED = -1e30
TILE = 256
LANES = 128
F32 = jnp.float32
BF16 = jnp.bfloat16
NT_DIMS = (((1,), (1,)), ((), ()))
TN_DIMS = (((0,), (0,)), ((), ()))


def dot(left, right):
    return jnp.dot(left, right, preferred_element_type=F32)


def dot_nt(left, right):
    return lax.dot_general(left, right, NT_DIMS, preferred_element_type=F32)


def dot_tn(left, right):
    return lax.dot_general(left, right, TN_DIMS, preferred_element_type=F32)


def normalize(value):
    center = value - jnp.mean(value, axis=-1, keepdims=True)
    spread = jnp.mean(center * center, axis=-1, keepdims=True)
    return center * lax.rsqrt(spread + EPS)


def angle_parts(length):
    dim = np.arange(LANES) % HDIM
    inverse = np.where(dim < ROT, 10000.0 ** (-2.0 * (dim % (ROT // 2)) / ROT), 0.0)
    high = (np.arange(length // LANES) * LANES)[:, None] * inverse
    low = np.arange(LANES)[:, None] * inverse
    parts = np.stack([np.cos(low), np.sin(low)]), np.stack([np.cos(high), np.sin(high)])
    return tuple(jnp.asarray(part, F32) for part in parts)


def rotation(low_ref, high_ref, tile):
    lane = lax.broadcasted_iota(jnp.int32, (1, LANES), 1) % HDIM
    sign = jnp.where(lane < ROT // 2, -1.0, 1.0)
    cos_rows, sin_rows = [], []
    for part in range(TILE // LANES):
        row = tile * (TILE // LANES) + part
        cos_high = high_ref[0, pl.ds(row, 1), :]
        sin_high = high_ref[1, pl.ds(row, 1), :]
        cos_rows.append(low_ref[0] * cos_high - low_ref[1] * sin_high)
        sin_rows.append((low_ref[1] * cos_high + low_ref[0] * sin_high) * sign)
    return jnp.concatenate(cos_rows, axis=0), jnp.concatenate(sin_rows, axis=0)


def swap_halves(value):
    lane = lax.broadcasted_iota(jnp.int32, value.shape, 1) % HDIM
    half = ROT // 2
    return jnp.where(
        lane < half, pltpu.roll(value, LANES - half, 1), pltpu.roll(value, half, 1)
    )


def true_block(meta_ref, slot):
    return jnp.bitwise_xor(meta_ref[0], slot)


def params(*semantics, vmem=None):
    return pltpu.CompilerParams(
        dimension_semantics=semantics or ("arbitrary",), vmem_limit_bytes=vmem or 60 * 2**20
    )


def whole(shape):
    return pl.BlockSpec(shape, lambda *_: (0,) * len(shape))


def qkv_kernel(slot, meta, x_ref, gain, shift, w_ref, b_ref, low, high, *refs):
    q_ref, k_ref, v_ref = refs[-3:]
    per = x_ref.shape[0] // TILE
    for part in range(per):
        rows = pl.ds(part * TILE, TILE)
        normed = normalize(x_ref[rows, :].astype(F32))
        attn_in = (normed * gain[...] + shift[...]).astype(BF16)
        joined = dot(attn_in, w_ref[...]) + b_ref[...]
        cos, sin = rotation(low, high, true_block(meta, slot) * per + part)
        scale = HDIM**-0.5

        def turn(block):
            return block * cos + swap_halves(block) * sin

        query = turn(joined[:, 0:128]) * scale
        keys = turn(joined[:, 128:256])
        mixed = turn(joined[:, 256:384])
        q_ref[rows, 0:128] = query.astype(BF16)
        k_ref[rows, 0:128] = keys.astype(BF16)
        q_ref[rows, 128:192] = (mixed[:, 0:64] * scale).astype(BF16)
        k_ref[rows, 128:192] = mixed[:, 64:128].astype(BF16)
        v_ref[rows, :] = joined[:, 384:576].astype(BF16)


def project(slot, meta, x, gain, shift, w, b, low, high, filled):
    seq = x.shape[0]
    width = w.shape[1] // 3
    total = 4 * seq
    out = jax.ShapeDtypeStruct((total, width), BF16)
    out_spec = pl.BlockSpec((seq, width), lambda i, m: (slot, 0))
    args = [x, gain, shift, w, b, low, high]
    specs = [whole(a.shape) for a in args]
    aliases = {}
    if filled is not None:
        aliases = {1 + len(args) + i: i for i in range(3)}
        args += list(filled)
        specs += [pl.BlockSpec(memory_space=pl.ANY)] * 3
    return pl.pallas_call(
        partial(qkv_kernel, slot),
        out_shape=[out] * 3,
        grid_spec=pltpu.PrefetchScalarGridSpec(
            num_scalar_prefetch=1, grid=(1,), in_specs=specs, out_specs=[out_spec] * 3
        ),
        input_output_aliases=aliases,
        compiler_params=params(),
        cost_estimate=pl.CostEstimate(
            flops=2 * seq * D * 3 * width, bytes_accessed=4 * seq * D, transcendentals=0
        ),
        name=f"qkv_{slot}",
    )(meta, *args)


def mlp_kernel(final, meta, *refs):
    if final:
        (xa, xb, ca, cb, gain, shift, w_up, b_up, w_down, w_out) = refs[:10]
        (up_in, down_in, b_in, g_in, s_in) = refs[10:15]
    else:
        (xa, xb, ca, cb, gain, shift, w_up, b_up, w_down, w_out) = refs[:10]
    (mo_ref, e_ref, gv_ref, gup_ref, gdown_ref, gb_ref, gg_ref, gs_ref) = refs[-12:-4]
    x_s, c_s, up_s, down_s = refs[-4:]
    step = pl.program_id(0)
    half = pl.num_programs(0) // 2

    @pl.when(step < half)
    def _():
        x_s[...] = xa[...]
        c_s[...] = ca[...]

    @pl.when(step >= half)
    def _():
        x_s[...] = xb[...]
        c_s[...] = cb[...]

    @pl.when(step == 0)
    def _():
        if final:
            up_s[...] = up_in[...]
            down_s[...] = down_in[...]
            gb_ref[...] = b_in[...]
            gg_ref[...] = g_in[...]
            gs_ref[...] = s_in[...]
        else:
            up_s[...] = jnp.zeros_like(up_s)
            down_s[...] = jnp.zeros_like(down_s)
            gb_ref[...] = jnp.zeros_like(gb_ref)
            gg_ref[...] = jnp.zeros_like(gg_ref)
            gs_ref[...] = jnp.zeros_like(gs_ref)

    normed = normalize(x_s[...].astype(F32))
    mlp_in = (normed * gain[...] + shift[...]).astype(BF16)
    upstream = c_s[...]
    hidden = dot(mlp_in, w_up[...]) + b_up[...]
    cdf = 0.5 * (1.0 + lax.erf(hidden * (0.5**0.5)))
    act = (hidden * cdf).astype(BF16)
    slope = cdf + hidden * jnp.exp(-0.5 * hidden * hidden) * ((2.0 * math.pi) ** -0.5)
    mo_ref[...] = dot(act, w_down[...]).astype(BF16)
    grad_act = dot_nt(upstream, w_down[...])
    grad_hidden = slope * grad_act
    grad_low = grad_hidden.astype(BF16)
    gb_ref[...] += jnp.sum(grad_low.astype(F32), axis=0, keepdims=True)
    grad_norm = dot_nt(grad_low, w_up[...])
    gg_ref[...] += jnp.sum(grad_norm * normed, axis=0, keepdims=True)
    gs_ref[...] += jnp.sum(grad_norm, axis=0, keepdims=True)
    e_ref[...] = (grad_norm * gain[...]).astype(BF16)
    gv_ref[...] = dot_nt(upstream, w_out[...]).astype(BF16)
    up_s[...] += dot_tn(mlp_in, grad_low)
    down_s[...] += dot_tn(act, upstream)

    @pl.when(step == pl.num_programs(0) - 1)
    def _():
        gup_ref[...] = up_s[...].astype(gup_ref.dtype)
        gdown_ref[...] = down_s[...].astype(gdown_ref.dtype)


def feed_forward(pair, meta, xs, cs, gain, shift, w_up, b_up, w_down, w_out, before):
    seq = xs[0].shape[0]
    per = seq // TILE
    steps = 2 * per
    hid = FF // 4
    width = D // 4
    first = pl.BlockSpec((TILE, D), lambda i, m: (jnp.minimum(i, per - 1), 0))
    second = pl.BlockSpec((TILE, D), lambda i, m: (jnp.maximum(i - per, 0), 0))
    row = whole((1, D))
    specs = [
        first,
        second,
        first,
        second,
        row,
        row,
        pl.BlockSpec((D, hid), lambda i, m: (0, m[0])),
        pl.BlockSpec((1, hid), lambda i, m: (0, m[0])),
        pl.BlockSpec((hid, D), lambda i, m: (m[0], 0)),
        pl.BlockSpec((width, D), lambda i, m: (m[0], 0)),
    ]
    args = [*xs, *cs, gain, shift, w_up, b_up, w_down, w_out]
    aliases = {}
    grad_type = F32
    if before is not None:
        grad_type = BF16
        args += list(before[3:]) + list(before[:3])
        specs += [whole(a.shape) for a in before[3:]]
        specs += [pl.BlockSpec(memory_space=pl.ANY)] * 3
        aliases = {1 + len(args) - 3 + i: i for i in range(3)}
    base = pair * steps

    def rows(cols):
        return pl.BlockSpec((TILE, cols), lambda i, m: (i + base, 0))

    total = 4 * seq
    return pl.pallas_call(
        partial(mlp_kernel, before is not None),
        out_shape=[
            jax.ShapeDtypeStruct((total, D), BF16),
            jax.ShapeDtypeStruct((total, D), BF16),
            jax.ShapeDtypeStruct((total, width), BF16),
            jax.ShapeDtypeStruct((D, hid), grad_type),
            jax.ShapeDtypeStruct((hid, D), grad_type),
            jax.ShapeDtypeStruct((1, hid), F32),
            jax.ShapeDtypeStruct((1, D), F32),
            jax.ShapeDtypeStruct((1, D), F32),
        ],
        grid_spec=pltpu.PrefetchScalarGridSpec(
            num_scalar_prefetch=1,
            grid=(steps,),
            in_specs=specs,
            out_specs=[
                rows(D),
                rows(D),
                rows(width),
                whole((D, hid)),
                whole((hid, D)),
                whole((1, hid)),
                row,
                row,
            ],
            scratch_shapes=[
                pltpu.VMEM((TILE, D), BF16),
                pltpu.VMEM((TILE, D), BF16),
                pltpu.VMEM((D, hid), F32),
                pltpu.VMEM((hid, D), F32),
            ],
        ),
        input_output_aliases=aliases,
        compiler_params=params(),
        cost_estimate=pl.CostEstimate(
            flops=2 * 6 * 2 * seq * D * hid, bytes_accessed=20 * seq * D, transcendentals=0
        ),
        name=f"mlp_{pair}",
    )(meta, *args)


def head_masks():
    lane = lax.broadcasted_iota(jnp.int32, (1, LANES), 1)
    first = jnp.where(lane < HDIM, 1.0, 0.0).astype(BF16)
    second = jnp.where(lane < HDIM, 0.0, 1.0).astype(BF16)
    return first, second


def slot_rows(meta, per, tile):
    slot = jnp.bitwise_xor(tile // per, meta[0])
    return pl.multiple_of((slot * per + tile % per) * TILE, TILE), slot * per + tile % per


def by_head(first, second, block, third):
    return (block * first, block * second, third)


def attend_kernel(per, meta, lo, q_ref, k_ref, v_ref, start_ref, o_ref, lse_ref, vt_ref, acc):
    tiles = q_ref.shape[0] // TILE
    mask0, mask1 = head_masks()

    @pl.loop(0, tiles)
    def _(tile):
        rows = pl.ds(pl.multiple_of(tile * TILE, TILE), TILE)
        vt_ref[:, rows] = v_ref[rows, :].astype(F32).T.astype(BF16)

    key_iota = lax.broadcasted_iota(jnp.int32, (TILE, TILE), 0)
    query_iota = lax.broadcasted_iota(jnp.int32, (TILE, TILE), 1)

    @pl.loop(0, tiles)
    def _(qi):
        q_at, q_slot = slot_rows(meta, per, qi)
        q_rows = pl.ds(q_at, TILE)
        queries = by_head(mask0, mask1, q_ref[q_rows, 0:128], q_ref[q_rows, 128:192])
        starts = start_ref[q_slot]
        acc[...] = jnp.zeros_like(acc)

        def visit(ki, carry):
            k_at, _ = slot_rows(meta, per, ki)
            k_rows = pl.ds(k_at, TILE)
            pair, third = k_ref[k_rows, 0:128], k_ref[k_rows, 128:192]
            key_pos = key_iota + ki * TILE
            allowed = (key_pos >= starts) & (key_pos <= query_iota + qi * TILE)
            after = []
            for head in range(3):
                top, total = carry[head]
                scores = dot_nt(third if head == 2 else pair, queries[head])
                scores = jnp.where(allowed, scores, MASKED)
                new_top = jnp.maximum(top, jnp.max(scores, axis=0, keepdims=True))
                fade = jnp.exp(top - new_top)
                weights = jnp.exp(scores - new_top)
                total = total * fade + jnp.sum(weights, axis=0, keepdims=True)
                cols = pl.ds(head * HDIM, HDIM)
                acc[cols, :] = acc[cols, :] * fade + dot(vt_ref[cols, k_rows], weights.astype(BF16))
                after.append((new_top, total))
            return tuple(after)

        begin = (jnp.full((1, TILE), MASKED, F32), jnp.zeros((1, TILE), F32))
        stats = lax.fori_loop(lo[qi], qi + 1, visit, (begin,) * 3)
        for head, (top, total) in enumerate(stats):
            cols = pl.ds(head * HDIM, HDIM)
            acc[cols, :] = acc[cols, :] / total
            lse_ref[head, q_slot] = top + jnp.log(total)
        o_ref[q_rows, :] = acc[...].T.astype(BF16)


def attend(meta, lo, query, keys, values, starts, per):
    total, width = query.shape
    tiles = total // TILE
    args = [query, keys, values, starts]
    return pl.pallas_call(
        partial(attend_kernel, per),
        out_shape=[
            jax.ShapeDtypeStruct((total, width), BF16),
            jax.ShapeDtypeStruct((3, tiles, 1, TILE), F32),
        ],
        grid_spec=pltpu.PrefetchScalarGridSpec(
            num_scalar_prefetch=2,
            grid=(1,),
            in_specs=[whole(a.shape) for a in args],
            out_specs=[whole((total, width)), whole((3, tiles, 1, TILE))],
            scratch_shapes=[pltpu.VMEM((width, total), BF16), pltpu.VMEM((width, TILE), F32)],
        ),
        compiler_params=params(),
        cost_estimate=pl.CostEstimate(
            flops=60 * 4 * 256 * 256 * 256, bytes_accessed=8 * total * width, transcendentals=0
        ),
        name="attend",
    )(meta, lo, *args)


def attend_back_kernel(
    per, meta, lo, q_ref, k_ref, v_ref, o_ref, gv_ref, start_ref, lse_ref, low, high,
    gj_ref, kt_ref, dk_ref, dv_ref, dqt_ref,
):
    tiles = q_ref.shape[0] // TILE
    mask0, mask1 = head_masks()

    @pl.loop(0, tiles)
    def _(tile):
        rows = pl.ds(pl.multiple_of(tile * TILE, TILE), TILE)
        kt_ref[:, rows] = k_ref[rows, :].astype(F32).T.astype(BF16)

    dk_ref[...] = jnp.zeros_like(dk_ref)
    dv_ref[...] = jnp.zeros_like(dv_ref)
    key_iota = lax.broadcasted_iota(jnp.int32, (TILE, TILE), 0)
    query_iota = lax.broadcasted_iota(jnp.int32, (TILE, TILE), 1)

    @pl.loop(0, tiles)
    def _(turn):
        qi = tiles - 1 - turn
        q_at, q_slot = slot_rows(meta, per, qi)
        q_rows = pl.ds(q_at, TILE)
        queries = by_head(mask0, mask1, q_ref[q_rows, 0:128], q_ref[q_rows, 128:192])
        grads = by_head(mask0, mask1, gv_ref[q_rows, 0:128], gv_ref[q_rows, 128:192])
        starts = start_ref[q_slot]
        lses = [lse_ref[head, q_slot] for head in range(3)]
        product = (gv_ref[q_rows, :].astype(F32) * o_ref[q_rows, :].astype(F32)).T
        deltas = [
            jnp.sum(product[head * HDIM : (head + 1) * HDIM], axis=0, keepdims=True)
            for head in range(3)
        ]
        dqt_ref[...] = jnp.zeros_like(dqt_ref)

        @pl.loop(lo[qi], qi + 1)
        def _(ki):
            k_at, _ = slot_rows(meta, per, ki)
            k_rows = pl.ds(k_at, TILE)
            pair, third = k_ref[k_rows, 0:128], k_ref[k_rows, 128:192]
            v_pair, v_third = v_ref[k_rows, 0:128], v_ref[k_rows, 128:192]
            key_pos = key_iota + ki * TILE
            allowed = (key_pos >= starts) & (key_pos <= query_iota + qi * TILE)
            dk, dv = [], []
            for head in range(3):
                scores = dot_nt(third if head == 2 else pair, queries[head])
                probs = jnp.exp(jnp.where(allowed, scores - lses[head], MASKED))
                grad_probs = dot_nt(v_third if head == 2 else v_pair, grads[head])
                grad_scores = (probs * (grad_probs - deltas[head])).astype(BF16)
                dv.append(dot(probs.astype(BF16), grads[head]))
                dk.append(dot(grad_scores, queries[head]))
                cols = pl.ds(head * HDIM, HDIM)
                dqt_ref[cols, :] += dot(kt_ref[cols, k_rows], grad_scores)
            dk_ref[k_rows, 0:128] += dk[0] + dk[1]
            dk_ref[k_rows, 128:192] += dk[2]
            dv_ref[k_rows, 0:128] += dv[0] + dv[1]
            dv_ref[k_rows, 128:192] += dv[2]

        cos, sin = rotation(low, high, qi)

        def turn_back(block):
            return (block * cos - swap_halves(block) * sin).astype(BF16)

        dq = dqt_ref[...].T * (HDIM**-0.5)
        gj_ref[q_rows, 0:128] = turn_back(dq[:, 0:128])
        mixed = jnp.concatenate([dq[:, 128:192], dk_ref[q_rows, 128:192]], axis=1)
        gj_ref[q_rows, 128:256] = turn_back(dk_ref[q_rows, 0:128])
        gj_ref[q_rows, 256:384] = turn_back(mixed)
        gj_ref[q_rows, 384:576] = dv_ref[q_rows, :].astype(BF16)


def attend_back(meta, lo, query, keys, values, attn, grad_vec, starts, lse, low, high, per):
    total, width = query.shape
    args = [query, keys, values, attn, grad_vec, starts, lse, low, high]
    return pl.pallas_call(
        partial(attend_back_kernel, per),
        out_shape=jax.ShapeDtypeStruct((total, 3 * width), BF16),
        grid_spec=pltpu.PrefetchScalarGridSpec(
            num_scalar_prefetch=2,
            grid=(1,),
            in_specs=[whole(a.shape) for a in args],
            out_specs=whole((total, 3 * width)),
            scratch_shapes=[
                pltpu.VMEM((width, total), BF16),
                pltpu.VMEM((total, width), F32),
                pltpu.VMEM((total, width), F32),
                pltpu.VMEM((width, TILE), F32),
            ],
        ),
        compiler_params=params(),
        cost_estimate=pl.CostEstimate(
            flops=60 * 10 * 256 * 256 * 256, bytes_accessed=16 * total * width, transcendentals=0
        ),
        name="attend_back",
    )(meta, lo, *args)


def pick(refs, into, per):
    step = pl.program_id(0)
    for slot, ref in enumerate(refs):

        @pl.when(step // per == slot)
        def _(ref=ref):
            into[...] = ref[...]


def slot_specs(per, cols):
    def spec(slot):
        return pl.BlockSpec(
            (TILE, cols), lambda i, m: (jnp.clip(i - slot * per, 0, per - 1), 0)
        )

    return [spec(slot) for slot in range(4)]


def output_kernel(per, meta, o_ref, mo_ref, c0, c1, c2, c3, w_ref, out_ref, gw_ref, c_s, gw_s):
    step = pl.program_id(0)
    pick((c0, c1, c2, c3), c_s, per)

    @pl.when(step == 0)
    def _():
        gw_s[...] = jnp.zeros_like(gw_s)

    attn = o_ref[...]
    out_ref[...] = (dot(attn, w_ref[...]) + mo_ref[...].astype(F32)).astype(BF16)
    gw_s[...] += dot_tn(attn, c_s[...])

    @pl.when(step == pl.num_programs(0) - 1)
    def _():
        gw_ref[...] = gw_s[...].astype(BF16)


def output(meta, attn, mlp, cots, w_out):
    total, width = attn.shape
    per = cots[0].shape[0] // TILE
    return pl.pallas_call(
        partial(output_kernel, per),
        out_shape=[
            jax.ShapeDtypeStruct((total, D), BF16),
            jax.ShapeDtypeStruct((width, D), BF16),
        ],
        grid_spec=pltpu.PrefetchScalarGridSpec(
            num_scalar_prefetch=1,
            grid=(4 * per,),
            in_specs=[
                pl.BlockSpec((TILE, width), lambda i, m: (i, 0)),
                pl.BlockSpec((TILE, D), lambda i, m: (i, 0)),
                *slot_specs(per, D),
                pl.BlockSpec((width, D), lambda i, m: (m[0], 0)),
            ],
            out_specs=[pl.BlockSpec((TILE, D), lambda i, m: (i, 0)), whole((width, D))],
            scratch_shapes=[pltpu.VMEM((TILE, D), BF16), pltpu.VMEM((width, D), F32)],
        ),
        compiler_params=params(),
        cost_estimate=pl.CostEstimate(
            flops=4 * total * width * D, bytes_accessed=6 * total * D, transcendentals=0
        ),
        name="output",
    )(meta, attn, mlp, *cots, w_out)


def joined_kernel(
    per, meta, gj_ref, e_in, t0, t1, t2, t3, gain, shift, w_ref,
    e_ref, gw_ref, gb_ref, gg_ref, gs_ref, x_s, gw_s,
):
    step = pl.program_id(0)
    pick((t0, t1, t2, t3), x_s, per)

    @pl.when(step == 0)
    def _():
        gw_s[...] = jnp.zeros_like(gw_s)
        gb_ref[...] = jnp.zeros_like(gb_ref)
        gg_ref[...] = jnp.zeros_like(gg_ref)
        gs_ref[...] = jnp.zeros_like(gs_ref)

    normed = normalize(x_s[...].astype(F32))
    attn_in = (normed * gain[...] + shift[...]).astype(BF16)
    grad = gj_ref[...]
    grad_norm = dot_nt(grad, w_ref[...])
    e_ref[...] = (grad_norm * gain[...] + e_in[...].astype(F32)).astype(BF16)
    gg_ref[...] += jnp.sum(grad_norm * normed, axis=0, keepdims=True)
    gs_ref[...] += jnp.sum(grad_norm, axis=0, keepdims=True)
    gb_ref[...] += jnp.sum(grad.astype(F32), axis=0, keepdims=True)
    gw_s[...] += dot_tn(attn_in, grad)

    @pl.when(step == pl.num_programs(0) - 1)
    def _():
        gw_ref[...] = gw_s[...].astype(BF16)


def joined_back(meta, grad, e_mlp, toks, gain, shift, w):
    total, width = grad.shape
    per = toks[0].shape[0] // TILE
    row = whole((1, D))
    return pl.pallas_call(
        partial(joined_kernel, per),
        out_shape=[
            jax.ShapeDtypeStruct((total, D), BF16),
            jax.ShapeDtypeStruct((D, width), BF16),
            jax.ShapeDtypeStruct((1, width), F32),
            jax.ShapeDtypeStruct((1, D), F32),
            jax.ShapeDtypeStruct((1, D), F32),
        ],
        grid_spec=pltpu.PrefetchScalarGridSpec(
            num_scalar_prefetch=1,
            grid=(4 * per,),
            in_specs=[
                pl.BlockSpec((TILE, width), lambda i, m: (i, 0)),
                pl.BlockSpec((TILE, D), lambda i, m: (i, 0)),
                *slot_specs(per, D),
                row,
                row,
                whole((D, width)),
            ],
            out_specs=[
                pl.BlockSpec((TILE, D), lambda i, m: (i, 0)),
                whole((D, width)),
                whole((1, width)),
                row,
                row,
            ],
            scratch_shapes=[pltpu.VMEM((TILE, D), BF16), pltpu.VMEM((D, width), F32)],
        ),
        compiler_params=params(),
        cost_estimate=pl.CostEstimate(
            flops=4 * total * width * D, bytes_accessed=8 * total * D, transcendentals=0
        ),
        name="joined_back",
    )(meta, grad, e_mlp, *toks, gain, shift, w)


def swap(value, axis, mask):
    size = lax.axis_size(axis)
    return lax.ppermute(value, axis, [(i, i ^ mask) for i in range(size)])


def reduce_rows(value):
    index = lax.axis_index("rows")
    mask = 1
    while value.shape[0] > 1:
        bit = (index // mask) % 2
        value = value.reshape(value.shape[0] // 2, 2, *value.shape[1:])
        mine = lax.dynamic_index_in_dim(value, bit, 1, keepdims=False)
        other = lax.dynamic_index_in_dim(value, 1 - bit, 1, keepdims=False)
        got = swap(other, "rows", mask)
        value = mine.astype(F32) + got.astype(F32)
        mask *= 2
        if value.shape[0] > 1:
            value = value.astype(BF16)
    return value[0]


def spread_rows(chunk, col_width):
    rows, blk = lax.axis_size("rows"), lax.axis_size("blk")
    r, b = lax.axis_index("rows"), lax.axis_index("blk")
    pieces = chunk.reshape(chunk.shape[0], blk, col_width)
    got = []
    for turn in range(blk):
        moves = []
        for rr in range(rows):
            for bb in range(blk):
                moves.append((rr * blk + bb, (rows * bb + rr) // blk * blk + ((rr % blk) ^ turn)))
        piece = lax.dynamic_index_in_dim(pieces, (r % blk) ^ turn, 1, keepdims=False)
        got.append(lax.ppermute(piece, ("rows", "blk"), moves))
    got = jnp.stack(got)
    return [lax.dynamic_index_in_dim(got, b ^ part, 0, keepdims=False) for part in range(blk)]


def spread_columns(chunk):
    blk = lax.axis_size("blk")
    b = lax.axis_index("blk")
    parts = jnp.stack(
        [
            jnp.concatenate([chunk[:, 0:128], chunk[:, 256:320]], axis=1),
            jnp.concatenate([chunk[:, 128:256], chunk[:, 320:384]], axis=1),
            chunk[:, 384:576],
        ]
    )
    got = []
    for turn in range(3):
        moves = [((3 * to + turn) % blk, to) for to in range(blk)]
        to = (3 * (b - turn)) % blk
        piece = lax.dynamic_index_in_dim(parts, (3 * to + turn) // blk, 0, keepdims=False)
        got.append(lax.ppermute(piece, "blk", moves))
    return jnp.concatenate(got, axis=1)


def gather_slots(own, after=None):
    near = swap(own, "blk", 1)
    if after is not None:
        own = lax.optimization_barrier((own, after))[0]
    far = swap(own, "blk", 2)
    return [own, near, far, swap(far, "blk", 1)]


def scatter_slots(parts):
    near = swap(parts[1], "blk", 1)
    far = swap(parts[3], "blk", 1)
    send = (parts[2].astype(F32) + far.astype(F32)).astype(BF16)
    across = swap(send, "blk", 2)
    return parts[0].astype(F32) + near.astype(F32) + across.astype(F32)


def local(
    tokens, seg_ids, valid_len, ln1_gain, ln1_bias, w_qkv, b_qkv, w_out, b_out,
    ln2_gain, ln2_bias, w_up, b_up, w_down, b_down, cotangent,
):
    rows = lax.axis_size("rows")
    blk = lax.axis_index("blk")
    seq = tokens.shape[1]
    per = seq // TILE
    width = D // 4
    meta = blk.astype(jnp.int32).reshape(1)
    low, high = angle_parts(4 * seq)

    tok = gather_slots(tokens[0])
    cot = gather_slots(cotangent[0], tok[2])
    seg = [seg_ids[0]] + [swap(seg_ids[0], "blk", mask) for mask in (1, 2, 3)]

    def own_columns(array, at, size):
        return lax.dynamic_slice_in_dim(array, at + width * blk, size, axis=-1)

    def own_joined(array):
        order = ((0, 128), (D, 128), (128, 64), (D + 128, 64), (2 * D, 192))
        return jnp.concatenate([own_columns(array, at, size) for at, size in order], axis=-1)

    w_own = own_joined(w_qkv)
    b_own = own_joined(b_qkv)[None]
    gain1, shift1, gain2, shift2 = (v[None] for v in (ln1_gain, ln1_bias, ln2_gain, ln2_bias))

    seg_all = jnp.stack(seg)
    pos = (jnp.arange(4, dtype=jnp.int32) ^ blk)[:, None] * seq + jnp.arange(seq, dtype=jnp.int32)
    starts = jnp.zeros_like(seg_all)
    for number in (1, 2, 3):
        starts = jnp.where(seg_all == number, jnp.sum(seg_all < number), starts)
    starts = jnp.where(pos < valid_len[0], starts, pos).astype(jnp.int32)
    starts = starts.reshape(4 * per, 1, TILE)
    tile_at = jnp.arange(4 * per, dtype=jnp.int32)
    tile_slot = (tile_at // per ^ blk) * per + tile_at % per
    lo = starts[:, 0, 0][tile_slot] // TILE

    joined = None
    for slot in range(4):
        joined = project(slot, meta, tok[slot], gain1, shift1, w_own, b_own, low, high, joined)
    query, keys, values = joined

    mlp_args = (gain2, shift2, w_up, b_up[None], w_down, w_out)
    first = feed_forward(0, meta, tok[:2], cot[:2], *mlp_args, None)
    attn, lse = attend(meta, lo, query, keys, values, starts, per)
    second = feed_forward(1, meta, tok[2:], cot[2:], *mlp_args, first)
    mlp_part, e_mlp, grad_vec, gw_up, gw_down, gb_up, g_ln2, s_ln2 = second

    out_part, gw_out = output(meta, attn, mlp_part, cot, w_out)
    grad_joined = attend_back(
        meta, lo, query, keys, values, attn, grad_vec, starts, lse, low, high, per
    )
    e_part, gw_qkv, gb_joined, g_ln1, s_ln1 = joined_back(
        meta, grad_joined, e_mlp, tok, gain1, shift1, w_own
    )

    summed = scatter_slots(out_part.reshape(4, seq, D))
    result = (tokens[0].astype(F32) + (b_out + b_down) + summed).astype(BF16)[None]

    hid = FF // 4
    up = reduce_rows(gw_up.reshape(rows, D // rows, hid))
    lower = jnp.concatenate(
        [gw_down.reshape(rows, hid // rows, D), gw_out.reshape(rows, width // rows, D)], axis=1
    )
    lower = spread_rows(reduce_rows(lower).astype(BF16), width)
    cut = hid // rows
    down = jnp.concatenate([part[:cut] for part in lower]).astype(F32)
    out_w = jnp.concatenate([part[cut:] for part in lower]).astype(F32)
    qkv = spread_columns(reduce_rows(gw_qkv.reshape(rows, D // rows, 3 * width)).astype(BF16))

    e_sum = scatter_slots(e_part.reshape(4, seq, D))
    wide = tokens[0].astype(F32)
    center = wide - jnp.mean(wide, axis=-1, keepdims=True)
    rate = lax.rsqrt(jnp.mean(center * center, axis=-1, keepdims=True) + EPS)
    normed = center * rate
    back = rate * (
        e_sum
        - jnp.mean(e_sum, axis=-1, keepdims=True)
        - normed * jnp.mean(e_sum * normed, axis=-1, keepdims=True)
    )
    up_wide = cotangent[0].astype(F32)
    grad_tokens = (up_wide + back).astype(BF16)[None]

    gb = gb_joined[0]
    own_b = (
        jnp.concatenate([gb[0:128], gb[256:320]]),
        jnp.concatenate([gb[128:256], gb[320:384]]),
        gb[384:576],
    )
    gb_qkv = jnp.zeros((3 * D,), F32)
    for part, piece in enumerate(own_b):
        gb_qkv = lax.dynamic_update_slice(gb_qkv, piece, (part * D + width * blk,))
    gb_up_all = lax.dynamic_update_slice(jnp.zeros((FF,), F32), gb_up[0], (hid * blk,))
    small = lax.psum(
        (
            gb_qkv,
            jnp.sum(up_wide, axis=0),
            gb_up_all,
            g_ln1[0],
            s_ln1[0],
            g_ln2[0],
            s_ln2[0],
        ),
        ("rows", "blk"),
    )
    return (
        result,
        grad_tokens,
        qkv.astype(F32),
        out_w,
        up,
        down,
        small[0],
        small[1],
        small[2],
        small[1],
        small[3],
        small[4],
        small[5],
        small[6],
    )


def solution(mesh):
    split = P("rows", "blk")
    in_specs = (
        P("rows", "blk", None),
        split,
        P("rows"),
        *(P(),) * 12,
        P("rows", "blk", None),
    )
    out_specs = (
        P("rows", "blk", None),
        P("rows", "blk", None),
        *(split,) * 4,
        *(P(),) * 8,
    )
    return jax.shard_map(local, mesh=mesh, in_specs=in_specs, out_specs=out_specs, check_vma=False)
```

time: 943 us -> 350 us (0.37)
  waiting for transfers between devices: 605 us -> 71.7 us
  Pallas kernels: 0 us -> 126 us
  matrix products: 119 us -> 0 us
  local copies, waits for them, and re-layouts: 99 us -> 31.2 us
  starting transfers between devices: 1.09 us -> 44.7 us
  other arithmetic: 48 us -> 30.3 us
  between operations: 15 us -> 1.91 us
    reduce_scatter x6 -> x0, waiting for transfers between devices: 561 us -> none  [the longest x1 149 us: local(): lax.psum_scatter(weight_grads[2], 'rows', scatter_dimension=0, tiled=True)]
    pallas_call x0 -> x10, Pallas kernels: none -> 126 us  [the longest x2 32.5 us: feed_forward(): pl.pallas_call(partial(mlp_kernel, before is not None), out_shape=[jax.Sh...]
    dot_general x19 -> x0, matrix products: 119 us -> none  [the longest x4 28.3 us: times_transpose(): lax.dot_general(left, right, (((1,), (1,)), ((), ())), preferred_element_...]
    ppermute x0 -> x31, waiting for transfers between devices: none -> 71.7 us  [the longest x24 71.6 us: swap(): return lax.ppermute(value, axis, [(i, i ^ mask) for i in range(size)])]
    ppermute x0 -> x31, starting transfers between devices: none -> 44.7 us  [the longest x24 24.9 us: swap(): return lax.ppermute(value, axis, [(i, i ^ mask) for i in range(size)])]
    unnamed x14 -> x0, waiting for transfers between devices: 31.1 us -> none
    unnamed x72 -> x78, local copies, waits for them, and re-layouts: 31.5 us -> 4.21 us
    reshape x4 -> x0, local copies, waits for them, and re-layouts: 18.8 us -> none  [the longest x1 6.38 us: local(): value_blocks = all_values.reshape(num_blocks, seq_len, HEADS, HDIM)]
  transfers between devices with their start and end apart: 11 -> 31, of which waited for: 8 -> 10; matrix products, arithmetic and copies ran while one was open for 22% -> 14% of each run, Pallas kernels for 0% -> 16%
where the time goes in v1:
time: 350 us; the launch traced here: 349 us
  Pallas kernels  126 us (36%)
  waiting for transfers between devices  71.7 us (20%)
  starting transfers between devices  44.7 us (13%)
  blocking collectives  42.9 us (12%)
  local copies, waits for them, and re-layouts  31.2 us (9%)
  other arithmetic  30.3 us (9%)
    ppermute x24, waiting for transfers between devices, swap(): return lax.ppermute(value, axis, [(i, i ^ mask) for i in range(size)])  71.6 us
    psum x1, blocking collectives, local(): lax.psum((gb_qkv, jnp.sum(up_wide, axis=0), gb_up_all, g_ln1[0], s_ln1[0]...  42.9 us
    pallas_call x2, Pallas kernels, feed_forward(): pl.pallas_call(partial(mlp_kernel, before is not None), out_shape=[jax.Sh...  32.5 us
    pallas_call x1, Pallas kernels, attend_back(): pl.pallas_call(partial(attend_back_kernel, per), out_shape=jax.ShapeDtype...  31 us
    pallas_call x1, Pallas kernels, attend(): pl.pallas_call(partial(attend_kernel, per), out_shape=[jax.ShapeDtypeStru...  27.2 us
    ppermute x24, starting transfers between devices, swap(): return lax.ppermute(value, axis, [(i, i ^ mask) for i in range(size)])  24.9 us
    pallas_call x4, Pallas kernels, project(): pl.pallas_call(partial(qkv_kernel, slot), out_shape=[out] * 3, grid_spec=...  14.2 us
    ppermute x4, starting transfers between devices, spread_rows(): got.append(lax.ppermute(piece, ('rows', 'blk'), moves))  12.8 us
  transfers between devices with their start and end apart: 31, of which 10 were waited for; matrix products, arithmetic and copies ran while one was open for 14% of the time, Pallas kernels for 16%

profile of v1, /device:TPU:0, one launch (start us, length us, event | category | flops | bytes accessed | tf_op | source)
XLA Modules:
  0.0 349.0 jit_solution(2836947755705233350)
XLA Ops:
  1.2 2.6 collective-permute-start.3
  20.1 2.1 collective-permute-done.3.x_ref.refs_0_.t2
  24.0 3.6 %qkv_0.1 = (bf16[2048,192]{1,0:T(8,128)(2,1)}, bf16[2048,192]{1,0:T(8,128)(2,1)}, bf16[2048,192]{1,0:T(8,128)(2,1)}) custom-call(s32[1]{0:T(128)} %bitcast.1.meta, bf16[512,768]{1,0:T(8,128)(2,1)} %bitcast.122, f32[1,768]{1,0:T(1,128)} %broadcast_in_dim.55.gain, f32[1,768]{1,0:T(1,128)} %broadcast_in_dim.56.shift, bf16[768,576]{1,0:T(8,128)(2,1)} %concatenate.35.w_ref, ...), custom_call_target="tpu_custom_call" | custom-call | flops 452984832 | bytes 1572864 | tf_op jit(solution)/shard_map/qkv_0/pallas_call | solution.py:126
  30.3 10.3 %collective-permute-done.2 = s32[512]{0:T(512)S(1)} collective-permute-done((s32[512]{0:T(512)S(1)}, s32[512]{0:T(512)S(1)}, u32[]{:S(2)}, u32[]{:S(2)}) %collective-permute-start.2) | collective-permute-done | bytes 2080 | tf_op jit(solution)/shard_map/ppermute | solution.py:602
  42.0 2.6 select_select_fusion
  47.3 3.5 %qkv_1.1 = (bf16[2048,192]{1,0:T(8,128)(2,1)}, bf16[2048,192]{1,0:T(8,128)(2,1)}, bf16[2048,192]{1,0:T(8,128)(2,1)}) custom-call(s32[1]{0:T(128)} %bitcast.1.meta, bf16[512,768]{1,0:T(8,128)(2,1)} %collective-permute-done.5.x_ref.refs_1_.t1, f32[1,768]{1,0:T(1,128)} %broadcast_in_dim.55.gain, ...), custom_call_target="tpu_custom_call", output_to_operand_aliasing={{0}: (8, {}), {1}: (9, {}), {2}: (10, {})} | custom-call | flops 452984832 | bytes 1572864 | tf_op jit(solution)/shard_map/qkv_1/pallas_call | solution.py:126
  50.8 3.5 %qkv_2.1 = (bf16[2048,192]{1,0:T(8,128)(2,1)}, bf16[2048,192]{1,0:T(8,128)(2,1)}, bf16[2048,192]{1,0:T(8,128)(2,1)}) custom-call(s32[1]{0:T(128)} %bitcast.1.meta, bf16[512,768]{1,0:T(8,128)(2,1)} %collective-permute-done.3.x_ref.refs_0_.t2, f32[1,768]{1,0:T(1,128)} %broadcast_in_dim.55.gain, ...), custom_call_target="tpu_custom_call", output_to_operand_aliasing={{0}: (8, {}), {1}: (9, {}), {2}: (10, {})} | custom-call | flops 452984832 | bytes 1572864 | tf_op jit(solution)/shard_map/qkv_2/pallas_call | solution.py:126
  55.5 15.8 %mlp_0.1 = (bf16[2048,768]{1,0:T(8,128)(2,1)}, bf16[2048,768]{1,0:T(8,128)(2,1)}, bf16[2048,192]{1,0:T(8,128)(2,1)}, f32[768,768]{1,0:T(8,128)}, f32[768,768]{1,...) custom-call(s32[1]{0:T(128)} %bitcast.1.meta, bf16[512,768]{1,0:T(8,128)(2,1)} %bitcast.123, ...), custom_call_target="tpu_custom_call" | custom-call | flops 7247757312 | bytes 7864320 | tf_op jit(solution)/shard_map/mlp_0/pallas_call | solution.py:239
  72.2 3.5 %qkv_3.1 = (bf16[2048,192]{1,0:T(8,128)(2,1)}, bf16[2048,192]{1,0:T(8,128)(2,1)}, bf16[2048,192]{1,0:T(8,128)(2,1)}) custom-call(s32[1]{0:T(128)} %bitcast.1.meta, bf16[512,768]{1,0:T(8,128)(2,1)} %copy-done.14, f32[1,768]{1,0:T(1,128)} %broadcast_in_dim.55.gain, ...), custom_call_target="tpu_custom_call", output_to_operand_aliasing={{0}: (8, {}), {1}: (9, {}), {2}: (10, {})} | custom-call | flops 452984832 | bytes 1572864 | tf_op jit(solution)/shard_map/qkv_3/pallas_call | solution.py:126
  75.7 27.2 %attend.1 = (bf16[2048,192]{1,0:T(8,128)(2,1)}, f32[3,8,1,256]{3,2,1,0:T(1,128)}) custom-call(s32[1]{0:T(128)} %bitcast.1.meta, s32[8]{0:T(128)} %and_select_fusion.lo, bf16[2048,192]{1,0:T(8,128)(2,1)} %get-tuple-element.61.q_ref, bf16[2048,192]{1,0:T(8,128)(2,1)} %get-tuple-element.62.k_ref, bf16[2048,192]{1,0:T(8,128)(2,1)} %get-tuple-element.63.v_ref, ...), custom_call_target="tpu_custom_call" | custom-call | flops 4026531840 | bytes 3145728 | tf_op jit(solution)/shard_map/attend/pallas_call | solution.py:350
  103.8 16.7 %mlp_1.1 = (bf16[2048,768]{1,0:T(8,128)(2,1)}, bf16[2048,768]{1,0:T(8,128)(2,1)}, bf16[2048,192]{1,0:T(8,128)(2,1)}, bf16[768,768]{1,0:T(8,128)(2,1)}, bf16[768,...) custom-call(s32[1]{0:T(128)} %bitcast.1.meta, ...), custom_call_target="tpu_custom_call", output_to_operand_aliasing={{0}: (16, {}), {1}: (17, {}), {2}: (18, {})} | custom-call | flops 7247757312 | bytes 7864320 | tf_op jit(solution)/shard_map/mlp_1/pallas_call | solution.py:239
  120.5 31.0 %attend_back.1.gj_ref = bf16[2048,576]{1,0:T(8,128)(2,1)} custom-call(s32[1]{0:T(128)} %bitcast.1.meta, s32[8]{0:T(128)} %and_select_fusion.lo, bf16[2048,192]{1,0:T(8,128)(2,1)} %get-tuple-element.61.q_ref, bf16[2048,192]{1,0:T(8,128)(2,1)} %get-tuple-element.62.k_ref, bf16[2048,192]{1,0:T(8,128)(2,1)} %get-tuple-element.63.v_ref, ...), custom_call_target="tpu_custom_call" | custom-call | flops 10066329600 | bytes 6291456 | tf_op jit(solution)/shard_map/attend_back/pallas_call | solution.py:443
  151.5 12.6 %joined_back.1 = (bf16[2048,768]{1,0:T(8,128)(2,1)}, bf16[768,576]{1,0:T(8,128)(2,1)}, f32[1,576]{1,0:T(1,128)}, f32[1,768]{1,0:T(1,128)}, f32[1,768]{1,0:T(1,128)}) custom-call(s32[1]{0:T(128)} %bitcast.1.meta, bf16[2048,576]{1,0:T(8,128)(2,1)} %attend_back.1.gj_ref, bf16[2048,768]{1,0:T(8,128)(2,1)} %get-tuple-element.78.e_in, bf16[512,768]{1,0:T(8,128)(2,1)} %bitcast.124, ...), custom_call_target="tpu_custom_call" | custom-call | flops 3623878656 | bytes 12582912 | tf_op jit(solution)/shard_map/joined_back/pallas_call | solution.py:563
  166.3 8.8 %output.1 = (bf16[2048,768]{1,0:T(8,128)(2,1)}, bf16[192,768]{1,0:T(8,128)(2,1)}) custom-call(s32[1]{0:T(128)} %bitcast.1.meta, bf16[2048,192]{1,0:T(8,128)(2,1)} %get-tuple-element.64.o_ref, bf16[2048,768]{1,0:T(8,128)(2,1)} %get-tuple-element.74.mo_ref, bf16[512,768]{1,0:T(8,128)(2,1)} %bitcast.129, bf16[512,768]{1,0:T(8,128)(2,1)} %copy-done.9, ...), custom_call_target="tpu_custom_call" | custom-call | flops 1207959552 | bytes 9437184 | tf_op jit(solution)/shard_map/output/pallas_call | solution.py:504
  175.1 2.8 fusion.30
  190.3 8.4 %collective-permute-done.15 = bf16[4,96,576]{2,1,0:T(8,128)(2,1)} collective-permute-done((bf16[4,96,576]{2,1,0:T(8,128)(2,1)}, bf16[4,96,576]{2,1,0:T(8,128)(2,1)}, u32[]{:S(2)}, u32[]{:S(2)}) %collective-permute-start.15) | collective-permute-done | bytes 442400 | tf_op jit(solution)/shard_map/ppermute | solution.py:602
  201.6 9.8 %collective-permute-done.28 = bf16[4,96,768]{2,1,0:T(8,128)(2,1)} collective-permute-done((bf16[4,96,768]{2,1,0:T(8,128)(2,1)}, bf16[4,96,768]{2,1,0:T(8,128)(2,1)}, u32[]{:S(2)}, u32[]{:S(2)}) %collective-permute-start.28) | collective-permute-done | bytes 589856 | tf_op jit(solution)/shard_map/ppermute | solution.py:602
  214.3 3.4 collective-permute-done.16
  219.4 6.9 %collective-permute-done.21 = bf16[4,120,768]{2,1,0:T(8,128)(2,1)S(1)} collective-permute-done((bf16[4,120,768]{2,1,0:T(8,128)(2,1)S(1)}, bf16[4,120,768]{2,1,0:T(8,128)(2,1)S(1)}, u32[]{:S(2)}, u32[]{:S(2)}) %collective-permute-start.21) | collective-permute-done | bytes 737312 | tf_op jit(solution)/shard_map/ppermute | solution.py:602
  226.5 7.8 %collective-permute-done.17 = bf16[1,96,576]{2,1,0:T(8,128)(2,1)S(1)} collective-permute-done((bf16[1,96,576]{2,1,0:T(8,128)(2,1)S(1)}, bf16[1,96,576]{2,1,0:T(8,128)(2,1)S(1)}, u32[]{:S(2)}, u32[]{:S(2)}) %collective-permute-start.17) | collective-permute-done | bytes 110624 | tf_op jit(solution)/shard_map/ppermute | solution.py:602
  237.2 2.5 add_convert_fusion.1
  239.8 2.2 add_convert_fusion
  242.4 4.8 %collective-permute-start.20 = (bf16[96,192]{1,0:T(8,128)(2,1)S(1)}, bf16[96,192]{1,0:T(8,128)(2,1)}, u32[]{:S(2)}, u32[]{:S(2)}) collective-permute-start(bf16[96,192]{1,0:T(8,128)(2,1)S(1)} %get-tuple-element.153), channel_id=1, source_target_pairs={{2,0},{1,1},{0,2},{3,3},{6,4},{5,5},{4,6},{7,7},{10,8},{9,9},{8,10... | collective-permute-start | bytes 110600 | tf_op jit(solution)/shard_map/ppermute | solution.py:652
  249.3 7.0 %collective-permute-done.23 = bf16[1,120,768]{2,1,0:T(8,128)(2,1)S(1)} collective-permute-done((bf16[1,120,768]{2,1,0:T(8,128)(2,1)S(1)}, bf16[1,120,768]{2,1,0:T(8,128)(2,1)S(1)}, u32[]{:S(2)}, u32[]{:S(2)}) %collective-permute-start.23) | collective-permute-done | bytes 184352 | tf_op jit(solution)/shard_map/ppermute | solution.py:602
  259.6 4.7 %collective-permute-start.25 = (bf16[120,192]{0,1:T(8,128)(2,1)S(1)}, bf16[120,192]{0,1:T(8,128)(2,1)S(1)}, u32[]{:S(2)}, u32[]{:S(2)}) collective-permute-start(bf16[120,192]{0,1:T(8,128)(2,1)S(1)} %get-tuple-element.151), channel_id=1, source_target_pairs={{0,1},{1,9},{2,17},{3,25},{4,0},{5,8},{6,16},{7,24},{8,3},{9,11},{... | collective-permute-start | bytes 138248 | tf_op jit(solution)/shard_map/ppermute | solution.py:632
  264.3 2.4 collective-permute-start.26
  266.7 4.9 %collective-permute-start.27 = (bf16[120,192]{0,1:T(8,128)(2,1)S(1)}, bf16[120,192]{0,1:T(8,128)(2,1)S(1)}, u32[]{:S(2)}, u32[]{:S(2)}) collective-permute-start(bf16[120,192]{0,1:T(8,128)(2,1)S(1)} %get-tuple-element.149), channel_id=1, source_target_pairs={{0,3},{1,11},{2,19},{3,27},{4,2},{5,10},{6,18},{7,26},{8,1},{9,9},... | collective-permute-start | bytes 138248 | tf_op jit(solution)/shard_map/ppermute | solution.py:632
  273.3 8.8 %collective-permute-start.9 = (bf16[512,768]{1,0:T(8,128)(2,1)S(1)}, bf16[512,768]{1,0:T(8,128)(2,1)}, u32[]{:S(2)}, u32[]{:S(2)}) collective-permute-start(bf16[512,768]{1,0:T(8,128)(2,1)S(1)} %copy-done.12), channel_id=1, source_target_pairs={{0,1},{1,0},{2,3},{3,2},{4,5},{5,4},{6,7},{7,6},{8,9},{9,8},{10,11... | collective-permute-start | bytes 2359304 | tf_op jit(solution)/shard_map/ppermute | solution.py:602
  284.0 2.1 fusion.23
  286.2 15.5 %collective-permute-done.11 = bf16[512,768]{1,0:T(8,128)(2,1)} collective-permute-done((bf16[512,768]{1,0:T(8,128)(2,1)S(1)}, bf16[512,768]{1,0:T(8,128)(2,1)}, u32[]{:S(2)}, u32[]{:S(2)}) %collective-permute-start.11) | collective-permute-done | bytes 786464 | tf_op jit(solution)/shard_map/ppermute | solution.py:602
  301.8 3.7 %convert_reduce_fusion.1 = (f32[768]{0:T(1024)S(1)}, bf16[1,512,768]{2,1,0:T(8,128)(2,1)}, bf16[1,512,768]{2,1,0:T(8,128)(2,1)}) fusion(bf16[1,512,768]{2,1,0:T(8,128)(2,1)S(1)} %copy-done.5, f32[512]{0:T(512)S(1)} %get-tuple-element.168, f32[512]{0:T(512)S(1)} %broadcast_multiply_fusion.2, bf16[1,512,768]{2,1,0:T(8,128)(2,1)S(1)} %copy-done.1, ...), kind=kLoop, calls=%fused_computation.4 | loop fusion | flops 9436416 | bytes 7878656 | tf_op jit(solution)/shard_map/reduce_sum | solution.py:769
  305.5 42.9 %all-reduce = (f32[2304]{0:T(1024)}, f32[768]{0:T(1024)S(1)}, f32[3072]{0:T(1024)}, f32[768]{0:T(1024)}, f32[768]{0:T(1024)}, /*index=5*/f32[768]{0:T(1024)}, f32[768]{0:T(1024)}) all-reduce(f32[2304]{0:T(1024)S(1)} %dynamic_update_slice.14, f32[768]{0:T(1024)S(1)} %get-tuple-element.137, ...), channel_id=1, replica_groups=mesh['rows'=8,'blk'=4] {'rows','blk'}, use_global_device_ids=true, to_apply=%region_7.8 | all-reduce | flops 9216 | bytes 73728 | tf_op jit(solution)/shard_map/psum | solution.py:766
  (205 shorter events, 62.6 us)
Async XLA Ops:
  0.6 46.7 %collective-permute-start.5 = (bf16[512,768]{1,0:T(8,128)(2,1)}, bf16[512,768]{1,0:T(8,128)(2,1)}, u32[]{:S(2)}, u32[]{:S(2)}) collective-permute-start(bf16[512,768]{1,0:T(8,128)(2,1)} %bitcast.120), channel_id=1, source_target_pairs={{0,1},{1,0},{2,3},{3,2},{4,5},{5,4},{6,7},{7,6},{8,9},{9,8},{10,11... | collective-permute-start | bytes 2359304 | tf_op jit(solution)/shard_map/ppermute | solution.py:602
  1.2 21.0 %collective-permute-start.3 = (bf16[512,768]{1,0:T(8,128)(2,1)}, bf16[512,768]{1,0:T(8,128)(2,1)}, u32[]{:S(2)}, u32[]{:S(2)}) collective-permute-start(bf16[512,768]{1,0:T(8,128)(2,1)} %bitcast.121), channel_id=1, source_target_pairs={{0,2},{1,3},{2,0},{3,1},{4,6},{5,7},{6,4},{7,5},{8,10},{9,11},{10,... | collective-permute-start | bytes 2359304 | tf_op jit(solution)/shard_map/ppermute | solution.py:602
  3.7 23.8 %collective-permute-start = (s32[512]{0:T(512)}, s32[512]{0:T(512)}, u32[]{:S(2)}, u32[]{:S(2)}) collective-permute-start(s32[512]{0:T(512)} %bitcast.148), channel_id=1, source_target_pairs={{0,1},{1,0},{2,3},{3,2},{4,5},{5,4},{6,7},{7,6},{8,9},{9,8},{10,11... | collective-permute-start | bytes 6152 | tf_op jit(solution)/shard_map/ppermute | solution.py:602
  3.9 26.4 %collective-permute-start.1 = (s32[512]{0:T(512)}, s32[512]{0:T(512)}, u32[]{:S(2)}, u32[]{:S(2)}) collective-permute-start(s32[512]{0:T(512)} %bitcast.149), channel_id=1, source_target_pairs={{0,2},{1,3},{2,0},{3,1},{4,6},{5,7},{6,4},{7,5},{8,10},{9,11},{10,... | collective-permute-start | bytes 6152 | tf_op jit(solution)/shard_map/ppermute | solution.py:602
  4.2 50.3 %collective-permute-start.8 = (bf16[512,768]{1,0:T(8,128)(2,1)}, bf16[512,768]{1,0:T(8,128)(2,1)S(1)}, u32[]{:S(2)}, u32[]{:S(2)}) collective-permute-start(bf16[512,768]{1,0:T(8,128)(2,1)} %bitcast.127), channel_id=1, source_target_pairs={{0,1},{1,0},{2,3},{3,2},{4,5},{5,4},{6,7},{7,6},{8,9},{9,8},{10,11... | collective-permute-start | bytes 2359304 | tf_op jit(solution)/shard_map/ppermute | solution.py:602
  22.2 32.2 %collective-permute-start.6 = (bf16[512,768]{1,0:T(8,128)(2,1)S(1)}, bf16[512,768]{1,0:T(8,128)(2,1)S(1)}, u32[]{:S(2)}, u32[]{:S(2)}) collective-permute-start(bf16[512,768]{1,0:T(8,128)(2,1)S(1)} %bitcast.130), channel_id=1, source_target_pairs={{0,2},{1,3},{2,0},{3,1},{4,6},{5,7},{6,4},{7,5},{8,10},{9,11},{10,... | collective-permute-start | bytes 2359304 | tf_op jit(solution)/shard_map/ppermute | solution.py:602
  27.6 13.0 %collective-permute-start.2 = (s32[512]{0:T(512)S(1)}, s32[512]{0:T(512)S(1)}, u32[]{:S(2)}, u32[]{:S(2)}) collective-permute-start(s32[512]{0:T(512)S(1)} %bitcast.150), channel_id=1, source_target_pairs={{0,3},{1,2},{2,1},{3,0},{4,7},{5,6},{6,5},{7,4},{8,11},{9,10},{10,... | collective-permute-start | bytes 6152 | tf_op jit(solution)/shard_map/ppermute | solution.py:602
  45.7 25.6 %collective-permute-start.4 = (bf16[512,768]{1,0:T(8,128)(2,1)}, bf16[512,768]{1,0:T(8,128)(2,1)S(1)}, u32[]{:S(2)}, u32[]{:S(2)}) collective-permute-start(bf16[512,768]{1,0:T(8,128)(2,1)} %collective-permute-done.3.x_ref.refs_0_.t2), channel_id=1, source_target_pairs={{0,1},{1,0},{2,3},{3,2},{4,5},{5,4},{6,7},{7,6},{8,9},{9,8},{10,11... | collective-permute-start | bytes 2359304 | tf_op jit(solution)/shard_map/ppermute | solution.py:602
  54.4 48.5 %collective-permute-start.7 = (bf16[512,768]{1,0:T(8,128)(2,1)S(1)}, bf16[512,768]{1,0:T(8,128)(2,1)S(1)}, u32[]{:S(2)}, u32[]{:S(2)}) collective-permute-start(bf16[512,768]{1,0:T(8,128)(2,1)S(1)} %collective-permute-done.6.refs_2_.c2), channel_id=1, source_target_pairs={{0,1},{1,0},{2,3},{3,2},{4,5},{5,4},{6,7},{7,6},{8,9},{9,8},{10,11... | collective-permute-start | bytes 2359304 | tf_op jit(solution)/shard_map/ppermute | solution.py:602
  177.8 57.3 %collective-permute-start.10 = (bf16[512,768]{1,0:T(8,128)(2,1)}, bf16[512,768]{1,0:T(8,128)(2,1)}, u32[]{:S(2)}, u32[]{:S(2)}) collective-permute-start(bf16[512,768]{1,0:T(8,128)(2,1)} %get-tuple-element.136), channel_id=1, source_target_pairs={{0,1},{1,0},{2,3},{3,2},{4,5},{5,4},{6,7},{7,6},{8,9},{9,8},{10,11... | collective-permute-start | bytes 2359304 | tf_op jit(solution)/shard_map/ppermute | solution.py:602
  179.5 60.2 %collective-permute-start.13 = (bf16[512,768]{1,0:T(8,128)(2,1)}, bf16[512,768]{1,0:T(8,128)(2,1)}, u32[]{:S(2)}, u32[]{:S(2)}) collective-permute-start(bf16[512,768]{1,0:T(8,128)(2,1)} %get-tuple-element.134), channel_id=1, source_target_pairs={{0,1},{1,0},{2,3},{3,2},{4,5},{5,4},{6,7},{7,6},{8,9},{9,8},{10,11... | collective-permute-start | bytes 2359304 | tf_op jit(solution)/shard_map/ppermute | solution.py:602
  179.6 104.4 %collective-permute-start.12 = (bf16[512,768]{1,0:T(8,128)(2,1)}, bf16[512,768]{1,0:T(8,128)(2,1)}, u32[]{:S(2)}, u32[]{:S(2)}) collective-permute-start(bf16[512,768]{1,0:T(8,128)(2,1)} %get-tuple-element.133), channel_id=1, source_target_pairs={{0,1},{1,0},{2,3},{3,2},{4,5},{5,4},{6,7},{7,6},{8,9},{9,8},{10,11... | collective-permute-start | bytes 2359304 | tf_op jit(solution)/shard_map/ppermute | solution.py:602
  184.4 14.4 %collective-permute-start.15 = (bf16[4,96,576]{2,1,0:T(8,128)(2,1)}, bf16[4,96,576]{2,1,0:T(8,128)(2,1)}, u32[]{:S(2)}, u32[]{:S(2)}) collective-permute-start(bf16[4,96,576]{2,1,0:T(8,128)(2,1)} %dynamic-slice_bitcast_fusion.1), channel_id=1, source_target_pairs={{0,4},{4,0},{8,12},{12,8},{16,20},{20,16},{24,28},{28,24},{1,5},{5... | collective-permute-start | bytes 1327112 | tf_op jit(solution)/shard_map/ppermute | solution.py:602
  187.9 23.5 %collective-permute-start.28 = (bf16[4,96,768]{2,1,0:T(8,128)(2,1)}, bf16[4,96,768]{2,1,0:T(8,128)(2,1)}, u32[]{:S(2)}, u32[]{:S(2)}) collective-permute-start(bf16[4,96,768]{2,1,0:T(8,128)(2,1)} %dynamic-slice_bitcast_fusion), channel_id=1, source_target_pairs={{0,4},{4,0},{8,12},{12,8},{16,20},{20,16},{24,28},{28,24},{1,5},{5... | collective-permute-start | bytes 1769480 | tf_op jit(solution)/shard_map/ppermute | solution.py:602
  198.8 27.5 %collective-permute-start.21 = (bf16[4,120,768]{2,1,0:T(8,128)(2,1)S(1)}, bf16[4,120,768]{2,1,0:T(8,128)(2,1)S(1)}, u32[]{:S(2)}, u32[]{:S(2)}) collective-permute-start(bf16[4,120,768]{2,1,0:T(8,128)(2,1)S(1)} %fusion.17), channel_id=1, source_target_pairs={{0,4},{4,0},{8,12},{12,8},{16,20},{20,16},{24,28},{28,24},{1,5},{5... | collective-permute-start | bytes 2211848 | tf_op jit(solution)/shard_map/ppermute | solution.py:602
  211.4 6.3 %collective-permute-start.16 = (bf16[2,96,576]{2,1,0:T(8,128)(2,1)S(1)}, bf16[2,96,576]{2,1,0:T(8,128)(2,1)S(1)}, u32[]{:S(2)}, u32[]{:S(2)}) collective-permute-start(bf16[2,96,576]{2,1,0:T(8,128)(2,1)S(1)} %dynamic-slice_bitcast_fusion.4), channel_id=1, source_target_pairs={{0,8},{4,12},{8,0},{12,4},{16,24},{20,28},{24,16},{28,20},{1,9},{5... | collective-permute-start | bytes 663560 | tf_op jit(solution)/shard_map/ppermute | solution.py:602
  217.7 29.7 %collective-permute-start.29 = (bf16[2,96,768]{2,1,0:T(8,128)(2,1)S(1)}, bf16[2,96,768]{2,1,0:T(8,128)(2,1)S(1)}, u32[]{:S(2)}, u32[]{:S(2)}) collective-permute-start(bf16[2,96,768]{2,1,0:T(8,128)(2,1)S(1)} %dynamic-slice_bitcast_fusion.3), channel_id=1, source_target_pairs={{0,8},{4,12},{8,0},{12,4},{16,24},{20,28},{24,16},{28,20},{1,9},{5... | collective-permute-start | bytes 884744 | tf_op jit(solution)/shard_map/ppermute | solution.py:602
  226.2 8.0 %collective-permute-start.17 = (bf16[1,96,576]{2,1,0:T(8,128)(2,1)S(1)}, bf16[1,96,576]{2,1,0:T(8,128)(2,1)S(1)}, u32[]{:S(2)}, u32[]{:S(2)}) collective-permute-start(bf16[1,96,576]{2,1,0:T(8,128)(2,1)S(1)} %constant_dynamic-slice_fusion.2), channel_id=1, source_target_pairs={{0,16},{4,20},{8,24},{12,28},{16,0},{20,4},{24,8},{28,12},{1,17},{... | collective-permute-start | bytes 331784 | tf_op jit(solution)/shard_map/ppermute | solution.py:602
  234.3 8.1 %collective-permute-start.22 = (bf16[2,120,768]{2,1,0:T(8,128)(2,1)S(1)}, bf16[2,120,768]{2,1,0:T(8,128)(2,1)S(1)}, u32[]{:S(2)}, u32[]{:S(2)}) collective-permute-start(bf16[2,120,768]{2,1,0:T(8,128)(2,1)S(1)} %dynamic-slice_bitcast_fusion.2), channel_id=1, source_target_pairs={{0,8},{4,12},{8,0},{12,4},{16,24},{20,28},{24,16},{28,20},{1,9},{5... | collective-permute-start | bytes 1105928 | tf_op jit(solution)/shard_map/ppermute | solution.py:602
  235.1 21.4 %collective-permute-start.18 = (bf16[96,192]{1,0:T(8,128)(2,1)}, bf16[96,192]{1,0:T(8,128)(2,1)}, u32[]{:S(2)}, u32[]{:S(2)}) collective-permute-start(bf16[96,192]{1,0:T(8,128)(2,1)} %get-tuple-element.152), channel_id=1, source_target_pairs={{0,0},{3,1},{2,2},{1,3},{4,4},{7,5},{6,6},{5,7},{8,8},{11,9},{10,1... | collective-permute-start | bytes 110600 | tf_op jit(solution)/shard_map/ppermute | solution.py:652
  239.7 17.5 %collective-permute-start.19 = (bf16[96,192]{1,0:T(8,128)(2,1)S(1)}, bf16[96,192]{1,0:T(8,128)(2,1)}, u32[]{:S(2)}, u32[]{:S(2)}) collective-permute-start(bf16[96,192]{1,0:T(8,128)(2,1)S(1)} %get-tuple-element.154), channel_id=1, source_target_pairs={{1,0},{0,1},{3,2},{2,3},{5,4},{4,5},{7,6},{6,7},{9,8},{8,9},{11,10... | collective-permute-start | bytes 110600 | tf_op jit(solution)/shard_map/ppermute | solution.py:652
  242.4 15.6 %collective-permute-start.20 = (bf16[96,192]{1,0:T(8,128)(2,1)S(1)}, bf16[96,192]{1,0:T(8,128)(2,1)}, u32[]{:S(2)}, u32[]{:S(2)}) collective-permute-start(bf16[96,192]{1,0:T(8,128)(2,1)S(1)} %get-tuple-element.153), channel_id=1, source_target_pairs={{2,0},{1,1},{0,2},{3,3},{6,4},{5,5},{4,6},{7,7},{10,8},{9,9},{8,10... | collective-permute-start | bytes 110600 | tf_op jit(solution)/shard_map/ppermute | solution.py:652
  247.4 34.7 %copy-start.13 = (bf16[512,768]{1,0:T(8,128)(2,1)S(1)}, bf16[512,768]{1,0:T(8,128)(2,1)}, u32[]{:S(2)}) copy-start(bf16[512,768]{1,0:T(8,128)(2,1)} %add_convert_fusion.1) | copy-start | bytes 2359300
  247.4 8.9 %collective-permute-start.23 = (bf16[1,120,768]{2,1,0:T(8,128)(2,1)S(1)}, bf16[1,120,768]{2,1,0:T(8,128)(2,1)S(1)}, u32[]{:S(2)}, u32[]{:S(2)}) collective-permute-start(bf16[1,120,768]{2,1,0:T(8,128)(2,1)S(1)} %constant_dynamic-slice_fusion.1), channel_id=1, source_target_pairs={{0,16},{4,20},{8,24},{12,28},{16,0},{20,4},{24,8},{28,12},{1,17},{... | collective-permute-start | bytes 552968 | tf_op jit(solution)/shard_map/ppermute | solution.py:602
  256.3 8.0 %collective-permute-start.30 = (bf16[1,96,768]{2,1,0:T(8,128)(2,1)}, bf16[1,96,768]{2,1,0:T(8,128)(2,1)}, u32[]{:S(2)}, u32[]{:S(2)}) collective-permute-start(bf16[1,96,768]{2,1,0:T(8,128)(2,1)} %constant_dynamic-slice_fusion), channel_id=1, source_target_pairs={{0,16},{4,20},{8,24},{12,28},{16,0},{20,4},{24,8},{28,12},{1,17},{... | collective-permute-start | bytes 442376 | tf_op jit(solution)/shard_map/ppermute | solution.py:602
  256.5 27.5 %collective-permute-start.14 = (bf16[512,768]{1,0:T(8,128)(2,1)}, bf16[512,768]{1,0:T(8,128)(2,1)S(1)}, u32[]{:S(2)}, u32[]{:S(2)}) collective-permute-start(bf16[512,768]{1,0:T(8,128)(2,1)} %add_convert_fusion), channel_id=1, source_target_pairs={{0,2},{1,3},{2,0},{3,1},{4,6},{5,7},{6,4},{7,5},{8,10},{9,11},{10,... | collective-permute-start | bytes 2359304 | tf_op jit(solution)/shard_map/ppermute | solution.py:602
  257.2 9.5 %collective-permute-start.24 = (bf16[120,192]{0,1:T(8,128)(2,1)S(1)}, bf16[120,192]{0,1:T(8,128)(2,1)S(1)}, u32[]{:S(2)}, u32[]{:S(2)}) collective-permute-start(bf16[120,192]{0,1:T(8,128)(2,1)S(1)} %get-tuple-element.148), channel_id=1, source_target_pairs={{0,0},{1,8},{2,16},{3,24},{4,1},{5,9},{6,17},{7,25},{8,2},{9,10},{... | collective-permute-start | bytes 138248 | tf_op jit(solution)/shard_map/ppermute | solution.py:632
  259.6 13.7 %collective-permute-start.25 = (bf16[120,192]{0,1:T(8,128)(2,1)S(1)}, bf16[120,192]{0,1:T(8,128)(2,1)S(1)}, u32[]{:S(2)}, u32[]{:S(2)}) collective-permute-start(bf16[120,192]{0,1:T(8,128)(2,1)S(1)} %get-tuple-element.151), channel_id=1, source_target_pairs={{0,1},{1,9},{2,17},{3,25},{4,0},{5,8},{6,16},{7,24},{8,3},{9,11},{... | collective-permute-start | bytes 138248 | tf_op jit(solution)/shard_map/ppermute | solution.py:632
  264.3 17.8 %collective-permute-start.26 = (bf16[120,192]{0,1:T(8,128)(2,1)S(1)}, bf16[120,192]{0,1:T(8,128)(2,1)S(1)}, u32[]{:S(2)}, u32[]{:S(2)}) collective-permute-start(bf16[120,192]{0,1:T(8,128)(2,1)S(1)} %get-tuple-element.150), channel_id=1, source_target_pairs={{0,2},{1,10},{2,18},{3,26},{4,3},{5,11},{6,19},{7,27},{8,0},{9,8},... | collective-permute-start | bytes 138248 | tf_op jit(solution)/shard_map/ppermute | solution.py:632
  266.7 15.4 %collective-permute-start.27 = (bf16[120,192]{0,1:T(8,128)(2,1)S(1)}, bf16[120,192]{0,1:T(8,128)(2,1)S(1)}, u32[]{:S(2)}, u32[]{:S(2)}) collective-permute-start(bf16[120,192]{0,1:T(8,128)(2,1)S(1)} %get-tuple-element.149), channel_id=1, source_target_pairs={{0,3},{1,11},{2,19},{3,27},{4,2},{5,10},{6,18},{7,26},{8,1},{9,9},... | collective-permute-start | bytes 138248 | tf_op jit(solution)/shard_map/ppermute | solution.py:632
  273.3 12.9 %collective-permute-start.9 = (bf16[512,768]{1,0:T(8,128)(2,1)S(1)}, bf16[512,768]{1,0:T(8,128)(2,1)}, u32[]{:S(2)}, u32[]{:S(2)}) collective-permute-start(bf16[512,768]{1,0:T(8,128)(2,1)S(1)} %copy-done.12), channel_id=1, source_target_pairs={{0,1},{1,0},{2,3},{3,2},{4,5},{5,4},{6,7},{7,6},{8,9},{9,8},{10,11... | collective-permute-start | bytes 2359304 | tf_op jit(solution)/shard_map/ppermute | solution.py:602
  282.1 19.6 %collective-permute-start.11 = (bf16[512,768]{1,0:T(8,128)(2,1)S(1)}, bf16[512,768]{1,0:T(8,128)(2,1)}, u32[]{:S(2)}, u32[]{:S(2)}) collective-permute-start(bf16[512,768]{1,0:T(8,128)(2,1)S(1)} %copy-done.13), channel_id=1, source_target_pairs={{0,2},{1,3},{2,0},{3,1},{4,6},{5,7},{6,4},{7,5},{8,10},{9,11},{10,... | collective-permute-start | bytes 2359304 | tf_op jit(solution)/shard_map/ppermute | solution.py:602
  (37 other events, 356.2 us)

commit v2 on v1

v2 whole, which is shorter than its diff:
```python
import math
from functools import partial

import jax
import jax.numpy as jnp
import numpy as np
from jax import lax
from jax.experimental import pallas as pl
from jax.experimental.pallas import tpu as pltpu
from jax.sharding import PartitionSpec as P

D = 768
HEADS = 12
HDIM = 64
ROT = 16
FF = 3072
EPS = 1e-05
MASKED = -1e30
TILE = 256
LANES = 128
F32 = jnp.float32
BF16 = jnp.bfloat16
NT_DIMS = (((1,), (1,)), ((), ()))
TN_DIMS = (((0,), (0,)), ((), ()))


def dot(left, right):
    return jnp.dot(left, right, preferred_element_type=F32)


def dot_nt(left, right):
    return lax.dot_general(left, right, NT_DIMS, preferred_element_type=F32)


def dot_tn(left, right):
    return lax.dot_general(left, right, TN_DIMS, preferred_element_type=F32)


def normalize(value):
    center = value - jnp.mean(value, axis=-1, keepdims=True)
    spread = jnp.mean(center * center, axis=-1, keepdims=True)
    return center * lax.rsqrt(spread + EPS)


def angle_parts(length):
    dim = np.arange(LANES) % HDIM
    inverse = np.where(dim < ROT, 10000.0 ** (-2.0 * (dim % (ROT // 2)) / ROT), 0.0)
    high = (np.arange(length // LANES) * LANES)[:, None] * inverse
    low = np.arange(LANES)[:, None] * inverse
    parts = np.stack([np.cos(low), np.sin(low)]), np.stack([np.cos(high), np.sin(high)])
    return tuple(jnp.asarray(part, F32) for part in parts)


def rotation(low_ref, high_ref, tile):
    lane = lax.broadcasted_iota(jnp.int32, (1, LANES), 1) % HDIM
    sign = jnp.where(lane < ROT // 2, -1.0, 1.0)
    cos_rows, sin_rows = [], []
    for part in range(TILE // LANES):
        row = tile * (TILE // LANES) + part
        cos_high = high_ref[0, pl.ds(row, 1), :]
        sin_high = high_ref[1, pl.ds(row, 1), :]
        cos_rows.append(low_ref[0] * cos_high - low_ref[1] * sin_high)
        sin_rows.append((low_ref[1] * cos_high + low_ref[0] * sin_high) * sign)
    return jnp.concatenate(cos_rows, axis=0), jnp.concatenate(sin_rows, axis=0)


def swap_halves(value):
    lane = lax.broadcasted_iota(jnp.int32, value.shape, 1) % HDIM
    half = ROT // 2
    return jnp.where(
        lane < half, pltpu.roll(value, LANES - half, 1), pltpu.roll(value, half, 1)
    )


def true_block(meta_ref, slot):
    return jnp.bitwise_xor(meta_ref[0], slot)


def params(*semantics, vmem=None):
    return pltpu.CompilerParams(
        dimension_semantics=semantics or ("arbitrary",), vmem_limit_bytes=vmem or 60 * 2**20
    )


def whole(shape):
    return pl.BlockSpec(shape, lambda *_: (0,) * len(shape))


def own_blocks(refs, odd, into):
    places = ((0, 256), (128, 320), (384, 512))
    for part, (pair_at, third_at) in enumerate(places):
        left, right = refs[2 * part], refs[2 * part + 1]

        @pl.when(odd == 0)
        def _(left=left, right=right, pair_at=pair_at, third_at=third_at):
            into[:, pair_at : pair_at + 128] = left[...]
            into[:, third_at : third_at + 64] = right[:, 0:64]

        @pl.when(odd == 1)
        def _(left=left, right=right, pair_at=pair_at, third_at=third_at):
            into[:, pair_at : pair_at + 128] = jnp.concatenate(
                [left[:, 64:128], right[:, 0:64]], axis=1
            )
            into[:, third_at : third_at + 64] = right[:, 64:128]


def qkv_kernel(slot, meta, x_ref, gain, shift, low, high, *refs):
    if slot == 0:
        odd = meta[0] % 2
        q_ref, k_ref, v_ref, w_ref, b_ref = refs[-5:]
        own_blocks(refs[0:6], odd, w_ref)
        own_blocks(refs[6:12], odd, b_ref)
    else:
        w_ref, b_ref = refs[0:2]
        q_ref, k_ref, v_ref = refs[-3:]
    per = x_ref.shape[0] // TILE
    for part in range(per):
        rows = pl.ds(part * TILE, TILE)
        normed = normalize(x_ref[rows, :].astype(F32))
        attn_in = (normed * gain[...] + shift[...]).astype(BF16)
        joined = dot(attn_in, w_ref[...]) + b_ref[...]
        cos, sin = rotation(low, high, true_block(meta, slot) * per + part)
        scale = HDIM**-0.5

        def turn(block):
            return block * cos + swap_halves(block) * sin

        query = turn(joined[:, 0:128]) * scale
        keys = turn(joined[:, 128:256])
        mixed = turn(joined[:, 256:384])
        q_ref[rows, 0:128] = query.astype(BF16)
        k_ref[rows, 0:128] = keys.astype(BF16)
        q_ref[rows, 128:192] = (mixed[:, 0:64] * scale).astype(BF16)
        k_ref[rows, 128:192] = mixed[:, 64:128].astype(BF16)
        v_ref[rows, :] = joined[:, 384:576].astype(BF16)


def project(slot, meta, x, gain, shift, low, high, w, b, filled):
    seq = x.shape[0]
    width = D // 4
    total = 4 * seq
    out = jax.ShapeDtypeStruct((total, width), BF16)
    out_spec = pl.BlockSpec((seq, width), lambda i, m: (slot, 0))
    outs, out_specs = [out] * 3, [out_spec] * 3
    args = [x, gain, shift, low, high]
    specs = [whole(a.shape) for a in args]
    aliases = {}
    if slot == 0:
        for array in (w, b):
            for part in range(3):
                for side in range(2):
                    specs.append(
                        pl.BlockSpec(
                            (array.shape[0], LANES),
                            lambda i, m, at=part * D // LANES + side: (0, at + 3 * m[0] // 2),
                        )
                    )
                    args.append(array)
        for array in (w, b):
            shape = (array.shape[0], 3 * width)
            outs.append(jax.ShapeDtypeStruct(shape, array.dtype))
            out_specs.append(whole(shape))
    else:
        args += [w, b]
        specs += [whole(w.shape), whole(b.shape)]
        aliases = {1 + len(args) + i: i for i in range(3)}
        args += list(filled)
        specs += [pl.BlockSpec(memory_space=pl.ANY)] * 3
    return pl.pallas_call(
        partial(qkv_kernel, slot),
        out_shape=outs,
        grid_spec=pltpu.PrefetchScalarGridSpec(
            num_scalar_prefetch=1, grid=(1,), in_specs=specs, out_specs=out_specs
        ),
        input_output_aliases=aliases,
        compiler_params=params(),
        cost_estimate=pl.CostEstimate(
            flops=2 * seq * D * 3 * width, bytes_accessed=4 * seq * D, transcendentals=0
        ),
        name=f"qkv_{slot}",
    )(meta, *args)


def store_chunks(grad, keep, send, meta):
    if len(keep.shape) == 2:
        keep[...] = grad[...].astype(keep.dtype)
        return
    size = keep.shape[1]
    for place in range(2 * keep.shape[0]):
        at = pl.multiple_of(jnp.bitwise_xor(meta[1], place) * size, 8)
        into = send if place % 2 else keep
        into[place // 2] = grad[pl.ds(at, size), :].astype(into.dtype)


def chunk_shapes(size, cols, rows):
    if size // rows % 8 == 0 and rows > 1:
        return [(rows // 2, size // rows, cols)] * 2
    return [(size, cols), (8, LANES)]


def chunks_of(keep, send, rows):
    if keep.ndim == 3:
        return keep, send
    places = jnp.arange(rows) ^ lax.axis_index("rows")
    parts = jnp.take(keep.reshape(rows, keep.shape[0] // rows, keep.shape[1]), places, axis=0)
    return parts[0::2], parts[1::2]


def mlp_kernel(final, meta, *refs):
    (xa, xb, ca, cb, gain, shift, w_up, b_up, w_down, w_out) = refs[:10]
    if final:
        (up_in, down_in, b_in, g_in, s_in) = refs[10:15]
        mo_ref, e_ref, gv_ref, gb_ref, gg_ref, gs_ref = refs[-14:-8]
        up_keep, up_send, down_keep, down_send = refs[-8:-4]
        x_s, c_s, up_s, down_s = refs[-4:]
    else:
        mo_ref, e_ref, gv_ref, gb_ref, gg_ref, gs_ref, up_s, down_s = refs[-10:-2]
        x_s, c_s = refs[-2:]
    step = pl.program_id(0)
    half = pl.num_programs(0) // 2

    @pl.when(step < half)
    def _():
        x_s[...] = xa[...]
        c_s[...] = ca[...]

    @pl.when(step >= half)
    def _():
        x_s[...] = xb[...]
        c_s[...] = cb[...]

    @pl.when(step == 0)
    def _():
        if final:
            up_s[...] = up_in[...]
            down_s[...] = down_in[...]
            gb_ref[...] = b_in[...]
            gg_ref[...] = g_in[...]
            gs_ref[...] = s_in[...]
        else:
            up_s[...] = jnp.zeros_like(up_s)
            down_s[...] = jnp.zeros_like(down_s)
            gb_ref[...] = jnp.zeros_like(gb_ref)
            gg_ref[...] = jnp.zeros_like(gg_ref)
            gs_ref[...] = jnp.zeros_like(gs_ref)

    normed = normalize(x_s[...].astype(F32))
    mlp_in = (normed * gain[...] + shift[...]).astype(BF16)
    upstream = c_s[...]
    hidden = dot(mlp_in, w_up[...]) + b_up[...]
    cdf = 0.5 * (1.0 + lax.erf(hidden * (0.5**0.5)))
    act = (hidden * cdf).astype(BF16)
    slope = cdf + hidden * jnp.exp(-0.5 * hidden * hidden) * ((2.0 * math.pi) ** -0.5)
    mo_ref[...] = dot(act, w_down[...]).astype(BF16)
    grad_act = dot_nt(upstream, w_down[...])
    grad_hidden = slope * grad_act
    grad_low = grad_hidden.astype(BF16)
    gb_ref[...] += jnp.sum(grad_low.astype(F32), axis=0, keepdims=True)
    grad_norm = dot_nt(grad_low, w_up[...])
    gg_ref[...] += jnp.sum(grad_norm * normed, axis=0, keepdims=True)
    gs_ref[...] += jnp.sum(grad_norm, axis=0, keepdims=True)
    e_ref[...] = (grad_norm * gain[...]).astype(BF16)
    gv_ref[...] = dot_nt(upstream, w_out[...]).astype(BF16)
    up_s[...] += dot_tn(mlp_in, grad_low)
    down_s[...] += dot_tn(act, upstream)

    if final:

        @pl.when(step == pl.num_programs(0) - 1)
        def _():
            store_chunks(up_s, up_keep, up_send, meta)
            store_chunks(down_s, down_keep, down_send, meta)


def feed_forward(pair, meta, xs, cs, gain, shift, w_up, b_up, w_down, w_out, before, rows):
    seq = xs[0].shape[0]
    per = seq // TILE
    steps = 2 * per
    hid = FF // 4
    width = D // 4
    first = pl.BlockSpec((TILE, D), lambda i, m: (jnp.minimum(i, per - 1), 0))
    second = pl.BlockSpec((TILE, D), lambda i, m: (jnp.maximum(i - per, 0), 0))
    row = whole((1, D))
    specs = [
        first,
        second,
        first,
        second,
        row,
        row,
        pl.BlockSpec((D, hid), lambda i, m: (0, m[0])),
        pl.BlockSpec((1, hid), lambda i, m: (0, m[0])),
        pl.BlockSpec((hid, D), lambda i, m: (m[0], 0)),
        pl.BlockSpec((width, D), lambda i, m: (m[0], 0)),
    ]
    args = [*xs, *cs, gain, shift, w_up, b_up, w_down, w_out]
    aliases = {}
    shapes = [(jnp.float32, (D, hid)), (jnp.float32, (hid, D))]
    scratch = [pltpu.VMEM((TILE, D), BF16), pltpu.VMEM((TILE, D), BF16)]
    if before is not None:
        shapes = [
            (BF16, shape)
            for size, cols in ((D, hid), (hid, D))
            for shape in chunk_shapes(size, cols, rows)
        ]
        scratch += [pltpu.VMEM((D, hid), F32), pltpu.VMEM((hid, D), F32)]
        carried = list(before[6:8]) + list(before[3:6])
        args += carried + list(before[:3])
        specs += [whole(a.shape) for a in carried]
        specs += [pl.BlockSpec(memory_space=pl.ANY)] * 3
        aliases = {1 + len(args) - 3 + i: i for i in range(3)}
    base = pair * steps

    def tiles(cols):
        return pl.BlockSpec((TILE, cols), lambda i, m: (i + base, 0))

    total = 4 * seq
    return pl.pallas_call(
        partial(mlp_kernel, before is not None),
        out_shape=[
            jax.ShapeDtypeStruct((total, D), BF16),
            jax.ShapeDtypeStruct((total, D), BF16),
            jax.ShapeDtypeStruct((total, width), BF16),
            jax.ShapeDtypeStruct((1, hid), F32),
            jax.ShapeDtypeStruct((1, D), F32),
            jax.ShapeDtypeStruct((1, D), F32),
            *(jax.ShapeDtypeStruct(shape, kind) for kind, shape in shapes),
        ],
        grid_spec=pltpu.PrefetchScalarGridSpec(
            num_scalar_prefetch=1,
            grid=(steps,),
            in_specs=specs,
            out_specs=[
                tiles(D),
                tiles(D),
                tiles(width),
                whole((1, hid)),
                row,
                row,
                *(whole(shape) for _, shape in shapes),
            ],
            scratch_shapes=scratch,
        ),
        input_output_aliases=aliases,
        compiler_params=params(),
        cost_estimate=pl.CostEstimate(
            flops=2 * 6 * 2 * seq * D * hid, bytes_accessed=20 * seq * D, transcendentals=0
        ),
        name=f"mlp_{pair}",
    )(meta, *args)


def head_masks():
    lane = lax.broadcasted_iota(jnp.int32, (1, LANES), 1)
    first = jnp.where(lane < HDIM, 1.0, 0.0).astype(BF16)
    second = jnp.where(lane < HDIM, 0.0, 1.0).astype(BF16)
    return first, second


def slot_rows(meta, per, tile):
    slot = jnp.bitwise_xor(tile // per, meta[0])
    return pl.multiple_of((slot * per + tile % per) * TILE, TILE)


def by_head(first, second, block, third):
    return (block * first, block * second, third)


def transpose_all(from_ref, to_ref):
    @pl.loop(0, from_ref.shape[0] // TILE)
    def _(tile):
        rows = pl.ds(pl.multiple_of(tile * TILE, TILE), TILE)
        to_ref[:, rows] = from_ref[rows, :].astype(F32).T.astype(BF16)


def attend_kernel(base, per, meta, lo, q_ref, k_ref, v_ref, start_ref, *refs):
    o_ref, lse_ref, vt_ref, acc = refs[-4:]
    mask0, mask1 = head_masks()

    @pl.when(pl.program_id(0) == 0)
    def _():
        transpose_all(v_ref, vt_ref)

    key_iota = lax.broadcasted_iota(jnp.int32, (TILE, TILE), 0)
    query_iota = lax.broadcasted_iota(jnp.int32, (TILE, TILE), 1)

    @pl.loop(0, per)
    def _(part):
        qi = (base + pl.program_id(0)) * per + part
        q_rows = pl.ds(pl.multiple_of(part * TILE, TILE), TILE)
        queries = by_head(mask0, mask1, q_ref[q_rows, 0:128], q_ref[q_rows, 128:192])
        starts = start_ref[part]
        acc[...] = jnp.zeros_like(acc)

        def visit(ki, carry):
            k_rows = pl.ds(slot_rows(meta, per, ki), TILE)
            pair, third = k_ref[k_rows, 0:128], k_ref[k_rows, 128:192]
            key_pos = key_iota + ki * TILE
            allowed = (key_pos >= starts) & (key_pos <= query_iota + qi * TILE)
            after = []
            for head in range(3):
                top, total = carry[head]
                scores = dot_nt(third if head == 2 else pair, queries[head])
                scores = jnp.where(allowed, scores, MASKED)
                new_top = jnp.maximum(top, jnp.max(scores, axis=0, keepdims=True))
                fade = jnp.exp(top - new_top)
                weights = jnp.exp(scores - new_top)
                total = total * fade + jnp.sum(weights, axis=0, keepdims=True)
                cols = pl.ds(head * HDIM, HDIM)
                acc[cols, :] = acc[cols, :] * fade + dot(vt_ref[cols, k_rows], weights.astype(BF16))
                after.append((new_top, total))
            return tuple(after)

        begin = (jnp.full((1, TILE), MASKED, F32), jnp.zeros((1, TILE), F32))
        stats = lax.fori_loop(lo[qi], qi + 1, visit, (begin,) * 3)
        for head, (top, total) in enumerate(stats):
            cols = pl.ds(head * HDIM, HDIM)
            acc[cols, :] = acc[cols, :] / total
            lse_ref[head, part] = top + jnp.log(total)
        o_ref[q_rows, :] = acc[...].T.astype(BF16)


def block_specs(per, true_of, widths):
    seq = per * TILE
    specs = [
        pl.BlockSpec((seq, w), lambda i, m, lo: (jnp.bitwise_xor(true_of(i), m[0]), 0))
        for w in widths
    ]
    starts = pl.BlockSpec(
        (per, 1, TILE), lambda i, m, lo: (jnp.bitwise_xor(true_of(i), m[0]), 0, 0)
    )
    lse = pl.BlockSpec(
        (3, per, 1, TILE), lambda i, m, lo: (0, jnp.bitwise_xor(true_of(i), m[0]), 0, 0)
    )
    return specs, starts, lse


def attend(base, meta, lo, query, keys, values, starts, per, filled):
    total, width = query.shape
    tiles = total // TILE
    (q_spec,), start_spec, lse_spec = block_specs(per, lambda i: base + i, (width,))
    args = [query, keys, values, starts]
    specs = [q_spec, whole(keys.shape), whole(values.shape), start_spec]
    aliases = {}
    if filled is not None:
        aliases = {2 + len(args) + i: i for i in range(2)}
        args += list(filled)
        specs += [pl.BlockSpec(memory_space=pl.ANY)] * 2
    return pl.pallas_call(
        partial(attend_kernel, base, per),
        out_shape=[
            jax.ShapeDtypeStruct((total, width), BF16),
            jax.ShapeDtypeStruct((3, tiles, 1, TILE), F32),
        ],
        grid_spec=pltpu.PrefetchScalarGridSpec(
            num_scalar_prefetch=2,
            grid=(2,),
            in_specs=specs,
            out_specs=[q_spec, lse_spec],
            scratch_shapes=[pltpu.VMEM((width, total), BF16), pltpu.VMEM((width, TILE), F32)],
        ),
        input_output_aliases=aliases,
        compiler_params=params(),
        cost_estimate=pl.CostEstimate(
            flops=30 * 4 * 256 * 256 * 256, bytes_accessed=8 * total * width, transcendentals=0
        ),
        name=f"attend_{base}",
    )(meta, lo, *args)


def attend_back_kernel(
    top, per, meta, lo, q_ref, k_ref, v_ref, o_ref, gv_ref, start_ref, lse_ref, low, high, *refs
):
    if top == 3:
        gj_ref, dk_ref, dv_ref, kt_ref, dqt_ref = refs
    else:
        dk_in, dv_in = refs[0:2]
        gj_ref, dk_ref, dv_ref, kt_ref, dqt_ref = refs[-5:]
    mask0, mask1 = head_masks()

    @pl.when(pl.program_id(0) == 0)
    def _():
        transpose_all(k_ref, kt_ref)
        if top == 3:
            dk_ref[...] = jnp.zeros_like(dk_ref)
            dv_ref[...] = jnp.zeros_like(dv_ref)
        else:
            dk_ref[...] = dk_in[...]
            dv_ref[...] = dv_in[...]

    key_iota = lax.broadcasted_iota(jnp.int32, (TILE, TILE), 0)
    query_iota = lax.broadcasted_iota(jnp.int32, (TILE, TILE), 1)

    @pl.loop(0, per)
    def _(turn):
        part = per - 1 - turn
        qi = (top - pl.program_id(0)) * per + part
        own_rows = pl.ds(slot_rows(meta, per, qi), TILE)
        q_rows = pl.ds(pl.multiple_of(part * TILE, TILE), TILE)
        queries = by_head(mask0, mask1, q_ref[q_rows, 0:128], q_ref[q_rows, 128:192])
        grads = by_head(mask0, mask1, gv_ref[q_rows, 0:128], gv_ref[q_rows, 128:192])
        starts = start_ref[part]
        lses = [lse_ref[head, part] for head in range(3)]
        product = (gv_ref[q_rows, :].astype(F32) * o_ref[q_rows, :].astype(F32)).T
        deltas = [
            jnp.sum(product[head * HDIM : (head + 1) * HDIM], axis=0, keepdims=True)
            for head in range(3)
        ]
        dqt_ref[...] = jnp.zeros_like(dqt_ref)

        @pl.loop(lo[qi], qi + 1)
        def _(ki):
            k_rows = pl.ds(slot_rows(meta, per, ki), TILE)
            pair, third = k_ref[k_rows, 0:128], k_ref[k_rows, 128:192]
            v_pair, v_third = v_ref[k_rows, 0:128], v_ref[k_rows, 128:192]
            key_pos = key_iota + ki * TILE
            allowed = (key_pos >= starts) & (key_pos <= query_iota + qi * TILE)
            dk, dv = [], []
            for head in range(3):
                scores = dot_nt(third if head == 2 else pair, queries[head])
                probs = jnp.exp(jnp.where(allowed, scores - lses[head], MASKED))
                grad_probs = dot_nt(v_third if head == 2 else v_pair, grads[head])
                grad_scores = (probs * (grad_probs - deltas[head])).astype(BF16)
                dv.append(dot(probs.astype(BF16), grads[head]))
                dk.append(dot(grad_scores, queries[head]))
                cols = pl.ds(head * HDIM, HDIM)
                dqt_ref[cols, :] += dot(kt_ref[cols, k_rows], grad_scores)
            dk_ref[k_rows, 0:128] += dk[0] + dk[1]
            dk_ref[k_rows, 128:192] += dk[2]
            dv_ref[k_rows, 0:128] += dv[0] + dv[1]
            dv_ref[k_rows, 128:192] += dv[2]

        cos, sin = rotation(low, high, qi)

        def turn_back(block):
            return (block * cos - swap_halves(block) * sin).astype(BF16)

        dq = dqt_ref[...].T * (HDIM**-0.5)
        gj_ref[q_rows, 0:128] = turn_back(dq[:, 0:128])
        mixed = jnp.concatenate([dq[:, 128:192], dk_ref[own_rows, 128:192]], axis=1)
        gj_ref[q_rows, 128:256] = turn_back(dk_ref[own_rows, 0:128])
        gj_ref[q_rows, 256:384] = turn_back(mixed)
        gj_ref[q_rows, 384:576] = dv_ref[own_rows, :].astype(BF16)


def attend_back(
    top, meta, lo, query, keys, values, attn, grad_vec, starts, lse, low, high, per, filled
):
    total, width = query.shape
    (q_spec, gj_spec), start_spec, lse_spec = block_specs(
        per, lambda i: top - i, (width, 3 * width)
    )
    args = [query, keys, values, attn, grad_vec, starts, lse, low, high]
    specs = [
        q_spec,
        whole(keys.shape),
        whole(values.shape),
        q_spec,
        q_spec,
        start_spec,
        lse_spec,
        whole(low.shape),
        whole(high.shape),
    ]
    aliases = {}
    if filled is not None:
        args += [filled[1], filled[2], filled[0]]
        specs += [whole(filled[1].shape)] * 2 + [pl.BlockSpec(memory_space=pl.ANY)]
        aliases = {2 + len(args) - 1: 0}
    return pl.pallas_call(
        partial(attend_back_kernel, top, per),
        out_shape=[
            jax.ShapeDtypeStruct((total, 3 * width), BF16),
            jax.ShapeDtypeStruct((total, width), F32),
            jax.ShapeDtypeStruct((total, width), F32),
        ],
        grid_spec=pltpu.PrefetchScalarGridSpec(
            num_scalar_prefetch=2,
            grid=(2,),
            in_specs=specs,
            out_specs=[gj_spec, whole((total, width)), whole((total, width))],
            scratch_shapes=[pltpu.VMEM((width, total), BF16), pltpu.VMEM((width, TILE), F32)],
        ),
        input_output_aliases=aliases,
        compiler_params=params(),
        cost_estimate=pl.CostEstimate(
            flops=30 * 10 * 256 * 256 * 256, bytes_accessed=16 * total * width, transcendentals=0
        ),
        name=f"attend_back_{top}",
    )(meta, lo, *args)


def pick(refs, into, per):
    step = pl.program_id(0)
    for slot, ref in enumerate(refs):

        @pl.when(step // per == slot)
        def _(ref=ref):
            into[...] = ref[...]


def put(refs, value, per):
    step = pl.program_id(0)
    for slot, ref in enumerate(refs):

        @pl.when(step // per == slot)
        def _(ref=ref):
            ref[...] = value


def slot_specs(per, cols, count):
    def spec(slot):
        return pl.BlockSpec(
            (TILE, cols), lambda i, m: (jnp.clip(i - slot * per, 0, per - 1), 0)
        )

    return [spec(slot) for slot in range(count)]


def output_kernel(per, meta, o_ref, mo_ref, c0, c1, c2, c3, w_ref, *refs):
    outs, (keep, send, c_s, gw_s) = refs[:4], refs[4:]
    step = pl.program_id(0)
    pick((c0, c1, c2, c3), c_s, per)

    @pl.when(step == 0)
    def _():
        gw_s[...] = jnp.zeros_like(gw_s)

    attn = o_ref[...]
    put(outs, (dot(attn, w_ref[...]) + mo_ref[...].astype(F32)).astype(BF16), per)
    gw_s[...] += dot_tn(attn, c_s[...])

    @pl.when(step == pl.num_programs(0) - 1)
    def _():
        store_chunks(gw_s, keep, send, meta)


def output(meta, attn, mlp, cots, w_out, rows):
    total, width = attn.shape
    seq = cots[0].shape[0]
    per = seq // TILE
    chunks = chunk_shapes(width, D, rows)
    return pl.pallas_call(
        partial(output_kernel, per),
        out_shape=[jax.ShapeDtypeStruct((seq, D), BF16)] * 4
        + [jax.ShapeDtypeStruct(shape, BF16) for shape in chunks],
        grid_spec=pltpu.PrefetchScalarGridSpec(
            num_scalar_prefetch=1,
            grid=(4 * per,),
            in_specs=[
                pl.BlockSpec((TILE, width), lambda i, m: (i, 0)),
                pl.BlockSpec((TILE, D), lambda i, m: (i, 0)),
                *slot_specs(per, D, 4),
                pl.BlockSpec((width, D), lambda i, m: (m[0], 0)),
            ],
            out_specs=[*slot_specs(per, D, 4), *(whole(shape) for shape in chunks)],
            scratch_shapes=[pltpu.VMEM((TILE, D), BF16), pltpu.VMEM((width, D), F32)],
        ),
        compiler_params=params(),
        cost_estimate=pl.CostEstimate(
            flops=4 * total * width * D, bytes_accessed=6 * total * D, transcendentals=0
        ),
        name="output",
    )(meta, attn, mlp, *cots, w_out)


def norm_grad_kernel(slots, per, meta, *refs):
    count = len(slots)
    gjs, es, toks = refs[0:count], refs[count : 2 * count], refs[2 * count : 3 * count]
    gain, w_ref, gg_in, gs_in = refs[3 * count : 3 * count + 4]
    outs, (gg_ref, gs_ref, gj_s, e_s, x_s) = refs[-5 - count : -5], refs[-5:]
    step = pl.program_id(0)
    pick(gjs, gj_s, per)
    pick(es, e_s, per)
    pick(toks, x_s, per)

    @pl.when(step == 0)
    def _():
        gg_ref[...] = gg_in[...]
        gs_ref[...] = gs_in[...]

    normed = normalize(x_s[...].astype(F32))
    grad_norm = dot_nt(gj_s[...], w_ref[...])
    put(outs, (grad_norm * gain[...] + e_s[...].astype(F32)).astype(BF16), per)
    gg_ref[...] += jnp.sum(grad_norm * normed, axis=0, keepdims=True)
    gs_ref[...] += jnp.sum(grad_norm, axis=0, keepdims=True)


def norm_grad(slots, meta, grad, e_mlp, toks, gain, w, sums):
    width = grad.shape[1]
    seq = toks[0].shape[0]
    per = seq // TILE
    count = len(slots)
    row = whole((1, D))

    def at_slot(place, slot, cols):
        return pl.BlockSpec(
            (TILE, cols), lambda i, m: (slot * per + jnp.clip(i - place * per, 0, per - 1), 0)
        )

    return pl.pallas_call(
        partial(norm_grad_kernel, slots, per),
        out_shape=[jax.ShapeDtypeStruct((seq, D), BF16)] * count
        + [jax.ShapeDtypeStruct((1, D), F32)] * 2,
        grid_spec=pltpu.PrefetchScalarGridSpec(
            num_scalar_prefetch=1,
            grid=(count * per,),
            in_specs=[
                *(at_slot(place, slot, width) for place, slot in enumerate(slots)),
                *(at_slot(place, slot, D) for place, slot in enumerate(slots)),
                *slot_specs(per, D, count),
                row,
                whole((D, width)),
                row,
                row,
            ],
            out_specs=[*slot_specs(per, D, count), row, row],
            scratch_shapes=[
                pltpu.VMEM((TILE, width), BF16),
                pltpu.VMEM((TILE, D), BF16),
                pltpu.VMEM((TILE, D), BF16),
            ],
        ),
        compiler_params=params(),
        cost_estimate=pl.CostEstimate(
            flops=2 * count * seq * width * D, bytes_accessed=8 * count * seq * D, transcendentals=0
        ),
        name=f"norm_grad_{slots[0]}",
    )(
        meta,
        *[grad] * count,
        *[e_mlp] * count,
        *[toks[slot] for slot in slots],
        gain,
        w,
        *sums,
    )


def joined_weight_kernel(per, meta, gj_ref, t0, t1, t2, t3, gain, shift, keep, send, gb_ref, x_s, gw_s):
    step = pl.program_id(0)
    pick((t0, t1, t2, t3), x_s, per)

    @pl.when(step == 0)
    def _():
        gw_s[...] = jnp.zeros_like(gw_s)
        gb_ref[...] = jnp.zeros_like(gb_ref)

    attn_in = (normalize(x_s[...].astype(F32)) * gain[...] + shift[...]).astype(BF16)
    grad = gj_ref[...]
    gb_ref[...] += jnp.sum(grad.astype(F32), axis=0, keepdims=True)
    gw_s[...] += dot_tn(attn_in, grad)

    @pl.when(step == pl.num_programs(0) - 1)
    def _():
        store_chunks(gw_s, keep, send, meta)


def joined_weight(meta, grad, toks, gain, shift, rows):
    total, width = grad.shape
    per = toks[0].shape[0] // TILE
    row = whole((1, D))
    chunks = chunk_shapes(D, width, rows)
    return pl.pallas_call(
        partial(joined_weight_kernel, per),
        out_shape=[
            *(jax.ShapeDtypeStruct(shape, BF16) for shape in chunks),
            jax.ShapeDtypeStruct((1, width), F32),
        ],
        grid_spec=pltpu.PrefetchScalarGridSpec(
            num_scalar_prefetch=1,
            grid=(4 * per,),
            in_specs=[
                pl.BlockSpec((TILE, width), lambda i, m: (i, 0)),
                *slot_specs(per, D, 4),
                row,
                row,
            ],
            out_specs=[*(whole(shape) for shape in chunks), whole((1, width))],
            scratch_shapes=[pltpu.VMEM((TILE, D), BF16), pltpu.VMEM((D, width), F32)],
        ),
        compiler_params=params(),
        cost_estimate=pl.CostEstimate(
            flops=2 * total * width * D, bytes_accessed=4 * total * D, transcendentals=0
        ),
        name="joined_weight",
    )(meta, grad, *toks, gain, shift)


def after(value, *others):
    return lax.optimization_barrier((value, others))[0]


def swap(value, axis, mask):
    size = lax.axis_size(axis)
    return lax.ppermute(value, axis, [(i, i ^ mask) for i in range(size)])


def add_pair(keep, got):
    return [
        (keep[i].astype(F32) + got[i].astype(F32)).astype(BF16) for i in range(keep.shape[0])
    ]


def exchange(parts):
    total = parts[0].astype(F32)
    for place in range(1, len(parts)):
        total += swap(parts[place], "rows", 2 * place).astype(F32)
    return total


def spread_rows(chunk, col_width):
    rows, blk = lax.axis_size("rows"), lax.axis_size("blk")
    r, b = lax.axis_index("rows"), lax.axis_index("blk")
    pieces = chunk.reshape(chunk.shape[0], blk, col_width)
    got = []
    for turn in range(blk):
        moves = []
        for rr in range(rows):
            for bb in range(blk):
                moves.append((rr * blk + bb, (rows * bb + rr) // blk * blk + ((rr % blk) ^ turn)))
        piece = lax.dynamic_index_in_dim(pieces, (r % blk) ^ turn, 1, keepdims=False)
        got.append(lax.ppermute(piece, ("rows", "blk"), moves))
    got = jnp.stack(got)
    return [lax.dynamic_index_in_dim(got, b ^ part, 0, keepdims=False) for part in range(blk)]


def spread_columns(chunk):
    blk = lax.axis_size("blk")
    b = lax.axis_index("blk")
    parts = jnp.stack(
        [
            jnp.concatenate([chunk[:, 0:128], chunk[:, 256:320]], axis=1),
            jnp.concatenate([chunk[:, 128:256], chunk[:, 320:384]], axis=1),
            chunk[:, 384:576],
        ]
    )
    got = []
    for turn in range(3):
        moves = [((3 * to + turn) % blk, to) for to in range(blk)]
        to = (3 * (b - turn)) % blk
        piece = lax.dynamic_index_in_dim(parts, (3 * to + turn) // blk, 0, keepdims=False)
        got.append(lax.ppermute(piece, "blk", moves))
    return jnp.concatenate(got, axis=1)


def add_low(left, right):
    return (left.astype(F32) + right.astype(F32)).astype(BF16)


def local(
    tokens, seg_ids, valid_len, ln1_gain, ln1_bias, w_qkv, b_qkv, w_out, b_out,
    ln2_gain, ln2_bias, w_up, b_up, w_down, b_down, cotangent,
):
    rows = lax.axis_size("rows")
    blk = lax.axis_index("blk")
    seq = tokens.shape[1]
    per = seq // TILE
    width = D // 4
    hid = FF // 4
    meta = jnp.stack([blk, lax.axis_index("rows")]).astype(jnp.int32)
    low, high = angle_parts(4 * seq)
    tok_own, cot_own = tokens[0], cotangent[0]
    gain1, shift1, gain2, shift2 = (v[None] for v in (ln1_gain, ln1_bias, ln2_gain, ln2_bias))

    tok_near = swap(tok_own, "blk", 1)
    tok_far = swap(tok_own, "blk", 2)
    cot_near = swap(cot_own, "blk", 1)
    seg = [seg_ids[0]] + [swap(seg_ids[0], "blk", mask) for mask in (1, 2, 3)]

    *joined, w_own, b_own = project(
        0, meta, tok_own, gain1, shift1, low, high, w_qkv, b_qkv[None], None
    )
    cot_far = swap(after(cot_own, b_own), "blk", 2)

    def more(slot, m, tok, filled):
        return project(slot, m, tok, gain1, shift1, low, high, w_own, b_own, filled)

    joined = more(1, meta, tok_near, joined)
    mlp_args = (gain2, shift2, w_up, b_up[None], w_down, w_out)
    meta = after(meta, joined[0])
    first = feed_forward(
        0, meta, (tok_own, tok_near), (cot_own, cot_near), *mlp_args, None, rows
    )
    meta = after(meta, first[3])
    tok_last = swap(tok_far, "blk", 1)
    joined = more(2, meta, tok_far, joined)

    seg_all = jnp.stack(seg)
    pos = (jnp.arange(4, dtype=jnp.int32) ^ blk)[:, None] * seq + jnp.arange(seq, dtype=jnp.int32)
    starts = jnp.zeros_like(seg_all)
    for number in (1, 2, 3):
        starts = jnp.where(seg_all == number, jnp.sum(seg_all < number), starts)
    starts = jnp.where(pos < valid_len[0], starts, pos).astype(jnp.int32)
    starts = starts.reshape(4 * per, 1, TILE)
    tile_at = jnp.arange(4 * per, dtype=jnp.int32)
    tile_slot = (tile_at // per ^ blk) * per + tile_at % per
    lo = starts[:, 0, 0][tile_slot] // TILE

    query, keys, values = more(3, meta, tok_last, joined)
    toks = (tok_own, tok_near, tok_far, tok_last)

    attended = attend(0, meta, lo, query, keys, values, starts, per, None)
    cot_far = after(cot_far, attended[1])
    cot_last = swap(cot_far, "blk", 1)
    cots = (cot_own, cot_near, cot_far, cot_last)
    meta = after(meta, cot_far)
    attn, lse = attend(2, meta, lo, query, keys, values, starts, per, attended)

    meta = after(meta, lse)
    second = feed_forward(1, meta, toks[2:], cots[2:], *mlp_args, first, rows)
    mlp_part, e_mlp, grad_vec, gb_up, g_ln2, s_ln2 = second[:6]
    up_keep, up_send = chunks_of(*second[6:8], rows)
    down_keep, down_send = chunks_of(*second[8:10], rows)
    up_got = swap(up_send, "rows", 1)
    meta = after(meta, gb_up)
    *out_parts, wo_keep, wo_send = output(meta, attn, mlp_part, cots, w_out, rows)
    wo_keep, wo_send = chunks_of(wo_keep, wo_send, rows)
    down_got = swap(after(down_send, wo_send), "rows", 1)
    wo_got = swap(wo_send, "rows", 1)
    out_near = swap(out_parts[1], "blk", 1)
    out_last = swap(out_parts[3], "blk", 1)

    meta = after(meta, wo_send)
    back_args = (query, keys, values, attn, grad_vec, starts, lse, low, high, per)
    back = attend_back(3, meta, lo, *back_args, None)

    out_send = add_low(out_parts[2], after(out_last, back[1]))
    out_far = swap(out_send, "blk", 2)
    up_parts = add_pair(up_keep, after(up_got, back[1]))
    up = exchange(up_parts)
    meta = after(meta, out_send, up_parts)
    grad_joined = attend_back(1, meta, lo, *back_args, back)[0]

    down_parts = add_pair(down_keep, after(down_got, grad_joined))
    wo_parts = add_pair(wo_keep, after(wo_got, grad_joined))
    down = exchange(down_parts)
    wo = exchange(wo_parts)
    meta = after(meta, down_parts, wo_parts)
    sums = (jnp.zeros((1, D), F32),) * 2
    e_last, e_far, *sums = norm_grad(
        (3, 2), meta, grad_joined, e_mlp, toks, gain1, w_own, sums
    )
    e_got = swap(e_last, "blk", 1)
    meta = after(meta, e_far)
    qkv_keep, qkv_send, gb_joined = joined_weight(meta, grad_joined, toks, gain1, shift1, rows)
    qkv_keep, qkv_send = chunks_of(qkv_keep, qkv_send, rows)
    qkv_got = swap(qkv_send, "rows", 1)
    e_send = add_low(e_far, after(e_got, gb_joined))
    e_across = swap(e_send, "blk", 2)
    meta = after(meta, e_send, qkv_send)
    e_near, e_own, g_ln1, s_ln1 = norm_grad(
        (1, 0), meta, grad_joined, e_mlp, toks, gain1, w_own, sums
    )
    e_got = swap(e_near, "blk", 1)

    up_wide = cot_own.astype(F32)
    own_sums = jnp.concatenate(
        [gb_up, g_ln1, s_ln1, g_ln2, s_ln2, jnp.sum(up_wide, axis=0)[None], gb_joined], axis=1
    )
    own_sums = own_sums + swap(own_sums, "rows", 1)
    qkv_parts = add_pair(qkv_keep, qkv_got)
    qkv = exchange(qkv_parts)
    own_sums = exchange([own_sums] * (rows // 2))
    qkv = spread_columns(qkv.astype(BF16))
    all_sums = jnp.concatenate([own_sums] + [swap(own_sums, "blk", mask) for mask in (1, 2, 3)])
    true = jnp.take(all_sums, jnp.arange(4) ^ blk, axis=0)
    gb_up_all = true[:, :hid].reshape(FF)
    norm_sums = jnp.sum(all_sums[:, hid : hid + 5 * D], axis=0).reshape(5, D)
    gj = true[:, hid + 5 * D :]
    gb_qkv = jnp.concatenate(
        [
            jnp.concatenate([gj[:, 0:128], gj[:, 256:320]], axis=1).reshape(D),
            jnp.concatenate([gj[:, 128:256], gj[:, 320:384]], axis=1).reshape(D),
            gj[:, 384:576].reshape(D),
        ]
    )

    lower = spread_rows(jnp.concatenate([down, wo], axis=0).astype(BF16), width)
    cut = hid // rows
    down = jnp.concatenate([part[:cut] for part in lower]).astype(F32)
    out_w = jnp.concatenate([part[cut:] for part in lower]).astype(F32)

    wide = tok_own.astype(F32)
    summed = out_parts[0].astype(F32) + out_near.astype(F32) + out_far.astype(F32)
    result = (wide + (b_out + b_down) + summed).astype(BF16)[None]

    e_sum = e_own.astype(F32) + e_got.astype(F32) + e_across.astype(F32)
    center = wide - jnp.mean(wide, axis=-1, keepdims=True)
    rate = lax.rsqrt(jnp.mean(center * center, axis=-1, keepdims=True) + EPS)
    normed = center * rate
    grad = rate * (
        e_sum
        - jnp.mean(e_sum, axis=-1, keepdims=True)
        - normed * jnp.mean(e_sum * normed, axis=-1, keepdims=True)
    )
    grad_tokens = (up_wide + grad).astype(BF16)[None]
    return (
        result,
        grad_tokens,
        qkv.astype(F32),
        out_w,
        up,
        down,
        gb_qkv,
        norm_sums[4],
        gb_up_all,
        norm_sums[4],
        norm_sums[0],
        norm_sums[1],
        norm_sums[2],
        norm_sums[3],
    )


def solution(mesh):
    split = P("rows", "blk")
    in_specs = (
        P("rows", "blk", None),
        split,
        P("rows"),
        *(P(),) * 12,
        P("rows", "blk", None),
    )
    out_specs = (
        P("rows", "blk", None),
        P("rows", "blk", None),
        *(split,) * 4,
        *(P(),) * 8,
    )
    return jax.shard_map(local, mesh=mesh, in_specs=in_specs, out_specs=out_specs, check_vma=False)
```

time: 350 us -> 314 us (0.90)
  blocking collectives: 42.9 us -> 0 us
  Pallas kernels: 126 us -> 158 us
  waiting for transfers between devices: 71.7 us -> 57.2 us
  starting transfers between devices: 44.7 us -> 59 us
  local copies, waits for them, and re-layouts: 31.2 us -> 17.6 us
  other arithmetic: 30.3 us -> 19.8 us
    psum x1 -> x0, blocking collectives: 42.9 us -> none  [local(): lax.psum((gb_qkv, jnp.sum(up_wide, axis=0), gb_up_all, g_ln1[0], s_ln1[0]...]
    pallas_call x7 -> x11, Pallas kernels: 85 us -> 114 us  [the longest x2 38.9 us: attend_back(): pl.pallas_call(partial(attend_back_kernel, top, per), out_shape=[jax.Shap...]
    ppermute x24 -> x38, starting transfers between devices: 24.9 us -> 45.1 us  [swap(): return lax.ppermute(value, axis, [(i, i ^ mask) for i in range(size)])]
    ppermute x24 -> x38, waiting for transfers between devices: 71.6 us -> 57.2 us  [swap(): return lax.ppermute(value, axis, [(i, i ^ mask) for i in range(size)])]
    dynamic_slice x6 -> x5, local copies, waits for them, and re-layouts: 7.88 us -> 1.02 us  [spread_rows(): piece = lax.dynamic_index_in_dim(pieces, r % blk ^ turn, 1, keepdims=False)]
    slice x5, local copies, waits for them, and re-layouts: 6.18 us -> 0.69 us  [the longest x1 0.61 us: local(): norm_sums[3]]
    convert_element_type x10 -> x7, other arithmetic: 7.56 us -> 2.41 us  [the longest x4 1.05 us: add_pair(): (keep[i].astype(F32) + got[i].astype(F32)).astype(BF16)]
    squeeze x9 -> x0, local copies, waits for them, and re-layouts: 4.63 us -> none  [the longest x8 4.6 us: reduce_rows(): other = lax.dynamic_index_in_dim(value, 1 - bit, 1, keepdims=False)]
  transfers between devices with their start and end apart: 31 -> 45, of which waited for: 10 -> 15; matrix products, arithmetic and copies ran while one was open for 14% -> 9% of each run, Pallas kernels for 16% -> 45%
where the time goes in v2:
time: 314 us
  Pallas kernels  158 us (50%)
  starting transfers between devices  59 us (19%)
  waiting for transfers between devices  57.2 us (18%)
  other arithmetic  19.8 us (6%)
  local copies, waits for them, and re-layouts  17.6 us (6%)
    ppermute x38, waiting for transfers between devices, swap(): return lax.ppermute(value, axis, [(i, i ^ mask) for i in range(size)])  57.2 us
    ppermute x38, starting transfers between devices, swap(): return lax.ppermute(value, axis, [(i, i ^ mask) for i in range(size)])  45.1 us
    pallas_call x2, Pallas kernels, attend_back(): pl.pallas_call(partial(attend_back_kernel, top, per), out_shape=[jax.Shap...  38.9 us
    pallas_call x2, Pallas kernels, feed_forward(): pl.pallas_call(partial(mlp_kernel, before is not None), out_shape=[jax.Sh...  33.2 us
    pallas_call x2, Pallas kernels, attend(): pl.pallas_call(partial(attend_kernel, base, per), out_shape=[jax.ShapeDty...  31 us
    pallas_call x4, Pallas kernels, project(): pl.pallas_call(partial(qkv_kernel, slot), out_shape=outs, grid_spec=pltpu...  17.9 us
    pallas_call x2, Pallas kernels, norm_grad(): pl.pallas_call(partial(norm_grad_kernel, slots, per), out_shape=[jax.Shap...  14.7 us
    pallas_call x1, Pallas kernels, joined_weight(): pl.pallas_call(partial(joined_weight_kernel, per), out_shape=[*(jax.Shape...  11.1 us
  transfers between devices with their start and end apart: 45, of which 15 were waited for; matrix products, arithmetic and copies ran while one was open for 9% of the time, Pallas kernels for 45%

profile of v2, /device:TPU:0, one launch (start us, length us, event | category | flops | bytes accessed | tf_op | source)
XLA Modules:
  0.0 313.5 jit_solution(9852023436551060148)
XLA Ops:
  1.2 2.6 collective-permute-start.6
  12.5 5.2 %qkv_0.1 = (bf16[2048,192]{1,0:T(8,128)(2,1)}, bf16[2048,192]{1,0:T(8,128)(2,1)}, bf16[2048,192]{1,0:T(8,128)(2,1)}, bf16[768,576]{1,0:T(8,128)(2,1)}, f32[1,576]{1,0:T(1,128)}) custom-call(s32[2]{0:T(128)} %pad_add_fusion.1.meta, bf16[512,768]{1,0:T(8,128)(2,1)} %bitcast.102, f32[1,768]{1,0:T(1,128)} %broadcast_in_dim.61.gain.refs_6_, ...), custom_call_target="tpu_custom_call" | custom-call | flops 452984832 | bytes 1572864 | tf_op jit(solution)/shard_map/qkv_0/pallas_call | solution.py:169
  19.7 2.5 collective-permute-done.4
  29.2 4.3 %qkv_1.1 = (bf16[2048,192]{1,0:T(8,128)(2,1)}, bf16[2048,192]{1,0:T(8,128)(2,1)}, bf16[2048,192]{1,0:T(8,128)(2,1)}) custom-call(s32[2]{0:T(128)} %pad_add_fusion.1.meta, bf16[512,768]{1,0:T(8,128)(2,1)} %copy-done.5, f32[1,768]{1,0:T(1,128)} %broadcast_in_dim.61.gain.refs_6_, ...), custom_call_target="tpu_custom_call", output_to_operand_aliasing={{0}: (8, {}), {1}: (9, {}), {2}: (10, {})} | custom-call | flops 452984832 | bytes 1572864 | tf_op jit(solution)/shard_map/qkv_1/pallas_call | solution.py:169
  33.5 15.9 %mlp_0.1 = (bf16[2048,768]{1,0:T(8,128)(2,1)}, bf16[2048,768]{1,0:T(8,128)(2,1)}, bf16[2048,192]{1,0:T(8,128)(2,1)}, f32[1,768]{1,0:T(1,128)}, f32[1,768]{1,0:T(...) custom-call(s32[2]{0:T(128)} %pad_add_fusion.1.meta, bf16[512,768]{1,0:T(8,128)(2,1)} %bitcast.103, ...), custom_call_target="tpu_custom_call" | custom-call | flops 7247757312 | bytes 7864320 | tf_op jit(solution)/shard_map/mlp_0/pallas_call | solution.py:318
  49.4 4.3 %qkv_2.1 = (bf16[2048,192]{1,0:T(8,128)(2,1)}, bf16[2048,192]{1,0:T(8,128)(2,1)}, bf16[2048,192]{1,0:T(8,128)(2,1)}) custom-call(s32[2]{0:T(128)} %pad_add_fusion.1.meta, bf16[512,768]{1,0:T(8,128)(2,1)} %copy-done.6, f32[1,768]{1,0:T(1,128)} %broadcast_in_dim.61.gain.refs_6_, ...), custom_call_target="tpu_custom_call", output_to_operand_aliasing={{0}: (8, {}), {1}: (9, {}), {2}: (10, {})} | custom-call | flops 452984832 | bytes 1572864 | tf_op jit(solution)/shard_map/qkv_2/pallas_call | solution.py:169
  54.5 4.2 %qkv_3.1 = (bf16[2048,192]{1,0:T(8,128)(2,1)}, bf16[2048,192]{1,0:T(8,128)(2,1)}, bf16[2048,192]{1,0:T(8,128)(2,1)}) custom-call(s32[2]{0:T(128)} %pad_add_fusion.1.meta, bf16[512,768]{1,0:T(8,128)(2,1)} %copy-done.7, f32[1,768]{1,0:T(1,128)} %broadcast_in_dim.61.gain.refs_6_, ...), custom_call_target="tpu_custom_call", output_to_operand_aliasing={{0}: (8, {}), {1}: (9, {}), {2}: (10, {})} | custom-call | flops 452984832 | bytes 1572864 | tf_op jit(solution)/shard_map/qkv_3/pallas_call | solution.py:169
  58.7 14.6 %attend_0.1 = (bf16[2048,192]{1,0:T(8,128)(2,1)}, f32[3,8,1,256]{3,2,1,0:T(1,128)}) custom-call(s32[2]{0:T(128)} %pad_add_fusion.1.meta, s32[8]{0:T(128)} %and_select_fusion.lo, bf16[2048,192]{1,0:T(8,128)(2,1)} %get-tuple-element.104.q_ref, bf16[2048,192]{1,0:T(8,128)(2,1)} %get-tuple-element.105.k_ref, bf16[2048,192]{1,0:T(8,128)(2,1)} %get-tuple-element.106.v_ref, ...), custom_call_target="tpu_custom_call" | custom-call | flops 2013265920 | bytes 3145728 | tf_op jit(solution)/shard_map/attend_0/pallas_call | solution.py:449
  74.2 16.4 %attend_2.1 = (bf16[2048,192]{1,0:T(8,128)(2,1)}, f32[3,8,1,256]{3,2,1,0:T(1,128)}) custom-call(s32[2]{0:T(128)} %pad_add_fusion.1.meta, s32[8]{0:T(128)} %and_select_fusion.lo, bf16[2048,192]{1,0:T(8,128)(2,1)} %get-tuple-element.104.q_ref, bf16[2048,192]{1,0:T(8,128)(2,1)} %get-tuple-element.105.k_ref, ...), custom_call_target="tpu_custom_call", output_to_operand_aliasing={{0}: (6, {}), {1}: (7, {})} | custom-call | flops 2013265920 | bytes 3145728 | tf_op jit(solution)/shard_map/attend_2/pallas_call | solution.py:449
  91.5 17.4 %mlp_1.1 = (bf16[2048,768]{1,0:T(8,128)(2,1)}, bf16[2048,768]{1,0:T(8,128)(2,1)}, bf16[2048,192]{1,0:T(8,128)(2,1)}, f32[1,768]{1,0:T(1,128)}, f32[1,768]{1,0:T(...) custom-call(s32[2]{0:T(128)} %pad_add_fusion.1.meta, ...), custom_call_target="tpu_custom_call", output_to_operand_aliasing={{0}: (16, {}), {1}: (17, {}), {2}: (18, {})} | custom-call | flops 7247757312 | bytes 7864320 | tf_op jit(solution)/shard_map/mlp_1/pallas_call | solution.py:318
  109.0 10.9 %output.1 = (bf16[512,768]{1,0:T(8,128)(2,1)}, bf16[512,768]{1,0:T(8,128)(2,1)}, bf16[512,768]{1,0:T(8,128)(2,1)}, bf16[512,768]{1,0:T(8,128)(2,1)}, bf16[4,24,7...) custom-call(s32[2]{0:T(128)} %pad_add_fusion.1.meta, bf16[2048,192]{1,0:T(8,128)(2,1)} %get-tuple-element.122.o_ref, ...), custom_call_target="tpu_custom_call" | custom-call | flops 1207959552 | bytes 9437184 | tf_op jit(solution)/shard_map/output/pallas_call | solution.py:643
  120.1 19.8 %attend_back_3.1 = (bf16[2048,576]{1,0:T(8,128)(2,1)}, f32[2048,192]{1,0:T(8,128)}, f32[2048,192]{1,0:T(8,128)}) custom-call(s32[2]{0:T(128)} %pad_add_fusion.1.meta, s32[8]{0:T(128)} %and_select_fusion.lo, bf16[2048,192]{1,0:T(8,128)(2,1)} %get-tuple-element.104.q_ref, bf16[2048,192]{1,0:T(8,128)(2,1)} %get-tuple-element.105.k_ref, ...), custom_call_target="tpu_custom_call" | custom-call | flops 5033164800 | bytes 6291456 | tf_op jit(solution)/shard_map/attend_back_3/pallas_call | solution.py:570
  140.7 5.9 %collective-permute-start.36 = (bf16[96,768]{1,0:T(8,128)(2,1)}, bf16[96,768]{1,0:T(8,128)(2,1)}, u32[]{:S(2)}, u32[]{:S(2)}) collective-permute-start(bf16[96,768]{1,0:T(8,128)(2,1)} %get-tuple-element.208), channel_id=1, source_target_pairs={{0,16},{4,20},{8,24},{12,28},{16,0},{20,4},{24,8},{28,12},{1,17},{... | collective-permute-start | bytes 442376 | tf_op jit(solution)/shard_map/ppermute | solution.py:796
  151.7 7.2 %collective-permute-done.37 = bf16[96,768]{1,0:T(8,128)(2,1)} collective-permute-done((bf16[96,768]{1,0:T(8,128)(2,1)}, bf16[96,768]{1,0:T(8,128)(2,1)}, u32[]{:S(2)}, u32[]{:S(2)}) %collective-permute-start.37) | collective-permute-done | bytes 147488 | tf_op jit(solution)/shard_map/ppermute | solution.py:796
  160.9 19.2 %attend_back_1.1 = (bf16[2048,576]{1,0:T(8,128)(2,1)}, f32[2048,192]{1,0:T(8,128)}, f32[2048,192]{1,0:T(8,128)}) custom-call(s32[2]{0:T(128)} %pad_add_fusion.1.meta, s32[8]{0:T(128)} %and_select_fusion.lo, bf16[2048,192]{1,0:T(8,128)(2,1)} %get-tuple-element.104.q_ref, ...), custom_call_target="tpu_custom_call", output_to_operand_aliasing={{0}: (13, {})} | custom-call | flops 5033164800 | bytes 6291456 | tf_op jit(solution)/shard_map/attend_back_1/pallas_call | solution.py:570
  180.1 2.9 collective-permute-start.28
  190.5 4.0 %collective-permute-done.25 = bf16[96,768]{1,0:T(8,128)(2,1)S(1)} collective-permute-done((bf16[96,768]{1,0:T(8,128)(2,1)S(1)}, bf16[96,768]{1,0:T(8,128)(2,1)S(1)}, u32[]{:S(2)}, u32[]{:S(2)}) %collective-permute-start.25) | collective-permute-done | bytes 147488 | tf_op jit(solution)/shard_map/ppermute | solution.py:796
  194.5 5.6 %collective-permute-done.26 = bf16[96,768]{1,0:T(8,128)(2,1)S(1)} collective-permute-done((bf16[96,768]{1,0:T(8,128)(2,1)S(1)}, bf16[96,768]{1,0:T(8,128)(2,1)S(1)}, u32[]{:S(2)}, u32[]{:S(2)}) %collective-permute-start.26) | collective-permute-done | bytes 147488 | tf_op jit(solution)/shard_map/ppermute | solution.py:796
  200.8 7.2 %norm_grad_3.1 = (bf16[512,768]{1,0:T(8,128)(2,1)}, bf16[512,768]{1,0:T(8,128)(2,1)}, f32[1,768]{1,0:T(1,128)}, f32[1,768]{1,0:T(1,128)}) custom-call(s32[2]{0:T(128)} %pad_add_fusion.1.meta, bf16[2048,576]{1,0:T(8,128)(2,1)} %get-tuple-element.142.refs_0_.refs_1_.gj_ref, bf16[2048,576]{1,0:T(8,128)(2,1)} %get-tuple-element.142.refs_0_.refs_1_.gj_ref, ...), custom_call_target="tpu_custom_call" | custom-call | flops 905969664 | bytes 6291456 | tf_op jit(solution)/shard_map/norm_grad_3/pallas_call | solution.py:701
  209.8 3.8 %collective-permute-start.32 = (bf16[120,192]{0,1:T(8,128)(2,1)S(1)}, bf16[120,192]{0,1:T(8,128)(2,1)S(1)}, u32[]{:S(2)}, u32[]{:S(2)}) collective-permute-start(bf16[120,192]{0,1:T(8,128)(2,1)S(1)} %bitcast.115), channel_id=1, source_target_pairs={{0,1},{1,9},{2,17},{3,25},{4,0},{5,8},{6,16},{7,24},{8,3},{9,11},{... | collective-permute-start | bytes 138248 | tf_op jit(solution)/shard_map/ppermute | solution.py:823
  213.7 2.5 collective-permute-start.33
  216.4 2.5 collective-permute-start.34
  218.9 11.1 %joined_weight.1 = (bf16[4,96,576]{2,1,0:T(8,128)(2,1)}, bf16[4,96,576]{2,1,0:T(8,128)(2,1)}, f32[1,576]{1,0:T(1,128)}) custom-call(s32[2]{0:T(128)} %pad_add_fusion.1.meta, bf16[2048,576]{1,0:T(8,128)(2,1)} %get-tuple-element.142.refs_0_.refs_1_.gj_ref, bf16[512,768]{1,0:T(8,128)(2,1)} %bitcast.104, bf16[512,768]{1,0:T(8,128)(2,1)} %copy-done.5, ...), custom_call_target="tpu_custom_call" | custom-call | flops 1811939328 | bytes 6291456 | tf_op jit(solution)/shard_map/joined_weight/pallas_call | solution.py:764
  234.6 9.4 %collective-permute-done.18 = bf16[4,96,576]{2,1,0:T(8,128)(2,1)S(1)} collective-permute-done((bf16[4,96,576]{2,1,0:T(8,128)(2,1)}, bf16[4,96,576]{2,1,0:T(8,128)(2,1)S(1)}, u32[]{:S(2)}, u32[]{:S(2)}) %collective-permute-start.18) | collective-permute-done | bytes 442400 | tf_op jit(solution)/shard_map/ppermute | solution.py:796
  245.3 3.0 collective-permute-start.20
  252.8 4.9 %collective-permute-done.20 = bf16[96,576]{1,0:T(8,128)(2,1)S(1)} collective-permute-done((bf16[96,576]{1,0:T(8,128)(2,1)S(1)}, bf16[96,576]{1,0:T(8,128)(2,1)S(1)}, u32[]{:S(2)}, u32[]{:S(2)}) %collective-permute-start.20) | collective-permute-done | bytes 110624 | tf_op jit(solution)/shard_map/ppermute | solution.py:796
  261.3 7.5 %norm_grad_1.1 = (bf16[512,768]{1,0:T(8,128)(2,1)}, bf16[512,768]{1,0:T(8,128)(2,1)}, f32[1,768]{1,0:T(1,128)}, f32[1,768]{1,0:T(1,128)}) custom-call(s32[2]{0:T(128)} %pad_add_fusion.1.meta, bf16[2048,576]{1,0:T(8,128)(2,1)} %get-tuple-element.142.refs_0_.refs_1_.gj_ref, bf16[2048,576]{1,0:T(8,128)(2,1)} %get-tuple-element.142.refs_0_.refs_1_.gj_ref, ...), custom_call_target="tpu_custom_call" | custom-call | flops 905969664 | bytes 6291456 | tf_op jit(solution)/shard_map/norm_grad_1/pallas_call | solution.py:701
  271.3 14.2 %collective-permute-done.17 = bf16[512,768]{1,0:T(8,128)(2,1)S(1)} collective-permute-done((bf16[512,768]{1,0:T(8,128)(2,1)S(1)}, bf16[512,768]{1,0:T(8,128)(2,1)S(1)}, u32[]{:S(2)}, u32[]{:S(2)}) %collective-permute-start.17) | collective-permute-done | bytes 786464 | tf_op jit(solution)/shard_map/ppermute | solution.py:796
  287.6 3.3 %convert_reduce_fusion.1 = (f32[768]{0:T(1024)S(1)}, bf16[1,512,768]{2,1,0:T(8,128)(2,1)}, bf16[1,512,768]{2,1,0:T(8,128)(2,1)}) fusion(bf16[1,512,768]{2,1,0:T(8,128)(2,1)S(1)} %copy-done.3, f32[512]{0:T(512)S(1)} %get-tuple-element.246, f32[512]{0:T(512)S(1)} %broadcast_multiply_fusion.2, bf16[1,512,768]{2,1,0:T(8,128)(2,1)S(1)} %copy-done.1, ...), kind=kLoop, calls=%fused_computation.5 | loop fusion | flops 9436416 | bytes 7878656 | tf_op jit(solution)/shard_map/reduce_sum | solution.py:959
  292.2 2.7 collective-permute-done.38
  295.9 3.3 %collective-permute-start.40 = (f32[1,5184]{1,0:T(1,128)S(1)}, f32[1,5184]{1,0:T(1,128)S(1)}, u32[]{:S(2)}, u32[]{:S(2)}) collective-permute-start(f32[1,5184]{1,0:T(1,128)S(1)} %add.386), channel_id=1, source_target_pairs={{0,16},{4,20},{8,24},{12,28},{16,0},{20,4},{24,8},{28,12},{1,17},{... | collective-permute-start | bytes 62216 | tf_op jit(solution)/shard_map/ppermute | solution.py:796
  300.1 3.7 %collective-permute-start.24 = (bf16[96,192]{1,0:T(8,128)(2,1)S(1)}, bf16[96,192]{1,0:T(8,128)(2,1)S(1)}, u32[]{:S(2)}, u32[]{:S(2)}) collective-permute-start(bf16[96,192]{1,0:T(8,128)(2,1)S(1)} %get-tuple-element.231), channel_id=1, source_target_pairs={{2,0},{1,1},{0,2},{3,3},{6,4},{5,5},{4,6},{7,7},{10,8},{9,9},{8,10... | collective-permute-start | bytes 110600 | tf_op jit(solution)/shard_map/ppermute | solution.py:843
  (225 shorter events, 69.7 us)
Async XLA Ops:
  0.6 27.7 %collective-permute-start = (bf16[512,768]{1,0:T(8,128)(2,1)}, bf16[512,768]{1,0:T(8,128)(2,1)S(1)}, u32[]{:S(2)}, u32[]{:S(2)}) collective-permute-start(bf16[512,768]{1,0:T(8,128)(2,1)} %bitcast.100), channel_id=1, source_target_pairs={{0,1},{1,0},{2,3},{3,2},{4,5},{5,4},{6,7},{7,6},{8,9},{9,8},{10,11... | collective-permute-start | bytes 2359304 | tf_op jit(solution)/shard_map/ppermute | solution.py:796
  1.2 26.4 %collective-permute-start.6 = (bf16[512,768]{1,0:T(8,128)(2,1)}, bf16[512,768]{1,0:T(8,128)(2,1)S(1)}, u32[]{:S(2)}, u32[]{:S(2)}) collective-permute-start(bf16[512,768]{1,0:T(8,128)(2,1)} %bitcast.101), channel_id=1, source_target_pairs={{0,2},{1,3},{2,0},{3,1},{4,6},{5,7},{6,4},{7,5},{8,10},{9,11},{10,... | collective-permute-start | bytes 2359304 | tf_op jit(solution)/shard_map/ppermute | solution.py:796
  3.9 18.2 %collective-permute-start.4 = (s32[512]{0:T(512)}, s32[512]{0:T(512)S(1)}, u32[]{:S(2)}, u32[]{:S(2)}) collective-permute-start(s32[512]{0:T(512)} %bitcast.119), channel_id=1, source_target_pairs={{0,2},{1,3},{2,0},{3,1},{4,6},{5,7},{6,4},{7,5},{8,10},{9,11},{10,... | collective-permute-start | bytes 6152 | tf_op jit(solution)/shard_map/ppermute | solution.py:796
  4.2 29.3 %collective-permute-start.1 = (bf16[512,768]{1,0:T(8,128)(2,1)}, bf16[512,768]{1,0:T(8,128)(2,1)}, u32[]{:S(2)}, u32[]{:S(2)}) collective-permute-start(bf16[512,768]{1,0:T(8,128)(2,1)} %bitcast.106), channel_id=1, source_target_pairs={{0,1},{1,0},{2,3},{3,2},{4,5},{5,4},{6,7},{7,6},{8,9},{9,8},{10,11... | collective-permute-start | bytes 2359304 | tf_op jit(solution)/shard_map/ppermute | solution.py:796
  10.6 13.3 %collective-permute-start.5 = (s32[512]{0:T(512)}, s32[512]{0:T(512)S(1)}, u32[]{:S(2)}, u32[]{:S(2)}) collective-permute-start(s32[512]{0:T(512)} %bitcast.120), channel_id=1, source_target_pairs={{0,3},{1,2},{2,1},{3,0},{4,7},{5,6},{6,5},{7,4},{8,11},{9,10},{10,... | collective-permute-start | bytes 6152 | tf_op jit(solution)/shard_map/ppermute | solution.py:796
  22.1 51.2 %collective-permute-start.2 = (bf16[512,768]{1,0:T(8,128)(2,1)S(1)}, bf16[512,768]{1,0:T(8,128)(2,1)}, u32[]{:S(2)}, u32[]{:S(2)}) collective-permute-start(bf16[512,768]{1,0:T(8,128)(2,1)S(1)} %bitcast.109), channel_id=1, source_target_pairs={{0,2},{1,3},{2,0},{3,1},{4,6},{5,7},{6,4},{7,5},{8,10},{9,11},{10,... | collective-permute-start | bytes 2359304 | tf_op jit(solution)/shard_map/ppermute | solution.py:796
  27.6 26.0 %collective-permute-start.7 = (bf16[512,768]{1,0:T(8,128)(2,1)S(1)}, bf16[512,768]{1,0:T(8,128)(2,1)S(1)}, u32[]{:S(2)}, u32[]{:S(2)}) collective-permute-start(bf16[512,768]{1,0:T(8,128)(2,1)S(1)} %collective-permute-done.6.x_ref.refs_0_.refs_5_.t2), channel_id=1, source_target_pairs={{0,1},{1,0},{2,3},{3,2},{4,5},{5,4},{6,7},{7,6},{8,9},{9,8},{10,11... | collective-permute-start | bytes 2359304 | tf_op jit(solution)/shard_map/ppermute | solution.py:796
  73.3 17.3 %collective-permute-start.8 = (bf16[512,768]{1,0:T(8,128)(2,1)}, bf16[512,768]{1,0:T(8,128)(2,1)S(1)}, u32[]{:S(2)}, u32[]{:S(2)}) collective-permute-start(bf16[512,768]{1,0:T(8,128)(2,1)} %collective-permute-done.2.refs_2_.c2), channel_id=1, source_target_pairs={{0,1},{1,0},{2,3},{3,2},{4,5},{5,4},{6,7},{7,6},{8,9},{9,8},{10,11... | collective-permute-start | bytes 2359304 | tf_op jit(solution)/shard_map/ppermute | solution.py:796
  108.9 31.0 %collective-permute-start.12 = (bf16[4,96,768]{2,1,0:T(8,128)(2,1)}, bf16[4,96,768]{2,1,0:T(8,128)(2,1)S(1)}, u32[]{:S(2)}, u32[]{:S(2)}) collective-permute-start(bf16[4,96,768]{2,1,0:T(8,128)(2,1)} %get-tuple-element.134), channel_id=1, source_target_pairs={{0,4},{4,0},{8,12},{12,8},{16,20},{20,16},{24,28},{28,24},{1,5},{5... | collective-permute-start | bytes 1769480 | tf_op jit(solution)/shard_map/ppermute | solution.py:796
  119.9 40.8 %collective-permute-start.10 = (bf16[512,768]{1,0:T(8,128)(2,1)}, bf16[512,768]{1,0:T(8,128)(2,1)S(1)}, u32[]{:S(2)}, u32[]{:S(2)}) collective-permute-start(bf16[512,768]{1,0:T(8,128)(2,1)} %get-tuple-element.127), channel_id=1, source_target_pairs={{0,1},{1,0},{2,3},{3,2},{4,5},{5,4},{6,7},{7,6},{8,9},{9,8},{10,11... | collective-permute-start | bytes 2359304 | tf_op jit(solution)/shard_map/ppermute | solution.py:796
  140.7 9.1 %collective-permute-start.35 = (bf16[96,768]{1,0:T(8,128)(2,1)S(1)}, bf16[96,768]{1,0:T(8,128)(2,1)S(1)}, u32[]{:S(2)}, u32[]{:S(2)}) collective-permute-start(bf16[96,768]{1,0:T(8,128)(2,1)S(1)} %get-tuple-element.206), channel_id=1, source_target_pairs={{0,8},{4,12},{8,0},{12,4},{16,24},{20,28},{24,16},{28,20},{1,9},{5... | collective-permute-start | bytes 442376 | tf_op jit(solution)/shard_map/ppermute | solution.py:796
  140.7 10.9 %collective-permute-start.36 = (bf16[96,768]{1,0:T(8,128)(2,1)}, bf16[96,768]{1,0:T(8,128)(2,1)}, u32[]{:S(2)}, u32[]{:S(2)}) collective-permute-start(bf16[96,768]{1,0:T(8,128)(2,1)} %get-tuple-element.208), channel_id=1, source_target_pairs={{0,16},{4,20},{8,24},{12,28},{16,0},{20,4},{24,8},{28,12},{1,17},{... | collective-permute-start | bytes 442376 | tf_op jit(solution)/shard_map/ppermute | solution.py:796
  146.6 12.3 %collective-permute-start.37 = (bf16[96,768]{1,0:T(8,128)(2,1)}, bf16[96,768]{1,0:T(8,128)(2,1)}, u32[]{:S(2)}, u32[]{:S(2)}) collective-permute-start(bf16[96,768]{1,0:T(8,128)(2,1)} %get-tuple-element.207), channel_id=1, source_target_pairs={{0,24},{4,28},{8,16},{12,20},{16,8},{20,12},{24,0},{28,4},{1,25},{... | collective-permute-start | bytes 442376 | tf_op jit(solution)/shard_map/ppermute | solution.py:796
  148.7 31.4 %collective-permute-start.14 = (bf16[4,24,768]{2,1,0:T(8,128)(2,1)}, bf16[4,24,768]{2,1,0:T(8,128)(2,1)S(1)}, u32[]{:S(2)}, u32[]{:S(2)}) collective-permute-start(bf16[4,24,768]{2,1,0:T(8,128)(2,1)} %get-tuple-element.128), channel_id=1, source_target_pairs={{0,4},{4,0},{8,12},{12,8},{16,20},{20,16},{24,28},{28,24},{1,5},{5... | collective-permute-start | bytes 442376 | tf_op jit(solution)/shard_map/ppermute | solution.py:796
  149.9 35.6 %collective-permute-start.13 = (bf16[4,96,768]{2,1,0:T(8,128)(2,1)}, bf16[4,96,768]{2,1,0:T(8,128)(2,1)S(1)}, u32[]{:S(2)}, u32[]{:S(2)}) collective-permute-start(bf16[4,96,768]{2,1,0:T(8,128)(2,1)} %get-tuple-element.139), channel_id=1, source_target_pairs={{0,4},{4,0},{8,12},{12,8},{16,20},{20,16},{24,28},{28,24},{1,5},{5... | collective-permute-start | bytes 1769480 | tf_op jit(solution)/shard_map/ppermute | solution.py:796
  151.7 135.9 %collective-permute-start.9 = (bf16[512,768]{1,0:T(8,128)(2,1)}, bf16[512,768]{1,0:T(8,128)(2,1)}, u32[]{:S(2)}, u32[]{:S(2)}) collective-permute-start(bf16[512,768]{1,0:T(8,128)(2,1)} %get-tuple-element.125), channel_id=1, source_target_pairs={{0,1},{1,0},{2,3},{3,2},{4,5},{5,4},{6,7},{7,6},{8,9},{9,8},{10,11... | collective-permute-start | bytes 2359304 | tf_op jit(solution)/shard_map/ppermute | solution.py:796
  183.1 7.2 %collective-permute-start.30 = (bf16[24,768]{1,0:T(8,128)(2,1)S(1)}, bf16[24,768]{1,0:T(8,128)(2,1)S(1)}, u32[]{:S(2)}, u32[]{:S(2)}) collective-permute-start(bf16[24,768]{1,0:T(8,128)(2,1)S(1)} %get-tuple-element.216), channel_id=1, source_target_pairs={{0,24},{4,28},{8,16},{12,20},{16,8},{20,12},{24,0},{28,4},{1,25},{... | collective-permute-start | bytes 110600 | tf_op jit(solution)/shard_map/ppermute | solution.py:796
  185.5 8.9 %collective-permute-start.25 = (bf16[96,768]{1,0:T(8,128)(2,1)S(1)}, bf16[96,768]{1,0:T(8,128)(2,1)S(1)}, u32[]{:S(2)}, u32[]{:S(2)}) collective-permute-start(bf16[96,768]{1,0:T(8,128)(2,1)S(1)} %get-tuple-element.203), channel_id=1, source_target_pairs={{0,8},{4,12},{8,0},{12,4},{16,24},{20,28},{24,16},{28,20},{1,9},{5... | collective-permute-start | bytes 442376 | tf_op jit(solution)/shard_map/ppermute | solution.py:796
  186.7 13.4 %collective-permute-start.26 = (bf16[96,768]{1,0:T(8,128)(2,1)S(1)}, bf16[96,768]{1,0:T(8,128)(2,1)S(1)}, u32[]{:S(2)}, u32[]{:S(2)}) collective-permute-start(bf16[96,768]{1,0:T(8,128)(2,1)S(1)} %get-tuple-element.205), channel_id=1, source_target_pairs={{0,16},{4,20},{8,24},{12,28},{16,0},{20,4},{24,8},{28,12},{1,17},{... | collective-permute-start | bytes 442376 | tf_op jit(solution)/shard_map/ppermute | solution.py:796
  188.5 11.6 %collective-permute-start.27 = (bf16[96,768]{1,0:T(8,128)(2,1)S(1)}, bf16[96,768]{1,0:T(8,128)(2,1)S(1)}, u32[]{:S(2)}, u32[]{:S(2)}) collective-permute-start(bf16[96,768]{1,0:T(8,128)(2,1)S(1)} %get-tuple-element.204), channel_id=1, source_target_pairs={{0,24},{4,28},{8,16},{12,20},{16,8},{20,12},{24,0},{28,4},{1,25},{... | collective-permute-start | bytes 442376 | tf_op jit(solution)/shard_map/ppermute | solution.py:796
  209.0 21.1 %collective-permute-start.31 = (bf16[120,192]{0,1:T(8,128)(2,1)S(1)}, bf16[120,192]{0,1:T(8,128)(2,1)S(1)}, u32[]{:S(2)}, u32[]{:S(2)}) collective-permute-start(bf16[120,192]{0,1:T(8,128)(2,1)S(1)} %bitcast.117), channel_id=1, source_target_pairs={{0,0},{1,8},{2,16},{3,24},{4,1},{5,9},{6,17},{7,25},{8,2},{9,10},{... | collective-permute-start | bytes 138248 | tf_op jit(solution)/shard_map/ppermute | solution.py:823
  209.8 20.3 %collective-permute-start.32 = (bf16[120,192]{0,1:T(8,128)(2,1)S(1)}, bf16[120,192]{0,1:T(8,128)(2,1)S(1)}, u32[]{:S(2)}, u32[]{:S(2)}) collective-permute-start(bf16[120,192]{0,1:T(8,128)(2,1)S(1)} %bitcast.115), channel_id=1, source_target_pairs={{0,1},{1,9},{2,17},{3,25},{4,0},{5,8},{6,16},{7,24},{8,3},{9,11},{... | collective-permute-start | bytes 138248 | tf_op jit(solution)/shard_map/ppermute | solution.py:823
  213.7 18.2 %collective-permute-start.33 = (bf16[120,192]{0,1:T(8,128)(2,1)S(1)}, bf16[120,192]{0,1:T(8,128)(2,1)S(1)}, u32[]{:S(2)}, u32[]{:S(2)}) collective-permute-start(bf16[120,192]{0,1:T(8,128)(2,1)S(1)} %bitcast.114), channel_id=1, source_target_pairs={{0,2},{1,10},{2,18},{3,26},{4,3},{5,11},{6,19},{7,27},{8,0},{9,8},... | collective-permute-start | bytes 138248 | tf_op jit(solution)/shard_map/ppermute | solution.py:823
  216.4 15.5 %collective-permute-start.34 = (bf16[120,192]{0,1:T(8,128)(2,1)S(1)}, bf16[120,192]{0,1:T(8,128)(2,1)S(1)}, u32[]{:S(2)}, u32[]{:S(2)}) collective-permute-start(bf16[120,192]{0,1:T(8,128)(2,1)S(1)} %bitcast.116), channel_id=1, source_target_pairs={{0,3},{1,11},{2,19},{3,27},{4,2},{5,10},{6,18},{7,26},{8,1},{9,9},... | collective-permute-start | bytes 138248 | tf_op jit(solution)/shard_map/ppermute | solution.py:823
  230.1 28.7 %collective-permute-start.15 = (bf16[512,768]{1,0:T(8,128)(2,1)}, bf16[512,768]{1,0:T(8,128)(2,1)S(1)}, u32[]{:S(2)}, u32[]{:S(2)}) collective-permute-start(bf16[512,768]{1,0:T(8,128)(2,1)} %get-tuple-element.150), channel_id=1, source_target_pairs={{0,1},{1,0},{2,3},{3,2},{4,5},{5,4},{6,7},{7,6},{8,9},{9,8},{10,11... | collective-permute-start | bytes 2359304 | tf_op jit(solution)/shard_map/ppermute | solution.py:796
  230.1 13.8 %collective-permute-start.18 = (bf16[4,96,576]{2,1,0:T(8,128)(2,1)}, bf16[4,96,576]{2,1,0:T(8,128)(2,1)S(1)}, u32[]{:S(2)}, u32[]{:S(2)}) collective-permute-start(bf16[4,96,576]{2,1,0:T(8,128)(2,1)} %get-tuple-element.153), channel_id=1, source_target_pairs={{0,4},{4,0},{8,12},{12,8},{16,20},{20,16},{24,28},{28,24},{1,5},{5... | collective-permute-start | bytes 1327112 | tf_op jit(solution)/shard_map/ppermute | solution.py:796
  245.3 12.4 %collective-permute-start.20 = (bf16[96,576]{1,0:T(8,128)(2,1)S(1)}, bf16[96,576]{1,0:T(8,128)(2,1)S(1)}, u32[]{:S(2)}, u32[]{:S(2)}) collective-permute-start(bf16[96,576]{1,0:T(8,128)(2,1)S(1)} %get-tuple-element.211), channel_id=1, source_target_pairs={{0,16},{4,20},{8,24},{12,28},{16,0},{20,4},{24,8},{28,12},{1,17},{... | collective-permute-start | bytes 331784 | tf_op jit(solution)/shard_map/ppermute | solution.py:796
  248.2 9.5 %collective-permute-start.21 = (bf16[96,576]{1,0:T(8,128)(2,1)S(1)}, bf16[96,576]{1,0:T(8,128)(2,1)S(1)}, u32[]{:S(2)}, u32[]{:S(2)}) collective-permute-start(bf16[96,576]{1,0:T(8,128)(2,1)S(1)} %get-tuple-element.210), channel_id=1, source_target_pairs={{0,24},{4,28},{8,16},{12,20},{16,8},{20,12},{24,0},{28,4},{1,25},{... | collective-permute-start | bytes 331784 | tf_op jit(solution)/shard_map/ppermute | solution.py:796
  250.5 37.1 %collective-permute-start.11 = (bf16[512,768]{1,0:T(8,128)(2,1)S(1)}, bf16[512,768]{1,0:T(8,128)(2,1)}, u32[]{:S(2)}, u32[]{:S(2)}) collective-permute-start(bf16[512,768]{1,0:T(8,128)(2,1)S(1)} %add_convert_fusion.1), channel_id=1, source_target_pairs={{0,2},{1,3},{2,0},{3,1},{4,6},{5,7},{6,4},{7,5},{8,10},{9,11},{10,... | collective-permute-start | bytes 2359304 | tf_op jit(solution)/shard_map/ppermute | solution.py:796
  259.0 26.5 %collective-permute-start.17 = (bf16[512,768]{1,0:T(8,128)(2,1)S(1)}, bf16[512,768]{1,0:T(8,128)(2,1)S(1)}, u32[]{:S(2)}, u32[]{:S(2)}) collective-permute-start(bf16[512,768]{1,0:T(8,128)(2,1)S(1)} %add_convert_fusion), channel_id=1, source_target_pairs={{0,2},{1,3},{2,0},{3,1},{4,6},{5,7},{6,4},{7,5},{8,10},{9,11},{10,... | collective-permute-start | bytes 2359304 | tf_op jit(solution)/shard_map/ppermute | solution.py:796
  295.9 7.8 %collective-permute-start.40 = (f32[1,5184]{1,0:T(1,128)S(1)}, f32[1,5184]{1,0:T(1,128)S(1)}, u32[]{:S(2)}, u32[]{:S(2)}) collective-permute-start(f32[1,5184]{1,0:T(1,128)S(1)} %add.386), channel_id=1, source_target_pairs={{0,16},{4,20},{8,24},{12,28},{16,0},{20,4},{24,8},{28,12},{1,17},{... | collective-permute-start | bytes 62216 | tf_op jit(solution)/shard_map/ppermute | solution.py:796
  299.3 7.4 %collective-permute-start.22 = (bf16[96,192]{1,0:T(8,128)(2,1)S(1)}, bf16[96,192]{1,0:T(8,128)(2,1)S(1)}, u32[]{:S(2)}, u32[]{:S(2)}) collective-permute-start(bf16[96,192]{1,0:T(8,128)(2,1)S(1)} %get-tuple-element.230), channel_id=1, source_target_pairs={{0,0},{3,1},{2,2},{1,3},{4,4},{7,5},{6,6},{5,7},{8,8},{11,9},{10,1... | collective-permute-start | bytes 110600 | tf_op jit(solution)/shard_map/ppermute | solution.py:843
  (44 other events, 414.3 us)

commit v3 on v0

v3 whole, which is shorter than its diff:
```python
import math
from functools import partial

import jax
import jax.numpy as jnp
import numpy as np
from jax import lax
from jax.experimental import pallas as pl
from jax.experimental.pallas import tpu as pltpu
from jax.sharding import PartitionSpec as P

D = 768
HEADS = 12
HDIM = 64
ROT = 16
FF = 3072
EPS = 1e-05
MASKED = -1e30
TILE = 256
VROWS = 80
LN2 = math.log(2.0)
EXTRA = 16
LANES = 128
F32 = jnp.float32
BF16 = jnp.bfloat16
COST = pl.CostEstimate(flops=1000, bytes_accessed=1000, transcendentals=0)
NT_DIMS = (((1,), (1,)), ((), ()))
TN_DIMS = (((0,), (0,)), ((), ()))


def dot(left, right):
    return jnp.dot(left, right, preferred_element_type=F32)


def dot_nt(left, right):
    return lax.dot_general(left, right, NT_DIMS, preferred_element_type=F32)


def dot_tn(left, right):
    return lax.dot_general(left, right, TN_DIMS, preferred_element_type=F32)


def normalize(value):
    center = value - jnp.mean(value, axis=-1, keepdims=True)
    spread = jnp.mean(center * center, axis=-1, keepdims=True)
    return center * lax.rsqrt(spread + EPS)


def angle_parts(length):
    dim = np.arange(LANES) % HDIM
    inverse = np.where(dim < ROT, 10000.0 ** (-2.0 * (dim % (ROT // 2)) / ROT), 0.0)
    high = (np.arange(length // LANES) * LANES)[:, None] * inverse
    low = np.arange(LANES)[:, None] * inverse
    parts = np.stack([np.cos(low), np.sin(low)]), np.stack([np.cos(high), np.sin(high)])
    return tuple(jnp.asarray(part, F32) for part in parts)


def rotation(low_ref, high_ref, tile):
    lane = lax.broadcasted_iota(jnp.int32, (1, LANES), 1) % HDIM
    sign = jnp.where(lane < ROT // 2, -1.0, 1.0)
    cos_rows, sin_rows = [], []
    for part in range(TILE // LANES):
        row = tile * (TILE // LANES) + part
        cos_high = high_ref[0, pl.ds(row, 1), :]
        sin_high = high_ref[1, pl.ds(row, 1), :]
        cos_rows.append(low_ref[0] * cos_high - low_ref[1] * sin_high)
        sin_rows.append((low_ref[1] * cos_high + low_ref[0] * sin_high) * sign)
    return jnp.concatenate(cos_rows, axis=0), jnp.concatenate(sin_rows, axis=0)


def swap_halves(value):
    lane = lax.broadcasted_iota(jnp.int32, value.shape, 1) % HDIM
    half = ROT // 2
    return jnp.where(
        lane < half, pltpu.roll(value, LANES - half, 1), pltpu.roll(value, half, 1)
    )


def true_block(meta_ref, slot):
    return jnp.bitwise_xor(meta_ref[0], slot)


def params(*semantics, vmem=None):
    return pltpu.CompilerParams(
        dimension_semantics=semantics or ("arbitrary",), vmem_limit_bytes=vmem or 60 * 2**20
    )


def whole(shape):
    return pl.BlockSpec(shape, lambda *_: (0,) * len(shape))


def own_blocks(refs, odd, into):
    places = ((0, 256), (128, 320), (384, 512))
    for part, (pair_at, third_at) in enumerate(places):
        left, right = refs[2 * part], refs[2 * part + 1]

        @pl.when(odd == 0)
        def _(left=left, right=right, pair_at=pair_at, third_at=third_at):
            into[:, pair_at : pair_at + 128] = left[...]
            into[:, third_at : third_at + 64] = right[:, 0:64]

        @pl.when(odd == 1)
        def _(left=left, right=right, pair_at=pair_at, third_at=third_at):
            into[:, pair_at : pair_at + 128] = jnp.concatenate(
                [left[:, 64:128], right[:, 0:64]], axis=1
            )
            into[:, third_at : third_at + 64] = right[:, 64:128]


def row(ref):
    return ref[...].reshape(1, ref.shape[0])


def own_bias(b_ref, odd, blk, into):
    blocks = []
    for part in range(3):
        for side in range(2):
            at = pl.multiple_of((part * (D // LANES) + side + 3 * blk // 2) * LANES, LANES)
            blocks.append(b_ref[pl.ds(at, LANES)].reshape(1, LANES))
    own_blocks(blocks, odd, into)


def project_tile(normed, gain, shift, w_ref, b_ref, low, high, tile, q_ref, k_ref, v_ref):
    attn_in = (normed * row(gain) + row(shift)).astype(BF16)
    joined = dot(attn_in, w_ref[...]) + b_ref[...]
    cos, sin = rotation(low, high, tile)
    scale = HDIM**-0.5 / LN2

    def turn(block):
        return block * cos + swap_halves(block) * sin

    query = turn(joined[:, 0:128]) * scale
    keys = turn(joined[:, 128:256])
    mixed = turn(joined[:, 256:384])
    q_ref[:, 0:128] = query.astype(BF16)
    k_ref[:, 0:128] = keys.astype(BF16)
    q_ref[:, 128:192] = (mixed[:, 0:64] * scale).astype(BF16)
    k_ref[:, 128:192] = mixed[:, 64:128].astype(BF16)
    v_ref[...] = joined[:, 384:576].astype(BF16)


def qkv_kernel(slot, meta, x_ref, gain, shift, low, high, w_ref, b_ref, *refs):
    per = pl.num_programs(0)
    tile = true_block(meta, slot) * per + pl.program_id(0)
    normed = normalize(x_ref[...].astype(F32))
    project_tile(normed, gain, shift, w_ref, b_ref, low, high, tile, *refs[-3:])


def project(slot, meta, x, gain, shift, low, high, w, b, filled, seq):
    width = D // 4
    per = seq // TILE
    out = jax.ShapeDtypeStruct((4 * seq, width), BF16)
    out_spec = pl.BlockSpec((TILE, width), lambda i, m: (slot * per + i, 0))
    args = [x, gain, shift, low, high, w, b, *filled]
    specs = [pl.BlockSpec((TILE, D), lambda i, m: (i, 0))]
    specs += [whole(a.shape) for a in args[1:7]]
    specs += [pl.BlockSpec(memory_space=pl.ANY)] * 3
    return pl.pallas_call(
        partial(qkv_kernel, slot),
        out_shape=[out] * 3,
        grid_spec=pltpu.PrefetchScalarGridSpec(
            num_scalar_prefetch=1, grid=(per,), in_specs=specs, out_specs=[out_spec] * 3
        ),
        input_output_aliases={8 + i: i for i in range(3)},
        compiler_params=params(),
        cost_estimate=COST,
        name=f"qkv_{slot}",
    )(meta, *args)


def starts_kernel(seq, meta, valid, s0, s1, s2, s3, start_ref, lo_ref, hi_ref):
    segs = [ref[0:1, 0:seq].astype(F32) for ref in (s0, s1, s2, s3)]
    below = [
        sum(jnp.sum((seg < number).astype(F32), axis=1, keepdims=True) for seg in segs)
        for number in (1, 2, 3)
    ]
    per = seq // TILE
    iota = lax.broadcasted_iota(jnp.int32, (1, seq), 1)
    for slot, seg in enumerate(segs):
        block = true_block(meta, slot)
        begin = jnp.zeros((1, seq), F32)
        for number in (1, 2, 3):
            begin = jnp.where(seg == number, below[number - 1], begin)
        pos = iota + block * seq
        begin = jnp.where(pos < valid[0], begin.astype(jnp.int32), pos)
        for part in range(per):
            tile = begin[:, part * TILE : (part + 1) * TILE]
            start_ref[slot * per + part] = tile
            lo_ref[block * per + part] = jnp.min(tile) // TILE
            hi_ref[block * per + part] = (jnp.max(tile) + (TILE - 1)) // TILE


def segment_starts(meta, valid_len, toks, seq):
    tiles = 4 * seq // TILE
    smem = pl.BlockSpec(memory_space=pltpu.SMEM)
    return pl.pallas_call(
        partial(starts_kernel, seq),
        out_shape=[
            jax.ShapeDtypeStruct((tiles, 1, TILE), jnp.int32),
            jax.ShapeDtypeStruct((tiles,), jnp.int32),
            jax.ShapeDtypeStruct((tiles,), jnp.int32),
        ],
        grid_spec=pltpu.PrefetchScalarGridSpec(
            num_scalar_prefetch=2,
            grid=(1,),
            in_specs=[pl.BlockSpec((EXTRA, D), lambda i, m, v: (seq // EXTRA, 0))] * 4,
            out_specs=[whole((tiles, 1, TILE)), smem, smem],
        ),
        compiler_params=params(),
        name="segment_starts",
    )(meta, valid_len, *toks)


def places(rows):
    order = [0]
    while len(order) < rows:
        order = [2 * i for i in order] + [2 * i + 1 for i in order]
    return order


def fits(rows):
    return rows == 8 and D // rows % 32 == 0


def store_chunks(grad, keep, send, meta, rows):
    size = grad.shape[0] // rows
    for index, place in enumerate(places(rows)):
        at = pl.multiple_of(jnp.bitwise_xor(meta[1], place) * size, 32)
        into = keep if index < rows // 2 else send
        row = index % (rows // 2) * size
        into[row : row + size, :] = grad[pl.ds(at, size), :].astype(into.dtype)


def chunk_shapes(cols, rows, extra=0):
    if fits(rows):
        return [(D // 2 + extra, cols)] * 2
    return [(D, cols), (8, LANES)]


def chunks_of(keep, send, rows):
    if fits(rows):
        return keep, send
    order = jnp.array(places(rows)) ^ lax.axis_index("rows")
    parts = keep.reshape(rows, D // rows, keep.shape[1])
    parts = jnp.take(parts, order, axis=0).reshape(keep.shape)
    return parts[: D // 2], parts[D // 2 :]


def feed(normed, upstream, gain, shift, w_up, b_up, w_down):
    mlp_in = (normed * row(gain) + row(shift)).astype(BF16)
    hidden = dot(mlp_in, w_up[...]) + b_up
    cdf = 0.5 * (1.0 + lax.erf(hidden * (0.5**0.5)))
    act = (hidden * cdf).astype(BF16)
    slope = cdf + hidden * jnp.exp(-0.5 * hidden * hidden) * ((2.0 * math.pi) ** -0.5)
    grad_low = (slope * dot_nt(upstream, w_down[...])).astype(BF16)
    grad_norm = dot_nt(grad_low, w_up[...])
    return mlp_in, act, grad_low, grad_norm


def add_sums(sums, grad_low, grad_norm, normed):
    sums[0:1, :] += jnp.sum(grad_low.astype(F32), axis=0, keepdims=True)
    sums[1:2, :] += jnp.sum(grad_norm * normed, axis=0, keepdims=True)
    sums[2:3, :] += jnp.sum(grad_norm, axis=0, keepdims=True)


def own_row(ref, blk, size):
    return ref[pl.ds(pl.multiple_of(blk * size, LANES), size)].reshape(1, size)


def mlp_first_kernel(
    half, meta, xa, xb, ca, cb, gain, shift, b_up, w_up, w_down, w_out,
    gain1, shift1, b_qkv, low, high, w0, w1, w2, w3, w4, w5,
    mo_ref, e_ref, gv_ref, sums, gup, gdown, q_ref, k_ref, v_ref, w_own, b_own, x_s, c_s,
):
    step = pl.program_id(0)

    @pl.when(step < half)
    def _():
        x_s[...] = xa[...]
        c_s[...] = ca[...]

    @pl.when(step >= half)
    def _():
        x_s[...] = xb[...]
        c_s[...] = cb[...]

    @pl.when(step == 0)
    def _():
        sums[...] = jnp.zeros_like(sums)
        gup[...] = jnp.zeros_like(gup)
        gdown[...] = jnp.zeros_like(gdown)
        odd = meta[0] % 2
        own_blocks((w0, w1, w2, w3, w4, w5), odd, w_own)
        own_bias(b_qkv, odd, meta[0], b_own)

    upstream = c_s[...]

    @pl.when(step < half)
    def _():
        sums[3:4, :] += jnp.sum(upstream.astype(F32), axis=0, keepdims=True)

    normed = normalize(x_s[...].astype(F32))
    tile = true_block(meta, step // half) * half + step % half
    project_tile(normed, gain1, shift1, w_own, b_own, low, high, tile, q_ref, k_ref, v_ref)
    bias = own_row(b_up, meta[0], gup.shape[1])
    mlp_in, act, grad_low, grad_norm = feed(normed, upstream, gain, shift, w_up, bias, w_down)
    mo_ref[...] = dot(act, w_down[...]).astype(BF16)
    add_sums(sums, grad_low, grad_norm, normed)
    e_ref[...] = (grad_norm * row(gain)).astype(BF16)
    gv_ref[...] = dot_nt(upstream, w_out[...]).astype(BF16)
    gup[...] += dot_tn(mlp_in, grad_low)
    gdown[...] += dot_tn(upstream, act)


def mlp_second_kernel(
    half, rows, meta, xa, xb, ca, cb, gain, shift, b_up, w_up, w_down, w_out,
    c0, c1, mo_in, o_near, o_far, sums_in, gup, gdown, _,
    e_ref, gv_ref, sums, even, odd, keep, send, x_s, c_s, n_s, grad,
):
    step = pl.program_id(0)
    hid = gup.shape[1]

    @pl.when(step < half)
    def _():
        x_s[...] = xa[...]
        c_s[...] = ca[...]
        n_s[...] = c0[...]

    @pl.when(step >= half)
    def _():
        x_s[...] = xb[...]
        c_s[...] = cb[...]
        n_s[...] = c1[...]

    @pl.when(step == 0)
    def _():
        sums[...] = sums_in[...]
        grad[:, 0:hid] = gup[...]
        grad[:, hid : 2 * hid] = gdown[...]
        grad[:, 2 * hid :] = jnp.zeros_like(grad[:, 2 * hid :])

    upstream = c_s[...]
    normed = normalize(x_s[...].astype(F32))
    bias = own_row(b_up, meta[0], hid)
    mlp_in, act, grad_low, grad_norm = feed(normed, upstream, gain, shift, w_up, bias, w_down)
    add_sums(sums, grad_low, grad_norm, normed)
    e_ref[...] = (grad_norm * row(gain)).astype(BF16)
    gv_ref[...] = dot_nt(upstream, w_out[...]).astype(BF16)
    grad[:, 0:hid] += dot_tn(mlp_in, grad_low)
    grad[:, hid : 2 * hid] += dot_tn(upstream, act)
    grad[:, 2 * hid : 2 * hid + D // 4] += dot_tn(upstream, o_far[...]) + dot_tn(
        n_s[...], o_near[...]
    )
    far = (dot(act, w_down[...]) + dot(o_far[...], w_out[...])).astype(BF16)
    near = (mo_in[...].astype(F32) + dot(o_near[...], w_out[...])).astype(BF16)

    @pl.when(step < half)
    def _():
        even[0] = near
        even[1] = far

    @pl.when(step >= half)
    def _():
        odd[0] = near
        odd[1] = far

    @pl.when(step == pl.num_programs(0) - 1)
    def _():
        if fits(rows):
            store_chunks(grad, keep, send, meta, rows)
        else:
            keep[...] = grad[...].astype(BF16)


def feed_forward(
    meta, xs, cs, gain, shift, b_up, w_up, w_down, w_out, rows, seq,
    joined=None, before=None, near=None, attn=None,
):
    per = seq // TILE
    steps = 2 * per
    hid = FF // 4
    width = D // 4
    total = 4 * seq
    first = pl.BlockSpec((TILE, D), lambda i, m: (jnp.minimum(i, per - 1), 0))
    second = pl.BlockSpec((TILE, D), lambda i, m: (jnp.maximum(i - per, 0), 0))
    specs = [
        first,
        second,
        first,
        second,
        whole((D,)),
        whole((D,)),
        whole((FF,)),
        pl.BlockSpec((D, hid), lambda i, m: (0, m[0])),
        pl.BlockSpec((hid, D), lambda i, m: (m[0], 0)),
        pl.BlockSpec((width, D), lambda i, m: (m[0], 0)),
    ]
    args = [*xs, *cs, gain, shift, b_up, w_up, w_down, w_out]
    tile = pl.BlockSpec((TILE, D), lambda i, m: (i, 0))
    narrow = pl.BlockSpec((TILE, width), lambda i, m: (i, 0))
    sums = (8, D)
    scratch = [pltpu.VMEM((TILE, D), BF16), pltpu.VMEM((TILE, D), BF16)]
    pair = jax.ShapeDtypeStruct((steps * TILE, D), BF16)
    vec = jax.ShapeDtypeStruct((total, width), BF16)
    if before is None:
        body = partial(mlp_first_kernel, per)
        gain1, shift1, w_qkv, b_qkv, low, high = joined
        args += [gain1, shift1, b_qkv, low, high]
        specs += [whole(a.shape) for a in args[-5:]]
        for part in range(3):
            for side in range(2):
                specs.append(
                    pl.BlockSpec(
                        (D, LANES),
                        lambda i, m, at=part * D // LANES + side: (0, at + 3 * m[0] // 2),
                    )
                )
                args.append(w_qkv)
        outs = [pair, pair, vec, jax.ShapeDtypeStruct(sums, F32)]
        outs += [jax.ShapeDtypeStruct((D, hid), F32)] * 2 + [vec] * 3
        outs += [
            jax.ShapeDtypeStruct((D, 3 * width), BF16),
            jax.ShapeDtypeStruct((1, 3 * width), F32),
        ]
        out_specs = [tile, tile, narrow, whole(sums)]
        out_specs += [whole((D, hid))] * 2 + [narrow] * 3
        out_specs += [whole((D, 3 * width)), whole((1, 3 * width))]
        aliases = {}
    else:
        body = partial(mlp_second_kernel, per, rows)
        mlp_out, _, grad_vec, sums_in, gup, gdown = before
        chunks = chunk_shapes(2 * hid + 2 * LANES, rows)
        args += [*near, mlp_out, attn, attn, sums_in, gup, gdown, grad_vec]
        specs += [
            first,
            second,
            tile,
            narrow,
            pl.BlockSpec((TILE, width), lambda i, m: (i + steps, 0)),
            whole(sums),
            whole((D, hid)),
            whole((D, hid)),
            pl.BlockSpec(memory_space=pl.ANY),
        ]
        aliases = {len(args): 1}
        both = jax.ShapeDtypeStruct((2, seq, D), BF16)
        outs = [pair, vec, jax.ShapeDtypeStruct(sums, F32), both, both]
        outs += [jax.ShapeDtypeStruct(shape, BF16) for shape in chunks]
        out_specs = [
            tile,
            pl.BlockSpec((TILE, width), lambda i, m: (i + steps, 0)),
            whole(sums),
            pl.BlockSpec((2, TILE, D), lambda i, m: (0, jnp.minimum(i, per - 1), 0)),
            pl.BlockSpec((2, TILE, D), lambda i, m: (0, jnp.maximum(i - per, 0), 0)),
            *(whole(shape) for shape in chunks),
        ]
        scratch += [pltpu.VMEM((TILE, D), BF16), pltpu.VMEM((D, 2 * hid + 2 * LANES), F32)]
    return pl.pallas_call(
        body,
        out_shape=outs,
        grid_spec=pltpu.PrefetchScalarGridSpec(
            num_scalar_prefetch=1,
            grid=(steps,),
            in_specs=specs,
            out_specs=out_specs,
            scratch_shapes=scratch,
        ),
        input_output_aliases=aliases,
        compiler_params=params(),
        cost_estimate=COST,
        name="mlp_first" if before is None else "mlp_second",
    )(meta, *args)


def head_masks():
    lane = lax.broadcasted_iota(jnp.int32, (1, LANES), 1)
    first = jnp.where(lane < HDIM, 1.0, 0.0).astype(BF16)
    second = jnp.where(lane < HDIM, 0.0, 1.0).astype(BF16)
    return first, second


def slot_rows(meta, per, tile):
    slot = jnp.bitwise_xor(tile // per, meta[0])
    return pl.multiple_of((slot * per + tile % per) * TILE, TILE)


def by_head(first, second, block, third):
    return (block * first, block * second, third)


def transpose_all(from_ref, to_ref):
    @pl.loop(0, from_ref.shape[0] // TILE)
    def _(tile):
        rows = pl.ds(pl.multiple_of(tile * TILE, TILE), TILE)
        to_ref[:, rows] = from_ref[rows, :].astype(F32).T.astype(BF16)


def attend_kernel(per, meta, lo, hi, q_ref, k_ref, v_ref, start_ref, o_ref, lse_ref, vt_ref, acc, s_ref):
    mask0, mask1 = head_masks()
    tiles = k_ref.shape[0] // TILE
    qi = pl.program_id(0)

    @pl.when(qi == 0)
    def _():
        ones = jnp.where(lax.broadcasted_iota(jnp.int32, (VROWS - HDIM, TILE), 0) == 0, 1.0, 0.0)

        @pl.loop(0, tiles)
        def _(tile):
            rows = pl.ds(pl.multiple_of(tile * TILE, TILE), TILE)
            block = v_ref[rows, :].astype(F32).T
            for head in range(3):
                at = head * VROWS
                vt_ref[at : at + HDIM, rows] = block[head * HDIM : (head + 1) * HDIM].astype(BF16)
                vt_ref[at + HDIM : at + VROWS, rows] = ones.astype(BF16)

    key_iota = lax.broadcasted_iota(jnp.int32, (TILE, TILE), 0)
    query_iota = lax.broadcasted_iota(jnp.int32, (TILE, TILE), 1)
    queries = by_head(mask0, mask1, q_ref[:, 0:128], q_ref[:, 128:192])
    starts = start_ref[0]
    acc[...] = jnp.zeros_like(acc)

    def key_tile(turn):
        return jnp.where(turn == 0, qi, first + turn - 1)

    def score(masked, ki):
        k_rows = pl.ds(slot_rows(meta, per, ki), TILE)
        pair, third = k_ref[k_rows, 0:128], k_ref[k_rows, 128:192]
        scores = [dot_nt(third if head == 2 else pair, queries[head]) for head in range(3)]
        if masked:
            allowed = (key_iota >= starts - ki * TILE) & (key_iota <= query_iota + (qi - ki) * TILE)
            scores = [jnp.where(allowed, x, MASKED) for x in scores]
        return scores, [jnp.max(x, axis=0, keepdims=True) for x in scores]

    def value(ki, tops, peaks):
        k_rows = pl.ds(slot_rows(meta, per, ki), TILE)
        news = [jnp.maximum(top, peak) for top, peak in zip(tops, peaks)]
        fades = [jnp.exp2(top - new) for top, new in zip(tops, news)]
        weights = [jnp.exp2(s_ref[head] - news[head]).astype(BF16) for head in range(3)]
        terms = [
            dot(vt_ref[head * VROWS : (head + 1) * VROWS, k_rows], weights[head]) for head in range(3)
        ]
        return news, fades, terms

    def put(fades, terms):
        for head in range(3):
            cols = slice(head * VROWS, (head + 1) * VROWS)
            acc[cols, :] = acc[cols, :] * fades[head] + terms[head]

    def visit(masked, turn, carry):
        tops, peaks = carry
        scores, next_peaks = score(masked, key_tile(turn + 1))
        news, fades, terms = value(key_tile(turn), tops, peaks)
        peaks = next_peaks
        for head in range(3):
            s_ref[head] = scores[head]
        put(fades, terms)
        return tuple(news), tuple(peaks)

    first = lo[qi]
    full = jnp.minimum(hi[qi], qi)
    scores, peaks = score(True, qi)
    for head in range(3):
        s_ref[head] = scores[head]
    carry = ((jnp.full((1, TILE), MASKED, F32),) * 3, tuple(peaks))
    carry = lax.fori_loop(0, full - first, partial(visit, True), carry)
    carry = lax.fori_loop(full - first, qi - first, partial(visit, False), carry)
    tops, fades, terms = value(key_tile(qi - first), *carry)
    put(fades, terms)
    heads = []
    for head, top in enumerate(tops):
        at = head * VROWS
        total = acc[at + HDIM : at + HDIM + 1, :]
        heads.append(acc[at : at + HDIM, :] / total)
        lse_ref[head, 0] = top + jnp.log2(total)
    o_ref[...] = jnp.concatenate(heads, axis=0).T.astype(BF16)

def attend(meta, lo, hi, query, keys, values, starts, per):
    total, width = query.shape
    tiles = total // TILE
    def slot(i, m):
        return jnp.bitwise_xor(i // per, m[0]) * per + i % per
    q_spec = pl.BlockSpec((TILE, width), lambda i, m, lo, hi: (slot(i, m), 0))
    start_spec = pl.BlockSpec((1, 1, TILE), lambda i, m, lo, hi: (slot(i, m), 0, 0))
    lse_spec = pl.BlockSpec((3, 1, 1, TILE), lambda i, m, lo, hi: (0, slot(i, m), 0, 0))
    return pl.pallas_call(
        partial(attend_kernel, per),
        out_shape=[
            jax.ShapeDtypeStruct((total, width), BF16),
            jax.ShapeDtypeStruct((3, tiles, 1, TILE), F32),
        ],
        grid_spec=pltpu.PrefetchScalarGridSpec(
            num_scalar_prefetch=3,
            grid=(tiles,),
            in_specs=[q_spec, whole(keys.shape), whole(values.shape), start_spec],
            out_specs=[q_spec, lse_spec],
            scratch_shapes=[pltpu.VMEM((3 * VROWS, total), BF16), pltpu.VMEM((3 * VROWS, TILE), F32), pltpu.VMEM((3, TILE, TILE), F32)],
        ),
        compiler_params=params(),
        cost_estimate=COST,
        name="attend",
    )(meta, lo, hi, query, keys, values, starts)


def attend_back_kernel(
    per, meta, lo, hi, q_ref, k_ref, v_ref, o_ref, gv_ref, start_ref, lse_ref, low, high,
    gj_ref, kt_ref, dk_ref, dv_ref, dqt_ref
):
    mask0, mask1 = head_masks()
    tiles = k_ref.shape[0] // TILE
    qi = tiles - 1 - pl.program_id(0)

    @pl.when(pl.program_id(0) == 0)
    def _():
        transpose_all(k_ref, kt_ref)

    own_rows = pl.ds(slot_rows(meta, per, qi), TILE)
    key_iota = lax.broadcasted_iota(jnp.int32, (TILE, TILE), 0)
    query_iota = lax.broadcasted_iota(jnp.int32, (TILE, TILE), 1)
    queries = by_head(mask0, mask1, q_ref[:, 0:128], q_ref[:, 128:192])
    grads = by_head(mask0, mask1, gv_ref[:, 0:128], gv_ref[:, 128:192])
    starts = start_ref[0]
    lses = [lse_ref[head, 0] for head in range(3)]
    product = (gv_ref[...].astype(F32) * o_ref[...].astype(F32)).T
    deltas = [
        jnp.sum(product[head * HDIM : (head + 1) * HDIM], axis=0, keepdims=True)
        for head in range(3)
    ]
    dqt_ref[...] = jnp.zeros_like(dqt_ref)

    @pl.when(pl.program_id(0) == 0)
    def _():
        dk_ref[...] = jnp.zeros_like(dk_ref)
        dv_ref[...] = jnp.zeros_like(dv_ref)

    def load(ki):
        k_rows = pl.ds(slot_rows(meta, per, ki), TILE)
        return k_rows

    def score(masked, ki):
        k_rows = load(ki)
        pair, third = k_ref[k_rows, 0:128], k_ref[k_rows, 128:192]
        v_pair, v_third = v_ref[k_rows, 0:128], v_ref[k_rows, 128:192]
        scores = [dot_nt(third if head == 2 else pair, queries[head]) for head in range(3)]
        grad_probs = [dot_nt(v_third if head == 2 else v_pair, grads[head]) for head in range(3)]
        if masked:
            allowed = (key_iota >= starts - ki * TILE) & (key_iota <= query_iota + (qi - ki) * TILE)
            scores = [jnp.where(allowed, x, MASKED) for x in scores]
        return scores, grad_probs

    def terms(ki, scores, grad_probs):
        k_rows = load(ki)
        probs = [jnp.exp2(x - lse) for x, lse in zip(scores, lses)]
        grad_scores = [
            (p * (g - delta)).astype(BF16) for p, g, delta in zip(probs, grad_probs, deltas)
        ]
        dv = [dot(p.astype(BF16), g) for p, g in zip(probs, grads)]
        dk = [dot(g, q) for g, q in zip(grad_scores, queries)]
        dq = [
            dot(kt_ref[head * HDIM : (head + 1) * HDIM, k_rows], grad_scores[head])
            for head in range(3)
        ]
        return dk, dv, dq

    def add(ki, dk, dv, dq):
        k_rows = load(ki)
        for into, parts in ((dk_ref, dk), (dv_ref, dv)):
            into[k_rows, 0:128] += parts[0] + parts[1]
            into[k_rows, 128:192] += parts[2]
        for head in range(3):
            dqt_ref[head * HDIM : (head + 1) * HDIM, :] += dq[head]

    first = lo[qi]
    full = jnp.minimum(hi[qi], qi)

    def visit(masked, ki):
        add(ki, *terms(ki, *score(masked, ki)))

    @pl.loop(first, full)
    def _(ki):
        visit(True, ki)

    @pl.loop(full, qi)
    def _(ki):
        visit(False, ki)

    visit(True, qi)

    cos, sin = rotation(low, high, qi)

    def turn_back(block):
        return block * cos - swap_halves(block) * sin

    dq = dqt_ref[...].T * (HDIM**-0.5)
    dk = dk_ref[own_rows, :] * LN2
    gj_ref[:, 0:128] = turn_back(dq[:, 0:128]).astype(BF16)
    gj_ref[:, 128:256] = turn_back(dk[:, 0:128]).astype(BF16)
    mixed = jnp.concatenate([dq[:, 128:192], dk[:, 128:192]], axis=1)
    gj_ref[:, 256:384] = turn_back(mixed).astype(BF16)
    gj_ref[:, 384:576] = dv_ref[own_rows, :].astype(BF16)


def attend_back(
    meta, lo, hi, query, keys, values, attn, grad_vec, starts, lse, low, high, per
):
    total, width = query.shape
    tiles = total // TILE

    def slot(i, m):
        tile = tiles - 1 - i
        return jnp.bitwise_xor(tile // per, m[0]) * per + tile % per

    q_spec = pl.BlockSpec((TILE, width), lambda i, m, lo, hi: (slot(i, m), 0))
    gj_spec = pl.BlockSpec((TILE, 3 * width), lambda i, m, lo, hi: (slot(i, m), 0))
    start_spec = pl.BlockSpec((1, 1, TILE), lambda i, m, lo, hi: (slot(i, m), 0, 0))
    lse_spec = pl.BlockSpec((3, 1, 1, TILE), lambda i, m, lo, hi: (0, slot(i, m), 0, 0))
    return pl.pallas_call(
        partial(attend_back_kernel, per),
        out_shape=jax.ShapeDtypeStruct((total, 3 * width), BF16),
        grid_spec=pltpu.PrefetchScalarGridSpec(
            num_scalar_prefetch=3,
            grid=(tiles,),
            in_specs=[
                q_spec,
                whole(keys.shape),
                whole(values.shape),
                q_spec,
                q_spec,
                start_spec,
                lse_spec,
                whole(low.shape),
                whole(high.shape),
            ],
            out_specs=gj_spec,
            scratch_shapes=[
                pltpu.VMEM((width, total), BF16),
                pltpu.VMEM((total, width), F32),
                pltpu.VMEM((total, width), F32),
                pltpu.VMEM((width, TILE), F32),
            ],
        ),
        compiler_params=params(),
        cost_estimate=COST,
        name="attend_back",
    )(meta, lo, hi, query, keys, values, attn, grad_vec, starts, lse, low, high)


def joined_kernel(final, rows, meta, *refs):
    gj_a, gj_b, e_a, e_b, x_a, x_b, gain_ref, shift_ref, w_ref = refs[:9]
    if final:
        grad_in, bias_in, sums_in, mlp_sums = refs[9:13]
        e_ref, keep, send, grad, bias, sums = refs[13:]
    else:
        e_ref, grad, bias, sums = refs[9:]
    step = pl.program_id(0)

    @pl.when(step == 0)
    def _():
        if final:
            grad[...] = grad_in[...]
            bias[...] = bias_in[...]
            sums[...] = sums_in[...]
        else:
            grad[...] = jnp.zeros_like(grad)
            bias[...] = jnp.zeros_like(bias)
            sums[...] = jnp.zeros_like(sums)

    gain, shift = row(gain_ref), row(shift_ref)
    for index, (gj_ref, e_in, x_ref) in enumerate(((gj_a, e_a, x_a), (gj_b, e_b, x_b))):
        normed = normalize(x_ref[...].astype(F32))
        attn_in = (normed * gain + shift).astype(BF16)
        low = gj_ref[...]
        grad_norm = dot_nt(low, w_ref[...])
        e_ref[index] = (grad_norm * gain + e_in[...].astype(F32)).astype(BF16)
        sums[0:1, :] += jnp.sum(grad_norm * normed, axis=0, keepdims=True)
        sums[1:2, :] += jnp.sum(grad_norm, axis=0, keepdims=True)
        bias[0:1, :] += jnp.sum(low.astype(F32), axis=0, keepdims=True)
        grad[...] += dot_tn(attn_in, low)

    if final:

        @pl.when(step == pl.num_programs(0) - 1)
        def _():
            if fits(rows):
                store_chunks(grad, keep, send, meta, rows)
                small = pack_small(sums[...], mlp_sums[...], bias[...])
                keep[D // 2 :, :] = small
                send[D // 2 :, :] = small
            else:
                keep[...] = grad[...].astype(BF16)
                send[...] = jnp.zeros_like(send)


SMALL = 32


def pack_small(norm_sums, mlp_sums, bias):
    third = 3 * D // 4
    table = jnp.concatenate([norm_sums[0:4], mlp_sums[0:4]], axis=0)
    which = lax.broadcasted_iota(jnp.int32, (8, third), 0)
    head = jnp.where(which == 2, bias[0:1, :], table[:, :third])
    tail = jnp.concatenate([table[:, third:], jnp.zeros((8, 2 * third - D), F32)], axis=1)
    return split_small(jnp.concatenate([head, tail], axis=0))


def add_small(left, right):
    half = SMALL // 2
    total = left.astype(F32) + right.astype(F32)
    return total[:half] + total[half:]


def split_small(rows):
    high = rows.astype(BF16)
    return jnp.concatenate([high, (rows - high.astype(F32)).astype(BF16)], axis=0)


def joined_back(
    meta, slots, grad, e_mlp, toks, gain, shift, w, rows, seq, before=None, mlp_sums=None
):
    width = grad.shape[1]
    per = seq // TILE

    def at(slot, cols):
        return pl.BlockSpec((TILE, cols), lambda i, m: (slot * per + i, 0))

    sums = (8, D)
    args = [grad, grad, *e_mlp, *[toks[slot] for slot in slots], gain, shift, w]
    specs = [
        *(at(slot, width) for slot in slots),
        *(at(slot % 2, D) for slot in slots),
        *(pl.BlockSpec((TILE, D), lambda i, m: (i, 0)),) * 2,
        whole(gain.shape),
        whole(shift.shape),
        whole(w.shape),
    ]
    e_spec = pl.BlockSpec((2, TILE, D), lambda i, m: (0, i, 0))
    outs, out_specs = [jax.ShapeDtypeStruct((2, seq, D), BF16)], [e_spec]
    carried = [(D, width), (8, width), sums]
    scratch = []
    if before is None:
        outs += [jax.ShapeDtypeStruct(shape, F32) for shape in carried]
        out_specs += [whole(shape) for shape in carried]
    else:
        chunks = chunk_shapes(width, rows, SMALL)
        outs += [jax.ShapeDtypeStruct(shape, BF16) for shape in chunks]
        out_specs += [whole(shape) for shape in chunks]
        if not fits(rows):
            outs[-1] = jax.ShapeDtypeStruct((8, LANES), BF16)
        args += [*before, mlp_sums]
        specs += [whole(shape) for shape in carried] + [whole(sums)]
        scratch = [pltpu.VMEM(shape, F32) for shape in carried]
        if not fits(rows):
            outs += [jax.ShapeDtypeStruct(shape, F32) for shape in carried[1:]]
            out_specs += [whole(shape) for shape in carried[1:]]
            scratch = scratch[:1]
    body = partial(joined_kernel, before is not None, rows)
    if before is not None and not fits(rows):

        def body(meta, *refs):
            inputs, (e_ref, keep, send, bias, sums, grad) = refs[:13], refs[13:]
            joined_kernel(True, rows, meta, *inputs, e_ref, keep, send, grad, bias, sums)

    return pl.pallas_call(
        body,
        out_shape=outs,
        grid_spec=pltpu.PrefetchScalarGridSpec(
            num_scalar_prefetch=1,
            grid=(per,),
            in_specs=specs,
            out_specs=out_specs,
            scratch_shapes=scratch,
        ),
        compiler_params=params(),
        cost_estimate=COST,
        name="joined_first" if before is None else "joined_second",
    )(meta, *args)


def fold_kernel(extra, keep, got, *outs):
    size = keep.shape[0] - extra
    for index, out in enumerate(outs):
        rows = slice(index * size // 2, (index + 1) * size // 2)
        total = keep[rows, :].astype(F32) + got[rows, :].astype(F32)
        out[0 : size // 2, :] = total.astype(BF16)
    if extra:
        small = split_small(add_small(keep[size:, :], got[size:, :]))
        for out in outs:
            out[size // 2 :, :] = small


def simple(body, name, shapes, *args):
    return pl.pallas_call(
        body,
        out_shape=[jax.ShapeDtypeStruct(shape, kind) for shape, kind in shapes],
        grid_spec=pltpu.PrefetchScalarGridSpec(
            num_scalar_prefetch=1,
            grid=(1,),
            in_specs=[whole(a.shape) for a in args[1:]],
            out_specs=[whole(shape) for shape, _ in shapes],
        ),
        compiler_params=params(),
        cost_estimate=COST,
        name=name,
    )(*args)


def fold(meta, keep, got, extra):
    size, cols = keep.shape[0] - extra, keep.shape[1]
    shapes = [((size // 2 + extra, cols), BF16)] * 2
    return simple(lambda _, *refs: fold_kernel(extra, *refs), "fold", shapes, meta, keep, got)


def last_packet_kernel(meta, keep, got, up_ref, first, second):
    hid = up_ref.shape[1]
    up_ref[...] = keep[:, :hid].astype(F32) + got[:, :hid].astype(F32)
    low = (keep[:, hid:].astype(F32) + got[:, hid:].astype(F32)).astype(BF16)
    cut, side = hid // 2, D // 8
    even = jnp.concatenate([low[:, :cut], low[:, hid : hid + side]], axis=1)
    odd = jnp.concatenate([low[:, cut:hid], low[:, hid + side : hid + 2 * side]], axis=1)

    @pl.when(meta[1] % 2 == 0)
    def _():
        first[...] = even
        second[...] = odd

    @pl.when(meta[1] % 2 == 1)
    def _():
        first[...] = odd
        second[...] = even


def lower_kernel(meta, first, second, down_ref, out_ref):
    cut = down_ref.shape[0]
    size = first.shape[0]

    def store(ref, at):
        turned = ref[...].astype(F32).T
        down_ref[:, at : at + size] = turned[:cut]
        out_ref[:, at : at + size] = turned[cut:]

    @pl.when(meta[1] % 2 == 0)
    def _():
        store(first, 0)
        store(second, size)

    @pl.when(meta[1] % 2 == 1)
    def _():
        store(second, 0)
        store(first, size)


def last_qkv_kernel(meta, keep, got, kept, near, far, small):
    size = kept.shape[0]
    width = kept.shape[1]
    total = keep[0:size, :].astype(F32) + got[0:size, :].astype(F32)
    rows = add_small(keep[size:, :], got[size:, :])
    for part in range(3):
        small[part * 8 : part * 8 + 8, :] = rows[0:8, part * width : (part + 1) * width]
    small[24:32, :] = rows[8:16, 0:width]
    near[size:, :] = small[...]
    far[size:, :] = small[...]
    query = jnp.concatenate([total[:, 0:128], total[:, 256:320]], axis=1)
    keys = jnp.concatenate([total[:, 128:256], total[:, 320:384]], axis=1)
    values = total[:, 384:576]
    plans = (
        (query, keys, values),
        (keys, query, values),
        (keys, values, query),
        (values, keys, query),
    )
    for blk, plan in enumerate(plans):

        @pl.when(meta[0] == blk)
        def _(plan=plan):
            kept[...] = plan[0]
            near[0:size, :] = plan[1]
            far[0:size, :] = plan[2]


def assemble_kernel(
    meta, kept, small, near, far, diag,
    qkv, b_qkv, b_out, b_up, b_down, gain1, shift1, gain2, shift2, table,
):
    size, width = kept.shape

    @pl.when(meta[0] % 2 == 0)
    def _():
        qkv[:, 0:width] = kept[...]
        qkv[:, 2 * width :] = far[0:size, :]

    @pl.when(meta[0] % 2 == 1)
    def _():
        qkv[:, 0:width] = far[0:size, :]
        qkv[:, 2 * width :] = kept[...]

    qkv[:, width : 2 * width] = near[0:size, :]
    table[0] = small[...]
    table[1] = near[size:, :]
    table[2] = far[size:, :]
    table[3] = diag[...]
    total = table[0] + table[1] + table[2] + table[3]

    def vector(rows, index):
        parts = [rows[part * 8 + index : part * 8 + index + 1, :] for part in range(4)]
        return jnp.concatenate(parts, axis=1)

    for ref, index in ((gain1, 0), (shift1, 1), (gain2, 5), (shift2, 6), (b_out, 7), (b_down, 7)):
        ref[...] = vector(total, index).reshape(D)
    ups, parts = [], ([], [], [])
    for blk in range(4):
        rows = table[jnp.bitwise_xor(meta[0], blk)]
        ups.append(vector(rows, 4))
        joined = vector(rows, 2)
        parts[0].append(jnp.concatenate([joined[:, 0:128], joined[:, 256:320]], axis=1))
        parts[1].append(jnp.concatenate([joined[:, 128:256], joined[:, 320:384]], axis=1))
        parts[2].append(joined[:, 384:576])
    b_up[...] = jnp.concatenate(ups, axis=1).reshape(4 * D)
    b_qkv[...] = jnp.concatenate(parts[0] + parts[1] + parts[2], axis=1).reshape(3 * D)


def assemble(meta, kept, small, near, far, diag):
    size, width = kept.shape
    shapes = [((size, 3 * width), F32), ((3 * D,), F32), ((D,), F32), ((4 * D,), F32)]
    shapes += [((D,), F32)] * 5
    args = (kept, small, near, far, diag)
    return pl.pallas_call(
        assemble_kernel,
        out_shape=[jax.ShapeDtypeStruct(shape, kind) for shape, kind in shapes],
        grid_spec=pltpu.PrefetchScalarGridSpec(
            num_scalar_prefetch=1,
            grid=(1,),
            in_specs=[whole(a.shape) for a in args],
            out_specs=[whole(shape) for shape, _ in shapes],
            scratch_shapes=[pltpu.VMEM((4, 32, width), F32)],
        ),
        compiler_params=params(),
        cost_estimate=COST,
        name="assemble",
    )(meta, *args)


def fold_plain(keep, got, last):
    total = keep.astype(F32) + got.astype(F32)
    if last:
        return [total]
    half = total.shape[0] // 2
    return [total[:half].astype(BF16), total[half:].astype(BF16)]


def reduce_plain(keep, got, rows):
    mask = 2
    while mask < rows:
        keep, send = fold_plain(keep, got, False)
        got = swap(send, "rows", mask)
        mask *= 2
    return fold_plain(keep, got, True)[0]


def after(value, *others):
    return lax.optimization_barrier((value, others))[0]


def swap(value, axis, mask):
    size = lax.axis_size(axis)
    return lax.ppermute(value, axis, [(i, i ^ mask) for i in range(size)])


def add_low(left, right):
    return (left.astype(F32) + right.astype(F32)).astype(BF16)


def spread_rows(lower):
    rows, blk = lax.axis_size("rows"), lax.axis_size("blk")
    r = lax.axis_index("rows")
    count = rows // blk
    hid, width = FF // 4, D // 4
    chunk = lower.shape[0]
    down = lower[:, :hid].reshape(chunk, count, hid // count)
    out = lower[:, hid:].reshape(chunk, count, width // count)
    pieces = jnp.concatenate([down, out], axis=2).astype(BF16)
    got = []
    for turn in range(count):
        moves = spread_moves(rows, blk, turn)
        piece = lax.dynamic_index_in_dim(pieces, (r % count) ^ turn, 1, keepdims=False)
        got.append(lax.ppermute(piece, ("rows", "blk"), moves))
    got = jnp.stack(got)
    parts = [
        lax.dynamic_index_in_dim(got, (r % count) ^ part, 0, keepdims=False)
        for part in range(count)
    ]
    whole_cols = jnp.concatenate(parts, axis=0).astype(F32).T
    cut = hid // count
    return whole_cols[:cut], whole_cols[cut:]


def spread_moves(rows, blk, turn):
    count = rows // blk
    moves = []
    for r in range(rows):
        for b in range(blk):
            to = count * b + ((r % count) ^ turn)
            moves.append((r * blk + b, to * blk + r // count))
    return moves


def split_columns(chunk):
    b = lax.axis_index("blk")
    q = jnp.concatenate([chunk[:, 0:128], chunk[:, 256:320]], axis=1)
    k = jnp.concatenate([chunk[:, 128:256], chunk[:, 320:384]], axis=1)
    v = chunk[:, 384:576]

    def choose(zero, one, two, three):
        return jnp.where(b < 2, jnp.where(b == 0, zero, one), jnp.where(b == 2, two, three))

    return choose(q, k, k, v), choose(k, q, v, k), choose(v, v, q, q)


def result_kernel(x_ref, even, near, far, b_out, b_down, out_ref):
    bias = row(b_out) + row(b_down)
    total = even[0].astype(F32) + near[0].astype(F32) + far[...].astype(F32)
    out_ref[...] = (x_ref[...].astype(F32) + bias + total).astype(BF16)


def token_kernel(x_ref, even, near, far, c_ref, out_ref):
    wide = x_ref[...].astype(F32)
    center = wide - jnp.mean(wide, axis=-1, keepdims=True)
    rate = lax.rsqrt(jnp.mean(center * center, axis=-1, keepdims=True) + EPS)
    normed = center * rate
    grad = even[0].astype(F32) + near[0].astype(F32) + far[...].astype(F32)
    mean = jnp.mean(grad, axis=-1, keepdims=True)
    along = jnp.mean(grad * normed, axis=-1, keepdims=True)
    back = rate * (grad - mean - normed * along)
    out_ref[...] = (c_ref[...].astype(F32) + back).astype(BF16)


def finish(body, name, seq, x, even, near, far, *more):
    flat = pl.BlockSpec((TILE, D), lambda i: (i, 0))
    own = pl.BlockSpec((1, TILE, D), lambda i: (0, i, 0))
    return pl.pallas_call(
        body,
        out_shape=jax.ShapeDtypeStruct((seq, D), BF16),
        grid=(seq // TILE,),
        in_specs=[flat, own, own, flat, *(flat if a.ndim == 2 else whole(a.shape) for a in more)],
        out_specs=flat,
        compiler_params=params(),
        cost_estimate=COST,
        name=name,
    )(x, even, near, far, *more)


def local(
    tokens, seg_ids, valid_len, ln1_gain, ln1_bias, w_qkv, b_qkv, w_out, b_out,
    ln2_gain, ln2_bias, w_up, b_up, w_down, b_down, cotangent,
):
    rows = lax.axis_size("rows")
    blk = lax.axis_index("blk")
    seq = tokens.shape[1]
    per = seq // TILE
    width = D // 4
    hid = FF // 4
    low, high = angle_parts(4 * seq)
    seg_row = jnp.pad(seg_ids.astype(BF16), ((0, EXTRA - 1), (0, D - seq)))
    tok_own = jnp.concatenate([tokens[0], seg_row], axis=0)
    cot_own = cotangent[0]

    cot_near = swap(cot_own, "blk", 1)
    tok_far = swap(tok_own, "blk", 2)
    tok_near = swap(tok_own, "blk", 1)
    cot_far = swap(after(cot_own, tok_near), "blk", 2)

    meta = jnp.stack([blk, lax.axis_index("rows")]).astype(jnp.int32)
    mlp_args = (ln2_gain, ln2_bias, b_up, w_up, w_down, w_out, rows, seq)
    joined = (ln1_gain, ln1_bias, w_qkv, b_qkv, low, high)
    *first, query, keys, values, w_own, b_own = feed_forward(
        meta, (tok_own, tok_near), (cot_own, cot_near), *mlp_args, joined
    )
    meta = after(meta, b_own)

    def more(slot, m, tok, filled):
        return project(slot, m, tok, ln1_gain, ln1_bias, low, high, w_own, b_own, filled, seq)

    tok_last = swap(after(tok_far, b_own), "blk", 1)
    joined = more(2, meta, tok_far, (query, keys, values))
    toks = (tok_own, tok_near, tok_far, tok_last)
    query, keys, values = more(3, after(meta, joined[0]), tok_last, joined)
    starts, lo, hi = segment_starts(after(meta, query), valid_len, toks, seq)
    cot_last = swap(after(cot_far, lo), "blk", 1)
    cots = (cot_own, cot_near, cot_far, cot_last)
    attn, lse = attend(meta, lo, hi, query, keys, values, starts, per)

    meta = after(meta, lse)
    e_far, grad_vec, mlp_sums, out_even, out_odd, keep, send = feed_forward(
        meta, toks[2:], cots[2:], *mlp_args, before=first, near=cots[:2], attn=attn
    )
    e_mlp = (first[1], e_far)
    keep, send = chunks_of(keep, send, rows)
    out_got = swap(out_odd, "blk", 1)
    got = swap(send, "rows", 1)

    meta = after(meta, mlp_sums)
    grad_joined = attend_back(
        meta, lo, hi, query, keys, values, attn, grad_vec, starts, lse, low, high, per
    )

    out_send = add_low(after(out_even, grad_joined)[1], out_got[1])
    out_far = swap(out_send, "blk", 2)
    joined_args = (grad_joined, e_mlp, toks, ln1_gain, ln1_bias, w_own, rows, seq)
    meta = after(meta, out_send)
    e_odd, *carried = joined_back(meta, (1, 3), *joined_args)
    e_got = swap(e_odd, "blk", 1)
    meta = after(meta, carried[1])
    if fits(rows):
        keep, send = fold(meta, keep, got, 0)
        got = swap(send, "rows", 2)
        meta = after(meta, send)
    e_even, qkv_keep, qkv_send, *rest = joined_back(
        meta, (0, 2), *joined_args, carried, mlp_sums
    )
    qkv_keep, qkv_send = chunks_of(qkv_keep, qkv_send, rows)
    qkv_got = swap(qkv_send, "rows", 1)
    e_send = add_low(e_even[1], e_got[1])
    e_far = swap(e_send, "blk", 2)

    out_args = (after(tok_own, e_send), out_even, out_got, out_far, b_out, b_down)
    result = finish(result_kernel, "result", seq, *out_args)
    if fits(rows):
        meta = after(meta, result)
        keep, send = fold(meta, keep, got, 0)
        got = swap(send, "rows", 4)
        meta = after(meta, send)
        qkv_keep, qkv_send = fold(meta, qkv_keep, qkv_got, SMALL)
        qkv_got = swap(qkv_send, "rows", 2)
        tok_args = (after(tok_own, qkv_send), e_even, e_got, e_far, cot_own)
        grad_tokens = finish(token_kernel, "token_grad", seq, *tok_args)
        meta = after(meta, grad_tokens)
        qkv_keep, qkv_send = fold(meta, qkv_keep, qkv_got, SMALL)
        qkv_got = swap(qkv_send, "rows", 4)
        meta = after(meta, qkv_send)
        chunk = D // rows
        part = ((chunk, hid // 2 + width // 2), BF16)
        up, *pieces = simple(
            last_packet_kernel, "last_packet", [((chunk, hid), F32), part, part], meta, keep, got
        )
        pieces = [
            lax.ppermute(piece, ("rows", "blk"), spread_moves(rows, 4, turn))
            for turn, piece in enumerate(pieces)
        ]
        meta = after(meta, up)
        packet = ((chunk + 32, width), F32)
        kept, near, far, small = simple(
            last_qkv_kernel,
            "last_qkv",
            [((chunk, width), F32), packet, packet, ((32, width), F32)],
            meta,
            qkv_keep,
            qkv_got,
        )
        near, far, diag = swap(near, "blk", 1), swap(far, "blk", 2), swap(small, "blk", 3)
        lower = [((hid // 2, width), F32), ((width // 2, width), F32)]
        down, out_w = simple(lower_kernel, "lower", lower, meta, *pieces)
        meta = after(meta, down)
        qkv, gb_qkv, gb_out, gb_up, gb_down, *norms = assemble(
            meta, kept, small, near, far, diag
        )
    else:
        weights = reduce_plain(keep, got, rows)
        qkv = reduce_plain(qkv_keep, qkv_got, rows)
        up = weights[:, :hid]
        down, out_w = spread_rows(weights[:, hid : 2 * hid + width])
        kept, near, far = split_columns(qkv)
        near, far = swap(near, "blk", 1), swap(far, "blk", 2)
        ends = [jnp.where(blk % 2 == 0, a, b) for a, b in ((kept, far), (far, kept))]
        qkv = jnp.concatenate([ends[0], near, ends[1]], axis=1)
        tok_args = (tok_own, e_even, e_got, e_far, cot_own)
        grad_tokens = finish(token_kernel, "token_grad", seq, *tok_args)
        bias, sums = rest
        mine = (jnp.arange(4) == blk)[:, None]
        joined = lax.psum(jnp.where(mine, bias[0:1], 0.0), ("rows", "blk"))
        gb_up = lax.psum(jnp.where(mine, mlp_sums[0:1], 0.0), ("rows", "blk")).reshape(FF)
        gb_qkv = jnp.concatenate(
            [
                jnp.concatenate([joined[:, 0:128], joined[:, 256:320]], axis=1).reshape(D),
                jnp.concatenate([joined[:, 128:256], joined[:, 320:384]], axis=1).reshape(D),
                joined[:, 384:576].reshape(D),
            ]
        )
        sums = jnp.concatenate([sums[0:2], mlp_sums[1:4]])
        *norms, gb_out = lax.psum(sums, ("rows", "blk"))
        gb_down = gb_out
    return (
        result[None],
        grad_tokens[None],
        qkv,
        out_w,
        up,
        down,
        gb_qkv,
        gb_out,
        gb_up,
        gb_down,
        *norms,
    )


def solution(mesh):
    split = P("rows", "blk")
    in_specs = (
        P("rows", "blk", None),
        split,
        P("rows"),
        *(P(),) * 12,
        P("rows", "blk", None),
    )
    out_specs = (
        P("rows", "blk", None),
        P("rows", "blk", None),
        *(split,) * 4,
        *(P(),) * 8,
    )
    return jax.shard_map(local, mesh=mesh, in_specs=in_specs, out_specs=out_specs, check_vma=False)
```

time: 943 us -> 235 us (0.25)
  the two profiles are of different devices: /device:TPU:0 before, /device:TPU:2 now
where the time goes in v3:
time: 235 us; the launch traced here: 234 us
  Pallas kernels  129 us (55%)
  waiting for transfers between devices  63.9 us (27%)
  starting transfers between devices  23.7 us (10%)
  local copies, waits for them, and re-layouts  10.9 us (5%)
  other arithmetic  4.59 us (2%)
    ppermute x19, waiting for transfers between devices, swap(): return lax.ppermute(value, axis, [(i, i ^ mask) for i in range(size)])  56.5 us
    pallas_call x2, Pallas kernels, feed_forward(): pl.pallas_call(body, out_shape=outs, grid_spec=pltpu.PrefetchScalarGridSp...  38.8 us
    pallas_call x1, Pallas kernels, attend_back(): pl.pallas_call(partial(attend_back_kernel, per), out_shape=jax.ShapeDtype...  21.2 us
    pallas_call x7, Pallas kernels, simple(): pl.pallas_call(body, out_shape=[jax.ShapeDtypeStruct(shape, kind) for sha...  19.7 us
    ppermute x19, starting transfers between devices, swap(): return lax.ppermute(value, axis, [(i, i ^ mask) for i in range(size)])  17.8 us
    pallas_call x2, Pallas kernels, joined_back(): pl.pallas_call(body, out_shape=outs, grid_spec=pltpu.PrefetchScalarGridSp...  16.2 us
    pallas_call x1, Pallas kernels, attend(): pl.pallas_call(partial(attend_kernel, per), out_shape=[jax.ShapeDtypeStru...  13 us
    unnamed x41, local copies, waits for them, and re-layouts  10.9 us
  transfers between devices with their start and end apart: 21, of which 8 were waited for; matrix products, arithmetic and copies ran while one was open for 2% of the time, Pallas kernels for 41%

profile of v3, /device:TPU:2, one launch (start us, length us, event | category | flops | bytes accessed | tf_op | source)
XLA Modules:
  0.0 233.9 jit_solution(3001475120158513692)
XLA Ops:
  3.8 2.5 %collective-permute-done.1.cb.c1 = bf16[512,768]{1,0:T(8,128)(2,1)S(1)} collective-permute-done((bf16[512,768]{1,0:T(8,128)(2,1)}, bf16[512,768]{1,0:T(8,128)(2,1)S(1)}, u32[]{:S(2)}, u32[]{:S(2)}) %collective-permute-start.1) | collective-permute-done | bytes 786464 | tf_op jit(solution)/shard_map/ppermute | solution.py:1065
  8.1 18.6 %mlp_first.1 = (bf16[1024,768]{1,0:T(8,128)(2,1)}, bf16[1024,768]{1,0:T(8,128)(2,1)}, bf16[2048,192]{1,0:T(8,128)(2,1)}, f32[8,768]{1,0:T(8,128)}, f32[768,768]{...) custom-call(s32[2]{0:T(128)} %pad_add_fusion.meta._, ...), custom_call_target="tpu_custom_call" | custom-call | flops 1000 | bytes 1000 | tf_op jit(solution)/shard_map/mlp_first/pallas_call | solution.py:459
  29.1 4.6 %qkv_2.1 = (bf16[2048,192]{1,0:T(8,128)(2,1)}, bf16[2048,192]{1,0:T(8,128)(2,1)}, bf16[2048,192]{1,0:T(8,128)(2,1)}) custom-call(s32[2]{0:T(128)} %pad_add_fusion.meta._, bf16[528,768]{1,0:T(8,128)(2,1)} %copy-done.1, f32[768]{0:T(1024)} %refs_6_.3, f32[768]{0:T(1024)} %refs_7_.3, ...), custom_call_target="tpu_custom_call", output_to_operand_aliasing={{0}: (8, {}), {1}: (9, {}), {2}: (10, {})} | custom-call | flops 1000 | bytes 1000 | tf_op jit(solution)/shard_map/qkv_2/pallas_call | solution.py:159
  34.6 4.5 %qkv_3.1 = (bf16[2048,192]{1,0:T(8,128)(2,1)}, bf16[2048,192]{1,0:T(8,128)(2,1)}, bf16[2048,192]{1,0:T(8,128)(2,1)}) custom-call(s32[2]{0:T(128)} %pad_add_fusion.meta._, bf16[528,768]{1,0:T(8,128)(2,1)} %copy-done.2, f32[768]{0:T(1024)} %refs_6_.3, f32[768]{0:T(1024)} %refs_7_.3, ...), custom_call_target="tpu_custom_call", output_to_operand_aliasing={{0}: (8, {}), {1}: (9, {}), {2}: (10, {})} | custom-call | flops 1000 | bytes 1000 | tf_op jit(solution)/shard_map/qkv_3/pallas_call | solution.py:159
  39.1 2.4 %segment_starts.1 = (s32[8,1,256]{2,1,0:T(1,128)}, s32[8]{0:T(128)}, s32[8]{0:T(128)}) custom-call(s32[2]{0:T(128)} %pad_add_fusion.meta._, s32[1]{0:T(128)S(6)} %copy.47.valid, bf16[528,768]{1,0:T(8,128)(2,1)} %copy-done, bf16[528,768]{1,0:T(8,128)(2,1)} %copy-done.3, bf16[528,768]{1,0:T(8,128)(2,1)} %copy-done.1, bf16[528,768]{1,0:T(8,128)(2,1)} %copy-done.2), custom_call_target="tpu_custom_call" | custom-call | tf_op jit(solution)/shard_map/segment_starts/pallas_call | solution.py:197
  41.6 5.6 %collective-permute-done.4.ca = bf16[512,768]{1,0:T(8,128)(2,1)S(1)} collective-permute-done((bf16[512,768]{1,0:T(8,128)(2,1)}, bf16[512,768]{1,0:T(8,128)(2,1)S(1)}, u32[]{:S(2)}, u32[]{:S(2)}) %collective-permute-start.4) | collective-permute-done | bytes 786464 | tf_op jit(solution)/shard_map/ppermute | solution.py:1065
  47.2 13.0 %attend.1 = (bf16[2048,192]{1,0:T(8,128)(2,1)}, f32[3,8,1,256]{3,2,1,0:T(1,128)}) custom-call(s32[2]{0:T(128)} %pad_add_fusion.meta._, s32[8]{0:T(128)} %get-tuple-element.109.lo, s32[8]{0:T(128)} %get-tuple-element.110.hi, bf16[2048,192]{1,0:T(8,128)(2,1)} %get-tuple-element.107.q_ref, bf16[2048,192]{1,0:T(8,128)(2,1)} %get-tuple-element.111.k_ref, ...), custom_call_target="tpu_custom_call" | custom-call | flops 1000 | bytes 1000 | tf_op jit(solution)/shard_map/attend/pallas_call | solution.py:586
  61.1 20.2 %mlp_second.1 = (bf16[1024,768]{1,0:T(8,128)(2,1)}, bf16[2048,192]{1,0:T(8,128)(2,1)}, f32[8,768]{1,0:T(8,128)}, bf16[2,512,768]{2,1,0:T(8,128)(2,1)}, bf16[2,51...) custom-call(s32[2]{0:T(128)} %pad_add_fusion.meta._, ...), custom_call_target="tpu_custom_call", output_to_operand_aliasing={{1}: (19, {})} | custom-call | flops 1000 | bytes 1000 | tf_op jit(solution)/shard_map/mlp_second/pallas_call | solution.py:459
  81.8 21.2 %attend_back.1.refs_0_.refs_1_ = bf16[2048,576]{1,0:T(8,128)(2,1)} custom-call(s32[2]{0:T(128)} %pad_add_fusion.meta._, s32[8]{0:T(128)} %get-tuple-element.109.lo, s32[8]{0:T(128)} %get-tuple-element.110.hi, bf16[2048,192]{1,0:T(8,128)(2,1)} %get-tuple-element.107.q_ref, bf16[2048,192]{1,0:T(8,128)(2,1)} %get-tuple-element.111.k_ref, ...), custom_call_target="tpu_custom_call" | custom-call | flops 1000 | bytes 1000 | tf_op jit(solution)/shard_map/attend_back/pallas_call | solution.py:717
  103.2 7.9 %joined_first.1 = (bf16[2,512,768]{2,1,0:T(8,128)(2,1)}, f32[768,576]{1,0:T(8,128)}, f32[8,576]{1,0:T(8,128)}, f32[8,768]{1,0:T(8,128)}) custom-call(s32[2]{0:T(128)} %pad_add_fusion.meta._, bf16[2048,576]{1,0:T(8,128)(2,1)} %attend_back.1.refs_0_.refs_1_, bf16[2048,576]{1,0:T(8,128)(2,1)} %attend_back.1.refs_0_.refs_1_, ...), custom_call_target="tpu_custom_call" | custom-call | flops 1000 | bytes 1000 | tf_op jit(solution)/shard_map/joined_first/pallas_call | solution.py:863
  111.2 5.5 %collective-permute-start.7 = (bf16[384,1792]{1,0:T(8,128)(2,1)}, bf16[384,1792]{1,0:T(8,128)(2,1)S(1)}, u32[]{:S(2)}, u32[]{:S(2)}) collective-permute-start(bf16[384,1792]{1,0:T(8,128)(2,1)} %get-tuple-element.136), channel_id=1, source_target_pairs={{0,4},{4,0},{8,12},{12,8},{16,20},{20,16},{24,28},{28,24},{1,5},{5... | collective-permute-start | bytes 4128776 | tf_op jit(solution)/shard_map/ppermute | solution.py:1065
  117.6 30.0 %collective-permute-done.7.refs_1_ = bf16[384,1792]{1,0:T(8,128)(2,1)S(1)} collective-permute-done((bf16[384,1792]{1,0:T(8,128)(2,1)}, bf16[384,1792]{1,0:T(8,128)(2,1)S(1)}, u32[]{:S(2)}, u32[]{:S(2)}) %collective-permute-start.7) | collective-permute-done | bytes 1376288 | tf_op jit(solution)/shard_map/ppermute | solution.py:1065
  148.7 3.6 %fold.4 = (bf16[192,1792]{1,0:T(8,128)(2,1)}, bf16[192,1792]{1,0:T(8,128)(2,1)}) custom-call(s32[2]{0:T(128)} %pad_add_fusion.meta._, bf16[384,1792]{1,0:T(8,128)(2,1)} %get-tuple-element.135.refs_0_, bf16[384,1792]{1,0:T(8,128)(2,1)} %copy-done.8), custom_call_target="tpu_custom_call" | custom-call | flops 1000 | bytes 1000 | tf_op jit(solution)/shard_map/fold/pallas_call | solution.py:892
  154.0 8.3 %joined_second.1 = (bf16[2,512,768]{2,1,0:T(8,128)(2,1)}, bf16[416,576]{1,0:T(8,128)(2,1)}, bf16[416,576]{1,0:T(8,128)(2,1)}) custom-call(s32[2]{0:T(128)} %pad_add_fusion.meta._, bf16[2048,576]{1,0:T(8,128)(2,1)} %attend_back.1.refs_0_.refs_1_, bf16[2048,576]{1,0:T(8,128)(2,1)} %attend_back.1.refs_0_.refs_1_, bf16[1024,768]{1,0:T(8,128)(2,1)} %get-tuple-element.131.refs_2_, ...), custom_call_target="tpu_custom_call" | custom-call | flops 1000 | bytes 1000 | tf_op jit(solution)/shard_map/joined_second/pallas_call | solution.py:863
  162.3 1.9 fusion.3
  167.0 2.9 %result.1 = bf16[512,768]{1,0:T(8,128)(2,1)} custom-call(bf16[528,768]{1,0:T(8,128)(2,1)} %copy-done, bf16[2,512,768]{2,1,0:T(8,128)(2,1)} %get-tuple-element.128.even, bf16[2,512,768]{2,1,0:T(8,128)(2,1)} %copy-done.6, bf16[512,768]{1,0:T(8,128)(2,1)} %collective-permute-done.9.far, f32[768]{0:T(1024)} %b_out.1, f32[768]{0:T(1024)} %b_down.1), custom_call_target="tpu_custom_call" | custom-call | flops 1000 | bytes 1000 | tf_op jit(solution)/shard_map/result/pallas_call | solution.py:1139
  169.9 2.9 %fold.5 = (bf16[96,1792]{1,0:T(8,128)(2,1)}, bf16[96,1792]{1,0:T(8,128)(2,1)}) custom-call(s32[2]{0:T(128)} %pad_add_fusion.meta._, bf16[192,1792]{1,0:T(8,128)(2,1)} %get-tuple-element.145.refs_0_, bf16[192,1792]{1,0:T(8,128)(2,1)} %collective-permute-done.10.refs_1_), custom_call_target="tpu_custom_call" | custom-call | flops 1000 | bytes 1000 | tf_op jit(solution)/shard_map/fold/pallas_call | solution.py:892
  172.8 6.1 %collective-permute-done.11.refs_1_ = bf16[416,576]{1,0:T(8,128)(2,1)} collective-permute-done((bf16[416,576]{1,0:T(8,128)(2,1)}, bf16[416,576]{1,0:T(8,128)(2,1)}, u32[]{:S(2)}, u32[]{:S(2)}) %collective-permute-start.11) | collective-permute-done | bytes 479264 | tf_op jit(solution)/shard_map/ppermute | solution.py:1065
  178.9 2.8 %fold.6 = (bf16[224,576]{1,0:T(8,128)(2,1)}, bf16[224,576]{1,0:T(8,128)(2,1)}) custom-call(s32[2]{0:T(128)} %pad_add_fusion.meta._, bf16[416,576]{1,0:T(8,128)(2,1)} %get-tuple-element.148.refs_0_, bf16[416,576]{1,0:T(8,128)(2,1)} %collective-permute-done.11.refs_1_), custom_call_target="tpu_custom_call" | custom-call | flops 1000 | bytes 1000 | tf_op jit(solution)/shard_map/fold/pallas_call | solution.py:892
  182.1 2.6 %collective-permute-start.14 = (bf16[96,1792]{1,0:T(8,128)(2,1)}, bf16[96,1792]{1,0:T(8,128)(2,1)S(1)}, u32[]{:S(2)}, u32[]{:S(2)}) collective-permute-start(bf16[96,1792]{1,0:T(8,128)(2,1)} %get-tuple-element.146), channel_id=1, source_target_pairs={{0,16},{4,20},{8,24},{12,28},{16,0},{20,4},{24,8},{28,12},{1,17},{... | collective-permute-start | bytes 1032200 | tf_op jit(solution)/shard_map/ppermute | solution.py:1065
  185.6 3.4 %token_grad.1 = bf16[512,768]{1,0:T(8,128)(2,1)} custom-call(bf16[528,768]{1,0:T(8,128)(2,1)} %copy-done, bf16[2,512,768]{2,1,0:T(8,128)(2,1)} %get-tuple-element.141.even, bf16[2,512,768]{2,1,0:T(8,128)(2,1)} %copy-done.5, bf16[512,768]{1,0:T(8,128)(2,1)} %copy-done.11, bf16[512,768]{1,0:T(8,128)(2,1)} %bitcast.3.ca.c0.c_ref), custom_call_target="tpu_custom_call" | custom-call | flops 1000 | bytes 1000 | tf_op jit(solution)/shard_map/token_grad/pallas_call | solution.py:1139
  189.0 6.9 %collective-permute-done.13.refs_1_ = bf16[224,576]{1,0:T(8,128)(2,1)S(1)} collective-permute-done((bf16[224,576]{1,0:T(8,128)(2,1)}, bf16[224,576]{1,0:T(8,128)(2,1)S(1)}, u32[]{:S(2)}, u32[]{:S(2)}) %collective-permute-start.13) | collective-permute-done | bytes 258080 | tf_op jit(solution)/shard_map/ppermute | solution.py:1065
  196.7 2.5 %fold.7 = (bf16[128,576]{1,0:T(8,128)(2,1)}, bf16[128,576]{1,0:T(8,128)(2,1)}) custom-call(s32[2]{0:T(128)} %pad_add_fusion.meta._, bf16[224,576]{1,0:T(8,128)(2,1)} %get-tuple-element.153.refs_0_, bf16[224,576]{1,0:T(8,128)(2,1)} %copy-done.13), custom_call_target="tpu_custom_call" | custom-call | flops 1000 | bytes 1000 | tf_op jit(solution)/shard_map/fold/pallas_call | solution.py:892
  199.9 2.7 %last_packet.1 = (f32[96,768]{1,0:T(8,128)}, bf16[96,480]{1,0:T(8,128)(2,1)}, bf16[96,480]{1,0:T(8,128)(2,1)}) custom-call(s32[2]{0:T(128)} %pad_add_fusion.meta._, bf16[96,1792]{1,0:T(8,128)(2,1)} %get-tuple-element.156.keep, bf16[96,1792]{1,0:T(8,128)(2,1)} %copy-done.12), custom_call_target="tpu_custom_call" | custom-call | flops 1000 | bytes 1000 | tf_op jit(solution)/shard_map/last_packet/pallas_call | solution.py:892
  202.6 5.3 %collective-permute-done.17.got = bf16[128,576]{1,0:T(8,128)(2,1)S(1)} collective-permute-done((bf16[128,576]{1,0:T(8,128)(2,1)}, bf16[128,576]{1,0:T(8,128)(2,1)S(1)}, u32[]{:S(2)}, u32[]{:S(2)}) %collective-permute-start.17) | collective-permute-done | bytes 147488 | tf_op jit(solution)/shard_map/ppermute | solution.py:1065
  208.5 2.5 %last_qkv.1 = (f32[96,192]{1,0:T(8,128)}, f32[128,192]{1,0:T(8,128)}, f32[128,192]{1,0:T(8,128)}, f32[32,192]{1,0:T(8,128)}) custom-call(s32[2]{0:T(128)} %pad_add_fusion.meta._, bf16[128,576]{1,0:T(8,128)(2,1)} %get-tuple-element.163.keep, bf16[128,576]{1,0:T(8,128)(2,1)} %copy-done.14), custom_call_target="tpu_custom_call" | custom-call | flops 1000 | bytes 1000 | tf_op jit(solution)/shard_map/last_qkv/pallas_call | solution.py:892
  212.1 2.0 collective-permute-start.15
  214.1 3.9 %collective-permute-start.16 = (bf16[96,480]{1,0:T(8,128)(2,1)}, bf16[96,480]{1,0:T(8,128)(2,1)S(1)}, u32[]{:S(2)}, u32[]{:S(2)}) collective-permute-start(bf16[96,480]{1,0:T(8,128)(2,1)} %get-tuple-element.160), channel_id=1, source_target_pairs={{0,4},{1,12},{2,20},{3,28},{4,0},{5,8},{6,16},{7,24},{8,5},{9,13},... | collective-permute-start | bytes 276488 | tf_op jit(solution)/shard_map/ppermute | solution.py:1245
  218.0 5.9 %collective-permute-done.15.first = bf16[96,480]{1,0:T(8,128)(2,1)S(1)} collective-permute-done((bf16[96,480]{1,0:T(8,128)(2,1)}, bf16[96,480]{1,0:T(8,128)(2,1)S(1)}, u32[]{:S(2)}, u32[]{:S(2)}) %collective-permute-start.15) | collective-permute-done | bytes 92192 | tf_op jit(solution)/shard_map/ppermute | solution.py:1245
  226.1 2.6 %lower.1 = (f32[384,192]{1,0:T(8,128)}, f32[96,192]{1,0:T(8,128)}) custom-call(s32[2]{0:T(128)} %pad_add_fusion.meta._, bf16[96,480]{1,0:T(8,128)(2,1)} %copy-done.17, bf16[96,480]{1,0:T(8,128)(2,1)} %copy-done.18), custom_call_target="tpu_custom_call" | custom-call | flops 1000 | bytes 1000 | tf_op jit(solution)/shard_map/lower/pallas_call | solution.py:892
  228.7 1.9 copy.39
  231.2 2.7 %assemble.1 = (f32[96,576]{1,0:T(8,128)}, f32[2304]{0:T(1024)}, f32[768]{0:T(1024)}, f32[3072]{0:T(1024)}, f32[768]{0:T(1024)}, /*index=5*/f32[768]{0:T(1024)}, f32[768]{0:T(1024)}, f32[768]{0:T(1024)}, f32[768]{0:T(1024)}) custom-call(s32[2]{0:T(128)} %pad_add_fusion.meta._, f32[96,192]{1,0:T(8,128)} %get-tuple-element.164.kept, ...), custom_call_target="tpu_custom_call" | custom-call | flops 1000 | bytes 1000 | tf_op jit(solution)/shard_map/assemble/pallas_call | solution.py:1026
  (75 shorter events, 23.1 us)
Async XLA Ops:
  2.5 3.7 %copy-start = (bf16[528,768]{1,0:T(8,128)(2,1)}, bf16[528,768]{1,0:T(8,128)(2,1)S(1)}, u32[]{:S(2)}) copy-start(bf16[528,768]{1,0:T(8,128)(2,1)S(1)} %fusion.1.xa.s0.refs_4_.x_ref) | copy-start | bytes 2433028
  2.5 3.7 %collective-permute-start = (bf16[528,768]{1,0:T(8,128)(2,1)S(1)}, bf16[528,768]{1,0:T(8,128)(2,1)S(1)}, u32[]{:S(2)}, u32[]{:S(2)}) collective-permute-start(bf16[528,768]{1,0:T(8,128)(2,1)S(1)} %fusion.1.xa.s0.refs_4_.x_ref), channel_id=1, source_target_pairs={{0,1},{1,0},{2,3},{3,2},{4,5},{5,4},{6,7},{7,6},{8,9},{9,8},{10,11... | collective-permute-start | bytes 2433032 | tf_op jit(solution)/shard_map/ppermute | solution.py:1065
  2.6 24.1 %collective-permute-start.2 = (bf16[528,768]{1,0:T(8,128)(2,1)S(1)}, bf16[528,768]{1,0:T(8,128)(2,1)S(1)}, u32[]{:S(2)}, u32[]{:S(2)}) collective-permute-start(bf16[528,768]{1,0:T(8,128)(2,1)S(1)} %fusion.1.xa.s0.refs_4_.x_ref), channel_id=1, source_target_pairs={{0,2},{1,3},{2,0},{3,1},{4,6},{5,7},{6,4},{7,5},{8,10},{9,11},{10,... | collective-permute-start | bytes 2433032 | tf_op jit(solution)/shard_map/ppermute | solution.py:1065
  2.7 3.6 %collective-permute-start.1 = (bf16[512,768]{1,0:T(8,128)(2,1)}, bf16[512,768]{1,0:T(8,128)(2,1)S(1)}, u32[]{:S(2)}, u32[]{:S(2)}) collective-permute-start(bf16[512,768]{1,0:T(8,128)(2,1)} %bitcast.3.ca.c0.c_ref), channel_id=1, source_target_pairs={{0,1},{1,0},{2,3},{3,2},{4,5},{5,4},{6,7},{7,6},{8,9},{9,8},{10,11... | collective-permute-start | bytes 2359304 | tf_op jit(solution)/shard_map/ppermute | solution.py:1065
  6.3 0.9 copy-start.7
  7.2 0.9 copy-start.3
  26.7 2.4 %copy-start.1 = (bf16[528,768]{1,0:T(8,128)(2,1)}, bf16[528,768]{1,0:T(8,128)(2,1)S(1)}, u32[]{:S(2)}) copy-start(bf16[528,768]{1,0:T(8,128)(2,1)S(1)} %collective-permute-done.2.x_ref.s2.xa.refs_5_) | copy-start | bytes 2433028
  26.7 7.0 %collective-permute-start.3 = (bf16[528,768]{1,0:T(8,128)(2,1)S(1)}, bf16[528,768]{1,0:T(8,128)(2,1)S(1)}, u32[]{:S(2)}, u32[]{:S(2)}) collective-permute-start(bf16[528,768]{1,0:T(8,128)(2,1)S(1)} %collective-permute-done.2.x_ref.s2.xa.refs_5_), channel_id=1, source_target_pairs={{0,1},{1,0},{2,3},{3,2},{4,5},{5,4},{6,7},{7,6},{8,9},{9,8},{10,11... | collective-permute-start | bytes 2433032 | tf_op jit(solution)/shard_map/ppermute | solution.py:1065
  27.5 19.7 %collective-permute-start.4 = (bf16[512,768]{1,0:T(8,128)(2,1)}, bf16[512,768]{1,0:T(8,128)(2,1)S(1)}, u32[]{:S(2)}, u32[]{:S(2)}) collective-permute-start(bf16[512,768]{1,0:T(8,128)(2,1)} %bitcast.3.ca.c0.c_ref), channel_id=1, source_target_pairs={{0,2},{1,3},{2,0},{3,1},{4,6},{5,7},{6,4},{7,5},{8,10},{9,11},{10,... | collective-permute-start | bytes 2359304 | tf_op jit(solution)/shard_map/ppermute | solution.py:1065
  47.2 13.0 %copy-start.9 = (bf16[512,768]{1,0:T(8,128)(2,1)}, bf16[512,768]{1,0:T(8,128)(2,1)S(1)}, u32[]{:S(2)}) copy-start(bf16[512,768]{1,0:T(8,128)(2,1)S(1)} %collective-permute-done.4.ca) | copy-start | bytes 2359300
  47.2 13.0 %collective-permute-start.5 = (bf16[512,768]{1,0:T(8,128)(2,1)S(1)}, bf16[512,768]{1,0:T(8,128)(2,1)S(1)}, u32[]{:S(2)}, u32[]{:S(2)}) collective-permute-start(bf16[512,768]{1,0:T(8,128)(2,1)S(1)} %collective-permute-done.4.ca), channel_id=1, source_target_pairs={{0,1},{1,0},{2,3},{3,2},{4,5},{5,4},{6,7},{7,6},{8,9},{9,8},{10,11... | collective-permute-start | bytes 2359304 | tf_op jit(solution)/shard_map/ppermute | solution.py:1065
  60.2 0.9 copy-start.10
  81.3 21.7 %collective-permute-start.6 = (bf16[2,512,768]{2,1,0:T(8,128)(2,1)}, bf16[2,512,768]{2,1,0:T(8,128)(2,1)S(1)}, u32[]{:S(2)}, u32[]{:S(2)}) collective-permute-start(bf16[2,512,768]{2,1,0:T(8,128)(2,1)} %get-tuple-element.129), channel_id=1, source_target_pairs={{0,1},{1,0},{2,3},{3,2},{4,5},{5,4},{6,7},{7,6},{8,9},{9,8},{10,11... | collective-permute-start | bytes 4718600 | tf_op jit(solution)/shard_map/ppermute | solution.py:1065
  81.8 21.2 %copy-start.4 = (bf16[2,512,768]{2,1,0:T(8,128)(2,1)S(1)}, bf16[2,512,768]{2,1,0:T(8,128)(2,1)}, u32[]{:S(2)}) copy-start(bf16[2,512,768]{2,1,0:T(8,128)(2,1)} %get-tuple-element.128.even) | copy-start | bytes 4718596
  103.0 8.1 %copy-start.6 = (bf16[2,512,768]{2,1,0:T(8,128)(2,1)}, bf16[2,512,768]{2,1,0:T(8,128)(2,1)S(1)}, u32[]{:S(2)}) copy-start(bf16[2,512,768]{2,1,0:T(8,128)(2,1)S(1)} %collective-permute-done.6.near) | copy-start | bytes 4718596
  111.1 51.2 %collective-permute-start.8 = (bf16[2,512,768]{2,1,0:T(8,128)(2,1)}, bf16[2,512,768]{2,1,0:T(8,128)(2,1)S(1)}, u32[]{:S(2)}, u32[]{:S(2)}) collective-permute-start(bf16[2,512,768]{2,1,0:T(8,128)(2,1)} %get-tuple-element.142), channel_id=1, source_target_pairs={{0,1},{1,0},{2,3},{3,2},{4,5},{5,4},{6,7},{7,6},{8,9},{9,8},{10,11... | collective-permute-start | bytes 4718600 | tf_op jit(solution)/shard_map/ppermute | solution.py:1065
  111.2 36.4 %collective-permute-start.7 = (bf16[384,1792]{1,0:T(8,128)(2,1)}, bf16[384,1792]{1,0:T(8,128)(2,1)S(1)}, u32[]{:S(2)}, u32[]{:S(2)}) collective-permute-start(bf16[384,1792]{1,0:T(8,128)(2,1)} %get-tuple-element.136), channel_id=1, source_target_pairs={{0,4},{4,0},{8,12},{12,8},{16,20},{20,16},{24,28},{28,24},{1,5},{5... | collective-permute-start | bytes 4128776 | tf_op jit(solution)/shard_map/ppermute | solution.py:1065
  116.7 50.3 %collective-permute-start.9 = (bf16[512,768]{1,0:T(8,128)(2,1)S(1)}, bf16[512,768]{1,0:T(8,128)(2,1)}, u32[]{:S(2)}, u32[]{:S(2)}) collective-permute-start(bf16[512,768]{1,0:T(8,128)(2,1)S(1)} %fusion.2), channel_id=1, source_target_pairs={{0,2},{1,3},{2,0},{3,1},{4,6},{5,7},{6,4},{7,5},{8,10},{9,11},{10,... | collective-permute-start | bytes 2359304 | tf_op jit(solution)/shard_map/ppermute | solution.py:1065
  147.6 1.1 copy-start.8
  152.4 17.5 %collective-permute-start.10 = (bf16[192,1792]{1,0:T(8,128)(2,1)}, bf16[192,1792]{1,0:T(8,128)(2,1)}, u32[]{:S(2)}, u32[]{:S(2)}) collective-permute-start(bf16[192,1792]{1,0:T(8,128)(2,1)} %get-tuple-element.137), channel_id=1, source_target_pairs={{0,8},{4,12},{8,0},{12,4},{16,24},{20,28},{24,16},{28,20},{1,9},{5... | collective-permute-start | bytes 2064392 | tf_op jit(solution)/shard_map/ppermute | solution.py:1065
  162.3 7.6 %copy-start.5 = (bf16[2,512,768]{2,1,0:T(8,128)(2,1)}, bf16[2,512,768]{2,1,0:T(8,128)(2,1)S(1)}, u32[]{:S(2)}) copy-start(bf16[2,512,768]{2,1,0:T(8,128)(2,1)S(1)} %collective-permute-done.8.near) | copy-start | bytes 4718596
  164.2 20.5 %collective-permute-start.12 = (bf16[512,768]{1,0:T(8,128)(2,1)S(1)}, bf16[512,768]{1,0:T(8,128)(2,1)S(1)}, u32[]{:S(2)}, u32[]{:S(2)}) collective-permute-start(bf16[512,768]{1,0:T(8,128)(2,1)S(1)} %fusion.3), channel_id=1, source_target_pairs={{0,2},{1,3},{2,0},{3,1},{4,6},{5,7},{6,4},{7,5},{8,10},{9,11},{10,... | collective-permute-start | bytes 2359304 | tf_op jit(solution)/shard_map/ppermute | solution.py:1065
  165.2 13.6 %collective-permute-start.11 = (bf16[416,576]{1,0:T(8,128)(2,1)}, bf16[416,576]{1,0:T(8,128)(2,1)}, u32[]{:S(2)}, u32[]{:S(2)}) collective-permute-start(bf16[416,576]{1,0:T(8,128)(2,1)} %get-tuple-element.149), channel_id=1, source_target_pairs={{0,4},{4,0},{8,12},{12,8},{16,20},{20,16},{24,28},{28,24},{1,5},{5... | collective-permute-start | bytes 1437704 | tf_op jit(solution)/shard_map/ppermute | solution.py:1065
  181.7 14.3 %collective-permute-start.13 = (bf16[224,576]{1,0:T(8,128)(2,1)}, bf16[224,576]{1,0:T(8,128)(2,1)S(1)}, u32[]{:S(2)}, u32[]{:S(2)}) collective-permute-start(bf16[224,576]{1,0:T(8,128)(2,1)} %get-tuple-element.150), channel_id=1, source_target_pairs={{0,8},{4,12},{8,0},{12,4},{16,24},{20,28},{24,16},{28,20},{1,9},{5... | collective-permute-start | bytes 774152 | tf_op jit(solution)/shard_map/ppermute | solution.py:1065
  182.1 17.1 %collective-permute-start.14 = (bf16[96,1792]{1,0:T(8,128)(2,1)}, bf16[96,1792]{1,0:T(8,128)(2,1)S(1)}, u32[]{:S(2)}, u32[]{:S(2)}) collective-permute-start(bf16[96,1792]{1,0:T(8,128)(2,1)} %get-tuple-element.146), channel_id=1, source_target_pairs={{0,16},{4,20},{8,24},{12,28},{16,0},{20,4},{24,8},{28,12},{1,17},{... | collective-permute-start | bytes 1032200 | tf_op jit(solution)/shard_map/ppermute | solution.py:1065
  199.2 8.7 %collective-permute-start.17 = (bf16[128,576]{1,0:T(8,128)(2,1)}, bf16[128,576]{1,0:T(8,128)(2,1)S(1)}, u32[]{:S(2)}, u32[]{:S(2)}) collective-permute-start(bf16[128,576]{1,0:T(8,128)(2,1)} %get-tuple-element.154), channel_id=1, source_target_pairs={{0,16},{4,20},{8,24},{12,28},{16,0},{20,4},{24,8},{28,12},{1,17},{... | collective-permute-start | bytes 442376 | tf_op jit(solution)/shard_map/ppermute | solution.py:1065
  211.1 19.5 %collective-permute-start.18 = (f32[128,192]{1,0:T(8,128)}, f32[128,192]{1,0:T(8,128)S(1)}, u32[]{:S(2)}, u32[]{:S(2)}) collective-permute-start(f32[128,192]{1,0:T(8,128)} %get-tuple-element.166), channel_id=1, source_target_pairs={{0,1},{1,0},{2,3},{3,2},{4,5},{5,4},{6,7},{7,6},{8,9},{9,8},{10,11... | collective-permute-start | bytes 294920 | tf_op jit(solution)/shard_map/ppermute | solution.py:1065
  211.1 19.5 %collective-permute-start.19 = (f32[128,192]{1,0:T(8,128)}, f32[128,192]{1,0:T(8,128)S(1)}, u32[]{:S(2)}, u32[]{:S(2)}) collective-permute-start(f32[128,192]{1,0:T(8,128)} %get-tuple-element.167), channel_id=1, source_target_pairs={{0,2},{1,3},{2,0},{3,1},{4,6},{5,7},{6,4},{7,5},{8,10},{9,11},{10,... | collective-permute-start | bytes 294920 | tf_op jit(solution)/shard_map/ppermute | solution.py:1065
  212.1 11.7 %collective-permute-start.15 = (bf16[96,480]{1,0:T(8,128)(2,1)}, bf16[96,480]{1,0:T(8,128)(2,1)S(1)}, u32[]{:S(2)}, u32[]{:S(2)}) collective-permute-start(bf16[96,480]{1,0:T(8,128)(2,1)} %get-tuple-element.159), channel_id=1, source_target_pairs={{0,0},{1,8},{2,16},{3,24},{4,4},{5,12},{6,20},{7,28},{8,1},{9,9},{... | collective-permute-start | bytes 276488 | tf_op jit(solution)/shard_map/ppermute | solution.py:1245
  214.1 11.3 %collective-permute-start.16 = (bf16[96,480]{1,0:T(8,128)(2,1)}, bf16[96,480]{1,0:T(8,128)(2,1)S(1)}, u32[]{:S(2)}, u32[]{:S(2)}) collective-permute-start(bf16[96,480]{1,0:T(8,128)(2,1)} %get-tuple-element.160), channel_id=1, source_target_pairs={{0,4},{1,12},{2,20},{3,28},{4,0},{5,8},{6,16},{7,24},{8,5},{9,13},... | collective-permute-start | bytes 276488 | tf_op jit(solution)/shard_map/ppermute | solution.py:1245
  218.0 12.6 %collective-permute-start.20 = (f32[32,192]{1,0:T(8,128)}, f32[32,192]{1,0:T(8,128)S(1)}, u32[]{:S(2)}, u32[]{:S(2)}) collective-permute-start(f32[32,192]{1,0:T(8,128)} %get-tuple-element.165.small), channel_id=1, source_target_pairs={{0,3},{1,2},{2,1},{3,0},{4,7},{5,6},{6,5},{7,4},{8,11},{9,10},{10,... | collective-permute-start | bytes 73736 | tf_op jit(solution)/shard_map/ppermute | solution.py:1065
  223.8 1.6 copy-start.17
  (9 other events, 6.5 us)

commit v4 on v3

--- a/solution.py
+++ b/solution.py
@@ -23,7 +23,7 @@
 LANES = 128
 F32 = jnp.float32
 BF16 = jnp.bfloat16
-COST = pl.CostEstimate(flops=1000, bytes_accessed=1000, transcendentals=0)
+COST = pl.CostEstimate(flops=0, bytes_accessed=0, transcendentals=0)
 NT_DIMS = (((1,), (1,)), ((), ()))
 TN_DIMS = (((0,), (0,)), ((), ()))
 
@@ -208,6 +208,7 @@
             out_specs=[whole((tiles, 1, TILE)), smem, smem],
         ),
         compiler_params=params(),
+        cost_estimate=COST,
         name="segment_starts",
     )(meta, valid_len, *toks)
 
@@ -749,9 +750,9 @@
     gj_a, gj_b, e_a, e_b, x_a, x_b, gain_ref, shift_ref, w_ref = refs[:9]
     if final:
         grad_in, bias_in, sums_in, mlp_sums = refs[9:13]
-        e_ref, keep, send, grad, bias, sums = refs[13:]
+        *e_refs, keep, send, grad, bias, sums = refs[13:]
     else:
-        e_ref, grad, bias, sums = refs[9:]
+        *e_refs, grad, bias, sums = refs[9:]
     step = pl.program_id(0)
 
     @pl.when(step == 0)
@@ -771,7 +772,7 @@
         attn_in = (normed * gain + shift).astype(BF16)
         low = gj_ref[...]
         grad_norm = dot_nt(low, w_ref[...])
-        e_ref[index] = (grad_norm * gain + e_in[...].astype(F32)).astype(BF16)
+        e_refs[index][...] = (grad_norm * gain + e_in[...].astype(F32)).astype(BF16)
         sums[0:1, :] += jnp.sum(grad_norm * normed, axis=0, keepdims=True)
         sums[1:2, :] += jnp.sum(grad_norm, axis=0, keepdims=True)
         bias[0:1, :] += jnp.sum(low.astype(F32), axis=0, keepdims=True)
@@ -833,8 +834,8 @@
         whole(shift.shape),
         whole(w.shape),
     ]
-    e_spec = pl.BlockSpec((2, TILE, D), lambda i, m: (0, i, 0))
-    outs, out_specs = [jax.ShapeDtypeStruct((2, seq, D), BF16)], [e_spec]
+    e_spec = pl.BlockSpec((TILE, D), lambda i, m: (i, 0))
+    outs, out_specs = [jax.ShapeDtypeStruct((seq, D), BF16)] * 2, [e_spec] * 2
     carried = [(D, width), (8, width), sums]
     scratch = []
     if before is None:
@@ -857,8 +858,8 @@
     if before is not None and not fits(rows):
 
         def body(meta, *refs):
-            inputs, (e_ref, keep, send, bias, sums, grad) = refs[:13], refs[13:]
-            joined_kernel(True, rows, meta, *inputs, e_ref, keep, send, grad, bias, sums)
+            inputs, (e_a, e_b, keep, send, bias, sums, grad) = refs[:13], refs[13:]
+            joined_kernel(True, rows, meta, *inputs, e_a, e_b, keep, send, grad, bias, sums)
 
     return pl.pallas_call(
         body,
@@ -1126,7 +1127,7 @@
     center = wide - jnp.mean(wide, axis=-1, keepdims=True)
     rate = lax.rsqrt(jnp.mean(center * center, axis=-1, keepdims=True) + EPS)
     normed = center * rate
-    grad = even[0].astype(F32) + near[0].astype(F32) + far[...].astype(F32)
+    grad = even[...].astype(F32) + near[...].astype(F32) + far[...].astype(F32)
     mean = jnp.mean(grad, axis=-1, keepdims=True)
     along = jnp.mean(grad * normed, axis=-1, keepdims=True)
     back = rate * (grad - mean - normed * along)
@@ -1140,7 +1141,10 @@
         body,
         out_shape=jax.ShapeDtypeStruct((seq, D), BF16),
         grid=(seq // TILE,),
-        in_specs=[flat, own, own, flat, *(flat if a.ndim == 2 else whole(a.shape) for a in more)],
+        in_specs=[
+            *(own if a.ndim == 3 else flat for a in (x, even, near, far)),
+            *(flat if a.ndim == 2 else whole(a.shape) for a in more),
+        ],
         out_specs=flat,
         compiler_params=params(),
         cost_estimate=COST,
@@ -1166,7 +1170,8 @@
     cot_near = swap(cot_own, "blk", 1)
     tok_far = swap(tok_own, "blk", 2)
     tok_near = swap(tok_own, "blk", 1)
-    cot_far = swap(after(cot_own, tok_near), "blk", 2)
+    cot_long = jnp.pad(cot_own, ((0, 2 * EXTRA), (0, 0)))
+    cot_far = swap(cot_long, "blk", 2)
 
     meta = jnp.stack([blk, lax.axis_index("rows")]).astype(jnp.int32)
     mlp_args = (ln2_gain, ln2_bias, b_up, w_up, w_down, w_out, rows, seq)
@@ -1206,19 +1211,20 @@
     out_far = swap(out_send, "blk", 2)
     joined_args = (grad_joined, e_mlp, toks, ln1_gain, ln1_bias, w_own, rows, seq)
     meta = after(meta, out_send)
-    e_odd, *carried = joined_back(meta, (1, 3), *joined_args)
-    e_got = swap(e_odd, "blk", 1)
+    e_near, e_last, *carried = joined_back(meta, (1, 3), *joined_args)
+    e_last = swap(e_last, "blk", 1)
+    e_near = swap(e_near, "blk", 1)
     meta = after(meta, carried[1])
     if fits(rows):
         keep, send = fold(meta, keep, got, 0)
         got = swap(send, "rows", 2)
         meta = after(meta, send)
-    e_even, qkv_keep, qkv_send, *rest = joined_back(
+    e_own, e_send, qkv_keep, qkv_send, *rest = joined_back(
         meta, (0, 2), *joined_args, carried, mlp_sums
     )
     qkv_keep, qkv_send = chunks_of(qkv_keep, qkv_send, rows)
     qkv_got = swap(qkv_send, "rows", 1)
-    e_send = add_low(e_even[1], e_got[1])
+    e_send = add_low(e_send, e_last)
     e_far = swap(e_send, "blk", 2)
 
     out_args = (after(tok_own, e_send), out_even, out_got, out_far, b_out, b_down)
@@ -1230,7 +1236,7 @@
         meta = after(meta, send)
         qkv_keep, qkv_send = fold(meta, qkv_keep, qkv_got, SMALL)
         qkv_got = swap(qkv_send, "rows", 2)
-        tok_args = (after(tok_own, qkv_send), e_even, e_got, e_far, cot_own)
+        tok_args = (after(tok_own, qkv_send), e_own, e_near, e_far, cot_own)
         grad_tokens = finish(token_kernel, "token_grad", seq, *tok_args)
         meta = after(meta, grad_tokens)
         qkv_keep, qkv_send = fold(meta, qkv_keep, qkv_got, SMALL)
@@ -1271,7 +1277,7 @@
         near, far = swap(near, "blk", 1), swap(far, "blk", 2)
         ends = [jnp.where(blk % 2 == 0, a, b) for a, b in ((kept, far), (far, kept))]
         qkv = jnp.concatenate([ends[0], near, ends[1]], axis=1)
-        tok_args = (tok_own, e_even, e_got, e_far, cot_own)
+        tok_args = (tok_own, e_own, e_near, e_far, cot_own)
         grad_tokens = finish(token_kernel, "token_grad", seq, *tok_args)
         bias, sums = rest
         mine = (jnp.arange(4) == blk)[:, None]

time: 235 us -> 199 us (0.85)
  waiting for transfers between devices: 63.9 us -> 30.9 us
  starting transfers between devices: 23.7 us -> 17.1 us
  Pallas kernels: 129 us -> 133 us
    ppermute x19 -> x20, waiting for transfers between devices: 56.5 us -> 21.3 us  [swap(): return lax.ppermute(value, axis, [(i, i ^ mask) for i in range(size)])]
    ppermute x19 -> x20, starting transfers between devices: 17.8 us -> 11.4 us  [swap(): return lax.ppermute(value, axis, [(i, i ^ mask) for i in range(size)])]
    pallas_call x1, Pallas kernels: 21.2 us -> 23.8 us  [attend_back(): pl.pallas_call(partial(attend_back_kernel, per), out_shape=jax.ShapeDtype...]
    unnamed x41 -> x39, local copies, waits for them, and re-layouts: 10.9 us -> 10 us
  transfers between devices with their start and end apart: 21 -> 22, of which waited for: 8 -> 8; matrix products, arithmetic and copies ran while one was open for 2% -> 2% of each run, Pallas kernels for 41% -> 54%
where the time goes in v4:
time: 199 us; the launch traced here: 198 us
  Pallas kernels  133 us (67%)
  waiting for transfers between devices  30.9 us (16%)
  starting transfers between devices  17.1 us (9%)
  local copies, waits for them, and re-layouts  11 us (6%)
  other arithmetic  4.05 us (2%)
    pallas_call x2, Pallas kernels, feed_forward(): pl.pallas_call(body, out_shape=outs, grid_spec=pltpu.PrefetchScalarGridSp...  38.9 us
    pallas_call x1, Pallas kernels, attend_back(): pl.pallas_call(partial(attend_back_kernel, per), out_shape=jax.ShapeDtype...  23.8 us
    ppermute x20, waiting for transfers between devices, swap(): return lax.ppermute(value, axis, [(i, i ^ mask) for i in range(size)])  21.3 us
    pallas_call x7, Pallas kernels, simple(): pl.pallas_call(body, out_shape=[jax.ShapeDtypeStruct(shape, kind) for sha...  19.7 us
    pallas_call x2, Pallas kernels, joined_back(): pl.pallas_call(body, out_shape=outs, grid_spec=pltpu.PrefetchScalarGridSp...  15.9 us
    pallas_call x1, Pallas kernels, attend(): pl.pallas_call(partial(attend_kernel, per), out_shape=[jax.ShapeDtypeStru...  14.1 us
    ppermute x20, starting transfers between devices, swap(): return lax.ppermute(value, axis, [(i, i ^ mask) for i in range(size)])  11.4 us
    unnamed x39, local copies, waits for them, and re-layouts  10 us
  transfers between devices with their start and end apart: 22, of which 8 were waited for; matrix products, arithmetic and copies ran while one was open for 2% of the time, Pallas kernels for 54%

profile of v4, /device:TPU:2, one launch (start us, length us, event | category | flops | bytes accessed | tf_op | source)
XLA Modules:
  0.0 197.6 jit_solution(7642250419209367081)
XLA Ops:
  4.1 1.8 collective-permute-start.4
  7.4 18.7 %mlp_first.1 = (bf16[1024,768]{1,0:T(8,128)(2,1)}, bf16[1024,768]{1,0:T(8,128)(2,1)}, bf16[2048,192]{1,0:T(8,128)(2,1)}, f32[8,768]{1,0:T(8,128)}, f32[768,768]{...) custom-call(s32[2]{0:T(128)} %pad_add_fusion.meta._, ...), custom_call_target="tpu_custom_call" | custom-call | tf_op jit(solution)/shard_map/mlp_first/pallas_call | solution.py:460
  27.5 4.6 %qkv_2.1 = (bf16[2048,192]{1,0:T(8,128)(2,1)}, bf16[2048,192]{1,0:T(8,128)(2,1)}, bf16[2048,192]{1,0:T(8,128)(2,1)}) custom-call(s32[2]{0:T(128)} %pad_add_fusion.meta._, bf16[528,768]{1,0:T(8,128)(2,1)} %copy-done.1, f32[768]{0:T(1024)} %refs_6_.3, f32[768]{0:T(1024)} %refs_7_.3, ...), custom_call_target="tpu_custom_call", output_to_operand_aliasing={{0}: (8, {}), {1}: (9, {}), {2}: (10, {})} | custom-call | tf_op jit(solution)/shard_map/qkv_2/pallas_call | solution.py:159
  32.9 4.6 %qkv_3.1 = (bf16[2048,192]{1,0:T(8,128)(2,1)}, bf16[2048,192]{1,0:T(8,128)(2,1)}, bf16[2048,192]{1,0:T(8,128)(2,1)}) custom-call(s32[2]{0:T(128)} %pad_add_fusion.meta._, bf16[528,768]{1,0:T(8,128)(2,1)} %copy-done.2, f32[768]{0:T(1024)} %refs_6_.3, f32[768]{0:T(1024)} %refs_7_.3, ...), custom_call_target="tpu_custom_call", output_to_operand_aliasing={{0}: (8, {}), {1}: (9, {}), {2}: (10, {})} | custom-call | tf_op jit(solution)/shard_map/qkv_3/pallas_call | solution.py:159
  37.5 2.4 %segment_starts.1 = (s32[8,1,256]{2,1,0:T(1,128)}, s32[8]{0:T(128)}, s32[8]{0:T(128)}) custom-call(s32[2]{0:T(128)} %pad_add_fusion.meta._, s32[1]{0:T(128)S(6)} %copy.47.valid, bf16[528,768]{1,0:T(8,128)(2,1)} %copy-done, bf16[528,768]{1,0:T(8,128)(2,1)} %copy-done.4, bf16[528,768]{1,0:T(8,128)(2,1)} %copy-done.1, bf16[528,768]{1,0:T(8,128)(2,1)} %copy-done.2), custom_call_target="tpu_custom_call" | custom-call | tf_op jit(solution)/shard_map/segment_starts/pallas_call | solution.py:197
  41.2 14.1 %attend.1 = (bf16[2048,192]{1,0:T(8,128)(2,1)}, f32[3,8,1,256]{3,2,1,0:T(1,128)}) custom-call(s32[2]{0:T(128)} %pad_add_fusion.meta._, s32[8]{0:T(128)} %get-tuple-element.110.lo, s32[8]{0:T(128)} %get-tuple-element.111.hi, bf16[2048,192]{1,0:T(8,128)(2,1)} %get-tuple-element.108.q_ref, bf16[2048,192]{1,0:T(8,128)(2,1)} %get-tuple-element.112.k_ref, ...), custom_call_target="tpu_custom_call" | custom-call | tf_op jit(solution)/shard_map/attend/pallas_call | solution.py:587
  56.2 20.2 %mlp_second.1 = (bf16[1024,768]{1,0:T(8,128)(2,1)}, bf16[2048,192]{1,0:T(8,128)(2,1)}, f32[8,768]{1,0:T(8,128)}, bf16[2,512,768]{2,1,0:T(8,128)(2,1)}, bf16[2,51...) custom-call(s32[2]{0:T(128)} %pad_add_fusion.meta._, ...), custom_call_target="tpu_custom_call", output_to_operand_aliasing={{1}: (19, {})} | custom-call | tf_op jit(solution)/shard_map/mlp_second/pallas_call | solution.py:460
  77.3 23.8 %attend_back.1.refs_0_.refs_1_ = bf16[2048,576]{1,0:T(8,128)(2,1)} custom-call(s32[2]{0:T(128)} %pad_add_fusion.meta._, s32[8]{0:T(128)} %get-tuple-element.110.lo, s32[8]{0:T(128)} %get-tuple-element.111.hi, bf16[2048,192]{1,0:T(8,128)(2,1)} %get-tuple-element.108.q_ref, bf16[2048,192]{1,0:T(8,128)(2,1)} %get-tuple-element.112.k_ref, ...), custom_call_target="tpu_custom_call" | custom-call | tf_op jit(solution)/shard_map/attend_back/pallas_call | solution.py:718
  101.4 7.6 %joined_first.1 = (bf16[512,768]{1,0:T(8,128)(2,1)}, bf16[512,768]{1,0:T(8,128)(2,1)}, f32[768,576]{1,0:T(8,128)}, f32[8,576]{1,0:T(8,128)}, f32[8,768]{1,0:T(8,128)}) custom-call(s32[2]{0:T(128)} %pad_add_fusion.meta._, bf16[2048,576]{1,0:T(8,128)(2,1)} %attend_back.1.refs_0_.refs_1_, bf16[2048,576]{1,0:T(8,128)(2,1)} %attend_back.1.refs_0_.refs_1_, ...), custom_call_target="tpu_custom_call" | custom-call | tf_op jit(solution)/shard_map/joined_first/pallas_call | solution.py:864
  109.8 3.7 %fold.4 = (bf16[192,1792]{1,0:T(8,128)(2,1)}, bf16[192,1792]{1,0:T(8,128)(2,1)}) custom-call(s32[2]{0:T(128)} %pad_add_fusion.meta._, bf16[384,1792]{1,0:T(8,128)(2,1)} %get-tuple-element.135.refs_0_, bf16[384,1792]{1,0:T(8,128)(2,1)} %collective-permute-done.7.refs_1_), custom_call_target="tpu_custom_call" | custom-call | tf_op jit(solution)/shard_map/fold/pallas_call | solution.py:893
  114.4 8.3 %joined_second.1 = (bf16[512,768]{1,0:T(8,128)(2,1)}, bf16[512,768]{1,0:T(8,128)(2,1)}, bf16[416,576]{1,0:T(8,128)(2,1)}, bf16[416,576]{1,0:T(8,128)(2,1)}) custom-call(s32[2]{0:T(128)} %pad_add_fusion.meta._, bf16[2048,576]{1,0:T(8,128)(2,1)} %attend_back.1.refs_0_.refs_1_, bf16[2048,576]{1,0:T(8,128)(2,1)} %attend_back.1.refs_0_.refs_1_, ...), custom_call_target="tpu_custom_call" | custom-call | tf_op jit(solution)/shard_map/joined_second/pallas_call | solution.py:864
  122.7 1.3 add_convert_fusion
  125.2 4.3 %collective-permute-done.9.far = bf16[512,768]{1,0:T(8,128)(2,1)S(1)} collective-permute-done((bf16[512,768]{1,0:T(8,128)(2,1)S(1)}, bf16[512,768]{1,0:T(8,128)(2,1)S(1)}, u32[]{:S(2)}, u32[]{:S(2)}) %collective-permute-start.9) | collective-permute-done | bytes 786464 | tf_op jit(solution)/shard_map/ppermute | solution.py:1066
  130.4 2.8 %result.1 = bf16[512,768]{1,0:T(8,128)(2,1)} custom-call(bf16[528,768]{1,0:T(8,128)(2,1)} %copy-done, bf16[2,512,768]{2,1,0:T(8,128)(2,1)} %get-tuple-element.128.even, bf16[2,512,768]{2,1,0:T(8,128)(2,1)} %copy-done.6, bf16[512,768]{1,0:T(8,128)(2,1)} %copy-done.10, f32[768]{0:T(1024)} %b_out.1, f32[768]{0:T(1024)} %b_down.1), custom_call_target="tpu_custom_call" | custom-call | tf_op jit(solution)/shard_map/result/pallas_call | solution.py:1140
  133.3 2.9 %fold.5 = (bf16[96,1792]{1,0:T(8,128)(2,1)}, bf16[96,1792]{1,0:T(8,128)(2,1)}) custom-call(s32[2]{0:T(128)} %pad_add_fusion.meta._, bf16[192,1792]{1,0:T(8,128)(2,1)} %get-tuple-element.145.refs_0_, bf16[192,1792]{1,0:T(8,128)(2,1)} %collective-permute-done.10.refs_1_), custom_call_target="tpu_custom_call" | custom-call | tf_op jit(solution)/shard_map/fold/pallas_call | solution.py:893
  136.2 3.6 %collective-permute-done.11.refs_1_ = bf16[416,576]{1,0:T(8,128)(2,1)} collective-permute-done((bf16[416,576]{1,0:T(8,128)(2,1)}, bf16[416,576]{1,0:T(8,128)(2,1)}, u32[]{:S(2)}, u32[]{:S(2)}) %collective-permute-start.11) | collective-permute-done | bytes 479264 | tf_op jit(solution)/shard_map/ppermute | solution.py:1066
  139.8 2.8 %fold.6 = (bf16[224,576]{1,0:T(8,128)(2,1)}, bf16[224,576]{1,0:T(8,128)(2,1)}) custom-call(s32[2]{0:T(128)} %pad_add_fusion.meta._, bf16[416,576]{1,0:T(8,128)(2,1)} %get-tuple-element.148.refs_0_, bf16[416,576]{1,0:T(8,128)(2,1)} %collective-permute-done.11.refs_1_), custom_call_target="tpu_custom_call" | custom-call | tf_op jit(solution)/shard_map/fold/pallas_call | solution.py:893
  142.6 1.4 collective-permute-start.14
  144.0 2.3 %collective-permute-start.15 = (bf16[96,1792]{1,0:T(8,128)(2,1)}, bf16[96,1792]{1,0:T(8,128)(2,1)S(1)}, u32[]{:S(2)}, u32[]{:S(2)}) collective-permute-start(bf16[96,1792]{1,0:T(8,128)(2,1)} %get-tuple-element.146), channel_id=1, source_target_pairs={{0,16},{4,20},{8,24},{12,28},{16,0},{20,4},{24,8},{28,12},{1,17},{... | collective-permute-start | bytes 1032200 | tf_op jit(solution)/shard_map/ppermute | solution.py:1066
  147.5 3.4 %token_grad.1 = bf16[512,768]{1,0:T(8,128)(2,1)} custom-call(bf16[528,768]{1,0:T(8,128)(2,1)} %copy-done, bf16[512,768]{1,0:T(8,128)(2,1)} %get-tuple-element.152.even, bf16[512,768]{1,0:T(8,128)(2,1)} %copy-done.8, bf16[512,768]{1,0:T(8,128)(2,1)} %copy-done.9, bf16[512,768]{1,0:T(8,128)(2,1)} %bitcast.10), custom_call_target="tpu_custom_call" | custom-call | tf_op jit(solution)/shard_map/token_grad/pallas_call | solution.py:1140
  151.0 7.3 %collective-permute-done.14.refs_1_ = bf16[224,576]{1,0:T(8,128)(2,1)S(1)} collective-permute-done((bf16[224,576]{1,0:T(8,128)(2,1)}, bf16[224,576]{1,0:T(8,128)(2,1)S(1)}, u32[]{:S(2)}, u32[]{:S(2)}) %collective-permute-start.14) | collective-permute-done | bytes 258080 | tf_op jit(solution)/shard_map/ppermute | solution.py:1066
  159.0 2.5 %fold.7 = (bf16[128,576]{1,0:T(8,128)(2,1)}, bf16[128,576]{1,0:T(8,128)(2,1)}) custom-call(s32[2]{0:T(128)} %pad_add_fusion.meta._, bf16[224,576]{1,0:T(8,128)(2,1)} %get-tuple-element.155.refs_0_, bf16[224,576]{1,0:T(8,128)(2,1)} %copy-done.12), custom_call_target="tpu_custom_call" | custom-call | tf_op jit(solution)/shard_map/fold/pallas_call | solution.py:893
  162.3 2.7 %last_packet.1 = (f32[96,768]{1,0:T(8,128)}, bf16[96,480]{1,0:T(8,128)(2,1)}, bf16[96,480]{1,0:T(8,128)(2,1)}) custom-call(s32[2]{0:T(128)} %pad_add_fusion.meta._, bf16[96,1792]{1,0:T(8,128)(2,1)} %get-tuple-element.158.keep, bf16[96,1792]{1,0:T(8,128)(2,1)} %copy-done.11), custom_call_target="tpu_custom_call" | custom-call | tf_op jit(solution)/shard_map/last_packet/pallas_call | solution.py:893
  165.0 4.8 %collective-permute-done.18.got = bf16[128,576]{1,0:T(8,128)(2,1)S(1)} collective-permute-done((bf16[128,576]{1,0:T(8,128)(2,1)}, bf16[128,576]{1,0:T(8,128)(2,1)S(1)}, u32[]{:S(2)}, u32[]{:S(2)}) %collective-permute-start.18) | collective-permute-done | bytes 147488 | tf_op jit(solution)/shard_map/ppermute | solution.py:1066
  170.5 2.6 %last_qkv.1 = (f32[96,192]{1,0:T(8,128)}, f32[128,192]{1,0:T(8,128)}, f32[128,192]{1,0:T(8,128)}, f32[32,192]{1,0:T(8,128)}) custom-call(s32[2]{0:T(128)} %pad_add_fusion.meta._, bf16[128,576]{1,0:T(8,128)(2,1)} %get-tuple-element.165.keep, bf16[128,576]{1,0:T(8,128)(2,1)} %copy-done.13), custom_call_target="tpu_custom_call" | custom-call | tf_op jit(solution)/shard_map/last_qkv/pallas_call | solution.py:893
  173.9 2.1 %collective-permute-start.16 = (bf16[96,480]{1,0:T(8,128)(2,1)}, bf16[96,480]{1,0:T(8,128)(2,1)S(1)}, u32[]{:S(2)}, u32[]{:S(2)}) collective-permute-start(bf16[96,480]{1,0:T(8,128)(2,1)} %get-tuple-element.161), channel_id=1, source_target_pairs={{0,0},{1,8},{2,16},{3,24},{4,4},{5,12},{6,20},{7,28},{8,1},{9,9},{... | collective-permute-start | bytes 276488 | tf_op jit(solution)/shard_map/ppermute | solution.py:1251
  176.0 3.5 %collective-permute-start.17 = (bf16[96,480]{1,0:T(8,128)(2,1)}, bf16[96,480]{1,0:T(8,128)(2,1)S(1)}, u32[]{:S(2)}, u32[]{:S(2)}) collective-permute-start(bf16[96,480]{1,0:T(8,128)(2,1)} %get-tuple-element.162), channel_id=1, source_target_pairs={{0,4},{1,12},{2,20},{3,28},{4,0},{5,8},{6,16},{7,24},{8,5},{9,13},... | collective-permute-start | bytes 276488 | tf_op jit(solution)/shard_map/ppermute | solution.py:1251
  179.6 7.0 %collective-permute-done.16.first = bf16[96,480]{1,0:T(8,128)(2,1)S(1)} collective-permute-done((bf16[96,480]{1,0:T(8,128)(2,1)}, bf16[96,480]{1,0:T(8,128)(2,1)S(1)}, u32[]{:S(2)}, u32[]{:S(2)}) %collective-permute-start.16) | collective-permute-done | bytes 92192 | tf_op jit(solution)/shard_map/ppermute | solution.py:1251
  186.6 2.5 %collective-permute-done.17.second = bf16[96,480]{1,0:T(8,128)(2,1)S(1)} collective-permute-done((bf16[96,480]{1,0:T(8,128)(2,1)}, bf16[96,480]{1,0:T(8,128)(2,1)S(1)}, u32[]{:S(2)}, u32[]{:S(2)}) %collective-permute-start.17) | collective-permute-done | bytes 92192 | tf_op jit(solution)/shard_map/ppermute | solution.py:1251
  189.8 2.6 %lower.1 = (f32[384,192]{1,0:T(8,128)}, f32[96,192]{1,0:T(8,128)}) custom-call(s32[2]{0:T(128)} %pad_add_fusion.meta._, bf16[96,480]{1,0:T(8,128)(2,1)} %copy-done.16, bf16[96,480]{1,0:T(8,128)(2,1)} %copy-done.17), custom_call_target="tpu_custom_call" | custom-call | tf_op jit(solution)/shard_map/lower/pallas_call | solution.py:893
  192.4 1.9 copy.39
  195.0 2.7 %assemble.1 = (f32[96,576]{1,0:T(8,128)}, f32[2304]{0:T(1024)}, f32[768]{0:T(1024)}, f32[3072]{0:T(1024)}, f32[768]{0:T(1024)}, /*index=5*/f32[768]{0:T(1024)}, f32[768]{0:T(1024)}, f32[768]{0:T(1024)}, f32[768]{0:T(1024)}) custom-call(s32[2]{0:T(128)} %pad_add_fusion.meta._, f32[96,192]{1,0:T(8,128)} %get-tuple-element.166.kept, ...), custom_call_target="tpu_custom_call" | custom-call | tf_op jit(solution)/shard_map/assemble/pallas_call | solution.py:1027
  (76 shorter events, 19.1 us)
Async XLA Ops:
  0.6 2.1 %copy-start.3 = (bf16[1,512,768]{2,1,0:T(8,128)(2,1)S(1)}, bf16[1,512,768]{2,1,0:T(8,128)(2,1)}, u32[]{:S(2)}) copy-start(bf16[1,512,768]{2,1,0:T(8,128)(2,1)} %param.33) | copy-start | bytes 2359300
  2.6 3.9 %copy-start = (bf16[528,768]{1,0:T(8,128)(2,1)}, bf16[528,768]{1,0:T(8,128)(2,1)S(1)}, u32[]{:S(2)}) copy-start(bf16[528,768]{1,0:T(8,128)(2,1)S(1)} %fusion.1.xa.s0.refs_4_.x_ref) | copy-start | bytes 2433028
  2.6 3.9 %collective-permute-start = (bf16[528,768]{1,0:T(8,128)(2,1)S(1)}, bf16[528,768]{1,0:T(8,128)(2,1)S(1)}, u32[]{:S(2)}, u32[]{:S(2)}) collective-permute-start(bf16[528,768]{1,0:T(8,128)(2,1)S(1)} %fusion.1.xa.s0.refs_4_.x_ref), channel_id=1, source_target_pairs={{0,1},{1,0},{2,3},{3,2},{4,5},{5,4},{6,7},{7,6},{8,9},{9,8},{10,11... | collective-permute-start | bytes 2433032 | tf_op jit(solution)/shard_map/ppermute | solution.py:1066
  2.7 23.4 %collective-permute-start.2 = (bf16[528,768]{1,0:T(8,128)(2,1)S(1)}, bf16[528,768]{1,0:T(8,128)(2,1)S(1)}, u32[]{:S(2)}, u32[]{:S(2)}) collective-permute-start(bf16[528,768]{1,0:T(8,128)(2,1)S(1)} %fusion.1.xa.s0.refs_4_.x_ref), channel_id=1, source_target_pairs={{0,2},{1,3},{2,0},{3,1},{4,6},{5,7},{6,4},{7,5},{8,10},{9,11},{10,... | collective-permute-start | bytes 2433032 | tf_op jit(solution)/shard_map/ppermute | solution.py:1066
  2.8 3.7 %collective-permute-start.1 = (bf16[512,768]{1,0:T(8,128)(2,1)S(1)}, bf16[512,768]{1,0:T(8,128)(2,1)}, u32[]{:S(2)}, u32[]{:S(2)}) collective-permute-start(bf16[512,768]{1,0:T(8,128)(2,1)S(1)} %bitcast.11), channel_id=1, source_target_pairs={{0,1},{1,0},{2,3},{3,2},{4,5},{5,4},{6,7},{7,6},{8,9},{9,8},{10,11... | collective-permute-start | bytes 2359304 | tf_op jit(solution)/shard_map/ppermute | solution.py:1066
  4.1 37.0 %collective-permute-start.4 = (bf16[544,768]{1,0:T(8,128)(2,1)}, bf16[544,768]{1,0:T(8,128)(2,1)}, u32[]{:S(2)}, u32[]{:S(2)}) collective-permute-start(bf16[544,768]{1,0:T(8,128)(2,1)} %pad.9), channel_id=1, source_target_pairs={{0,2},{1,3},{2,0},{3,1},{4,6},{5,7},{6,4},{7,5},{8,10},{9,11},{10,... | collective-permute-start | bytes 2506760 | tf_op jit(solution)/shard_map/ppermute | solution.py:1066
  26.1 1.3 copy-start.1
  26.1 5.9 %collective-permute-start.3 = (bf16[528,768]{1,0:T(8,128)(2,1)S(1)}, bf16[528,768]{1,0:T(8,128)(2,1)S(1)}, u32[]{:S(2)}, u32[]{:S(2)}) collective-permute-start(bf16[528,768]{1,0:T(8,128)(2,1)S(1)} %collective-permute-done.2.x_ref.s2.xa.refs_5_), channel_id=1, source_target_pairs={{0,1},{1,0},{2,3},{3,2},{4,5},{5,4},{6,7},{7,6},{8,9},{9,8},{10,11... | collective-permute-start | bytes 2433032 | tf_op jit(solution)/shard_map/ppermute | solution.py:1066
  32.0 0.9 copy-start.2
  41.2 14.1 %collective-permute-start.5 = (bf16[544,768]{1,0:T(8,128)(2,1)}, bf16[544,768]{1,0:T(8,128)(2,1)S(1)}, u32[]{:S(2)}, u32[]{:S(2)}) collective-permute-start(bf16[544,768]{1,0:T(8,128)(2,1)} %collective-permute-done.4.ca), channel_id=1, source_target_pairs={{0,1},{1,0},{2,3},{3,2},{4,5},{5,4},{6,7},{7,6},{8,9},{9,8},{10,11... | collective-permute-start | bytes 2506760 | tf_op jit(solution)/shard_map/ppermute | solution.py:1066
  55.3 0.9 copy-start.7
  76.4 24.8 %collective-permute-start.6 = (bf16[2,512,768]{2,1,0:T(8,128)(2,1)}, bf16[2,512,768]{2,1,0:T(8,128)(2,1)S(1)}, u32[]{:S(2)}, u32[]{:S(2)}) collective-permute-start(bf16[2,512,768]{2,1,0:T(8,128)(2,1)} %get-tuple-element.129), channel_id=1, source_target_pairs={{0,1},{1,0},{2,3},{3,2},{4,5},{5,4},{6,7},{7,6},{8,9},{9,8},{10,11... | collective-permute-start | bytes 4718600 | tf_op jit(solution)/shard_map/ppermute | solution.py:1066
  77.0 32.8 %collective-permute-start.7 = (bf16[384,1792]{1,0:T(8,128)(2,1)}, bf16[384,1792]{1,0:T(8,128)(2,1)}, u32[]{:S(2)}, u32[]{:S(2)}) collective-permute-start(bf16[384,1792]{1,0:T(8,128)(2,1)} %get-tuple-element.136), channel_id=1, source_target_pairs={{0,4},{4,0},{8,12},{12,8},{16,20},{20,16},{24,28},{28,24},{1,5},{5... | collective-permute-start | bytes 4128776 | tf_op jit(solution)/shard_map/ppermute | solution.py:1066
  77.3 23.9 %copy-start.5 = (bf16[2,512,768]{2,1,0:T(8,128)(2,1)S(1)}, bf16[2,512,768]{2,1,0:T(8,128)(2,1)}, u32[]{:S(2)}) copy-start(bf16[2,512,768]{2,1,0:T(8,128)(2,1)} %get-tuple-element.128.even) | copy-start | bytes 4718596
  101.2 7.8 %copy-start.6 = (bf16[2,512,768]{2,1,0:T(8,128)(2,1)}, bf16[2,512,768]{2,1,0:T(8,128)(2,1)S(1)}, u32[]{:S(2)}) copy-start(bf16[2,512,768]{2,1,0:T(8,128)(2,1)S(1)} %collective-permute-done.6.near) | copy-start | bytes 4718596
  109.0 13.6 %collective-permute-start.8 = (bf16[512,768]{1,0:T(8,128)(2,1)}, bf16[512,768]{1,0:T(8,128)(2,1)S(1)}, u32[]{:S(2)}, u32[]{:S(2)}) collective-permute-start(bf16[512,768]{1,0:T(8,128)(2,1)} %get-tuple-element.142), channel_id=1, source_target_pairs={{0,1},{1,0},{2,3},{3,2},{4,5},{5,4},{6,7},{7,6},{8,9},{9,8},{10,11... | collective-permute-start | bytes 2359304 | tf_op jit(solution)/shard_map/ppermute | solution.py:1066
  109.1 20.4 %collective-permute-start.9 = (bf16[512,768]{1,0:T(8,128)(2,1)S(1)}, bf16[512,768]{1,0:T(8,128)(2,1)S(1)}, u32[]{:S(2)}, u32[]{:S(2)}) collective-permute-start(bf16[512,768]{1,0:T(8,128)(2,1)S(1)} %fusion.2), channel_id=1, source_target_pairs={{0,2},{1,3},{2,0},{3,1},{4,6},{5,7},{6,4},{7,5},{8,10},{9,11},{10,... | collective-permute-start | bytes 2359304 | tf_op jit(solution)/shard_map/ppermute | solution.py:1066
  113.4 19.8 %collective-permute-start.10 = (bf16[192,1792]{1,0:T(8,128)(2,1)}, bf16[192,1792]{1,0:T(8,128)(2,1)}, u32[]{:S(2)}, u32[]{:S(2)}) collective-permute-start(bf16[192,1792]{1,0:T(8,128)(2,1)} %get-tuple-element.137), channel_id=1, source_target_pairs={{0,8},{4,12},{8,0},{12,4},{16,24},{20,28},{24,16},{28,20},{1,9},{5... | collective-permute-start | bytes 2064392 | tf_op jit(solution)/shard_map/ppermute | solution.py:1066
  114.4 31.9 %collective-permute-start.12 = (bf16[512,768]{1,0:T(8,128)(2,1)}, bf16[512,768]{1,0:T(8,128)(2,1)S(1)}, u32[]{:S(2)}, u32[]{:S(2)}) collective-permute-start(bf16[512,768]{1,0:T(8,128)(2,1)} %get-tuple-element.153), channel_id=1, source_target_pairs={{0,1},{1,0},{2,3},{3,2},{4,5},{5,4},{6,7},{7,6},{8,9},{9,8},{10,11... | collective-permute-start | bytes 2359304 | tf_op jit(solution)/shard_map/ppermute | solution.py:1066
  124.0 22.3 %collective-permute-start.13 = (bf16[512,768]{1,0:T(8,128)(2,1)S(1)}, bf16[512,768]{1,0:T(8,128)(2,1)S(1)}, u32[]{:S(2)}, u32[]{:S(2)}) collective-permute-start(bf16[512,768]{1,0:T(8,128)(2,1)S(1)} %add_convert_fusion), channel_id=1, source_target_pairs={{0,2},{1,3},{2,0},{3,1},{4,6},{5,7},{6,4},{7,5},{8,10},{9,11},{10,... | collective-permute-start | bytes 2359304 | tf_op jit(solution)/shard_map/ppermute | solution.py:1066
  125.2 14.5 %collective-permute-start.11 = (bf16[416,576]{1,0:T(8,128)(2,1)}, bf16[416,576]{1,0:T(8,128)(2,1)}, u32[]{:S(2)}, u32[]{:S(2)}) collective-permute-start(bf16[416,576]{1,0:T(8,128)(2,1)} %get-tuple-element.149), channel_id=1, source_target_pairs={{0,4},{4,0},{8,12},{12,8},{16,20},{20,16},{24,28},{28,24},{1,5},{5... | collective-permute-start | bytes 1437704 | tf_op jit(solution)/shard_map/ppermute | solution.py:1066
  142.6 15.7 %collective-permute-start.14 = (bf16[224,576]{1,0:T(8,128)(2,1)}, bf16[224,576]{1,0:T(8,128)(2,1)S(1)}, u32[]{:S(2)}, u32[]{:S(2)}) collective-permute-start(bf16[224,576]{1,0:T(8,128)(2,1)} %get-tuple-element.150), channel_id=1, source_target_pairs={{0,8},{4,12},{8,0},{12,4},{16,24},{20,28},{24,16},{28,20},{1,9},{5... | collective-permute-start | bytes 774152 | tf_op jit(solution)/shard_map/ppermute | solution.py:1066
  144.0 17.6 %collective-permute-start.15 = (bf16[96,1792]{1,0:T(8,128)(2,1)}, bf16[96,1792]{1,0:T(8,128)(2,1)S(1)}, u32[]{:S(2)}, u32[]{:S(2)}) collective-permute-start(bf16[96,1792]{1,0:T(8,128)(2,1)} %get-tuple-element.146), channel_id=1, source_target_pairs={{0,16},{4,20},{8,24},{12,28},{16,0},{20,4},{24,8},{28,12},{1,17},{... | collective-permute-start | bytes 1032200 | tf_op jit(solution)/shard_map/ppermute | solution.py:1066
  146.3 0.9 copy-start.8
  146.3 1.2 copy-start.9
  161.5 8.3 %collective-permute-start.18 = (bf16[128,576]{1,0:T(8,128)(2,1)}, bf16[128,576]{1,0:T(8,128)(2,1)S(1)}, u32[]{:S(2)}, u32[]{:S(2)}) collective-permute-start(bf16[128,576]{1,0:T(8,128)(2,1)} %get-tuple-element.156), channel_id=1, source_target_pairs={{0,16},{4,20},{8,24},{12,28},{16,0},{20,4},{24,8},{28,12},{1,17},{... | collective-permute-start | bytes 442376 | tf_op jit(solution)/shard_map/ppermute | solution.py:1066
  173.0 21.3 %collective-permute-start.19 = (f32[128,192]{1,0:T(8,128)}, f32[128,192]{1,0:T(8,128)S(1)}, u32[]{:S(2)}, u32[]{:S(2)}) collective-permute-start(f32[128,192]{1,0:T(8,128)} %get-tuple-element.168), channel_id=1, source_target_pairs={{0,1},{1,0},{2,3},{3,2},{4,5},{5,4},{6,7},{7,6},{8,9},{9,8},{10,11... | collective-permute-start | bytes 294920 | tf_op jit(solution)/shard_map/ppermute | solution.py:1066
  173.0 21.3 %collective-permute-start.20 = (f32[128,192]{1,0:T(8,128)}, f32[128,192]{1,0:T(8,128)S(1)}, u32[]{:S(2)}, u32[]{:S(2)}) collective-permute-start(f32[128,192]{1,0:T(8,128)} %get-tuple-element.169), channel_id=1, source_target_pairs={{0,2},{1,3},{2,0},{3,1},{4,6},{5,7},{6,4},{7,5},{8,10},{9,11},{10,... | collective-permute-start | bytes 294920 | tf_op jit(solution)/shard_map/ppermute | solution.py:1066
  173.9 12.7 %collective-permute-start.16 = (bf16[96,480]{1,0:T(8,128)(2,1)}, bf16[96,480]{1,0:T(8,128)(2,1)S(1)}, u32[]{:S(2)}, u32[]{:S(2)}) collective-permute-start(bf16[96,480]{1,0:T(8,128)(2,1)} %get-tuple-element.161), channel_id=1, source_target_pairs={{0,0},{1,8},{2,16},{3,24},{4,4},{5,12},{6,20},{7,28},{8,1},{9,9},{... | collective-permute-start | bytes 276488 | tf_op jit(solution)/shard_map/ppermute | solution.py:1251
  176.0 13.1 %collective-permute-start.17 = (bf16[96,480]{1,0:T(8,128)(2,1)}, bf16[96,480]{1,0:T(8,128)(2,1)S(1)}, u32[]{:S(2)}, u32[]{:S(2)}) collective-permute-start(bf16[96,480]{1,0:T(8,128)(2,1)} %get-tuple-element.162), channel_id=1, source_target_pairs={{0,4},{1,12},{2,20},{3,28},{4,0},{5,8},{6,16},{7,24},{8,5},{9,13},... | collective-permute-start | bytes 276488 | tf_op jit(solution)/shard_map/ppermute | solution.py:1251
  179.6 14.7 %collective-permute-start.21 = (f32[32,192]{1,0:T(8,128)}, f32[32,192]{1,0:T(8,128)S(1)}, u32[]{:S(2)}, u32[]{:S(2)}) collective-permute-start(f32[32,192]{1,0:T(8,128)} %get-tuple-element.167.small), channel_id=1, source_target_pairs={{0,3},{1,2},{2,1},{3,0},{4,7},{5,6},{6,5},{7,4},{8,11},{9,10},{10,... | collective-permute-start | bytes 73736 | tf_op jit(solution)/shard_map/ppermute | solution.py:1066
  186.6 2.5 %copy-start.16 = (bf16[96,480]{1,0:T(8,128)(2,1)}, bf16[96,480]{1,0:T(8,128)(2,1)S(1)}, u32[]{:S(2)}) copy-start(bf16[96,480]{1,0:T(8,128)(2,1)S(1)} %collective-permute-done.16.first) | copy-start | bytes 276484
  (9 other events, 6.5 us)

commit v5 on v4

--- a/solution.py
+++ b/solution.py
@@ -213,10 +213,15 @@
     )(meta, valid_len, *toks)
 
 
-def places(rows):
+def mask_order(rows, first):
+    masks = [1 << bit for bit in range(rows.bit_length() - 1)]
+    return [m for m in masks if m >= first] + [m for m in masks if m < first]
+
+
+def places(masks):
     order = [0]
-    while len(order) < rows:
-        order = [2 * i for i in order] + [2 * i + 1 for i in order]
+    for mask in reversed(masks):
+        order = order + [mask + i for i in order]
     return order
 
 
@@ -224,13 +229,13 @@
     return rows == 8 and D // rows % 32 == 0
 
 
-def store_chunks(grad, keep, send, meta, rows):
-    size = grad.shape[0] // rows
-    for index, place in enumerate(places(rows)):
+def store_chunks(load, keep, send, meta, rows, first):
+    size = D // rows
+    for index, place in enumerate(places(mask_order(rows, first))):
         at = pl.multiple_of(jnp.bitwise_xor(meta[1], place) * size, 32)
         into = keep if index < rows // 2 else send
-        row = index % (rows // 2) * size
-        into[row : row + size, :] = grad[pl.ds(at, size), :].astype(into.dtype)
+        row_at = index % (rows // 2) * size
+        into[row_at : row_at + size, :] = load(pl.ds(at, size)).astype(into.dtype)
 
 
 def chunk_shapes(cols, rows, extra=0):
@@ -239,10 +244,10 @@
     return [(D, cols), (8, LANES)]
 
 
-def chunks_of(keep, send, rows):
+def chunks_of(keep, send, rows, first):
     if fits(rows):
         return keep, send
-    order = jnp.array(places(rows)) ^ lax.axis_index("rows")
+    order = jnp.array(places(mask_order(rows, first))) ^ lax.axis_index("rows")
     parts = keep.reshape(rows, D // rows, keep.shape[1])
     parts = jnp.take(parts, order, axis=0).reshape(keep.shape)
     return parts[: D // 2], parts[D // 2 :]
@@ -317,7 +322,7 @@
 def mlp_second_kernel(
     half, rows, meta, xa, xb, ca, cb, gain, shift, b_up, w_up, w_down, w_out,
     c0, c1, mo_in, o_near, o_far, sums_in, gup, gdown, _,
-    e_ref, gv_ref, sums, even, odd, keep, send, x_s, c_s, n_s, grad,
+    e_ref, gv_ref, sums, even, odd, up_keep, up_send, low_keep, low_send, x_s, c_s, n_s, grad,
 ):
     step = pl.program_id(0)
     hid = gup.shape[1]
@@ -369,9 +374,11 @@
     @pl.when(step == pl.num_programs(0) - 1)
     def _():
         if fits(rows):
-            store_chunks(grad, keep, send, meta, rows)
+            store_chunks(lambda at: grad[at, 0:hid], up_keep, up_send, meta, rows, 1)
+            store_chunks(lambda at: grad[at, hid:], low_keep, low_send, meta, rows, 2)
         else:
-            keep[...] = grad[...].astype(BF16)
+            up_keep[...] = grad[:, 0:hid].astype(BF16)
+            low_keep[...] = grad[:, hid:].astype(BF16)
 
 
 def feed_forward(
@@ -431,7 +438,7 @@
     else:
         body = partial(mlp_second_kernel, per, rows)
         mlp_out, _, grad_vec, sums_in, gup, gdown = before
-        chunks = chunk_shapes(2 * hid + 2 * LANES, rows)
+        chunks = chunk_shapes(hid, rows) + chunk_shapes(hid + 2 * LANES, rows)
         args += [*near, mlp_out, attn, attn, sums_in, gup, gdown, grad_vec]
         specs += [
             first,
@@ -746,147 +753,132 @@
     )(meta, lo, hi, query, keys, values, attn, grad_vec, starts, lse, low, high)
 
 
-def joined_kernel(final, rows, meta, *refs):
-    gj_a, gj_b, e_a, e_b, x_a, x_b, gain_ref, shift_ref, w_ref = refs[:9]
-    if final:
-        grad_in, bias_in, sums_in, mlp_sums = refs[9:13]
-        *e_refs, keep, send, grad, bias, sums = refs[13:]
-    else:
-        *e_refs, grad, bias, sums = refs[9:]
+SMALL = 16
+
+
+def pack_small(gain_sum, shift_sum, bias, mlp_sums):
+    third = 3 * D // 4
+    which = lax.broadcasted_iota(jnp.int32, (8, D), 0)
+    table = jnp.concatenate([jnp.zeros((4, D), F32), mlp_sums[0:4]], axis=0)
+    table = jnp.where(which == 0, gain_sum, jnp.where(which == 1, shift_sum, table))
+    head = jnp.where(which[:, :third] == 2, bias, table[:, :third])
+    tail = jnp.concatenate([table[:, third:], jnp.zeros((8, 2 * third - D), F32)], axis=1)
+    return jnp.concatenate([head, tail], axis=0)
+
+
+def high_low(value):
+    high = value.astype(BF16)
+    return high, (value - high.astype(F32)).astype(BF16)
+
+
+def weight_kernel(rows, meta, *refs):
+    gjs, xs = refs[0:4], refs[4:8]
+    gain, shift, w_ref, mlp_sums, keep, send, small, n_s, gj_s, grad, bias = refs[8:]
     step = pl.program_id(0)
 
     @pl.when(step == 0)
     def _():
-        if final:
-            grad[...] = grad_in[...]
-            bias[...] = bias_in[...]
-            sums[...] = sums_in[...]
+        grad[...] = jnp.zeros_like(grad)
+        bias[...] = jnp.zeros_like(bias)
+
+    for index, (gj_ref, x_ref) in enumerate(zip(gjs, xs)):
+        at = slice(index * TILE, (index + 1) * TILE)
+        n_s[at, :] = normalize(x_ref[...].astype(F32)).astype(BF16)
+        gj_s[at, :] = gj_ref[...]
+    bias[0:1, :] += jnp.sum(gj_s[...].astype(F32), axis=0, keepdims=True)
+    grad[...] += dot_tn(n_s[...], gj_s[...])
+
+    @pl.when(step == pl.num_programs(0) - 1)
+    def _():
+        total = bias[0:1, :]
+        width = total.shape[1]
+        parts = jnp.concatenate(
+            [*high_low(jnp.broadcast_to(total, (8, width)))], axis=0
+        )
+        shift_sum = dot_nt(parts, w_ref[...])
+        shift_sum = shift_sum[0:1] + shift_sum[8:9]
+        ones = jnp.ones((16, width), BF16)
+        high, low = high_low(grad[...] * w_ref[...].astype(F32))
+        gain_sum = (dot_nt(ones, high) + dot_nt(ones, low))[0:1]
+        columns = jnp.concatenate(
+            [jnp.broadcast_to(row(gain), (8, D)), jnp.broadcast_to(row(shift), (8, D))], axis=0
+        ).T
+        grad[...] = grad[...] * columns[:, 0:1] + columns[:, 8:9] * total
+        rest = pack_small(gain_sum, shift_sum, total, mlp_sums[...])
+        small[...] = rest
+        if fits(rows):
+            store_chunks(lambda at: grad[at, :], keep, send, meta, rows, 1)
+            keep[D // 2 :, :] = rest.astype(BF16)
+            send[D // 2 :, :] = rest.astype(BF16)
         else:
-            grad[...] = jnp.zeros_like(grad)
-            bias[...] = jnp.zeros_like(bias)
-            sums[...] = jnp.zeros_like(sums)
-
-    gain, shift = row(gain_ref), row(shift_ref)
-    for index, (gj_ref, e_in, x_ref) in enumerate(((gj_a, e_a, x_a), (gj_b, e_b, x_b))):
-        normed = normalize(x_ref[...].astype(F32))
-        attn_in = (normed * gain + shift).astype(BF16)
-        low = gj_ref[...]
-        grad_norm = dot_nt(low, w_ref[...])
-        e_refs[index][...] = (grad_norm * gain + e_in[...].astype(F32)).astype(BF16)
-        sums[0:1, :] += jnp.sum(grad_norm * normed, axis=0, keepdims=True)
-        sums[1:2, :] += jnp.sum(grad_norm, axis=0, keepdims=True)
-        bias[0:1, :] += jnp.sum(low.astype(F32), axis=0, keepdims=True)
-        grad[...] += dot_tn(attn_in, low)
-
-    if final:
-
-        @pl.when(step == pl.num_programs(0) - 1)
-        def _():
-            if fits(rows):
-                store_chunks(grad, keep, send, meta, rows)
-                small = pack_small(sums[...], mlp_sums[...], bias[...])
-                keep[D // 2 :, :] = small
-                send[D // 2 :, :] = small
-            else:
-                keep[...] = grad[...].astype(BF16)
-                send[...] = jnp.zeros_like(send)
-
-
-SMALL = 32
-
-
-def pack_small(norm_sums, mlp_sums, bias):
-    third = 3 * D // 4
-    table = jnp.concatenate([norm_sums[0:4], mlp_sums[0:4]], axis=0)
-    which = lax.broadcasted_iota(jnp.int32, (8, third), 0)
-    head = jnp.where(which == 2, bias[0:1, :], table[:, :third])
-    tail = jnp.concatenate([table[:, third:], jnp.zeros((8, 2 * third - D), F32)], axis=1)
-    return split_small(jnp.concatenate([head, tail], axis=0))
-
-
-def add_small(left, right):
-    half = SMALL // 2
-    total = left.astype(F32) + right.astype(F32)
-    return total[:half] + total[half:]
-
-
-def split_small(rows):
-    high = rows.astype(BF16)
-    return jnp.concatenate([high, (rows - high.astype(F32)).astype(BF16)], axis=0)
-
-
-def joined_back(
-    meta, slots, grad, e_mlp, toks, gain, shift, w, rows, seq, before=None, mlp_sums=None
-):
+            keep[...] = grad[...].astype(BF16)
+
+
+def slot_tiles(slot, cols, per):
+    return pl.BlockSpec((TILE, cols), lambda i, m: (slot * per + i, 0))
+
+
+def joined_weight(meta, grad, toks, gain, shift, w, mlp_sums, rows, seq):
     width = grad.shape[1]
     per = seq // TILE
-
-    def at(slot, cols):
-        return pl.BlockSpec((TILE, cols), lambda i, m: (slot * per + i, 0))
-
-    sums = (8, D)
-    args = [grad, grad, *e_mlp, *[toks[slot] for slot in slots], gain, shift, w]
-    specs = [
-        *(at(slot, width) for slot in slots),
-        *(at(slot % 2, D) for slot in slots),
-        *(pl.BlockSpec((TILE, D), lambda i, m: (i, 0)),) * 2,
-        whole(gain.shape),
-        whole(shift.shape),
-        whole(w.shape),
-    ]
-    e_spec = pl.BlockSpec((TILE, D), lambda i, m: (i, 0))
-    outs, out_specs = [jax.ShapeDtypeStruct((seq, D), BF16)] * 2, [e_spec] * 2
-    carried = [(D, width), (8, width), sums]
-    scratch = []
-    if before is None:
-        outs += [jax.ShapeDtypeStruct(shape, F32) for shape in carried]
-        out_specs += [whole(shape) for shape in carried]
-    else:
-        chunks = chunk_shapes(width, rows, SMALL)
-        outs += [jax.ShapeDtypeStruct(shape, BF16) for shape in chunks]
-        out_specs += [whole(shape) for shape in chunks]
-        if not fits(rows):
-            outs[-1] = jax.ShapeDtypeStruct((8, LANES), BF16)
-        args += [*before, mlp_sums]
-        specs += [whole(shape) for shape in carried] + [whole(sums)]
-        scratch = [pltpu.VMEM(shape, F32) for shape in carried]
-        if not fits(rows):
-            outs += [jax.ShapeDtypeStruct(shape, F32) for shape in carried[1:]]
-            out_specs += [whole(shape) for shape in carried[1:]]
-            scratch = scratch[:1]
-    body = partial(joined_kernel, before is not None, rows)
-    if before is not None and not fits(rows):
-
-        def body(meta, *refs):
-            inputs, (e_a, e_b, keep, send, bias, sums, grad) = refs[:13], refs[13:]
-            joined_kernel(True, rows, meta, *inputs, e_a, e_b, keep, send, grad, bias, sums)
-
+    chunks = chunk_shapes(width, rows, SMALL)
     return pl.pallas_call(
-        body,
-        out_shape=outs,
+        partial(weight_kernel, rows),
+        out_shape=[jax.ShapeDtypeStruct(shape, BF16) for shape in chunks]
+        + [jax.ShapeDtypeStruct((SMALL, width), F32)],
         grid_spec=pltpu.PrefetchScalarGridSpec(
             num_scalar_prefetch=1,
             grid=(per,),
-            in_specs=specs,
-            out_specs=out_specs,
-            scratch_shapes=scratch,
+            in_specs=[
+                *(slot_tiles(slot, width, per) for slot in range(4)),
+                *(slot_tiles(0, D, per) for _ in range(4)),
+                whole(gain.shape),
+                whole(shift.shape),
+                whole(w.shape),
+                whole(mlp_sums.shape),
+            ],
+            out_specs=[*(whole(shape) for shape in chunks), whole((SMALL, width))],
+            scratch_shapes=[
+                pltpu.VMEM((4 * TILE, D), BF16),
+                pltpu.VMEM((4 * TILE, width), BF16),
+                pltpu.VMEM((D, width), F32),
+                pltpu.VMEM((8, width), F32),
+            ],
         ),
         compiler_params=params(),
         cost_estimate=COST,
-        name="joined_first" if before is None else "joined_second",
-    )(meta, *args)
-
-
-def fold_kernel(extra, keep, got, *outs):
-    size = keep.shape[0] - extra
-    for index, out in enumerate(outs):
-        rows = slice(index * size // 2, (index + 1) * size // 2)
-        total = keep[rows, :].astype(F32) + got[rows, :].astype(F32)
-        out[0 : size // 2, :] = total.astype(BF16)
-    if extra:
-        small = split_small(add_small(keep[size:, :], got[size:, :]))
-        for out in outs:
-            out[size // 2 :, :] = small
+        name="joined_weight",
+    )(meta, *[grad] * 4, *toks, gain, shift, w, mlp_sums)
+
+
+def norm_kernel(meta, *refs):
+    gjs, es, (gain, w_ref), outs = refs[0:4], refs[4:8], refs[8:10], refs[10:]
+    for gj_ref, e_in, out in zip(gjs, es, outs):
+        grad_norm = dot_nt(gj_ref[...], w_ref[...])
+        out[...] = (grad_norm * row(gain) + e_in[...].astype(F32)).astype(BF16)
+
+
+def norm_grad(meta, grad, e_mlp, gain, w, seq):
+    width = grad.shape[1]
+    per = seq // TILE
+    return pl.pallas_call(
+        norm_kernel,
+        out_shape=[jax.ShapeDtypeStruct((seq, D), BF16)] * 4,
+        grid_spec=pltpu.PrefetchScalarGridSpec(
+            num_scalar_prefetch=1,
+            grid=(per,),
+            in_specs=[
+                *(slot_tiles(slot, width, per) for slot in range(4)),
+                *(slot_tiles(slot % 2, D, per) for slot in range(4)),
+                whole(gain.shape),
+                whole(w.shape),
+            ],
+            out_specs=[slot_tiles(0, D, per)] * 4,
+        ),
+        compiler_params=params(),
+        cost_estimate=COST,
+        name="norm_grad",
+    )(meta, *[grad] * 4, e_mlp[0], e_mlp[0], e_mlp[1], e_mlp[1], gain, w)
 
 
 def simple(body, name, shapes, *args):
@@ -905,17 +897,10 @@
     )(*args)
 
 
-def fold(meta, keep, got, extra):
-    size, cols = keep.shape[0] - extra, keep.shape[1]
-    shapes = [((size // 2 + extra, cols), BF16)] * 2
-    return simple(lambda _, *refs: fold_kernel(extra, *refs), "fold", shapes, meta, keep, got)
-
-
-def last_packet_kernel(meta, keep, got, up_ref, first, second):
-    hid = up_ref.shape[1]
-    up_ref[...] = keep[:, :hid].astype(F32) + got[:, :hid].astype(F32)
-    low = (keep[:, hid:].astype(F32) + got[:, hid:].astype(F32)).astype(BF16)
-    cut, side = hid // 2, D // 8
+def last_low_kernel(meta, keep, got, first, second):
+    low = (keep[...].astype(F32) + got[...].astype(F32)).astype(BF16)
+    hid, side = FF // 4, D // 8
+    cut = hid // 2
     even = jnp.concatenate([low[:, :cut], low[:, hid : hid + side]], axis=1)
     odd = jnp.concatenate([low[:, cut:hid], low[:, hid + side : hid + 2 * side]], axis=1)
 
@@ -953,8 +938,8 @@
 def last_qkv_kernel(meta, keep, got, kept, near, far, small):
     size = kept.shape[0]
     width = kept.shape[1]
-    total = keep[0:size, :].astype(F32) + got[0:size, :].astype(F32)
-    rows = add_small(keep[size:, :], got[size:, :])
+    both = keep[...].astype(F32) + got[...].astype(F32)
+    total, rows = both[0:size], both[size:]
     for part in range(3):
         small[part * 8 : part * 8 + 8, :] = rows[0:8, part * width : (part + 1) * width]
     small[24:32, :] = rows[8:16, 0:width]
@@ -999,7 +984,8 @@
     table[1] = near[size:, :]
     table[2] = far[size:, :]
     table[3] = diag[...]
-    total = table[0] + table[1] + table[2] + table[3]
+    blocks = [table[jnp.bitwise_xor(meta[0], blk)] for blk in range(4)]
+    total = blocks[0] + blocks[1] + blocks[2] + blocks[3]
 
     def vector(rows, index):
         parts = [rows[part * 8 + index : part * 8 + index + 1, :] for part in range(4)]
@@ -1008,8 +994,7 @@
     for ref, index in ((gain1, 0), (shift1, 1), (gain2, 5), (shift2, 6), (b_out, 7), (b_down, 7)):
         ref[...] = vector(total, index).reshape(D)
     ups, parts = [], ([], [], [])
-    for blk in range(4):
-        rows = table[jnp.bitwise_xor(meta[0], blk)]
+    for rows in blocks:
         ups.append(vector(rows, 4))
         joined = vector(rows, 2)
         parts[0].append(jnp.concatenate([joined[:, 0:128], joined[:, 256:320]], axis=1))
@@ -1040,21 +1025,26 @@
     )(meta, *args)
 
 
-def fold_plain(keep, got, last):
-    total = keep.astype(F32) + got.astype(F32)
-    if last:
-        return [total]
-    half = total.shape[0] // 2
-    return [total[:half].astype(BF16), total[half:].astype(BF16)]
-
-
-def reduce_plain(keep, got, rows):
-    mask = 2
-    while mask < rows:
-        keep, send = fold_plain(keep, got, False)
+def halve(keep, got):
+    half = keep.shape[0] // 2
+    send = add_low(keep[half:], got[half:])
+    return add_low(after(keep, send)[:half], got[:half]), send
+
+
+def halve_packet(keep, got, extra):
+    size = keep.shape[0] - extra
+    half = size // 2
+    tail = add_low(keep[size:], got[size:])
+    send = jnp.concatenate([add_low(keep[half:size], got[half:size]), tail])
+    first = add_low(after(keep, send)[:half], got[:half])
+    return jnp.concatenate([first, tail]), send
+
+
+def reduce_plain(keep, got, masks):
+    for mask in masks:
+        keep, send = halve(keep, got)
         got = swap(send, "rows", mask)
-        mask *= 2
-    return fold_plain(keep, got, True)[0]
+    return keep.astype(F32) + got.astype(F32)
 
 
 def after(value, *others):
@@ -1194,64 +1184,67 @@
     attn, lse = attend(meta, lo, hi, query, keys, values, starts, per)
 
     meta = after(meta, lse)
-    e_far, grad_vec, mlp_sums, out_even, out_odd, keep, send = feed_forward(
+    e_far, grad_vec, mlp_sums, out_even, out_odd, *packets = feed_forward(
         meta, toks[2:], cots[2:], *mlp_args, before=first, near=cots[:2], attn=attn
     )
     e_mlp = (first[1], e_far)
-    keep, send = chunks_of(keep, send, rows)
+    up_keep, up_send = chunks_of(*packets[:2], rows, 1)
+    low_keep, low_send = chunks_of(*packets[2:], rows, 2)
+    up_masks, low_masks = mask_order(rows, 1), mask_order(rows, 2)
     out_got = swap(out_odd, "blk", 1)
-    got = swap(send, "rows", 1)
+    up_got = swap(up_send, "rows", up_masks[0])
+    low_got = swap(low_send, "rows", low_masks[0])
 
     meta = after(meta, mlp_sums)
     grad_joined = attend_back(
         meta, lo, hi, query, keys, values, attn, grad_vec, starts, lse, low, high, per
     )
-
-    out_send = add_low(after(out_even, grad_joined)[1], out_got[1])
+    meta = after(meta, grad_joined)
+    qkv_keep, qkv_send, small = joined_weight(
+        meta, grad_joined, toks, ln1_gain, ln1_bias, w_own, mlp_sums, rows, seq
+    )
+    qkv_keep, qkv_send = chunks_of(qkv_keep, qkv_send, rows, 1)
+    qkv_got = swap(qkv_send, "rows", 1)
+
+    meta = after(meta, small)
+    out_send = add_low(after(out_even, small)[1], out_got[1])
     out_far = swap(out_send, "blk", 2)
-    joined_args = (grad_joined, e_mlp, toks, ln1_gain, ln1_bias, w_own, rows, seq)
+    if fits(rows):
+        up_keep, up_send = halve(after(up_keep, small), up_got)
+        up_got = swap(up_send, "rows", up_masks[1])
+        low_keep, low_send = halve(after(low_keep, small), low_got)
+        low_got = swap(low_send, "rows", low_masks[1])
+        meta = after(meta, up_send, low_send)
     meta = after(meta, out_send)
-    e_near, e_last, *carried = joined_back(meta, (1, 3), *joined_args)
+    e_own, e_near, e_send, e_last = norm_grad(meta, grad_joined, e_mlp, ln1_gain, w_own, seq)
     e_last = swap(e_last, "blk", 1)
     e_near = swap(e_near, "blk", 1)
-    meta = after(meta, carried[1])
     if fits(rows):
-        keep, send = fold(meta, keep, got, 0)
-        got = swap(send, "rows", 2)
-        meta = after(meta, send)
-    e_own, e_send, qkv_keep, qkv_send, *rest = joined_back(
-        meta, (0, 2), *joined_args, carried, mlp_sums
-    )
-    qkv_keep, qkv_send = chunks_of(qkv_keep, qkv_send, rows)
-    qkv_got = swap(qkv_send, "rows", 1)
+        chunk = D // rows
+        qkv_keep, qkv_send = halve_packet(after(qkv_keep, e_own), qkv_got, SMALL)
+        qkv_got = swap(qkv_send, "rows", 2)
+        e_send = after(e_send, qkv_send)
     e_send = add_low(e_send, e_last)
     e_far = swap(e_send, "blk", 2)
-
-    out_args = (after(tok_own, e_send), out_even, out_got, out_far, b_out, b_down)
-    result = finish(result_kernel, "result", seq, *out_args)
     if fits(rows):
-        meta = after(meta, result)
-        keep, send = fold(meta, keep, got, 0)
-        got = swap(send, "rows", 4)
-        meta = after(meta, send)
-        qkv_keep, qkv_send = fold(meta, qkv_keep, qkv_got, SMALL)
-        qkv_got = swap(qkv_send, "rows", 2)
+        out_args = (after(tok_own, e_send), out_even, out_got, out_far, b_out, b_down)
+        result = finish(result_kernel, "result", seq, *out_args)
+        low_keep, low_send = halve(after(low_keep, result), low_got)
+        low_got = swap(low_send, "rows", low_masks[2])
+        up_keep, up_send = halve(after(up_keep, low_send), up_got)
+        up_got = swap(up_send, "rows", up_masks[2])
+        qkv_keep, qkv_send = halve_packet(after(qkv_keep, up_send), qkv_got, SMALL)
+        qkv_got = swap(qkv_send, "rows", 4)
         tok_args = (after(tok_own, qkv_send), e_own, e_near, e_far, cot_own)
         grad_tokens = finish(token_kernel, "token_grad", seq, *tok_args)
         meta = after(meta, grad_tokens)
-        qkv_keep, qkv_send = fold(meta, qkv_keep, qkv_got, SMALL)
-        qkv_got = swap(qkv_send, "rows", 4)
-        meta = after(meta, qkv_send)
-        chunk = D // rows
         part = ((chunk, hid // 2 + width // 2), BF16)
-        up, *pieces = simple(
-            last_packet_kernel, "last_packet", [((chunk, hid), F32), part, part], meta, keep, got
-        )
+        pieces = simple(last_low_kernel, "last_low", [part, part], meta, low_keep, low_got)
+        meta = after(meta, pieces[0])
         pieces = [
             lax.ppermute(piece, ("rows", "blk"), spread_moves(rows, 4, turn))
             for turn, piece in enumerate(pieces)
         ]
-        meta = after(meta, up)
         packet = ((chunk + 32, width), F32)
         kept, near, far, small = simple(
             last_qkv_kernel,
@@ -1262,27 +1255,32 @@
             qkv_got,
         )
         near, far, diag = swap(near, "blk", 1), swap(far, "blk", 2), swap(small, "blk", 3)
+        up = after(up_keep, small).astype(F32) + up_got.astype(F32)
         lower = [((hid // 2, width), F32), ((width // 2, width), F32)]
+        meta = after(meta, up)
         down, out_w = simple(lower_kernel, "lower", lower, meta, *pieces)
         meta = after(meta, down)
         qkv, gb_qkv, gb_out, gb_up, gb_down, *norms = assemble(
             meta, kept, small, near, far, diag
         )
     else:
-        weights = reduce_plain(keep, got, rows)
-        qkv = reduce_plain(qkv_keep, qkv_got, rows)
-        up = weights[:, :hid]
-        down, out_w = spread_rows(weights[:, hid : 2 * hid + width])
+        up = reduce_plain(up_keep, up_got, up_masks[1:])
+        weights = reduce_plain(low_keep, low_got, low_masks[1:])
+        qkv = reduce_plain(qkv_keep, qkv_got, up_masks[1:])
+        down, out_w = spread_rows(weights[:, : hid + width])
         kept, near, far = split_columns(qkv)
         near, far = swap(near, "blk", 1), swap(far, "blk", 2)
         ends = [jnp.where(blk % 2 == 0, a, b) for a, b in ((kept, far), (far, kept))]
         qkv = jnp.concatenate([ends[0], near, ends[1]], axis=1)
+        out_args = (tok_own, out_even, out_got, out_far, b_out, b_down)
+        result = finish(result_kernel, "result", seq, *out_args)
         tok_args = (tok_own, e_own, e_near, e_far, cot_own)
         grad_tokens = finish(token_kernel, "token_grad", seq, *tok_args)
-        bias, sums = rest
+        third = 3 * width
+        table = jnp.concatenate([small[0:8], small[8:16, : D - third]], axis=1)
         mine = (jnp.arange(4) == blk)[:, None]
-        joined = lax.psum(jnp.where(mine, bias[0:1], 0.0), ("rows", "blk"))
-        gb_up = lax.psum(jnp.where(mine, mlp_sums[0:1], 0.0), ("rows", "blk")).reshape(FF)
+        joined = lax.psum(jnp.where(mine, small[2:3], 0.0), ("rows", "blk"))
+        gb_up = lax.psum(jnp.where(mine, table[4:5], 0.0), ("rows", "blk")).reshape(FF)
         gb_qkv = jnp.concatenate(
             [
                 jnp.concatenate([joined[:, 0:128], joined[:, 256:320]], axis=1).reshape(D),
@@ -1290,9 +1288,8 @@
                 joined[:, 384:576].reshape(D),
             ]
         )
-        sums = jnp.concatenate([sums[0:2], mlp_sums[1:4]])
-        *norms, gb_out = lax.psum(sums, ("rows", "blk"))
-        gb_down = gb_out
+        gain_1, shift_1, _, _, _, gain_2, shift_2, gb_out = lax.psum(table, ("rows", "blk"))
+        norms, gb_down = (gain_1, shift_1, gain_2, shift_2), gb_out
     return (
         result[None],
         grad_tokens[None],

time: 199 us -> 191 us (0.960)
  the two profiles are of different devices: /device:TPU:2 before, /device:TPU:0 now
where the time goes in v5:
time: 191 us; the launch traced here: 188 us
  Pallas kernels  118 us (62%)
  starting transfers between devices  29.9 us (16%)
  other arithmetic  19 us (10%)
  waiting for transfers between devices  10.6 us (6%)
  local copies, waits for them, and re-layouts  9.08 us (5%)
    pallas_call x2, Pallas kernels, feed_forward(): pl.pallas_call(body, out_shape=outs, grid_spec=pltpu.PrefetchScalarGridSp...  38.9 us
    ppermute x23, starting transfers between devices, swap(): return lax.ppermute(value, axis, [(i, i ^ mask) for i in range(size)])  27.5 us
    pallas_call x1, Pallas kernels, attend_back(): pl.pallas_call(partial(attend_back_kernel, per), out_shape=jax.ShapeDtype...  21 us
    pallas_call x1, Pallas kernels, attend(): pl.pallas_call(partial(attend_kernel, per), out_shape=[jax.ShapeDtypeStru...  13 us
    convert_element_type x16, other arithmetic, add_low(): return (left.astype(F32) + right.astype(F32)).astype(BF16)  12.6 us
    pallas_call x1, Pallas kernels, joined_weight(): pl.pallas_call(partial(weight_kernel, rows), out_shape=[jax.ShapeDtypeStr...  9.98 us
    ppermute x23, waiting for transfers between devices, swap(): return lax.ppermute(value, axis, [(i, i ^ mask) for i in range(size)])  9.61 us
    pallas_call x2, Pallas kernels, project(): pl.pallas_call(partial(qkv_kernel, slot), out_shape=[out] * 3, grid_spec=...  9.14 us
  transfers between devices with their start and end apart: 25, of which 5 were waited for; matrix products, arithmetic and copies ran while one was open for 11% of the time, Pallas kernels for 51%

profile of v5, /device:TPU:0, one launch (start us, length us, event | category | flops | bytes accessed | tf_op | source)
XLA Modules:
  0.0 188.1 jit_solution(15703711660401386365)
XLA Ops:
  3.1 2.6 %collective-permute-start.2 = (bf16[528,768]{1,0:T(8,128)(2,1)S(1)}, bf16[528,768]{1,0:T(8,128)(2,1)S(1)}, u32[]{:S(2)}, u32[]{:S(2)}) collective-permute-start(bf16[528,768]{1,0:T(8,128)(2,1)S(1)} %fusion.1.xa.s0.refs_4_.x_ref), channel_id=1, source_target_pairs={{0,2},{1,3},{2,0},{3,1},{4,6},{5,7},{6,4},{7,5},{8,10},{9,11},{10,... | collective-permute-start | bytes 2433032 | tf_op jit(solution)/shard_map/ppermute | solution.py:1056
  9.1 18.7 %mlp_first.1 = (bf16[1024,768]{1,0:T(8,128)(2,1)}, bf16[1024,768]{1,0:T(8,128)(2,1)}, bf16[2048,192]{1,0:T(8,128)(2,1)}, f32[8,768]{1,0:T(8,128)}, f32[768,768]{...) custom-call(s32[2]{0:T(128)} %pad_add_fusion.meta, ...), custom_call_target="tpu_custom_call" | custom-call | tf_op jit(solution)/shard_map/mlp_first/pallas_call | solution.py:467
  29.2 4.6 %qkv_2.1 = (bf16[2048,192]{1,0:T(8,128)(2,1)}, bf16[2048,192]{1,0:T(8,128)(2,1)}, bf16[2048,192]{1,0:T(8,128)(2,1)}) custom-call(s32[2]{0:T(128)} %pad_add_fusion.meta, bf16[528,768]{1,0:T(8,128)(2,1)} %copy-done.1, f32[768]{0:T(1024)} %refs_8_.3, f32[768]{0:T(1024)} %refs_9_.1, ...), custom_call_target="tpu_custom_call", output_to_operand_aliasing={{0}: (8, {}), {1}: (9, {}), {2}: (10, {})} | custom-call | tf_op jit(solution)/shard_map/qkv_2/pallas_call | solution.py:159
  34.7 4.6 %qkv_3.1 = (bf16[2048,192]{1,0:T(8,128)(2,1)}, bf16[2048,192]{1,0:T(8,128)(2,1)}, bf16[2048,192]{1,0:T(8,128)(2,1)}) custom-call(s32[2]{0:T(128)} %pad_add_fusion.meta, bf16[528,768]{1,0:T(8,128)(2,1)} %copy-done.2, f32[768]{0:T(1024)} %refs_8_.3, f32[768]{0:T(1024)} %refs_9_.1, ...), custom_call_target="tpu_custom_call", output_to_operand_aliasing={{0}: (8, {}), {1}: (9, {}), {2}: (10, {})} | custom-call | tf_op jit(solution)/shard_map/qkv_3/pallas_call | solution.py:159
  39.2 2.4 %segment_starts.1 = (s32[8,1,256]{2,1,0:T(1,128)}, s32[8]{0:T(128)}, s32[8]{0:T(128)}) custom-call(s32[2]{0:T(128)} %pad_add_fusion.meta, s32[1]{0:T(128)S(6)} %copy.47.valid, bf16[528,768]{1,0:T(8,128)(2,1)} %copy-done, bf16[528,768]{1,0:T(8,128)(2,1)} %copy-done.4, bf16[528,768]{1,0:T(8,128)(2,1)} %copy-done.1, bf16[528,768]{1,0:T(8,128)(2,1)} %copy-done.2), custom_call_target="tpu_custom_call" | custom-call | tf_op jit(solution)/shard_map/segment_starts/pallas_call | solution.py:197
  42.4 13.0 %attend.1 = (bf16[2048,192]{1,0:T(8,128)(2,1)}, f32[3,8,1,256]{3,2,1,0:T(1,128)}) custom-call(s32[2]{0:T(128)} %pad_add_fusion.meta, s32[8]{0:T(128)} %get-tuple-element.114.lo, s32[8]{0:T(128)} %get-tuple-element.115.hi, bf16[2048,192]{1,0:T(8,128)(2,1)} %get-tuple-element.112.q_ref, bf16[2048,192]{1,0:T(8,128)(2,1)} %get-tuple-element.116.k_ref, ...), custom_call_target="tpu_custom_call" | custom-call | tf_op jit(solution)/shard_map/attend/pallas_call | solution.py:594
  56.2 20.2 %mlp_second.1 = (bf16[1024,768]{1,0:T(8,128)(2,1)}, bf16[2048,192]{1,0:T(8,128)(2,1)}, f32[8,768]{1,0:T(8,128)}, bf16[2,512,768]{2,1,0:T(8,128)(2,1)}, bf16[2,51...) custom-call(s32[2]{0:T(128)} %pad_add_fusion.meta, ...), custom_call_target="tpu_custom_call", output_to_operand_aliasing={{1}: (19, {})} | custom-call | tf_op jit(solution)/shard_map/mlp_second/pallas_call | solution.py:467
  76.4 1.8 collective-permute-start.6
  78.5 1.3 collective-permute-start.7
  79.8 21.0 %attend_back.1.refs_0_.refs_1_.refs_2_.refs_3_ = bf16[2048,576]{1,0:T(8,128)(2,1)} custom-call(s32[2]{0:T(128)} %pad_add_fusion.meta, s32[8]{0:T(128)} %get-tuple-element.114.lo, s32[8]{0:T(128)} %get-tuple-element.115.hi, bf16[2048,192]{1,0:T(8,128)(2,1)} %get-tuple-element.112.q_ref, bf16[2048,192]{1,0:T(8,128)(2,1)} %get-tuple-element.116.k_ref, ...), custom_call_target="tpu_custom_call" | custom-call | tf_op jit(solution)/shard_map/attend_back/pallas_call | solution.py:725
  100.8 10.0 %joined_weight.1 = (bf16[400,576]{1,0:T(8,128)(2,1)}, bf16[400,576]{1,0:T(8,128)(2,1)}, f32[16,576]{1,0:T(8,128)}) custom-call(s32[2]{0:T(128)} %pad_add_fusion.meta, bf16[2048,576]{1,0:T(8,128)(2,1)} %attend_back.1.refs_0_.refs_1_.refs_2_.refs_3_, bf16[2048,576]{1,0:T(8,128)(2,1)} %attend_back.1.refs_0_.refs_1_.refs_2_.refs_3_, ...), custom_call_target="tpu_custom_call" | custom-call | tf_op jit(solution)/shard_map/joined_weight/pallas_call | solution.py:825
  112.5 2.0 %add_convert_fusion.3 = bf16[192,1024]{1,0:T(8,128)(2,1)} fusion(bf16[384,1024]{1,0:T(8,128)(2,1)} %collective-permute-done.7, bf16[384,1024]{1,0:T(8,128)(2,1)S(1)} %copy-done.10), kind=kLoop, calls=%fused_computation.7 | loop fusion | flops 786432 | bytes 1179648 | tf_op jit(solution)/shard_map/convert_element_type | solution.py:1060
  114.5 4.7 %collective-permute-start.12 = (bf16[192,1024]{1,0:T(8,128)(2,1)}, bf16[192,1024]{1,0:T(8,128)(2,1)}, u32[]{:S(2)}, u32[]{:S(2)}) collective-permute-start(bf16[192,1024]{1,0:T(8,128)(2,1)} %add_convert_fusion.3), channel_id=1, source_target_pairs={{0,16},{4,20},{8,24},{12,28},{16,0},{20,4},{24,8},{28,12},{1,17},{... | collective-permute-start | bytes 1179656 | tf_op jit(solution)/shard_map/ppermute | solution.py:1056
  121.6 1.5 collective-permute-start.11
  123.0 7.0 %norm_grad.1 = (bf16[512,768]{1,0:T(8,128)(2,1)}, bf16[512,768]{1,0:T(8,128)(2,1)}, bf16[512,768]{1,0:T(8,128)(2,1)}, bf16[512,768]{1,0:T(8,128)(2,1)}) custom-call(s32[2]{0:T(128)} %pad_add_fusion.meta, bf16[2048,576]{1,0:T(8,128)(2,1)} %attend_back.1.refs_0_.refs_1_.refs_2_.refs_3_, bf16[2048,576]{1,0:T(8,128)(2,1)} %attend_back.1.refs_0_.refs_1_.refs_2_.refs_3_, ...), custom_call_target="tpu_custom_call" | custom-call | tf_op jit(solution)/shard_map/norm_grad/pallas_call | solution.py:864
  131.0 1.9 %collective-permute-start.14 = (bf16[208,576]{1,0:T(8,128)(2,1)}, bf16[208,576]{1,0:T(8,128)(2,1)}, u32[]{:S(2)}, u32[]{:S(2)}) collective-permute-start(bf16[208,576]{1,0:T(8,128)(2,1)} %pad_maximum_fusion.1), channel_id=1, source_target_pairs={{0,8},{4,12},{8,0},{12,4},{16,24},{20,28},{24,16},{28,20},{1,9},{5... | collective-permute-start | bytes 718856 | tf_op jit(solution)/shard_map/ppermute | solution.py:1056
  133.5 7.3 %collective-permute-done.11.far = bf16[512,768]{1,0:T(8,128)(2,1)} collective-permute-done((bf16[512,768]{1,0:T(8,128)(2,1)}, bf16[512,768]{1,0:T(8,128)(2,1)}, u32[]{:S(2)}, u32[]{:S(2)}) %collective-permute-start.11) | collective-permute-done | bytes 786464 | tf_op jit(solution)/shard_map/ppermute | solution.py:1056
  140.7 1.5 collective-permute-start.16
  142.3 2.8 %result.1 = bf16[512,768]{1,0:T(8,128)(2,1)} custom-call(bf16[528,768]{1,0:T(8,128)(2,1)} %copy-done, bf16[2,512,768]{2,1,0:T(8,128)(2,1)} %get-tuple-element.142.even, bf16[2,512,768]{2,1,0:T(8,128)(2,1)} %copy-done.6, bf16[512,768]{1,0:T(8,128)(2,1)} %collective-permute-done.11.far, f32[768]{0:T(1024)} %b_out.1, f32[768]{0:T(1024)} %b_down.1), custom_call_target="tpu_custom_call" | custom-call | tf_op jit(solution)/shard_map/result/pallas_call | solution.py:1130
  149.7 2.6 %collective-permute-start.19 = (bf16[96,768]{1,0:T(8,128)(2,1)S(1)}, bf16[96,768]{1,0:T(8,128)(2,1)}, u32[]{:S(2)}, u32[]{:S(2)}) collective-permute-start(bf16[96,768]{1,0:T(8,128)(2,1)S(1)} %add_convert_fusion.11), channel_id=1, source_target_pairs={{0,16},{4,20},{8,24},{12,28},{16,0},{20,4},{24,8},{28,12},{1,17},{... | collective-permute-start | bytes 442376 | tf_op jit(solution)/shard_map/ppermute | solution.py:1056
  154.2 1.7 add_convert_fusion.8.keep
  157.4 1.2 collective-permute-done.16.far
  159.6 3.4 %token_grad.1 = bf16[512,768]{1,0:T(8,128)(2,1)} custom-call(bf16[528,768]{1,0:T(8,128)(2,1)} %copy-done, bf16[512,768]{1,0:T(8,128)(2,1)} %get-tuple-element.149.even, bf16[512,768]{1,0:T(8,128)(2,1)} %copy-done.8, bf16[512,768]{1,0:T(8,128)(2,1)} %copy-done.9, bf16[512,768]{1,0:T(8,128)(2,1)} %bitcast.10), custom_call_target="tpu_custom_call" | custom-call | tf_op jit(solution)/shard_map/token_grad/pallas_call | solution.py:1130
  163.7 2.5 %last_low.1 = (bf16[96,480]{1,0:T(8,128)(2,1)}, bf16[96,480]{1,0:T(8,128)(2,1)}) custom-call(s32[2]{0:T(128)} %pad_add_fusion.meta, bf16[96,1024]{1,0:T(8,128)(2,1)} %add_convert_fusion.8.keep, bf16[96,1024]{1,0:T(8,128)(2,1)} %copy-done.14), custom_call_target="tpu_custom_call" | custom-call | tf_op jit(solution)/shard_map/last_low/pallas_call | solution.py:885
  166.2 1.5 collective-permute-start.20
  167.7 2.5 %last_qkv.1 = (f32[96,192]{1,0:T(8,128)}, f32[128,192]{1,0:T(8,128)}, f32[128,192]{1,0:T(8,128)}, f32[32,192]{1,0:T(8,128)}) custom-call(s32[2]{0:T(128)} %pad_add_fusion.meta, bf16[112,576]{1,0:T(8,128)(2,1)} %pad_maximum_fusion.2.keep, bf16[112,576]{1,0:T(8,128)(2,1)} %collective-permute-done.18.got), custom_call_target="tpu_custom_call" | custom-call | tf_op jit(solution)/shard_map/last_qkv/pallas_call | solution.py:885
  170.2 2.9 %collective-permute-start.24 = (f32[32,192]{1,0:T(8,128)}, f32[32,192]{1,0:T(8,128)S(1)}, u32[]{:S(2)}, u32[]{:S(2)}) collective-permute-start(f32[32,192]{1,0:T(8,128)} %get-tuple-element.169.small), channel_id=1, source_target_pairs={{0,3},{1,2},{2,1},{3,0},{4,7},{5,6},{6,5},{7,4},{8,11},{9,10},{10,... | collective-permute-start | bytes 73736 | tf_op jit(solution)/shard_map/ppermute | solution.py:1056
  174.0 2.3 %collective-permute-start.23 = (f32[128,192]{1,0:T(8,128)}, f32[128,192]{1,0:T(8,128)S(1)}, u32[]{:S(2)}, u32[]{:S(2)}) collective-permute-start(f32[128,192]{1,0:T(8,128)} %get-tuple-element.177), channel_id=1, source_target_pairs={{0,2},{1,3},{2,0},{3,1},{4,6},{5,7},{6,4},{7,5},{8,10},{9,11},{10,... | collective-permute-start | bytes 294920 | tf_op jit(solution)/shard_map/ppermute | solution.py:1056
  176.4 1.7 convert_add_fusion
  180.3 2.6 %lower.1 = (f32[384,192]{1,0:T(8,128)}, f32[96,192]{1,0:T(8,128)}) custom-call(s32[2]{0:T(128)} %pad_add_fusion.meta, bf16[96,480]{1,0:T(8,128)(2,1)} %copy-done.17, bf16[96,480]{1,0:T(8,128)(2,1)} %copy-done.18), custom_call_target="tpu_custom_call" | custom-call | tf_op jit(solution)/shard_map/lower/pallas_call | solution.py:885
  182.9 1.9 copy.39
  185.5 2.7 %assemble.1 = (f32[96,576]{1,0:T(8,128)}, f32[2304]{0:T(1024)}, f32[768]{0:T(1024)}, f32[3072]{0:T(1024)}, f32[768]{0:T(1024)}, /*index=5*/f32[768]{0:T(1024)}, f32[768]{0:T(1024)}, f32[768]{0:T(1024)}, f32[768]{0:T(1024)}) custom-call(s32[2]{0:T(128)} %pad_add_fusion.meta, f32[96,192]{1,0:T(8,128)} %get-tuple-element.175.kept, ...), custom_call_target="tpu_custom_call" | custom-call | tf_op jit(solution)/shard_map/assemble/pallas_call | solution.py:1012
  (99 shorter events, 28.2 us)
Async XLA Ops:
  0.6 5.1 %copy-start.3 = (bf16[1,512,768]{2,1,0:T(8,128)(2,1)S(1)}, bf16[1,512,768]{2,1,0:T(8,128)(2,1)}, u32[]{:S(2)}) copy-start(bf16[1,512,768]{2,1,0:T(8,128)(2,1)} %param.33) | copy-start | bytes 2359300
  2.6 5.5 %copy-start = (bf16[528,768]{1,0:T(8,128)(2,1)}, bf16[528,768]{1,0:T(8,128)(2,1)S(1)}, u32[]{:S(2)}) copy-start(bf16[528,768]{1,0:T(8,128)(2,1)S(1)} %fusion.1.xa.s0.refs_4_.x_ref) | copy-start | bytes 2433028
  2.6 5.5 %collective-permute-start = (bf16[528,768]{1,0:T(8,128)(2,1)S(1)}, bf16[528,768]{1,0:T(8,128)(2,1)S(1)}, u32[]{:S(2)}, u32[]{:S(2)}) collective-permute-start(bf16[528,768]{1,0:T(8,128)(2,1)S(1)} %fusion.1.xa.s0.refs_4_.x_ref), channel_id=1, source_target_pairs={{0,1},{1,0},{2,3},{3,2},{4,5},{5,4},{6,7},{7,6},{8,9},{9,8},{10,11... | collective-permute-start | bytes 2433032 | tf_op jit(solution)/shard_map/ppermute | solution.py:1056
  3.1 24.6 %collective-permute-start.2 = (bf16[528,768]{1,0:T(8,128)(2,1)S(1)}, bf16[528,768]{1,0:T(8,128)(2,1)S(1)}, u32[]{:S(2)}, u32[]{:S(2)}) collective-permute-start(bf16[528,768]{1,0:T(8,128)(2,1)S(1)} %fusion.1.xa.s0.refs_4_.x_ref), channel_id=1, source_target_pairs={{0,2},{1,3},{2,0},{3,1},{4,6},{5,7},{6,4},{7,5},{8,10},{9,11},{10,... | collective-permute-start | bytes 2433032 | tf_op jit(solution)/shard_map/ppermute | solution.py:1056
  5.7 2.4 %collective-permute-start.1 = (bf16[512,768]{1,0:T(8,128)(2,1)S(1)}, bf16[512,768]{1,0:T(8,128)(2,1)}, u32[]{:S(2)}, u32[]{:S(2)}) collective-permute-start(bf16[512,768]{1,0:T(8,128)(2,1)S(1)} %bitcast.11), channel_id=1, source_target_pairs={{0,1},{1,0},{2,3},{3,2},{4,5},{5,4},{6,7},{7,6},{8,9},{9,8},{10,11... | collective-permute-start | bytes 2359304 | tf_op jit(solution)/shard_map/ppermute | solution.py:1056
  6.8 35.5 %collective-permute-start.4 = (bf16[544,768]{1,0:T(8,128)(2,1)}, bf16[544,768]{1,0:T(8,128)(2,1)}, u32[]{:S(2)}, u32[]{:S(2)}) collective-permute-start(bf16[544,768]{1,0:T(8,128)(2,1)} %pad.9), channel_id=1, source_target_pairs={{0,2},{1,3},{2,0},{3,1},{4,6},{5,7},{6,4},{7,5},{8,10},{9,11},{10,... | collective-permute-start | bytes 2506760 | tf_op jit(solution)/shard_map/ppermute | solution.py:1056
  27.8 6.0 %collective-permute-start.3 = (bf16[528,768]{1,0:T(8,128)(2,1)S(1)}, bf16[528,768]{1,0:T(8,128)(2,1)S(1)}, u32[]{:S(2)}, u32[]{:S(2)}) collective-permute-start(bf16[528,768]{1,0:T(8,128)(2,1)S(1)} %collective-permute-done.2.x_ref.s2.xa.refs_6_), channel_id=1, source_target_pairs={{0,1},{1,0},{2,3},{3,2},{4,5},{5,4},{6,7},{7,6},{8,9},{9,8},{10,11... | collective-permute-start | bytes 2433032 | tf_op jit(solution)/shard_map/ppermute | solution.py:1056
  42.4 13.0 %collective-permute-start.5 = (bf16[544,768]{1,0:T(8,128)(2,1)}, bf16[544,768]{1,0:T(8,128)(2,1)S(1)}, u32[]{:S(2)}, u32[]{:S(2)}) collective-permute-start(bf16[544,768]{1,0:T(8,128)(2,1)} %collective-permute-done.4.ca), channel_id=1, source_target_pairs={{0,1},{1,0},{2,3},{3,2},{4,5},{5,4},{6,7},{7,6},{8,9},{9,8},{10,11... | collective-permute-start | bytes 2506760 | tf_op jit(solution)/shard_map/ppermute | solution.py:1056
  76.4 35.2 %collective-permute-start.6 = (bf16[384,768]{1,0:T(8,128)(2,1)}, bf16[384,768]{1,0:T(8,128)(2,1)S(1)}, u32[]{:S(2)}, u32[]{:S(2)}) collective-permute-start(bf16[384,768]{1,0:T(8,128)(2,1)} %get-tuple-element.136), channel_id=1, source_target_pairs={{0,4},{4,0},{8,12},{12,8},{16,20},{20,16},{24,28},{28,24},{1,5},{5... | collective-permute-start | bytes 1769480 | tf_op jit(solution)/shard_map/ppermute | solution.py:1056
  78.2 42.1 %collective-permute-start.8 = (bf16[2,512,768]{2,1,0:T(8,128)(2,1)}, bf16[2,512,768]{2,1,0:T(8,128)(2,1)S(1)}, u32[]{:S(2)}, u32[]{:S(2)}) collective-permute-start(bf16[2,512,768]{2,1,0:T(8,128)(2,1)} %get-tuple-element.143), channel_id=1, source_target_pairs={{0,1},{1,0},{2,3},{3,2},{4,5},{5,4},{6,7},{7,6},{8,9},{9,8},{10,11... | collective-permute-start | bytes 4718600 | tf_op jit(solution)/shard_map/ppermute | solution.py:1056
  78.5 34.0 %collective-permute-start.7 = (bf16[384,1024]{1,0:T(8,128)(2,1)}, bf16[384,1024]{1,0:T(8,128)(2,1)}, u32[]{:S(2)}, u32[]{:S(2)}) collective-permute-start(bf16[384,1024]{1,0:T(8,128)(2,1)} %get-tuple-element.139), channel_id=1, source_target_pairs={{0,8},{4,12},{8,0},{12,4},{16,24},{20,28},{24,16},{28,20},{1,9},{5... | collective-permute-start | bytes 2359304 | tf_op jit(solution)/shard_map/ppermute | solution.py:1056
  100.8 10.9 %copy-start.12 = (bf16[384,768]{1,0:T(8,128)(2,1)S(1)}, bf16[384,768]{1,0:T(8,128)(2,1)}, u32[]{:S(2)}) copy-start(bf16[384,768]{1,0:T(8,128)(2,1)} %get-tuple-element.156) | copy-start | bytes 1769476
  110.8 19.3 %collective-permute-start.9 = (bf16[400,576]{1,0:T(8,128)(2,1)}, bf16[400,576]{1,0:T(8,128)(2,1)S(1)}, u32[]{:S(2)}, u32[]{:S(2)}) collective-permute-start(bf16[400,576]{1,0:T(8,128)(2,1)} %get-tuple-element.151), channel_id=1, source_target_pairs={{0,4},{4,0},{8,12},{12,8},{16,20},{20,16},{24,28},{28,24},{1,5},{5... | collective-permute-start | bytes 1382408 | tf_op jit(solution)/shard_map/ppermute | solution.py:1056
  112.4 7.9 %copy-start.5 = (bf16[2,512,768]{2,1,0:T(8,128)(2,1)S(1)}, bf16[2,512,768]{2,1,0:T(8,128)(2,1)}, u32[]{:S(2)}) copy-start(bf16[2,512,768]{2,1,0:T(8,128)(2,1)} %get-tuple-element.142.even) | copy-start | bytes 4718596
  112.4 33.7 %collective-permute-start.13 = (bf16[192,768]{1,0:T(8,128)(2,1)}, bf16[192,768]{1,0:T(8,128)(2,1)}, u32[]{:S(2)}, u32[]{:S(2)}) collective-permute-start(bf16[192,768]{1,0:T(8,128)(2,1)} %add_convert_fusion.5), channel_id=1, source_target_pairs={{0,8},{4,12},{8,0},{12,4},{16,24},{20,28},{24,16},{28,20},{1,9},{5... | collective-permute-start | bytes 884744 | tf_op jit(solution)/shard_map/ppermute | solution.py:1056
  114.5 30.6 %collective-permute-start.12 = (bf16[192,1024]{1,0:T(8,128)(2,1)}, bf16[192,1024]{1,0:T(8,128)(2,1)}, u32[]{:S(2)}, u32[]{:S(2)}) collective-permute-start(bf16[192,1024]{1,0:T(8,128)(2,1)} %add_convert_fusion.3), channel_id=1, source_target_pairs={{0,16},{4,20},{8,24},{12,28},{16,0},{20,4},{24,8},{28,12},{1,17},{... | collective-permute-start | bytes 1179656 | tf_op jit(solution)/shard_map/ppermute | solution.py:1056
  120.4 9.7 %copy-start.6 = (bf16[2,512,768]{2,1,0:T(8,128)(2,1)}, bf16[2,512,768]{2,1,0:T(8,128)(2,1)S(1)}, u32[]{:S(2)}) copy-start(bf16[2,512,768]{2,1,0:T(8,128)(2,1)S(1)} %collective-permute-done.8.near) | copy-start | bytes 4718596
  121.6 19.2 %collective-permute-start.11 = (bf16[512,768]{1,0:T(8,128)(2,1)}, bf16[512,768]{1,0:T(8,128)(2,1)}, u32[]{:S(2)}, u32[]{:S(2)}) collective-permute-start(bf16[512,768]{1,0:T(8,128)(2,1)} %fusion.2), channel_id=1, source_target_pairs={{0,2},{1,3},{2,0},{3,1},{4,6},{5,7},{6,4},{7,5},{8,10},{9,11},{10,... | collective-permute-start | bytes 2359304 | tf_op jit(solution)/shard_map/ppermute | solution.py:1056
  123.0 7.1 %copy-start.13 = (bf16[400,576]{1,0:T(8,128)(2,1)S(1)}, bf16[400,576]{1,0:T(8,128)(2,1)}, u32[]{:S(2)}) copy-start(bf16[400,576]{1,0:T(8,128)(2,1)} %get-tuple-element.155) | copy-start | bytes 1382404
  130.0 3.2 %copy-start.11 = (bf16[512,768]{1,0:T(8,128)(2,1)S(1)}, bf16[512,768]{1,0:T(8,128)(2,1)}, u32[]{:S(2)}) copy-start(bf16[512,768]{1,0:T(8,128)(2,1)} %get-tuple-element.152) | copy-start | bytes 2359300
  130.0 3.0 %collective-permute-start.10 = (bf16[512,768]{1,0:T(8,128)(2,1)}, bf16[512,768]{1,0:T(8,128)(2,1)S(1)}, u32[]{:S(2)}, u32[]{:S(2)}) collective-permute-start(bf16[512,768]{1,0:T(8,128)(2,1)} %get-tuple-element.153), channel_id=1, source_target_pairs={{0,1},{1,0},{2,3},{3,2},{4,5},{5,4},{6,7},{7,6},{8,9},{9,8},{10,11... | collective-permute-start | bytes 2359304 | tf_op jit(solution)/shard_map/ppermute | solution.py:1056
  131.0 16.1 %collective-permute-start.14 = (bf16[208,576]{1,0:T(8,128)(2,1)}, bf16[208,576]{1,0:T(8,128)(2,1)}, u32[]{:S(2)}, u32[]{:S(2)}) collective-permute-start(bf16[208,576]{1,0:T(8,128)(2,1)} %pad_maximum_fusion.1), channel_id=1, source_target_pairs={{0,8},{4,12},{8,0},{12,4},{16,24},{20,28},{24,16},{28,20},{1,9},{5... | collective-permute-start | bytes 718856 | tf_op jit(solution)/shard_map/ppermute | solution.py:1056
  133.0 24.4 %collective-permute-start.15 = (bf16[512,768]{1,0:T(8,128)(2,1)}, bf16[512,768]{1,0:T(8,128)(2,1)S(1)}, u32[]{:S(2)}, u32[]{:S(2)}) collective-permute-start(bf16[512,768]{1,0:T(8,128)(2,1)} %get-tuple-element.162), channel_id=1, source_target_pairs={{0,1},{1,0},{2,3},{3,2},{4,5},{5,4},{6,7},{7,6},{8,9},{9,8},{10,11... | collective-permute-start | bytes 2359304 | tf_op jit(solution)/shard_map/ppermute | solution.py:1056
  140.7 17.9 %collective-permute-start.16 = (bf16[512,768]{1,0:T(8,128)(2,1)S(1)}, bf16[512,768]{1,0:T(8,128)(2,1)S(1)}, u32[]{:S(2)}, u32[]{:S(2)}) collective-permute-start(bf16[512,768]{1,0:T(8,128)(2,1)S(1)} %add_convert_fusion), channel_id=1, source_target_pairs={{0,2},{1,3},{2,0},{3,1},{4,6},{5,7},{6,4},{7,5},{8,10},{9,11},{10,... | collective-permute-start | bytes 2359304 | tf_op jit(solution)/shard_map/ppermute | solution.py:1056
  149.4 18.3 %collective-permute-start.18 = (bf16[112,576]{1,0:T(8,128)(2,1)}, bf16[112,576]{1,0:T(8,128)(2,1)}, u32[]{:S(2)}, u32[]{:S(2)}) collective-permute-start(bf16[112,576]{1,0:T(8,128)(2,1)} %pad_maximum_fusion.3), channel_id=1, source_target_pairs={{0,16},{4,20},{8,24},{12,28},{16,0},{20,4},{24,8},{28,12},{1,17},{... | collective-permute-start | bytes 387080 | tf_op jit(solution)/shard_map/ppermute | solution.py:1056
  149.7 24.3 %collective-permute-start.19 = (bf16[96,768]{1,0:T(8,128)(2,1)S(1)}, bf16[96,768]{1,0:T(8,128)(2,1)}, u32[]{:S(2)}, u32[]{:S(2)}) collective-permute-start(bf16[96,768]{1,0:T(8,128)(2,1)S(1)} %add_convert_fusion.11), channel_id=1, source_target_pairs={{0,16},{4,20},{8,24},{12,28},{16,0},{20,4},{24,8},{28,12},{1,17},{... | collective-permute-start | bytes 442376 | tf_op jit(solution)/shard_map/ppermute | solution.py:1056
  152.3 10.7 %collective-permute-start.17 = (bf16[96,1024]{1,0:T(8,128)(2,1)S(1)}, bf16[96,1024]{1,0:T(8,128)(2,1)S(1)}, u32[]{:S(2)}, u32[]{:S(2)}) collective-permute-start(bf16[96,1024]{1,0:T(8,128)(2,1)S(1)} %add_convert_fusion.9), channel_id=1, source_target_pairs={{0,4},{4,0},{8,12},{12,8},{16,20},{20,16},{24,28},{28,24},{1,5},{5... | collective-permute-start | bytes 589832 | tf_op jit(solution)/shard_map/ppermute | solution.py:1056
  166.2 12.8 %collective-permute-start.20 = (bf16[96,480]{1,0:T(8,128)(2,1)}, bf16[96,480]{1,0:T(8,128)(2,1)S(1)}, u32[]{:S(2)}, u32[]{:S(2)}) collective-permute-start(bf16[96,480]{1,0:T(8,128)(2,1)} %get-tuple-element.165), channel_id=1, source_target_pairs={{0,0},{1,8},{2,16},{3,24},{4,4},{5,12},{6,20},{7,28},{8,1},{9,9},{... | collective-permute-start | bytes 276488 | tf_op jit(solution)/shard_map/ppermute | solution.py:1245
  170.2 14.5 %collective-permute-start.24 = (f32[32,192]{1,0:T(8,128)}, f32[32,192]{1,0:T(8,128)S(1)}, u32[]{:S(2)}, u32[]{:S(2)}) collective-permute-start(f32[32,192]{1,0:T(8,128)} %get-tuple-element.169.small), channel_id=1, source_target_pairs={{0,3},{1,2},{2,1},{3,0},{4,7},{5,6},{6,5},{7,4},{8,11},{9,10},{10,... | collective-permute-start | bytes 73736 | tf_op jit(solution)/shard_map/ppermute | solution.py:1056
  173.1 5.9 %collective-permute-start.21 = (bf16[96,480]{1,0:T(8,128)(2,1)}, bf16[96,480]{1,0:T(8,128)(2,1)S(1)}, u32[]{:S(2)}, u32[]{:S(2)}) collective-permute-start(bf16[96,480]{1,0:T(8,128)(2,1)} %get-tuple-element.172), channel_id=1, source_target_pairs={{0,4},{1,12},{2,20},{3,28},{4,0},{5,8},{6,16},{7,24},{8,5},{9,13},... | collective-permute-start | bytes 276488 | tf_op jit(solution)/shard_map/ppermute | solution.py:1245
  174.0 10.7 %collective-permute-start.22 = (f32[128,192]{1,0:T(8,128)}, f32[128,192]{1,0:T(8,128)S(1)}, u32[]{:S(2)}, u32[]{:S(2)}) collective-permute-start(f32[128,192]{1,0:T(8,128)} %get-tuple-element.176), channel_id=1, source_target_pairs={{0,1},{1,0},{2,3},{3,2},{4,5},{5,4},{6,7},{7,6},{8,9},{9,8},{10,11... | collective-permute-start | bytes 294920 | tf_op jit(solution)/shard_map/ppermute | solution.py:1056
  174.0 10.7 %collective-permute-start.23 = (f32[128,192]{1,0:T(8,128)}, f32[128,192]{1,0:T(8,128)S(1)}, u32[]{:S(2)}, u32[]{:S(2)}) collective-permute-start(f32[128,192]{1,0:T(8,128)} %get-tuple-element.177), channel_id=1, source_target_pairs={{0,2},{1,3},{2,0},{3,1},{4,6},{5,7},{6,4},{7,5},{8,10},{9,11},{10,... | collective-permute-start | bytes 294920 | tf_op jit(solution)/shard_map/ppermute | solution.py:1056
  (13 other events, 11.9 us)

commit v6 on v5

--- a/solution.py
+++ b/solution.py
@@ -140,37 +140,8 @@
     v_ref[...] = joined[:, 384:576].astype(BF16)
 
 
-def qkv_kernel(slot, meta, x_ref, gain, shift, low, high, w_ref, b_ref, *refs):
-    per = pl.num_programs(0)
-    tile = true_block(meta, slot) * per + pl.program_id(0)
-    normed = normalize(x_ref[...].astype(F32))
-    project_tile(normed, gain, shift, w_ref, b_ref, low, high, tile, *refs[-3:])
-
-
-def project(slot, meta, x, gain, shift, low, high, w, b, filled, seq):
-    width = D // 4
-    per = seq // TILE
-    out = jax.ShapeDtypeStruct((4 * seq, width), BF16)
-    out_spec = pl.BlockSpec((TILE, width), lambda i, m: (slot * per + i, 0))
-    args = [x, gain, shift, low, high, w, b, *filled]
-    specs = [pl.BlockSpec((TILE, D), lambda i, m: (i, 0))]
-    specs += [whole(a.shape) for a in args[1:7]]
-    specs += [pl.BlockSpec(memory_space=pl.ANY)] * 3
-    return pl.pallas_call(
-        partial(qkv_kernel, slot),
-        out_shape=[out] * 3,
-        grid_spec=pltpu.PrefetchScalarGridSpec(
-            num_scalar_prefetch=1, grid=(per,), in_specs=specs, out_specs=[out_spec] * 3
-        ),
-        input_output_aliases={8 + i: i for i in range(3)},
-        compiler_params=params(),
-        cost_estimate=COST,
-        name=f"qkv_{slot}",
-    )(meta, *args)
-
-
-def starts_kernel(seq, meta, valid, s0, s1, s2, s3, start_ref, lo_ref, hi_ref):
-    segs = [ref[0:1, 0:seq].astype(F32) for ref in (s0, s1, s2, s3)]
+def find_starts(seq, meta, valid, rows, start_ref, lo_ref, hi_ref):
+    segs = [ref[0:1, 0:seq].astype(F32) for ref in rows]
     below = [
         sum(jnp.sum((seg < number).astype(F32), axis=1, keepdims=True) for seg in segs)
         for number in (1, 2, 3)
@@ -191,26 +162,48 @@
             hi_ref[block * per + part] = (jnp.max(tile) + (TILE - 1)) // TILE
 
 
-def segment_starts(meta, valid_len, toks, seq):
-    tiles = 4 * seq // TILE
-    smem = pl.BlockSpec(memory_space=pltpu.SMEM)
+def qkv_kernel(slot, meta, valid, x_ref, gain, shift, low, high, w_ref, b_ref, *refs):
+    per = pl.num_programs(0)
+    tile = true_block(meta, slot) * per + pl.program_id(0)
+    normed = normalize(x_ref[...].astype(F32))
+    if slot == 3:
+        segs, (*outs, start_ref, lo_ref, hi_ref) = refs[3:7], refs[7:]
+
+        @pl.when(pl.program_id(0) == 0)
+        def _():
+            find_starts(per * TILE, meta, valid, segs, start_ref, lo_ref, hi_ref)
+    else:
+        outs = refs[3:]
+    project_tile(normed, gain, shift, w_ref, b_ref, low, high, tile, *outs)
+
+
+def project(slot, meta, valid, x, gain, shift, low, high, w, b, filled, seq, toks=()):
+    width = D // 4
+    per = seq // TILE
+    tiles = 4 * per
+    outs = [jax.ShapeDtypeStruct((4 * seq, width), BF16)] * 3
+    out_specs = [pl.BlockSpec((TILE, width), lambda i, m, v: (slot * per + i, 0))] * 3
+    args = [x, gain, shift, low, high, w, b, *filled, *toks]
+    specs = [pl.BlockSpec((TILE, D), lambda i, m, v: (i, 0))]
+    specs += [whole(a.shape) for a in args[1:7]]
+    specs += [pl.BlockSpec(memory_space=pl.ANY)] * 3
+    specs += [pl.BlockSpec((EXTRA, D), lambda i, m, v: (seq // EXTRA, 0)) for _ in toks]
+    if toks:
+        smem = pl.BlockSpec(memory_space=pltpu.SMEM)
+        outs.append(jax.ShapeDtypeStruct((tiles, 1, TILE), jnp.int32))
+        outs += [jax.ShapeDtypeStruct((tiles,), jnp.int32)] * 2
+        out_specs += [whole((tiles, 1, TILE)), smem, smem]
     return pl.pallas_call(
-        partial(starts_kernel, seq),
-        out_shape=[
-            jax.ShapeDtypeStruct((tiles, 1, TILE), jnp.int32),
-            jax.ShapeDtypeStruct((tiles,), jnp.int32),
-            jax.ShapeDtypeStruct((tiles,), jnp.int32),
-        ],
+        partial(qkv_kernel, slot),
+        out_shape=outs,
         grid_spec=pltpu.PrefetchScalarGridSpec(
-            num_scalar_prefetch=2,
-            grid=(1,),
-            in_specs=[pl.BlockSpec((EXTRA, D), lambda i, m, v: (seq // EXTRA, 0))] * 4,
-            out_specs=[whole((tiles, 1, TILE)), smem, smem],
+            num_scalar_prefetch=2, grid=(per,), in_specs=specs, out_specs=out_specs
         ),
+        input_output_aliases={9 + i: i for i in range(3)},
         compiler_params=params(),
         cost_estimate=COST,
-        name="segment_starts",
-    )(meta, valid_len, *toks)
+        name=f"qkv_{slot}",
+    )(meta, valid, *args)
 
 
 def mask_order(rows, first):
@@ -236,6 +229,39 @@
         into = keep if index < rows // 2 else send
         row_at = index % (rows // 2) * size
         into[row_at : row_at + size, :] = load(pl.ds(at, size)).astype(into.dtype)
+
+
+def store_low(grad, keep, send, meta, rows):
+    size, hid = D // 4, FF // 4
+    for index, place in enumerate(places(mask_order(rows, 2))):
+        chunk = jnp.bitwise_xor(meta[1], place)
+        at = pl.ds(pl.multiple_of(chunk % 4 * size, 64), size)
+        down = pl.multiple_of(hid + chunk // 4 * (hid // 2), LANES)
+        out = pl.multiple_of(2 * hid + chunk // 4 * LANES, LANES)
+        into = keep if index < rows // 2 else send
+        row_at = slice(index % (rows // 2) * size, (index % (rows // 2) + 1) * size)
+        into[row_at, : hid // 2] = grad[at, pl.ds(down, hid // 2)].astype(BF16)
+        into[row_at, hid // 2 :] = grad[at, pl.ds(out, LANES)].astype(BF16)
+
+
+def low_shapes(rows):
+    if fits(rows):
+        return [(D, FF // 8 + LANES)] * 2
+    return [(D, FF // 4 + 2 * LANES), (8, LANES)]
+
+
+def low_chunks(keep, send, rows):
+    if fits(rows):
+        return keep, send
+    hid, width, count = FF // 4, D // 4, rows // 4
+    parts = [
+        part.reshape(4, width, count, part.shape[1] // count).transpose(2, 0, 1, 3)
+        for part in (keep[:, :hid], keep[:, hid : hid + width])
+    ]
+    chunks = jnp.concatenate(parts, axis=3).reshape(rows, width, -1)
+    order = jnp.array(places(mask_order(rows, 2))) ^ lax.axis_index("rows")
+    chunks = jnp.take(chunks, order, axis=0).reshape(rows * width, -1)
+    return chunks[: rows * width // 2], chunks[rows * width // 2 :]
 
 
 def chunk_shapes(cols, rows, extra=0):
@@ -277,7 +303,7 @@
 def mlp_first_kernel(
     half, meta, xa, xb, ca, cb, gain, shift, b_up, w_up, w_down, w_out,
     gain1, shift1, b_qkv, low, high, w0, w1, w2, w3, w4, w5,
-    mo_ref, e_ref, gv_ref, sums, gup, gdown, q_ref, k_ref, v_ref, w_own, b_own, x_s, c_s,
+    mo_ref, e_ref, n_ref, gv_ref, sums, gup, gdown, q_ref, k_ref, v_ref, w_own, b_own, x_s, c_s,
 ):
     step = pl.program_id(0)
 
@@ -307,6 +333,7 @@
         sums[3:4, :] += jnp.sum(upstream.astype(F32), axis=0, keepdims=True)
 
     normed = normalize(x_s[...].astype(F32))
+    n_ref[...] = normed.astype(BF16)
     tile = true_block(meta, step // half) * half + step % half
     project_tile(normed, gain1, shift1, w_own, b_own, low, high, tile, q_ref, k_ref, v_ref)
     bias = own_row(b_up, meta[0], gup.shape[1])
@@ -321,9 +348,10 @@
 
 def mlp_second_kernel(
     half, rows, meta, xa, xb, ca, cb, gain, shift, b_up, w_up, w_down, w_out,
-    c0, c1, mo_in, o_near, o_far, sums_in, gup, gdown, _,
-    e_ref, gv_ref, sums, even, odd, up_keep, up_send, low_keep, low_send, x_s, c_s, n_s, grad,
+    c0, c1, mo_in, o_near, o_far, sums_in, gup, gdown, *refs
 ):
+    e_ref, n_ref, gv_ref, sums, even, odd, up_keep, up_send, low_keep, low_send = refs[3:13]
+    x_s, c_s, n_s, grad = refs[13:]
     step = pl.program_id(0)
     hid = gup.shape[1]
 
@@ -348,6 +376,7 @@
 
     upstream = c_s[...]
     normed = normalize(x_s[...].astype(F32))
+    n_ref[...] = normed.astype(BF16)
     bias = own_row(b_up, meta[0], hid)
     mlp_in, act, grad_low, grad_norm = feed(normed, upstream, gain, shift, w_up, bias, w_down)
     add_sums(sums, grad_low, grad_norm, normed)
@@ -355,9 +384,13 @@
     gv_ref[...] = dot_nt(upstream, w_out[...]).astype(BF16)
     grad[:, 0:hid] += dot_tn(mlp_in, grad_low)
     grad[:, hid : 2 * hid] += dot_tn(upstream, act)
-    grad[:, 2 * hid : 2 * hid + D // 4] += dot_tn(upstream, o_far[...]) + dot_tn(
-        n_s[...], o_near[...]
-    )
+    out_grad = dot_tn(upstream, o_far[...]) + dot_tn(n_s[...], o_near[...])
+    side = out_grad.shape[1] // 2
+    if fits(rows):
+        grad[:, 2 * hid : 2 * hid + side] += out_grad[:, :side]
+        grad[:, 2 * hid + LANES : 2 * hid + LANES + side] += out_grad[:, side:]
+    else:
+        grad[:, 2 * hid : 2 * hid + 2 * side] += out_grad
     far = (dot(act, w_down[...]) + dot(o_far[...], w_out[...])).astype(BF16)
     near = (mo_in[...].astype(F32) + dot(o_near[...], w_out[...])).astype(BF16)
 
@@ -375,7 +408,7 @@
     def _():
         if fits(rows):
             store_chunks(lambda at: grad[at, 0:hid], up_keep, up_send, meta, rows, 1)
-            store_chunks(lambda at: grad[at, hid:], low_keep, low_send, meta, rows, 2)
+            store_low(grad, low_keep, low_send, meta, rows)
         else:
             up_keep[...] = grad[:, 0:hid].astype(BF16)
             low_keep[...] = grad[:, hid:].astype(BF16)
@@ -410,6 +443,7 @@
     sums = (8, D)
     scratch = [pltpu.VMEM((TILE, D), BF16), pltpu.VMEM((TILE, D), BF16)]
     pair = jax.ShapeDtypeStruct((steps * TILE, D), BF16)
+    full = jax.ShapeDtypeStruct((total, D), BF16)
     vec = jax.ShapeDtypeStruct((total, width), BF16)
     if before is None:
         body = partial(mlp_first_kernel, per)
@@ -425,21 +459,21 @@
                     )
                 )
                 args.append(w_qkv)
-        outs = [pair, pair, vec, jax.ShapeDtypeStruct(sums, F32)]
+        outs = [pair, full, full, vec, jax.ShapeDtypeStruct(sums, F32)]
         outs += [jax.ShapeDtypeStruct((D, hid), F32)] * 2 + [vec] * 3
         outs += [
             jax.ShapeDtypeStruct((D, 3 * width), BF16),
             jax.ShapeDtypeStruct((1, 3 * width), F32),
         ]
-        out_specs = [tile, tile, narrow, whole(sums)]
+        out_specs = [tile, tile, tile, narrow, whole(sums)]
         out_specs += [whole((D, hid))] * 2 + [narrow] * 3
         out_specs += [whole((D, 3 * width)), whole((1, 3 * width))]
         aliases = {}
     else:
         body = partial(mlp_second_kernel, per, rows)
-        mlp_out, _, grad_vec, sums_in, gup, gdown = before
-        chunks = chunk_shapes(hid, rows) + chunk_shapes(hid + 2 * LANES, rows)
-        args += [*near, mlp_out, attn, attn, sums_in, gup, gdown, grad_vec]
+        mlp_out, norm_part, normed, grad_vec, sums_in, gup, gdown = before
+        chunks = chunk_shapes(hid, rows) + low_shapes(rows)
+        args += [*near, mlp_out, attn, attn, sums_in, gup, gdown, norm_part, normed, grad_vec]
         specs += [
             first,
             second,
@@ -449,14 +483,16 @@
             whole(sums),
             whole((D, hid)),
             whole((D, hid)),
-            pl.BlockSpec(memory_space=pl.ANY),
+            *(pl.BlockSpec(memory_space=pl.ANY),) * 3,
         ]
-        aliases = {len(args): 1}
+        aliases = {len(args) - 2 + i: i for i in range(3)}
         both = jax.ShapeDtypeStruct((2, seq, D), BF16)
-        outs = [pair, vec, jax.ShapeDtypeStruct(sums, F32), both, both]
+        outs = [full, full, vec, jax.ShapeDtypeStruct(sums, F32), both, both]
+        late = pl.BlockSpec((TILE, D), lambda i, m: (i + steps, 0))
         outs += [jax.ShapeDtypeStruct(shape, BF16) for shape in chunks]
         out_specs = [
-            tile,
+            late,
+            late,
             pl.BlockSpec((TILE, width), lambda i, m: (i + steps, 0)),
             whole(sums),
             pl.BlockSpec((2, TILE, D), lambda i, m: (0, jnp.minimum(i, per - 1), 0)),
@@ -772,8 +808,7 @@
 
 
 def weight_kernel(rows, meta, *refs):
-    gjs, xs = refs[0:4], refs[4:8]
-    gain, shift, w_ref, mlp_sums, keep, send, small, n_s, gj_s, grad, bias = refs[8:]
+    gj_ref, n_ref, gain, shift, w_ref, mlp_sums, keep, send, small, grad, bias = refs
     step = pl.program_id(0)
 
     @pl.when(step == 0)
@@ -781,12 +816,9 @@
         grad[...] = jnp.zeros_like(grad)
         bias[...] = jnp.zeros_like(bias)
 
-    for index, (gj_ref, x_ref) in enumerate(zip(gjs, xs)):
-        at = slice(index * TILE, (index + 1) * TILE)
-        n_s[at, :] = normalize(x_ref[...].astype(F32)).astype(BF16)
-        gj_s[at, :] = gj_ref[...]
-    bias[0:1, :] += jnp.sum(gj_s[...].astype(F32), axis=0, keepdims=True)
-    grad[...] += dot_tn(n_s[...], gj_s[...])
+    joined = gj_ref[...]
+    bias[0:1, :] += jnp.sum(joined.astype(F32), axis=0, keepdims=True)
+    grad[...] += dot_tn(n_ref[...], joined)
 
     @pl.when(step == pl.num_programs(0) - 1)
     def _():
@@ -814,81 +846,76 @@
             keep[...] = grad[...].astype(BF16)
 
 
-def slot_tiles(slot, cols, per):
-    return pl.BlockSpec((TILE, cols), lambda i, m: (slot * per + i, 0))
-
-
-def joined_weight(meta, grad, toks, gain, shift, w, mlp_sums, rows, seq):
-    width = grad.shape[1]
-    per = seq // TILE
+def row_tiles(cols, tile=TILE):
+    return pl.BlockSpec((tile, cols), lambda i, m: (i, 0))
+
+
+def joined_weight(meta, grad, normed, gain, shift, w, mlp_sums, rows):
+    total, width = grad.shape
+    tile = 2 * TILE
     chunks = chunk_shapes(width, rows, SMALL)
+    args = [gain, shift, w, mlp_sums]
     return pl.pallas_call(
         partial(weight_kernel, rows),
         out_shape=[jax.ShapeDtypeStruct(shape, BF16) for shape in chunks]
         + [jax.ShapeDtypeStruct((SMALL, width), F32)],
         grid_spec=pltpu.PrefetchScalarGridSpec(
             num_scalar_prefetch=1,
-            grid=(per,),
-            in_specs=[
-                *(slot_tiles(slot, width, per) for slot in range(4)),
-                *(slot_tiles(0, D, per) for _ in range(4)),
-                whole(gain.shape),
-                whole(shift.shape),
-                whole(w.shape),
-                whole(mlp_sums.shape),
-            ],
+            grid=(total // tile,),
+            in_specs=[row_tiles(width, tile), row_tiles(D, tile), *(whole(a.shape) for a in args)],
             out_specs=[*(whole(shape) for shape in chunks), whole((SMALL, width))],
-            scratch_shapes=[
-                pltpu.VMEM((4 * TILE, D), BF16),
-                pltpu.VMEM((4 * TILE, width), BF16),
-                pltpu.VMEM((D, width), F32),
-                pltpu.VMEM((8, width), F32),
-            ],
+            scratch_shapes=[pltpu.VMEM((D, width), F32), pltpu.VMEM((8, width), F32)],
         ),
         compiler_params=params(),
         cost_estimate=COST,
         name="joined_weight",
-    )(meta, *[grad] * 4, *toks, gain, shift, w, mlp_sums)
-
-
-def norm_kernel(meta, *refs):
-    gjs, es, (gain, w_ref), outs = refs[0:4], refs[4:8], refs[8:10], refs[10:]
-    for gj_ref, e_in, out in zip(gjs, es, outs):
-        grad_norm = dot_nt(gj_ref[...], w_ref[...])
-        out[...] = (grad_norm * row(gain) + e_in[...].astype(F32)).astype(BF16)
+    )(meta, grad, normed, *args)
+
+
+def norm_kernel(per, meta, gj_ref, e_in, gain, w_ref, *outs):
+    grad_norm = dot_nt(gj_ref[...], w_ref[...])
+    value = (grad_norm * row(gain) + e_in[...].astype(F32)).astype(BF16)
+    for slot, out in enumerate(outs):
+
+        @pl.when(pl.program_id(0) // per == slot)
+        def _(out=out):
+            out[...] = value
 
 
 def norm_grad(meta, grad, e_mlp, gain, w, seq):
-    width = grad.shape[1]
     per = seq // TILE
+
+    def slot_out(slot):
+        return pl.BlockSpec((TILE, D), lambda i, m: (jnp.clip(i - slot * per, 0, per - 1), 0))
+
     return pl.pallas_call(
-        norm_kernel,
+        partial(norm_kernel, per),
         out_shape=[jax.ShapeDtypeStruct((seq, D), BF16)] * 4,
         grid_spec=pltpu.PrefetchScalarGridSpec(
             num_scalar_prefetch=1,
-            grid=(per,),
+            grid=(4 * per,),
             in_specs=[
-                *(slot_tiles(slot, width, per) for slot in range(4)),
-                *(slot_tiles(slot % 2, D, per) for slot in range(4)),
+                row_tiles(grad.shape[1]),
+                row_tiles(D),
                 whole(gain.shape),
                 whole(w.shape),
             ],
-            out_specs=[slot_tiles(0, D, per)] * 4,
+            out_specs=[slot_out(slot) for slot in range(4)],
         ),
         compiler_params=params(),
         cost_estimate=COST,
         name="norm_grad",
-    )(meta, *[grad] * 4, e_mlp[0], e_mlp[0], e_mlp[1], e_mlp[1], gain, w)
-
-
-def simple(body, name, shapes, *args):
+    )(meta, grad, e_mlp, gain, w)
+
+
+def simple(body, name, shapes, *args, specs=None):
     return pl.pallas_call(
         body,
         out_shape=[jax.ShapeDtypeStruct(shape, kind) for shape, kind in shapes],
         grid_spec=pltpu.PrefetchScalarGridSpec(
             num_scalar_prefetch=1,
             grid=(1,),
-            in_specs=[whole(a.shape) for a in args[1:]],
+            in_specs=specs or [whole(a.shape) for a in args[1:]],
             out_specs=[whole(shape) for shape, _ in shapes],
         ),
         compiler_params=params(),
@@ -897,49 +924,25 @@
     )(*args)
 
 
-def last_low_kernel(meta, keep, got, first, second):
-    low = (keep[...].astype(F32) + got[...].astype(F32)).astype(BF16)
-    hid, side = FF // 4, D // 8
-    cut = hid // 2
-    even = jnp.concatenate([low[:, :cut], low[:, hid : hid + side]], axis=1)
-    odd = jnp.concatenate([low[:, cut:hid], low[:, hid + side : hid + 2 * side]], axis=1)
-
-    @pl.when(meta[1] % 2 == 0)
-    def _():
-        first[...] = even
-        second[...] = odd
-
-    @pl.when(meta[1] % 2 == 1)
-    def _():
-        first[...] = odd
-        second[...] = even
-
-
-def lower_kernel(meta, first, second, down_ref, out_ref):
-    cut = down_ref.shape[0]
-    size = first.shape[0]
-
-    def store(ref, at):
-        turned = ref[...].astype(F32).T
-        down_ref[:, at : at + size] = turned[:cut]
-        out_ref[:, at : at + size] = turned[cut:]
-
-    @pl.when(meta[1] % 2 == 0)
-    def _():
-        store(first, 0)
-        store(second, size)
-
-    @pl.when(meta[1] % 2 == 1)
-    def _():
-        store(second, 0)
-        store(first, size)
-
-
-def last_qkv_kernel(meta, keep, got, kept, near, far, small):
+def add_up(refs):
+    total = refs[0][...].astype(F32)
+    for ref in refs[1:]:
+        total += ref[...].astype(F32)
+    return total
+
+
+def lower_kernel(meta, piece, down_ref, out_ref):
+    cut = down_ref.shape[1]
+    down_ref[...] = piece[:, :cut].astype(F32)
+    out_ref[...] = piece[:, cut:].astype(F32).T[: out_ref.shape[0]]
+
+
+def last_qkv_kernel(meta, *refs):
+    *terms, sums, got_sums, kept, near, far, small = refs
     size = kept.shape[0]
     width = kept.shape[1]
-    both = keep[...].astype(F32) + got[...].astype(F32)
-    total, rows = both[0:size], both[size:]
+    total = add_up(terms)
+    rows = sums[...].astype(F32) + got_sums[...].astype(F32)
     for part in range(3):
         small[part * 8 : part * 8 + 8, :] = rows[0:8, part * width : (part + 1) * width]
     small[24:32, :] = rows[8:16, 0:width]
@@ -1025,26 +1028,16 @@
     )(meta, *args)
 
 
-def halve(keep, got):
-    half = keep.shape[0] // 2
-    send = add_low(keep[half:], got[half:])
-    return add_low(after(keep, send)[:half], got[:half]), send
-
-
-def halve_packet(keep, got, extra):
-    size = keep.shape[0] - extra
-    half = size // 2
-    tail = add_low(keep[size:], got[size:])
-    send = jnp.concatenate([add_low(keep[half:size], got[half:size]), tail])
-    first = add_low(after(keep, send)[:half], got[:half])
-    return jnp.concatenate([first, tail]), send
+def next_send(terms, size):
+    return sum(term[size // 2 : size].astype(F32) for term in terms).astype(BF16)
 
 
 def reduce_plain(keep, got, masks):
+    terms, size = [keep, got], keep.shape[0]
     for mask in masks:
-        keep, send = halve(keep, got)
-        got = swap(send, "rows", mask)
-    return keep.astype(F32) + got.astype(F32)
+        terms.append(swap(next_send(terms, size), "rows", mask))
+        size //= 2
+    return sum(term[:size].astype(F32) for term in terms)
 
 
 def after(value, *others):
@@ -1060,38 +1053,12 @@
     return (left.astype(F32) + right.astype(F32)).astype(BF16)
 
 
-def spread_rows(lower):
-    rows, blk = lax.axis_size("rows"), lax.axis_size("blk")
-    r = lax.axis_index("rows")
-    count = rows // blk
-    hid, width = FF // 4, D // 4
-    chunk = lower.shape[0]
-    down = lower[:, :hid].reshape(chunk, count, hid // count)
-    out = lower[:, hid:].reshape(chunk, count, width // count)
-    pieces = jnp.concatenate([down, out], axis=2).astype(BF16)
-    got = []
-    for turn in range(count):
-        moves = spread_moves(rows, blk, turn)
-        piece = lax.dynamic_index_in_dim(pieces, (r % count) ^ turn, 1, keepdims=False)
-        got.append(lax.ppermute(piece, ("rows", "blk"), moves))
-    got = jnp.stack(got)
-    parts = [
-        lax.dynamic_index_in_dim(got, (r % count) ^ part, 0, keepdims=False)
-        for part in range(count)
+def spread_rows(chunk):
+    rows = lax.axis_size("rows")
+    moves = [
+        (r * 4 + b, (rows // 4 * b + r // 4) * 4 + r % 4) for r in range(rows) for b in range(4)
     ]
-    whole_cols = jnp.concatenate(parts, axis=0).astype(F32).T
-    cut = hid // count
-    return whole_cols[:cut], whole_cols[cut:]
-
-
-def spread_moves(rows, blk, turn):
-    count = rows // blk
-    moves = []
-    for r in range(rows):
-        for b in range(blk):
-            to = count * b + ((r % count) ^ turn)
-            moves.append((r * blk + b, to * blk + r // count))
-    return moves
+    return lax.ppermute(chunk, ("rows", "blk"), moves)
 
 
 def split_columns(chunk):
@@ -1171,25 +1138,26 @@
     )
     meta = after(meta, b_own)
 
-    def more(slot, m, tok, filled):
-        return project(slot, m, tok, ln1_gain, ln1_bias, low, high, w_own, b_own, filled, seq)
+    def more(slot, m, tok, filled, slots=()):
+        args = (ln1_gain, ln1_bias, low, high, w_own, b_own, filled, seq, slots)
+        return project(slot, m, valid_len, tok, *args)
 
     tok_last = swap(after(tok_far, b_own), "blk", 1)
     joined = more(2, meta, tok_far, (query, keys, values))
     toks = (tok_own, tok_near, tok_far, tok_last)
-    query, keys, values = more(3, after(meta, joined[0]), tok_last, joined)
-    starts, lo, hi = segment_starts(after(meta, query), valid_len, toks, seq)
+    query, keys, values, starts, lo, hi = more(
+        3, after(meta, joined[0]), tok_last, joined, toks
+    )
     cot_last = swap(after(cot_far, lo), "blk", 1)
     cots = (cot_own, cot_near, cot_far, cot_last)
     attn, lse = attend(meta, lo, hi, query, keys, values, starts, per)
 
     meta = after(meta, lse)
-    e_far, grad_vec, mlp_sums, out_even, out_odd, *packets = feed_forward(
+    e_mlp, normed, grad_vec, mlp_sums, out_even, out_odd, *packets = feed_forward(
         meta, toks[2:], cots[2:], *mlp_args, before=first, near=cots[:2], attn=attn
     )
-    e_mlp = (first[1], e_far)
     up_keep, up_send = chunks_of(*packets[:2], rows, 1)
-    low_keep, low_send = chunks_of(*packets[2:], rows, 2)
+    low_keep, low_send = low_chunks(*packets[2:], rows)
     up_masks, low_masks = mask_order(rows, 1), mask_order(rows, 2)
     out_got = swap(out_odd, "blk", 1)
     up_got = swap(up_send, "rows", up_masks[0])
@@ -1201,19 +1169,22 @@
     )
     meta = after(meta, grad_joined)
     qkv_keep, qkv_send, small = joined_weight(
-        meta, grad_joined, toks, ln1_gain, ln1_bias, w_own, mlp_sums, rows, seq
+        meta, grad_joined, normed, ln1_gain, ln1_bias, w_own, mlp_sums, rows
     )
     qkv_keep, qkv_send = chunks_of(qkv_keep, qkv_send, rows, 1)
     qkv_got = swap(qkv_send, "rows", 1)
 
-    meta = after(meta, small)
-    out_send = add_low(after(out_even, small)[1], out_got[1])
+    meta = after(meta, qkv_keep)
+    out_send = add_low(after(out_even, qkv_keep)[1], out_got[1])
     out_far = swap(out_send, "blk", 2)
+    half = D // 2
     if fits(rows):
-        up_keep, up_send = halve(after(up_keep, small), up_got)
-        up_got = swap(up_send, "rows", up_masks[1])
-        low_keep, low_send = halve(after(low_keep, small), low_got)
-        low_got = swap(low_send, "rows", low_masks[1])
+        up = [after(up_keep, qkv_keep), up_got]
+        up_send = next_send(up, half)
+        up.append(swap(up_send, "rows", up_masks[1]))
+        lower = [after(low_keep, qkv_keep), low_got]
+        low_send = next_send(lower, D)
+        lower.append(swap(low_send, "rows", low_masks[1]))
         meta = after(meta, up_send, low_send)
     meta = after(meta, out_send)
     e_own, e_near, e_send, e_last = norm_grad(meta, grad_joined, e_mlp, ln1_gain, w_own, seq)
@@ -1221,45 +1192,53 @@
     e_near = swap(e_near, "blk", 1)
     if fits(rows):
         chunk = D // rows
-        qkv_keep, qkv_send = halve_packet(after(qkv_keep, e_own), qkv_got, SMALL)
-        qkv_got = swap(qkv_send, "rows", 2)
+        joined = [after(qkv_keep, e_own), qkv_got]
+        tail = add_low(joined[0][half:], qkv_got[half:])
+        qkv_send = jnp.concatenate([next_send(joined, half), tail])
+        joined.append(swap(qkv_send, "rows", 2))
         e_send = after(e_send, qkv_send)
     e_send = add_low(e_send, e_last)
     e_far = swap(e_send, "blk", 2)
     if fits(rows):
-        out_args = (after(tok_own, e_send), out_even, out_got, out_far, b_out, b_down)
+        lower[0] = after(lower[0], e_send)
+        low_send = next_send(lower, half)
+        lower.append(swap(low_send, "rows", low_masks[2]))
+        up[0] = after(up[0], low_send)
+        up_send = next_send(up, half // 2)
+        up.append(swap(up_send, "rows", up_masks[2]))
+        joined[0] = after(joined[0], up_send)
+        tail = add_low(after(qkv_send, up_send)[half // 2 :], joined[2][half // 2 :])
+        qkv_send = jnp.concatenate([next_send(joined, half // 2), tail])
+        joined.append(swap(qkv_send, "rows", 4))
+        out_args = (after(tok_own, qkv_send), out_even, out_got, out_far, b_out, b_down)
         result = finish(result_kernel, "result", seq, *out_args)
-        low_keep, low_send = halve(after(low_keep, result), low_got)
-        low_got = swap(low_send, "rows", low_masks[2])
-        up_keep, up_send = halve(after(up_keep, low_send), up_got)
-        up_got = swap(up_send, "rows", up_masks[2])
-        qkv_keep, qkv_send = halve_packet(after(qkv_keep, up_send), qkv_got, SMALL)
-        qkv_got = swap(qkv_send, "rows", 4)
-        tok_args = (after(tok_own, qkv_send), e_own, e_near, e_far, cot_own)
-        grad_tokens = finish(token_kernel, "token_grad", seq, *tok_args)
-        meta = after(meta, grad_tokens)
-        part = ((chunk, hid // 2 + width // 2), BF16)
-        pieces = simple(last_low_kernel, "last_low", [part, part], meta, low_keep, low_got)
-        meta = after(meta, pieces[0])
-        pieces = [
-            lax.ppermute(piece, ("rows", "blk"), spread_moves(rows, 4, turn))
-            for turn, piece in enumerate(pieces)
-        ]
+        meta = after(meta, result)
+        lower[0] = after(lower[0], result)
+        piece = sum(term[:width].astype(F32) for term in lower).astype(BF16)
+        meta = after(meta, piece)
+        piece = spread_rows(piece)
         packet = ((chunk + 32, width), F32)
+        last = pl.BlockSpec((SMALL, 3 * width), lambda i, m: (chunk // SMALL, 0))
         kept, near, far, small = simple(
             last_qkv_kernel,
             "last_qkv",
             [((chunk, width), F32), packet, packet, ((32, width), F32)],
             meta,
-            qkv_keep,
-            qkv_got,
+            *joined,
+            qkv_send,
+            joined[3],
+            specs=[pl.BlockSpec((chunk, 3 * width), lambda i, m: (0, 0))] * 4 + [last] * 2,
         )
         near, far, diag = swap(near, "blk", 1), swap(far, "blk", 2), swap(small, "blk", 3)
-        up = after(up_keep, small).astype(F32) + up_got.astype(F32)
-        lower = [((hid // 2, width), F32), ((width // 2, width), F32)]
+        tok_args = (after(tok_own, small), e_own, e_near, e_far, cot_own)
+        grad_tokens = finish(token_kernel, "token_grad", seq, *tok_args)
+        up[0] = after(up[0], grad_tokens)
+        up = sum(term[:chunk].astype(F32) for term in up)
+        ends = [((width, hid // 2), F32), ((width // 2, width), F32)]
         meta = after(meta, up)
-        down, out_w = simple(lower_kernel, "lower", lower, meta, *pieces)
+        down, out_w = simple(lower_kernel, "lower", ends, meta, piece)
         meta = after(meta, down)
+        down = down.T
         qkv, gb_qkv, gb_out, gb_up, gb_down, *norms = assemble(
             meta, kept, small, near, far, diag
         )
@@ -1267,7 +1246,9 @@
         up = reduce_plain(up_keep, up_got, up_masks[1:])
         weights = reduce_plain(low_keep, low_got, low_masks[1:])
         qkv = reduce_plain(qkv_keep, qkv_got, up_masks[1:])
-        down, out_w = spread_rows(weights[:, : hid + width])
+        piece = spread_rows(weights).T
+        cut = 4 * hid // rows
+        down, out_w = piece[:cut], piece[cut:]
         kept, near, far = split_columns(qkv)
         near, far = swap(near, "blk", 1), swap(far, "blk", 2)
         ends = [jnp.where(blk % 2 == 0, a, b) for a, b in ((kept, far), (far, kept))]

time: 191 us -> 190 us (level)
  waiting for transfers between devices: 10.6 us -> 21.9 us
  other arithmetic: 19 us -> 13.1 us
  local copies, waits for them, and re-layouts: 9.08 us -> 5.75 us
  Pallas kernels: 118 us -> 116 us
    ppermute x23, waiting for transfers between devices: 9.61 us -> 21.9 us  [swap(): return lax.ppermute(value, axis, [(i, i ^ mask) for i in range(size)])]
    convert_element_type x16 -> x4, other arithmetic: 12.6 us -> 1.51 us  [add_low(): return (left.astype(F32) + right.astype(F32)).astype(BF16)]
    convert_element_type x0 -> x7, other arithmetic: none -> 7.14 us  [the longest x6 5.92 us: next_send(): sum((term[size // 2:size].astype(F32) for term in terms)).astype(BF16)]
    unnamed x41 -> x52, local copies, waits for them, and re-layouts: 8.12 us -> 4.75 us
    pallas_call x3 -> x2, Pallas kernels: 7.59 us -> 5.01 us  [simple(): pl.pallas_call(body, out_shape=[jax.ShapeDtypeStruct(shape, kind) for sha...]
    ppermute x23, starting transfers between devices: 27.5 us -> 29.6 us  [swap(): return lax.ppermute(value, axis, [(i, i ^ mask) for i in range(size)])]
    concatenate x4 -> x2, other arithmetic: 2.12 us -> 0.05 us  [the longest x1 0.03 us: local(): qkv_send = jnp.concatenate([next_send(joined, half), tail])]
    pallas_call x4 -> x3, Pallas kernels: 18.6 us -> 19.8 us  [the longest x1 10.1 us: norm_grad(): pl.pallas_call(partial(norm_kernel, per), out_shape=[jax.ShapeDtypeStruct...]
  transfers between devices with their start and end apart: 25 -> 24, of which waited for: 5 -> 4; matrix products, arithmetic and copies ran while one was open for 11% -> 6% of each run, Pallas kernels for 51% -> 49%
where the time goes in v6:
time: 190 us; the launch traced here: 188 us
  Pallas kernels  116 us (61%)
  starting transfers between devices  30.2 us (16%)
  waiting for transfers between devices  21.9 us (12%)
  other arithmetic  13.1 us (7%)
  local copies, waits for them, and re-layouts  5.75 us (3%)
    pallas_call x2, Pallas kernels, feed_forward(): pl.pallas_call(body, out_shape=outs, grid_spec=pltpu.PrefetchScalarGridSp...  39.3 us
    ppermute x23, starting transfers between devices, swap(): return lax.ppermute(value, axis, [(i, i ^ mask) for i in range(size)])  29.6 us
    ppermute x23, waiting for transfers between devices, swap(): return lax.ppermute(value, axis, [(i, i ^ mask) for i in range(size)])  21.9 us
    pallas_call x1, Pallas kernels, attend_back(): pl.pallas_call(partial(attend_back_kernel, per), out_shape=jax.ShapeDtype...  21 us
    pallas_call x1, Pallas kernels, attend(): pl.pallas_call(partial(attend_kernel, per), out_shape=[jax.ShapeDtypeStru...  13 us
    pallas_call x1, Pallas kernels, norm_grad(): pl.pallas_call(partial(norm_kernel, per), out_shape=[jax.ShapeDtypeStruct...  10.1 us
    pallas_call x2, Pallas kernels, project(): pl.pallas_call(partial(qkv_kernel, slot), out_shape=outs, grid_spec=pltpu...  9.74 us
    pallas_call x1, Pallas kernels, joined_weight(): pl.pallas_call(partial(weight_kernel, rows), out_shape=[jax.ShapeDtypeStr...  8.68 us
  transfers between devices with their start and end apart: 24, of which 4 were waited for; matrix products, arithmetic and copies ran while one was open for 6% of the time, Pallas kernels for 49%

profile of v6, /device:TPU:0, one launch (start us, length us, event | category | flops | bytes accessed | tf_op | source)
XLA Modules:
  0.0 188.4 jit_solution(13630446461826115423)
XLA Ops:
  3.1 2.6 %collective-permute-start.2 = (bf16[528,768]{1,0:T(8,128)(2,1)S(1)}, bf16[528,768]{1,0:T(8,128)(2,1)S(1)}, u32[]{:S(2)}, u32[]{:S(2)}) collective-permute-start(bf16[528,768]{1,0:T(8,128)(2,1)S(1)} %fusion.1.xa.refs_3_.x_ref), channel_id=1, source_target_pairs={{0,2},{1,3},{2,0},{3,1},{4,6},{5,7},{6,4},{7,5},{8,10},{9,11},{10,... | collective-permute-start | bytes 2433032 | tf_op jit(solution)/shard_map/ppermute | solution.py:1049
  9.2 18.9 %mlp_first.1 = (bf16[1024,768]{1,0:T(8,128)(2,1)}, bf16[2048,768]{1,0:T(8,128)(2,1)}, bf16[2048,768]{1,0:T(8,128)(2,1)}, bf16[2048,192]{1,0:T(8,128)(2,1)}, f32[...) custom-call(s32[2]{0:T(128)} %pad_add_fusion.meta, ...), custom_call_target="tpu_custom_call" | custom-call | tf_op jit(solution)/shard_map/mlp_first/pallas_call | solution.py:503
  29.6 4.6 %qkv_2.1 = (bf16[2048,192]{1,0:T(8,128)(2,1)}, bf16[2048,192]{1,0:T(8,128)(2,1)}, bf16[2048,192]{1,0:T(8,128)(2,1)}) custom-call(s32[2]{0:T(128)} %pad_add_fusion.meta, s32[1]{0:T(128)S(6)} %copy.50.valid, bf16[528,768]{1,0:T(8,128)(2,1)} %copy-done.3, f32[768]{0:T(1024)} %gain.9, ...), custom_call_target="tpu_custom_call", output_to_operand_aliasing={{0}: (9, {}), {1}: (10, {}), {2}: (11, {})} | custom-call | tf_op jit(solution)/shard_map/qkv_2/pallas_call | solution.py:196
  35.1 5.2 %qkv_3.1 = (bf16[2048,192]{1,0:T(8,128)(2,1)}, bf16[2048,192]{1,0:T(8,128)(2,1)}, bf16[2048,192]{1,0:T(8,128)(2,1)}, s32[8,1,256]{2,1,0:T(1,128)}, s32[8]{0:T(128)}, /*index=5*/s32[8]{0:T(128)}) custom-call(s32[2]{0:T(128)} %pad_add_fusion.meta, s32[1]{0:T(128)S(6)} %copy.50.valid, ...), custom_call_target="tpu_custom_call", output_to_operand_aliasing={{0}: (9, {}), {1}: (10, {}), {2}: (11, {})} | custom-call | tf_op jit(solution)/shard_map/qkv_3/pallas_call | solution.py:196
  40.2 2.1 %collective-permute-done.4.ca = bf16[544,768]{1,0:T(8,128)(2,1)} collective-permute-done((bf16[544,768]{1,0:T(8,128)(2,1)}, bf16[544,768]{1,0:T(8,128)(2,1)}, u32[]{:S(2)}, u32[]{:S(2)}) %collective-permute-start.4) | collective-permute-done | bytes 835616 | tf_op jit(solution)/shard_map/ppermute | solution.py:1049
  42.4 13.0 %attend.1 = (bf16[2048,192]{1,0:T(8,128)(2,1)}, f32[3,8,1,256]{3,2,1,0:T(1,128)}) custom-call(s32[2]{0:T(128)} %pad_add_fusion.meta, s32[8]{0:T(128)} %get-tuple-element.106.lo, s32[8]{0:T(128)} %get-tuple-element.107.hi, bf16[2048,192]{1,0:T(8,128)(2,1)} %get-tuple-element.108.q_ref, bf16[2048,192]{1,0:T(8,128)(2,1)} %get-tuple-element.109.k_ref, ...), custom_call_target="tpu_custom_call" | custom-call | tf_op jit(solution)/shard_map/attend/pallas_call | solution.py:630
  56.3 20.4 %mlp_second.1 = (bf16[2048,768]{1,0:T(8,128)(2,1)}, bf16[2048,768]{1,0:T(8,128)(2,1)}, bf16[2048,192]{1,0:T(8,128)(2,1)}, f32[8,768]{1,0:T(8,128)}, bf16[2,512,7...) custom-call(s32[2]{0:T(128)} %pad_add_fusion.meta, ...), custom_call_target="tpu_custom_call", output_to_operand_aliasing={{0}: (19, {}), {1}: (20, {}), {2}: (21, {})} | custom-call | tf_op jit(solution)/shard_map/mlp_second/pallas_call | solution.py:503
  77.2 2.6 %collective-permute-start.6 = (bf16[384,768]{1,0:T(8,128)(2,1)}, bf16[384,768]{1,0:T(8,128)(2,1)}, u32[]{:S(2)}, u32[]{:S(2)}) collective-permute-start(bf16[384,768]{1,0:T(8,128)(2,1)} %get-tuple-element.132), channel_id=1, source_target_pairs={{0,4},{4,0},{8,12},{12,8},{16,20},{20,16},{24,28},{28,24},{1,5},{5... | collective-permute-start | bytes 1769480 | tf_op jit(solution)/shard_map/ppermute | solution.py:1049
  80.2 21.0 %attend_back.1.refs_0_.gj_ref = bf16[2048,576]{1,0:T(8,128)(2,1)} custom-call(s32[2]{0:T(128)} %pad_add_fusion.meta, s32[8]{0:T(128)} %get-tuple-element.106.lo, s32[8]{0:T(128)} %get-tuple-element.107.hi, bf16[2048,192]{1,0:T(8,128)(2,1)} %get-tuple-element.108.q_ref, bf16[2048,192]{1,0:T(8,128)(2,1)} %get-tuple-element.109.k_ref, ...), custom_call_target="tpu_custom_call" | custom-call | tf_op jit(solution)/shard_map/attend_back/pallas_call | solution.py:761
  101.3 8.7 %joined_weight.1 = (bf16[400,576]{1,0:T(8,128)(2,1)}, bf16[400,576]{1,0:T(8,128)(2,1)}, f32[16,576]{1,0:T(8,128)}) custom-call(s32[2]{0:T(128)} %pad_add_fusion.meta, bf16[2048,576]{1,0:T(8,128)(2,1)} %attend_back.1.refs_0_.gj_ref, bf16[2048,768]{1,0:T(8,128)(2,1)} %get-tuple-element.127.refs_1_, f32[768]{0:T(1024)} %gain.9, f32[768]{0:T(1024)} %refs_3_.1, ...), custom_call_target="tpu_custom_call" | custom-call | tf_op jit(solution)/shard_map/joined_weight/pallas_call | solution.py:858
  109.9 3.0 %collective-permute-start.9 = (bf16[400,576]{1,0:T(8,128)(2,1)}, bf16[400,576]{1,0:T(8,128)(2,1)S(1)}, u32[]{:S(2)}, u32[]{:S(2)}) collective-permute-start(bf16[400,576]{1,0:T(8,128)(2,1)} %get-tuple-element.145), channel_id=1, source_target_pairs={{0,4},{4,0},{8,12},{12,8},{16,20},{20,16},{24,28},{28,24},{1,5},{5... | collective-permute-start | bytes 1382408 | tf_op jit(solution)/shard_map/ppermute | solution.py:1049
  112.9 1.8 add_convert_fusion.3
  115.8 1.3 fusion.2
  117.1 10.1 %norm_grad.1 = (bf16[512,768]{1,0:T(8,128)(2,1)}, bf16[512,768]{1,0:T(8,128)(2,1)}, bf16[512,768]{1,0:T(8,128)(2,1)}, bf16[512,768]{1,0:T(8,128)(2,1)}) custom-call(s32[2]{0:T(128)} %pad_add_fusion.meta, bf16[2048,576]{1,0:T(8,128)(2,1)} %attend_back.1.refs_0_.gj_ref, bf16[2048,768]{1,0:T(8,128)(2,1)} %get-tuple-element.141.e_in, f32[768]{0:T(1024)} %gain.9, ...), custom_call_target="tpu_custom_call" | custom-call | tf_op jit(solution)/shard_map/norm_grad/pallas_call | solution.py:891
  127.3 4.3 %collective-permute-start.11 = (bf16[384,512]{1,0:T(8,128)(2,1)S(1)}, bf16[384,512]{1,0:T(8,128)(2,1)S(1)}, u32[]{:S(2)}, u32[]{:S(2)}) collective-permute-start(bf16[384,512]{1,0:T(8,128)(2,1)S(1)} %add_convert_fusion.2), channel_id=1, source_target_pairs={{0,16},{4,20},{8,24},{12,28},{16,0},{20,4},{24,8},{28,12},{1,17},{... | collective-permute-start | bytes 1179656 | tf_op jit(solution)/shard_map/ppermute | solution.py:1049
  131.6 1.5 collective-permute-start.14
  133.3 1.8 collective-permute-start.13
  135.3 14.4 %collective-permute-done.11 = bf16[384,512]{1,0:T(8,128)(2,1)S(1)} collective-permute-done((bf16[384,512]{1,0:T(8,128)(2,1)S(1)}, bf16[384,512]{1,0:T(8,128)(2,1)S(1)}, u32[]{:S(2)}, u32[]{:S(2)}) %collective-permute-start.11) | collective-permute-done | bytes 393248 | tf_op jit(solution)/shard_map/ppermute | solution.py:1049
  150.8 1.8 add_convert_fusion.7
  152.6 1.4 collective-permute-start.15
  154.0 1.5 collective-permute-start.18
  155.8 2.9 %collective-permute-start.19 = (bf16[96,768]{1,0:T(8,128)(2,1)}, bf16[96,768]{1,0:T(8,128)(2,1)}, u32[]{:S(2)}, u32[]{:S(2)}) collective-permute-start(bf16[96,768]{1,0:T(8,128)(2,1)} %add_convert_fusion.7), channel_id=1, source_target_pairs={{0,16},{4,20},{8,24},{12,28},{16,0},{20,4},{24,8},{28,12},{1,17},{... | collective-permute-start | bytes 442376 | tf_op jit(solution)/shard_map/ppermute | solution.py:1049
  158.7 2.8 %result.1 = bf16[512,768]{1,0:T(8,128)(2,1)} custom-call(bf16[528,768]{1,0:T(8,128)(2,1)} %copy-done, bf16[2,512,768]{2,1,0:T(8,128)(2,1)} %get-tuple-element.138.even, bf16[2,512,768]{2,1,0:T(8,128)(2,1)} %copy-done.5, bf16[512,768]{1,0:T(8,128)(2,1)} %collective-permute-done.14.far, f32[768]{0:T(1024)} %b_out.1, f32[768]{0:T(1024)} %b_down.1), custom_call_target="tpu_custom_call" | custom-call | tf_op jit(solution)/shard_map/result/pallas_call | solution.py:1097
  161.6 1.2 add_convert_fusion.5
  162.8 4.8 %collective-permute-done.16.refs_3_.refs_5_ = bf16[112,576]{1,0:T(8,128)(2,1)S(1)} collective-permute-done((bf16[112,576]{1,0:T(8,128)(2,1)S(1)}, bf16[112,576]{1,0:T(8,128)(2,1)S(1)}, u32[]{:S(2)}, u32[]{:S(2)}) %collective-permute-start.16) | collective-permute-done | bytes 129056 | tf_op jit(solution)/shard_map/ppermute | solution.py:1049
  168.2 2.6 %last_qkv.1 = (f32[96,192]{1,0:T(8,128)}, f32[128,192]{1,0:T(8,128)}, f32[128,192]{1,0:T(8,128)}, f32[32,192]{1,0:T(8,128)}) custom-call(s32[2]{0:T(128)} %pad_add_fusion.meta, bf16[400,576]{1,0:T(8,128)(2,1)} %get-tuple-element.150.refs_0_, bf16[400,576]{1,0:T(8,128)(2,1)} %copy-done.8, bf16[208,576]{1,0:T(8,128)(2,1)} %copy-done.14, ...), custom_call_target="tpu_custom_call" | custom-call | tf_op jit(solution)/shard_map/last_qkv/pallas_call | solution.py:912
  171.6 2.0 %collective-permute-start.21 = (f32[128,192]{1,0:T(8,128)}, f32[128,192]{1,0:T(8,128)S(1)}, u32[]{:S(2)}, u32[]{:S(2)}) collective-permute-start(f32[128,192]{1,0:T(8,128)} %get-tuple-element.164), channel_id=1, source_target_pairs={{0,1},{1,0},{2,3},{3,2},{4,5},{5,4},{6,7},{7,6},{8,9},{9,8},{10,11... | collective-permute-start | bytes 294920 | tf_op jit(solution)/shard_map/ppermute | solution.py:1049
  173.5 3.1 %collective-permute-start.22 = (f32[128,192]{1,0:T(8,128)}, f32[128,192]{1,0:T(8,128)S(1)}, u32[]{:S(2)}, u32[]{:S(2)}) collective-permute-start(f32[128,192]{1,0:T(8,128)} %get-tuple-element.165), channel_id=1, source_target_pairs={{0,2},{1,3},{2,0},{3,1},{4,6},{5,7},{6,4},{7,5},{8,10},{9,11},{10,... | collective-permute-start | bytes 294920 | tf_op jit(solution)/shard_map/ppermute | solution.py:1049
  176.7 3.5 %token_grad.1 = bf16[512,768]{1,0:T(8,128)(2,1)} custom-call(bf16[528,768]{1,0:T(8,128)(2,1)} %copy-done, bf16[512,768]{1,0:T(8,128)(2,1)} %get-tuple-element.142.even, bf16[512,768]{1,0:T(8,128)(2,1)} %copy-done.10, bf16[512,768]{1,0:T(8,128)(2,1)} %copy-done.11, bf16[512,768]{1,0:T(8,128)(2,1)} %bitcast.12), custom_call_target="tpu_custom_call" | custom-call | tf_op jit(solution)/shard_map/token_grad/pallas_call | solution.py:1097
  180.1 1.8 convert_add_fusion
  182.6 2.4 %lower.1 = (f32[192,384]{1,0:T(8,128)}, f32[96,192]{1,0:T(8,128)}) custom-call(s32[2]{0:T(128)} %pad_add_fusion.meta, bf16[192,512]{1,0:T(8,128)(2,1)} %copy-done.22), custom_call_target="tpu_custom_call" | custom-call | tf_op jit(solution)/shard_map/lower/pallas_call | solution.py:912
  185.7 2.7 %assemble.1 = (f32[96,576]{1,0:T(8,128)}, f32[2304]{0:T(1024)}, f32[768]{0:T(1024)}, f32[3072]{0:T(1024)}, f32[768]{0:T(1024)}, /*index=5*/f32[768]{0:T(1024)}, f32[768]{0:T(1024)}, f32[768]{0:T(1024)}, f32[768]{0:T(1024)}) custom-call(s32[2]{0:T(128)} %pad_add_fusion.meta, f32[96,192]{1,0:T(8,128)} %get-tuple-element.163.kept, ...), custom_call_target="tpu_custom_call" | custom-call | tf_op jit(solution)/shard_map/assemble/pallas_call | solution.py:1015
  (99 shorter events, 15.2 us)
Async XLA Ops:
  2.6 5.7 %collective-permute-start = (bf16[528,768]{1,0:T(8,128)(2,1)S(1)}, bf16[528,768]{1,0:T(8,128)(2,1)S(1)}, u32[]{:S(2)}, u32[]{:S(2)}) collective-permute-start(bf16[528,768]{1,0:T(8,128)(2,1)S(1)} %fusion.1.xa.refs_3_.x_ref), channel_id=1, source_target_pairs={{0,1},{1,0},{2,3},{3,2},{4,5},{5,4},{6,7},{7,6},{8,9},{9,8},{10,11... | collective-permute-start | bytes 2433032 | tf_op jit(solution)/shard_map/ppermute | solution.py:1049
  3.1 25.0 %collective-permute-start.2 = (bf16[528,768]{1,0:T(8,128)(2,1)S(1)}, bf16[528,768]{1,0:T(8,128)(2,1)S(1)}, u32[]{:S(2)}, u32[]{:S(2)}) collective-permute-start(bf16[528,768]{1,0:T(8,128)(2,1)S(1)} %fusion.1.xa.refs_3_.x_ref), channel_id=1, source_target_pairs={{0,2},{1,3},{2,0},{3,1},{4,6},{5,7},{6,4},{7,5},{8,10},{9,11},{10,... | collective-permute-start | bytes 2433032 | tf_op jit(solution)/shard_map/ppermute | solution.py:1049
  5.7 2.6 %collective-permute-start.1 = (bf16[512,768]{1,0:T(8,128)(2,1)}, bf16[512,768]{1,0:T(8,128)(2,1)}, u32[]{:S(2)}, u32[]{:S(2)}) collective-permute-start(bf16[512,768]{1,0:T(8,128)(2,1)} %bitcast.9), channel_id=1, source_target_pairs={{0,1},{1,0},{2,3},{3,2},{4,5},{5,4},{6,7},{7,6},{8,9},{9,8},{10,11... | collective-permute-start | bytes 2359304 | tf_op jit(solution)/shard_map/ppermute | solution.py:1049
  6.9 35.5 %collective-permute-start.4 = (bf16[544,768]{1,0:T(8,128)(2,1)}, bf16[544,768]{1,0:T(8,128)(2,1)}, u32[]{:S(2)}, u32[]{:S(2)}) collective-permute-start(bf16[544,768]{1,0:T(8,128)(2,1)} %pad.9), channel_id=1, source_target_pairs={{0,2},{1,3},{2,0},{3,1},{4,6},{5,7},{6,4},{7,5},{8,10},{9,11},{10,... | collective-permute-start | bytes 2506760 | tf_op jit(solution)/shard_map/ppermute | solution.py:1049
  28.2 6.0 %collective-permute-start.3 = (bf16[528,768]{1,0:T(8,128)(2,1)S(1)}, bf16[528,768]{1,0:T(8,128)(2,1)S(1)}, u32[]{:S(2)}, u32[]{:S(2)}) collective-permute-start(bf16[528,768]{1,0:T(8,128)(2,1)S(1)} %collective-permute-done.2.x_ref.refs_5_.xa), channel_id=1, source_target_pairs={{0,1},{1,0},{2,3},{3,2},{4,5},{5,4},{6,7},{7,6},{8,9},{9,8},{10,11... | collective-permute-start | bytes 2433032 | tf_op jit(solution)/shard_map/ppermute | solution.py:1049
  42.4 13.0 %collective-permute-start.5 = (bf16[544,768]{1,0:T(8,128)(2,1)}, bf16[544,768]{1,0:T(8,128)(2,1)S(1)}, u32[]{:S(2)}, u32[]{:S(2)}) collective-permute-start(bf16[544,768]{1,0:T(8,128)(2,1)} %collective-permute-done.4.ca), channel_id=1, source_target_pairs={{0,1},{1,0},{2,3},{3,2},{4,5},{5,4},{6,7},{7,6},{8,9},{9,8},{10,11... | collective-permute-start | bytes 2506760 | tf_op jit(solution)/shard_map/ppermute | solution.py:1049
  76.6 39.1 %collective-permute-start.8 = (bf16[2,512,768]{2,1,0:T(8,128)(2,1)}, bf16[2,512,768]{2,1,0:T(8,128)(2,1)S(1)}, u32[]{:S(2)}, u32[]{:S(2)}) collective-permute-start(bf16[2,512,768]{2,1,0:T(8,128)(2,1)} %get-tuple-element.139), channel_id=1, source_target_pairs={{0,1},{1,0},{2,3},{3,2},{4,5},{5,4},{6,7},{7,6},{8,9},{9,8},{10,11... | collective-permute-start | bytes 4718600 | tf_op jit(solution)/shard_map/ppermute | solution.py:1049
  77.2 35.7 %collective-permute-start.6 = (bf16[384,768]{1,0:T(8,128)(2,1)}, bf16[384,768]{1,0:T(8,128)(2,1)}, u32[]{:S(2)}, u32[]{:S(2)}) collective-permute-start(bf16[384,768]{1,0:T(8,128)(2,1)} %get-tuple-element.132), channel_id=1, source_target_pairs={{0,4},{4,0},{8,12},{12,8},{16,20},{20,16},{24,28},{28,24},{1,5},{5... | collective-permute-start | bytes 1769480 | tf_op jit(solution)/shard_map/ppermute | solution.py:1049
  79.8 34.9 %collective-permute-start.7 = (bf16[768,512]{1,0:T(8,128)(2,1)}, bf16[768,512]{1,0:T(8,128)(2,1)}, u32[]{:S(2)}, u32[]{:S(2)}) collective-permute-start(bf16[768,512]{1,0:T(8,128)(2,1)} %get-tuple-element.135), channel_id=1, source_target_pairs={{0,8},{4,12},{8,0},{12,4},{16,24},{20,28},{24,16},{28,20},{1,9},{5... | collective-permute-start | bytes 2359304 | tf_op jit(solution)/shard_map/ppermute | solution.py:1049
  101.2 11.7 %copy-start.15 = (bf16[384,768]{1,0:T(8,128)(2,1)S(1)}, bf16[384,768]{1,0:T(8,128)(2,1)}, u32[]{:S(2)}) copy-start(bf16[384,768]{1,0:T(8,128)(2,1)} %get-tuple-element.159) | copy-start | bytes 1769476
  101.2 13.4 %copy-start.13 = (bf16[768,512]{1,0:T(8,128)(2,1)S(1)}, bf16[768,512]{1,0:T(8,128)(2,1)}, u32[]{:S(2)}) copy-start(bf16[768,512]{1,0:T(8,128)(2,1)} %get-tuple-element.154) | copy-start | bytes 2359300
  109.9 23.2 %collective-permute-start.9 = (bf16[400,576]{1,0:T(8,128)(2,1)}, bf16[400,576]{1,0:T(8,128)(2,1)S(1)}, u32[]{:S(2)}, u32[]{:S(2)}) collective-permute-start(bf16[400,576]{1,0:T(8,128)(2,1)} %get-tuple-element.145), channel_id=1, source_target_pairs={{0,4},{4,0},{8,12},{12,8},{16,20},{20,16},{24,28},{28,24},{1,5},{5... | collective-permute-start | bytes 1382408 | tf_op jit(solution)/shard_map/ppermute | solution.py:1049
  115.8 11.4 %copy-start.5 = (bf16[2,512,768]{2,1,0:T(8,128)(2,1)}, bf16[2,512,768]{2,1,0:T(8,128)(2,1)S(1)}, u32[]{:S(2)}) copy-start(bf16[2,512,768]{2,1,0:T(8,128)(2,1)S(1)} %collective-permute-done.8.near) | copy-start | bytes 4718596
  117.1 16.1 %copy-start.7 = (bf16[400,576]{1,0:T(8,128)(2,1)S(1)}, bf16[400,576]{1,0:T(8,128)(2,1)}, u32[]{:S(2)}) copy-start(bf16[400,576]{1,0:T(8,128)(2,1)} %get-tuple-element.150.refs_0_) | copy-start | bytes 1382404
  127.2 7.9 %copy-start.12 = (bf16[512,768]{1,0:T(8,128)(2,1)S(1)}, bf16[512,768]{1,0:T(8,128)(2,1)}, u32[]{:S(2)}) copy-start(bf16[512,768]{1,0:T(8,128)(2,1)} %get-tuple-element.146) | copy-start | bytes 2359300
  127.2 7.9 %collective-permute-start.10 = (bf16[512,768]{1,0:T(8,128)(2,1)}, bf16[512,768]{1,0:T(8,128)(2,1)S(1)}, u32[]{:S(2)}, u32[]{:S(2)}) collective-permute-start(bf16[512,768]{1,0:T(8,128)(2,1)} %get-tuple-element.147), channel_id=1, source_target_pairs={{0,1},{1,0},{2,3},{3,2},{4,5},{5,4},{6,7},{7,6},{8,9},{9,8},{10,11... | collective-permute-start | bytes 2359304 | tf_op jit(solution)/shard_map/ppermute | solution.py:1049
  127.3 23.6 %collective-permute-start.12 = (bf16[192,768]{1,0:T(8,128)(2,1)}, bf16[192,768]{1,0:T(8,128)(2,1)S(1)}, u32[]{:S(2)}, u32[]{:S(2)}) collective-permute-start(bf16[192,768]{1,0:T(8,128)(2,1)} %add_convert_fusion.3), channel_id=1, source_target_pairs={{0,8},{4,12},{8,0},{12,4},{16,24},{20,28},{24,16},{28,20},{1,9},{5... | collective-permute-start | bytes 884744 | tf_op jit(solution)/shard_map/ppermute | solution.py:1049
  127.3 22.3 %collective-permute-start.11 = (bf16[384,512]{1,0:T(8,128)(2,1)S(1)}, bf16[384,512]{1,0:T(8,128)(2,1)S(1)}, u32[]{:S(2)}, u32[]{:S(2)}) collective-permute-start(bf16[384,512]{1,0:T(8,128)(2,1)S(1)} %add_convert_fusion.2), channel_id=1, source_target_pairs={{0,16},{4,20},{8,24},{12,28},{16,0},{20,4},{24,8},{28,12},{1,17},{... | collective-permute-start | bytes 1179656 | tf_op jit(solution)/shard_map/ppermute | solution.py:1049
  131.6 24.1 %collective-permute-start.14 = (bf16[512,768]{1,0:T(8,128)(2,1)}, bf16[512,768]{1,0:T(8,128)(2,1)}, u32[]{:S(2)}, u32[]{:S(2)}) collective-permute-start(bf16[512,768]{1,0:T(8,128)(2,1)} %fusion.2), channel_id=1, source_target_pairs={{0,2},{1,3},{2,0},{3,1},{4,6},{5,7},{6,4},{7,5},{8,10},{9,11},{10,... | collective-permute-start | bytes 2359304 | tf_op jit(solution)/shard_map/ppermute | solution.py:1049
  133.1 22.4 %copy-start.8 = (bf16[400,576]{1,0:T(8,128)(2,1)}, bf16[400,576]{1,0:T(8,128)(2,1)S(1)}, u32[]{:S(2)}) copy-start(bf16[400,576]{1,0:T(8,128)(2,1)S(1)} %collective-permute-done.9.refs_1_) | copy-start | bytes 1382404
  133.3 22.3 %collective-permute-start.13 = (bf16[208,576]{1,0:T(8,128)(2,1)S(1)}, bf16[208,576]{1,0:T(8,128)(2,1)S(1)}, u32[]{:S(2)}, u32[]{:S(2)}) collective-permute-start(bf16[208,576]{1,0:T(8,128)(2,1)S(1)} %pad_maximum_fusion), channel_id=1, source_target_pairs={{0,8},{4,12},{8,0},{12,4},{16,24},{20,28},{24,16},{28,20},{1,9},{5... | collective-permute-start | bytes 718856 | tf_op jit(solution)/shard_map/ppermute | solution.py:1049
  135.1 36.5 %collective-permute-start.17 = (bf16[512,768]{1,0:T(8,128)(2,1)}, bf16[512,768]{1,0:T(8,128)(2,1)S(1)}, u32[]{:S(2)}, u32[]{:S(2)}) collective-permute-start(bf16[512,768]{1,0:T(8,128)(2,1)} %get-tuple-element.158), channel_id=1, source_target_pairs={{0,1},{1,0},{2,3},{3,2},{4,5},{5,4},{6,7},{7,6},{8,9},{9,8},{10,11... | collective-permute-start | bytes 2359304 | tf_op jit(solution)/shard_map/ppermute | solution.py:1049
  152.6 8.9 %collective-permute-start.15 = (bf16[192,512]{1,0:T(8,128)(2,1)S(1)}, bf16[192,512]{1,0:T(8,128)(2,1)}, u32[]{:S(2)}, u32[]{:S(2)}) collective-permute-start(bf16[192,512]{1,0:T(8,128)(2,1)S(1)} %add_convert_fusion.6), channel_id=1, source_target_pairs={{0,4},{4,0},{8,12},{12,8},{16,20},{20,16},{24,28},{28,24},{1,5},{5... | collective-permute-start | bytes 589832 | tf_op jit(solution)/shard_map/ppermute | solution.py:1049
  154.0 19.5 %collective-permute-start.18 = (bf16[512,768]{1,0:T(8,128)(2,1)S(1)}, bf16[512,768]{1,0:T(8,128)(2,1)S(1)}, u32[]{:S(2)}, u32[]{:S(2)}) collective-permute-start(bf16[512,768]{1,0:T(8,128)(2,1)S(1)} %add_convert_fusion), channel_id=1, source_target_pairs={{0,2},{1,3},{2,0},{3,1},{4,6},{5,7},{6,4},{7,5},{8,10},{9,11},{10,... | collective-permute-start | bytes 2359304 | tf_op jit(solution)/shard_map/ppermute | solution.py:1049
  155.5 6.0 %copy-start.14 = (bf16[208,576]{1,0:T(8,128)(2,1)}, bf16[208,576]{1,0:T(8,128)(2,1)S(1)}, u32[]{:S(2)}) copy-start(bf16[208,576]{1,0:T(8,128)(2,1)S(1)} %collective-permute-done.13.refs_2_) | copy-start | bytes 718852
  155.6 11.9 %collective-permute-start.16 = (bf16[112,576]{1,0:T(8,128)(2,1)S(1)}, bf16[112,576]{1,0:T(8,128)(2,1)S(1)}, u32[]{:S(2)}, u32[]{:S(2)}) collective-permute-start(bf16[112,576]{1,0:T(8,128)(2,1)S(1)} %pad_maximum_fusion.1.refs_4_), channel_id=1, source_target_pairs={{0,16},{4,20},{8,24},{12,28},{16,0},{20,4},{24,8},{28,12},{1,17},{... | collective-permute-start | bytes 387080 | tf_op jit(solution)/shard_map/ppermute | solution.py:1049
  155.8 24.4 %collective-permute-start.19 = (bf16[96,768]{1,0:T(8,128)(2,1)}, bf16[96,768]{1,0:T(8,128)(2,1)}, u32[]{:S(2)}, u32[]{:S(2)}) collective-permute-start(bf16[96,768]{1,0:T(8,128)(2,1)} %add_convert_fusion.7), channel_id=1, source_target_pairs={{0,16},{4,20},{8,24},{12,28},{16,0},{20,4},{24,8},{28,12},{1,17},{... | collective-permute-start | bytes 442376 | tf_op jit(solution)/shard_map/ppermute | solution.py:1049
  170.9 14.1 %collective-permute-start.23 = (f32[32,192]{1,0:T(8,128)}, f32[32,192]{1,0:T(8,128)S(1)}, u32[]{:S(2)}, u32[]{:S(2)}) collective-permute-start(f32[32,192]{1,0:T(8,128)} %get-tuple-element.156.small), channel_id=1, source_target_pairs={{0,3},{1,2},{2,1},{3,0},{4,7},{5,6},{6,5},{7,4},{8,11},{9,10},{10,... | collective-permute-start | bytes 73736 | tf_op jit(solution)/shard_map/ppermute | solution.py:1049
  170.9 11.1 %collective-permute-start.20 = (bf16[192,512]{1,0:T(8,128)(2,1)S(1)}, bf16[192,512]{1,0:T(8,128)(2,1)S(1)}, u32[]{:S(2)}, u32[]{:S(2)}) collective-permute-start(bf16[192,512]{1,0:T(8,128)(2,1)S(1)} %add_convert_fusion.5), channel_id=1, source_target_pairs={{0,0},{1,8},{2,16},{3,24},{4,1},{5,9},{6,17},{7,25},{8,2},{9,10},{... | collective-permute-start | bytes 589832 | tf_op jit(solution)/shard_map/ppermute | solution.py:1061
  171.6 13.4 %collective-permute-start.21 = (f32[128,192]{1,0:T(8,128)}, f32[128,192]{1,0:T(8,128)S(1)}, u32[]{:S(2)}, u32[]{:S(2)}) collective-permute-start(f32[128,192]{1,0:T(8,128)} %get-tuple-element.164), channel_id=1, source_target_pairs={{0,1},{1,0},{2,3},{3,2},{4,5},{5,4},{6,7},{7,6},{8,9},{9,8},{10,11... | collective-permute-start | bytes 294920 | tf_op jit(solution)/shard_map/ppermute | solution.py:1049
  173.5 6.6 %copy-start.21 = (bf16[192,768]{1,0:T(8,128)(2,1)S(1)}, bf16[192,768]{1,0:T(8,128)(2,1)}, u32[]{:S(2)}) copy-start(bf16[192,768]{1,0:T(8,128)(2,1)} %copy-done.20) | copy-start | bytes 884740
  173.5 11.5 %collective-permute-start.22 = (f32[128,192]{1,0:T(8,128)}, f32[128,192]{1,0:T(8,128)S(1)}, u32[]{:S(2)}, u32[]{:S(2)}) collective-permute-start(f32[128,192]{1,0:T(8,128)} %get-tuple-element.165), channel_id=1, source_target_pairs={{0,2},{1,3},{2,0},{3,1},{4,6},{5,7},{6,4},{7,5},{8,10},{9,11},{10,... | collective-permute-start | bytes 294920 | tf_op jit(solution)/shard_map/ppermute | solution.py:1049
  (18 other events, 55.0 us)

commit v7 on v6

--- a/solution.py
+++ b/solution.py
@@ -82,7 +82,7 @@
 
 def params(*semantics, vmem=None):
     return pltpu.CompilerParams(
-        dimension_semantics=semantics or ("arbitrary",), vmem_limit_bytes=vmem or 60 * 2**20
+        dimension_semantics=semantics or ("arbitrary",), vmem_limit_bytes=vmem or 67_043_328
     )
 
 
@@ -208,7 +208,7 @@
 
 def mask_order(rows, first):
     masks = [1 << bit for bit in range(rows.bit_length() - 1)]
-    return [m for m in masks if m >= first] + [m for m in masks if m < first]
+    return masks if first == 1 else masks[1::-1] + masks[2:]
 
 
 def places(masks):
@@ -872,40 +872,38 @@
     )(meta, grad, normed, *args)
 
 
-def norm_kernel(per, meta, gj_ref, e_in, gain, w_ref, *outs):
-    grad_norm = dot_nt(gj_ref[...], w_ref[...])
-    value = (grad_norm * row(gain) + e_in[...].astype(F32)).astype(BF16)
-    for slot, out in enumerate(outs):
-
-        @pl.when(pl.program_id(0) // per == slot)
-        def _(out=out):
-            out[...] = value
+def norm_kernel(meta, *refs):
+    gjs, es, (gain, w_ref), outs = refs[0:4], refs[4:8], refs[8:10], refs[10:]
+    for gj_ref, e_in, out in zip(gjs, es, outs):
+        grad_norm = dot_nt(gj_ref[...], w_ref[...])
+        out[...] = (grad_norm * row(gain) + e_in[...].astype(F32)).astype(BF16)
 
 
 def norm_grad(meta, grad, e_mlp, gain, w, seq):
-    per = seq // TILE
-
-    def slot_out(slot):
-        return pl.BlockSpec((TILE, D), lambda i, m: (jnp.clip(i - slot * per, 0, per - 1), 0))
+    tile = TILE // 2
+    per = seq // tile
+
+    def slot_tiles(slot, cols):
+        return pl.BlockSpec((tile, cols), lambda i, m: (slot * per + i, 0))
 
     return pl.pallas_call(
-        partial(norm_kernel, per),
+        norm_kernel,
         out_shape=[jax.ShapeDtypeStruct((seq, D), BF16)] * 4,
         grid_spec=pltpu.PrefetchScalarGridSpec(
             num_scalar_prefetch=1,
-            grid=(4 * per,),
+            grid=(per,),
             in_specs=[
-                row_tiles(grad.shape[1]),
-                row_tiles(D),
+                *(slot_tiles(slot, grad.shape[1]) for slot in range(4)),
+                *(slot_tiles(slot, D) for slot in range(4)),
                 whole(gain.shape),
                 whole(w.shape),
             ],
-            out_specs=[slot_out(slot) for slot in range(4)],
+            out_specs=[slot_tiles(0, D)] * 4,
         ),
         compiler_params=params(),
         cost_estimate=COST,
         name="norm_grad",
-    )(meta, grad, e_mlp, gain, w)
+    )(meta, *[grad] * 4, *[e_mlp] * 4, gain, w)
 
 
 def simple(body, name, shapes, *args, specs=None):
@@ -1174,12 +1172,11 @@
     qkv_keep, qkv_send = chunks_of(qkv_keep, qkv_send, rows, 1)
     qkv_got = swap(qkv_send, "rows", 1)
 
-    meta = after(meta, qkv_keep)
     out_send = add_low(after(out_even, qkv_keep)[1], out_got[1])
     out_far = swap(out_send, "blk", 2)
     half = D // 2
     if fits(rows):
-        up = [after(up_keep, qkv_keep), up_got]
+        up = [up_keep, up_got]
         up_send = next_send(up, half)
         up.append(swap(up_send, "rows", up_masks[1]))
         lower = [after(low_keep, qkv_keep), low_got]
@@ -1213,7 +1210,6 @@
         out_args = (after(tok_own, qkv_send), out_even, out_got, out_far, b_out, b_down)
         result = finish(result_kernel, "result", seq, *out_args)
         meta = after(meta, result)
-        lower[0] = after(lower[0], result)
         piece = sum(term[:width].astype(F32) for term in lower).astype(BF16)
         meta = after(meta, piece)
         piece = spread_rows(piece)
@@ -1237,7 +1233,6 @@
         ends = [((width, hid // 2), F32), ((width // 2, width), F32)]
         meta = after(meta, up)
         down, out_w = simple(lower_kernel, "lower", ends, meta, piece)
-        meta = after(meta, down)
         down = down.T
         qkv, gb_qkv, gb_out, gb_up, gb_down, *norms = assemble(
             meta, kept, small, near, far, diag

time: 190 us -> 186 us (0.979)
  other arithmetic: 13.1 us -> 21.9 us
  starting transfers between devices: 30.2 us -> 23.7 us
  local copies, waits for them, and re-layouts: 5.75 us -> 1 us
  waiting for transfers between devices: 21.9 us -> 18 us
  Pallas kernels: 116 us -> 119 us
    ppermute x23, starting transfers between devices: 29.6 us -> 20.7 us  [swap(): return lax.ppermute(value, axis, [(i, i ^ mask) for i in range(size)])]
    unnamed x52 -> x12, local copies, waits for them, and re-layouts: 4.75 us -> 0.03 us
    ppermute x23, waiting for transfers between devices: 21.9 us -> 18 us  [swap(): return lax.ppermute(value, axis, [(i, i ^ mask) for i in range(size)])]
    convert_element_type x6, other arithmetic: 5.92 us -> 9.75 us  [next_send(): sum((term[size // 2:size].astype(F32) for term in terms)).astype(BF16)]
    pallas_call x1, Pallas kernels: 21 us -> 23.7 us  [attend_back(): pl.pallas_call(partial(attend_back_kernel, per), out_shape=jax.ShapeDtype...]
    convert_element_type x4, other arithmetic: 1.51 us -> 4.05 us  [add_low(): return (left.astype(F32) + right.astype(F32)).astype(BF16)]
    ppermute x1, starting transfers between devices: 0.66 us -> 2.99 us  [spread_rows(): return lax.ppermute(chunk, ('rows', 'blk'), moves)]
  transfers between devices with their start and end apart: 24 -> 24, of which waited for: 4 -> 5; matrix products, arithmetic and copies ran while one was open for 6% -> 11% of each run, Pallas kernels for 49% -> 52%
where the time goes in v7:
time: 186 us; the launch traced here: 184 us
  Pallas kernels  119 us (64%)
  starting transfers between devices  23.7 us (13%)
  other arithmetic  21.9 us (12%)
  waiting for transfers between devices  18 us (10%)
    pallas_call x2, Pallas kernels, feed_forward(): pl.pallas_call(body, out_shape=outs, grid_spec=pltpu.PrefetchScalarGridSp...  39.4 us
    pallas_call x1, Pallas kernels, attend_back(): pl.pallas_call(partial(attend_back_kernel, per), out_shape=jax.ShapeDtype...  23.7 us
    ppermute x23, starting transfers between devices, swap(): return lax.ppermute(value, axis, [(i, i ^ mask) for i in range(size)])  20.7 us
    ppermute x23, waiting for transfers between devices, swap(): return lax.ppermute(value, axis, [(i, i ^ mask) for i in range(size)])  18 us
    pallas_call x1, Pallas kernels, attend(): pl.pallas_call(partial(attend_kernel, per), out_shape=[jax.ShapeDtypeStru...  14.1 us
    pallas_call x2, Pallas kernels, project(): pl.pallas_call(partial(qkv_kernel, slot), out_shape=outs, grid_spec=pltpu...  9.77 us
    convert_element_type x6, other arithmetic, next_send(): sum((term[size // 2:size].astype(F32) for term in terms)).astype(BF16)  9.75 us
    pallas_call x1, Pallas kernels, norm_grad(): pl.pallas_call(norm_kernel, out_shape=[jax.ShapeDtypeStruct((seq, D), BF1...  9.02 us
  transfers between devices with their start and end apart: 24, of which 5 were waited for; matrix products, arithmetic and copies ran while one was open for 11% of the time, Pallas kernels for 52%

profile of v7, /device:TPU:0, one launch (start us, length us, event | category | flops | bytes accessed | tf_op | source)
XLA Modules:
  0.0 184.5 jit_solution(14534803938039386573)
XLA Ops:
  1.4 2.1 %fusion.1.xa.refs_3_.x_ref = bf16[528,768]{1,0:T(8,128)(2,1)} fusion(bf16[1,512]{1,0:T(2,128)(2,1)S(1)} %convert_element_type.138, bf16[512,768]{1,0:T(8,128)(2,1)} %bitcast.15), kind=kLoop, calls=%fused_computation.4 | loop fusion | flops 2433024 | bytes 1598464 | tf_op jit(solution)/shard_map/concatenate | solution.py:1122
  3.9 2.5 %collective-permute-start.2 = (bf16[528,768]{1,0:T(8,128)(2,1)}, bf16[528,768]{1,0:T(8,128)(2,1)}, u32[]{:S(2)}, u32[]{:S(2)}) collective-permute-start(bf16[528,768]{1,0:T(8,128)(2,1)} %fusion.1.xa.refs_3_.x_ref), channel_id=1, source_target_pairs={{0,2},{1,3},{2,0},{3,1},{4,6},{5,7},{6,4},{7,5},{8,10},{9,11},{10,... | collective-permute-start | bytes 2433032 | tf_op jit(solution)/shard_map/ppermute | solution.py:1047
  9.1 18.9 %mlp_first.1 = (bf16[1024,768]{1,0:T(8,128)(2,1)}, bf16[2048,768]{1,0:T(8,128)(2,1)}, bf16[2048,768]{1,0:T(8,128)(2,1)}, bf16[2048,192]{1,0:T(8,128)(2,1)}, f32[...) custom-call(s32[2]{0:T(128)} %pad_add_fusion.meta, ...), custom_call_target="tpu_custom_call" | custom-call | tf_op jit(solution)/shard_map/mlp_first/pallas_call | solution.py:503
  29.5 4.6 %qkv_2.1 = (bf16[2048,192]{1,0:T(8,128)(2,1)}, bf16[2048,192]{1,0:T(8,128)(2,1)}, bf16[2048,192]{1,0:T(8,128)(2,1)}) custom-call(s32[2]{0:T(128)} %pad_add_fusion.meta, s32[1]{0:T(128)S(6)} %copy.50.valid, bf16[528,768]{1,0:T(8,128)(2,1)} %collective-permute-done.2.x_ref.refs_5_.xa, ...), custom_call_target="tpu_custom_call", output_to_operand_aliasing={{0}: (9, {}), {1}: (10, {}), {2}: (11, {})} | custom-call | tf_op jit(solution)/shard_map/qkv_2/pallas_call | solution.py:196
  34.1 5.2 %qkv_3.1 = (bf16[2048,192]{1,0:T(8,128)(2,1)}, bf16[2048,192]{1,0:T(8,128)(2,1)}, bf16[2048,192]{1,0:T(8,128)(2,1)}, s32[8,1,256]{2,1,0:T(1,128)}, s32[8]{0:T(128)}, /*index=5*/s32[8]{0:T(128)}) custom-call(s32[2]{0:T(128)} %pad_add_fusion.meta, s32[1]{0:T(128)S(6)} %copy.50.valid, ...), custom_call_target="tpu_custom_call", output_to_operand_aliasing={{0}: (9, {}), {1}: (10, {}), {2}: (11, {})} | custom-call | tf_op jit(solution)/shard_map/qkv_3/pallas_call | solution.py:196
  39.3 4.1 %collective-permute-done.4.ca = bf16[544,768]{1,0:T(8,128)(2,1)} collective-permute-done((bf16[544,768]{1,0:T(8,128)(2,1)}, bf16[544,768]{1,0:T(8,128)(2,1)}, u32[]{:S(2)}, u32[]{:S(2)}) %collective-permute-start.4) | collective-permute-done | bytes 835616 | tf_op jit(solution)/shard_map/ppermute | solution.py:1047
  43.4 14.1 %attend.1 = (bf16[2048,192]{1,0:T(8,128)(2,1)}, f32[3,8,1,256]{3,2,1,0:T(1,128)}) custom-call(s32[2]{0:T(128)} %pad_add_fusion.meta, s32[8]{0:T(128)} %get-tuple-element.102.lo, s32[8]{0:T(128)} %get-tuple-element.103.hi, bf16[2048,192]{1,0:T(8,128)(2,1)} %get-tuple-element.104.q_ref, bf16[2048,192]{1,0:T(8,128)(2,1)} %get-tuple-element.105.k_ref, ...), custom_call_target="tpu_custom_call" | custom-call | tf_op jit(solution)/shard_map/attend/pallas_call | solution.py:630
  57.5 20.4 %mlp_second.1 = (bf16[2048,768]{1,0:T(8,128)(2,1)}, bf16[2048,768]{1,0:T(8,128)(2,1)}, bf16[2048,192]{1,0:T(8,128)(2,1)}, f32[8,768]{1,0:T(8,128)}, bf16[2,512,7...) custom-call(s32[2]{0:T(128)} %pad_add_fusion.meta, ...), custom_call_target="tpu_custom_call", output_to_operand_aliasing={{0}: (19, {}), {1}: (20, {}), {2}: (21, {})} | custom-call | tf_op jit(solution)/shard_map/mlp_second/pallas_call | solution.py:503
  78.5 1.5 collective-permute-start.6
  80.7 23.7 %attend_back.1.refs_0_.refs_1_.refs_2_.refs_3_ = bf16[2048,576]{1,0:T(8,128)(2,1)} custom-call(s32[2]{0:T(128)} %pad_add_fusion.meta, s32[8]{0:T(128)} %get-tuple-element.102.lo, s32[8]{0:T(128)} %get-tuple-element.103.hi, bf16[2048,192]{1,0:T(8,128)(2,1)} %get-tuple-element.104.q_ref, bf16[2048,192]{1,0:T(8,128)(2,1)} %get-tuple-element.105.k_ref, ...), custom_call_target="tpu_custom_call" | custom-call | tf_op jit(solution)/shard_map/attend_back/pallas_call | solution.py:761
  104.4 8.5 %joined_weight.1 = (bf16[400,576]{1,0:T(8,128)(2,1)}, bf16[400,576]{1,0:T(8,128)(2,1)}, f32[16,576]{1,0:T(8,128)}) custom-call(s32[2]{0:T(128)} %pad_add_fusion.meta, bf16[2048,576]{1,0:T(8,128)(2,1)} %attend_back.1.refs_0_.refs_1_.refs_2_.refs_3_, bf16[2048,768]{1,0:T(8,128)(2,1)} %get-tuple-element.123.refs_1_, f32[768]{0:T(1024)} %refs_8_.1, ...), custom_call_target="tpu_custom_call" | custom-call | tf_op jit(solution)/shard_map/joined_weight/pallas_call | solution.py:858
  114.1 1.8 add_convert_fusion.3
  115.9 1.9 %add_convert_fusion.2 = bf16[384,512]{1,0:T(8,128)(2,1)} fusion(bf16[768,512]{1,0:T(8,128)(2,1)} %collective-permute-done.7, bf16[768,512]{1,0:T(8,128)(2,1)} %get-tuple-element.142), kind=kLoop, calls=%fused_computation.6 | loop fusion | flops 786432 | bytes 1179648 | tf_op jit(solution)/shard_map/convert_element_type | solution.py:1030
  117.9 2.2 %fusion.2 = bf16[512,768]{1,0:T(8,128)(2,1)} fusion(bf16[2,512,768]{2,1,0:T(8,128)(2,1)} %collective-permute-done.8.near, bf16[2,512,768]{2,1,0:T(8,128)(2,1)S(1)} %copy-done.1), kind=kLoop, calls=%fused_computation.5 | loop fusion | flops 1572864 | bytes 2359296 | tf_op jit(solution)/shard_map/convert_element_type | solution.py:1051
  120.1 9.0 %norm_grad.1 = (bf16[512,768]{1,0:T(8,128)(2,1)}, bf16[512,768]{1,0:T(8,128)(2,1)}, bf16[512,768]{1,0:T(8,128)(2,1)}, bf16[512,768]{1,0:T(8,128)(2,1)}) custom-call(s32[2]{0:T(128)} %pad_add_fusion.meta, bf16[2048,576]{1,0:T(8,128)(2,1)} %attend_back.1.refs_0_.refs_1_.refs_2_.refs_3_, bf16[2048,576]{1,0:T(8,128)(2,1)} %attend_back.1.refs_0_.refs_1_.refs_2_.refs_3_, ...), custom_call_target="tpu_custom_call" | custom-call | tf_op jit(solution)/shard_map/norm_grad/pallas_call | solution.py:889
  129.6 1.9 %collective-permute-start.11 = (bf16[384,512]{1,0:T(8,128)(2,1)}, bf16[384,512]{1,0:T(8,128)(2,1)S(1)}, u32[]{:S(2)}, u32[]{:S(2)}) collective-permute-start(bf16[384,512]{1,0:T(8,128)(2,1)} %add_convert_fusion.2), channel_id=1, source_target_pairs={{0,4},{4,0},{8,12},{12,8},{16,20},{20,16},{24,28},{28,24},{1,5},{5... | collective-permute-start | bytes 1179656 | tf_op jit(solution)/shard_map/ppermute | solution.py:1047
  131.5 1.6 collective-permute-start.14
  136.9 4.3 %collective-permute-done.11 = bf16[384,512]{1,0:T(8,128)(2,1)S(1)} collective-permute-done((bf16[384,512]{1,0:T(8,128)(2,1)}, bf16[384,512]{1,0:T(8,128)(2,1)S(1)}, u32[]{:S(2)}, u32[]{:S(2)}) %collective-permute-start.11) | collective-permute-done | bytes 393248 | tf_op jit(solution)/shard_map/ppermute | solution.py:1047
  141.2 1.9 %add_convert_fusion.6 = bf16[192,512]{1,0:T(8,128)(2,1)} fusion(bf16[384,512]{1,0:T(8,128)(2,1)S(1)} %collective-permute-done.11, bf16[768,512]{1,0:T(8,128)(2,1)} %collective-permute-done.7, bf16[768,512]{1,0:T(8,128)(2,1)} %get-tuple-element.142), kind=kLoop, calls=%fused_computation.10 | loop fusion | flops 589824 | bytes 786432 | tf_op jit(solution)/shard_map/convert_element_type | solution.py:1030
  143.1 1.8 add_convert_fusion.7
  144.9 1.8 collective-permute-start.15
  146.8 1.5 collective-permute-start.18
  153.1 2.8 %result.1 = bf16[512,768]{1,0:T(8,128)(2,1)} custom-call(bf16[528,768]{1,0:T(8,128)(2,1)} %fusion.1.xa.refs_3_.x_ref, bf16[2,512,768]{2,1,0:T(8,128)(2,1)} %get-tuple-element.132.even, bf16[2,512,768]{2,1,0:T(8,128)(2,1)} %collective-permute-done.8.near, bf16[512,768]{1,0:T(8,128)(2,1)} %collective-permute-done.14.far, f32[768]{0:T(1024)} %b_out.1, f32[768]{0:T(1024)} %b_down.1), custom_call_target="tpu_custom_call" | custom-call | tf_op jit(solution)/shard_map/result/pallas_call | solution.py:1095
  155.9 8.0 %collective-permute-done.15 = bf16[192,512]{1,0:T(8,128)(2,1)} collective-permute-done((bf16[192,512]{1,0:T(8,128)(2,1)}, bf16[192,512]{1,0:T(8,128)(2,1)}, u32[]{:S(2)}, u32[]{:S(2)}) %collective-permute-start.15) | collective-permute-done | bytes 196640 | tf_op jit(solution)/shard_map/ppermute | solution.py:1047
  163.9 2.0 %add_convert_fusion.5 = bf16[192,512]{1,0:T(8,128)(2,1)} fusion(bf16[192,512]{1,0:T(8,128)(2,1)} %collective-permute-done.15, bf16[384,512]{1,0:T(8,128)(2,1)} %copy-done.4, bf16[768,512]{1,0:T(8,128)(2,1)} %collective-permute-done.7, bf16[768,512]{1,0:T(8,128)(2,1)} %get-tuple-element.142), kind=kLoop, calls=%fused_computation.9 | loop fusion | flops 786432 | bytes 983040 | tf_op jit(solution)/shard_map/convert_element_type | solution.py:1213
  165.9 3.0 %collective-permute-start.23 = (bf16[192,512]{1,0:T(8,128)(2,1)}, bf16[192,512]{1,0:T(8,128)(2,1)}, u32[]{:S(2)}, u32[]{:S(2)}) collective-permute-start(bf16[192,512]{1,0:T(8,128)(2,1)} %add_convert_fusion.5), channel_id=1, source_target_pairs={{0,0},{1,8},{2,16},{3,24},{4,1},{5,9},{6,17},{7,25},{8,2},{9,10},{... | collective-permute-start | bytes 589832 | tf_op jit(solution)/shard_map/ppermute | solution.py:1059
  168.9 2.6 %last_qkv.1 = (f32[96,192]{1,0:T(8,128)}, f32[128,192]{1,0:T(8,128)}, f32[128,192]{1,0:T(8,128)}, f32[32,192]{1,0:T(8,128)}) custom-call(s32[2]{0:T(128)} %pad_add_fusion.meta, bf16[400,576]{1,0:T(8,128)(2,1)} %get-tuple-element.144.refs_0_, bf16[400,576]{1,0:T(8,128)(2,1)} %collective-permute-done.9.refs_1_, bf16[208,576]{1,0:T(8,128)(2,1)} %copy-done.3, ...), custom_call_target="tpu_custom_call" | custom-call | tf_op jit(solution)/shard_map/last_qkv/pallas_call | solution.py:910
  171.5 2.1 %collective-permute-start.22 = (f32[32,192]{1,0:T(8,128)}, f32[32,192]{1,0:T(8,128)}, u32[]{:S(2)}, u32[]{:S(2)}) collective-permute-start(f32[32,192]{1,0:T(8,128)} %get-tuple-element.149.small), channel_id=1, source_target_pairs={{0,3},{1,2},{2,1},{3,0},{4,7},{5,6},{6,5},{7,4},{8,11},{9,10},{10,... | collective-permute-start | bytes 73736 | tf_op jit(solution)/shard_map/ppermute | solution.py:1047
  174.1 3.4 %token_grad.1 = bf16[512,768]{1,0:T(8,128)(2,1)} custom-call(bf16[528,768]{1,0:T(8,128)(2,1)} %fusion.1.xa.refs_3_.x_ref, bf16[512,768]{1,0:T(8,128)(2,1)} %get-tuple-element.136.even, bf16[512,768]{1,0:T(8,128)(2,1)} %collective-permute-done.17.near, bf16[512,768]{1,0:T(8,128)(2,1)} %collective-permute-done.18.far, bf16[512,768]{1,0:T(8,128)(2,1)} %bitcast.12), custom_call_target="tpu_custom_call" | custom-call | tf_op jit(solution)/shard_map/token_grad/pallas_call | solution.py:1095
  177.6 1.9 %convert_add_fusion = f32[96,768]{1,0:T(8,128)} fusion(bf16[96,768]{1,0:T(8,128)(2,1)} %collective-permute-done.19, bf16[192,768]{1,0:T(8,128)(2,1)} %copy-done.5, bf16[384,768]{1,0:T(8,128)(2,1)} %collective-permute-done.6, bf16[384,768]{1,0:T(8,128)(2,1)} %get-tuple-element.152), kind=kLoop, calls=%fused_computation.11 | loop fusion | flops 516096 | bytes 884736 | tf_op jit(solution)/shard_map/add | solution.py:1232
  179.5 2.4 %lower.1 = (f32[192,384]{1,0:T(8,128)}, f32[96,192]{1,0:T(8,128)}) custom-call(s32[2]{0:T(128)} %pad_add_fusion.meta, bf16[192,512]{1,0:T(8,128)(2,1)} %collective-permute-done.23.piece), custom_call_target="tpu_custom_call" | custom-call | tf_op jit(solution)/shard_map/lower/pallas_call | solution.py:910
  181.8 2.7 %assemble.1 = (f32[96,576]{1,0:T(8,128)}, f32[2304]{0:T(1024)}, f32[768]{0:T(1024)}, f32[3072]{0:T(1024)}, f32[768]{0:T(1024)}, /*index=5*/f32[768]{0:T(1024)}, f32[768]{0:T(1024)}, f32[768]{0:T(1024)}, f32[768]{0:T(1024)}) custom-call(s32[2]{0:T(128)} %pad_add_fusion.meta, f32[96,192]{1,0:T(8,128)} %get-tuple-element.154.kept, ...), custom_call_target="tpu_custom_call" | custom-call | tf_op jit(solution)/shard_map/assemble/pallas_call | solution.py:1013
  (59 shorter events, 16.6 us)
Async XLA Ops:
  0.6 6.0 %copy-start = (bf16[1,512,768]{2,1,0:T(8,128)(2,1)S(1)}, bf16[1,512,768]{2,1,0:T(8,128)(2,1)}, u32[]{:S(2)}) copy-start(bf16[1,512,768]{2,1,0:T(8,128)(2,1)} %param.33) | copy-start | bytes 2359300
  3.5 5.6 %collective-permute-start = (bf16[528,768]{1,0:T(8,128)(2,1)}, bf16[528,768]{1,0:T(8,128)(2,1)}, u32[]{:S(2)}, u32[]{:S(2)}) collective-permute-start(bf16[528,768]{1,0:T(8,128)(2,1)} %fusion.1.xa.refs_3_.x_ref), channel_id=1, source_target_pairs={{0,1},{1,0},{2,3},{3,2},{4,5},{5,4},{6,7},{7,6},{8,9},{9,8},{10,11... | collective-permute-start | bytes 2433032 | tf_op jit(solution)/shard_map/ppermute | solution.py:1047
  3.9 24.1 %collective-permute-start.2 = (bf16[528,768]{1,0:T(8,128)(2,1)}, bf16[528,768]{1,0:T(8,128)(2,1)}, u32[]{:S(2)}, u32[]{:S(2)}) collective-permute-start(bf16[528,768]{1,0:T(8,128)(2,1)} %fusion.1.xa.refs_3_.x_ref), channel_id=1, source_target_pairs={{0,2},{1,3},{2,0},{3,1},{4,6},{5,7},{6,4},{7,5},{8,10},{9,11},{10,... | collective-permute-start | bytes 2433032 | tf_op jit(solution)/shard_map/ppermute | solution.py:1047
  6.4 2.6 %collective-permute-start.1 = (bf16[512,768]{1,0:T(8,128)(2,1)}, bf16[512,768]{1,0:T(8,128)(2,1)}, u32[]{:S(2)}, u32[]{:S(2)}) collective-permute-start(bf16[512,768]{1,0:T(8,128)(2,1)} %bitcast.9), channel_id=1, source_target_pairs={{0,1},{1,0},{2,3},{3,2},{4,5},{5,4},{6,7},{7,6},{8,9},{9,8},{10,11... | collective-permute-start | bytes 2359304 | tf_op jit(solution)/shard_map/ppermute | solution.py:1047
  7.6 35.8 %collective-permute-start.4 = (bf16[544,768]{1,0:T(8,128)(2,1)}, bf16[544,768]{1,0:T(8,128)(2,1)}, u32[]{:S(2)}, u32[]{:S(2)}) collective-permute-start(bf16[544,768]{1,0:T(8,128)(2,1)} %pad.9), channel_id=1, source_target_pairs={{0,2},{1,3},{2,0},{3,1},{4,6},{5,7},{6,4},{7,5},{8,10},{9,11},{10,... | collective-permute-start | bytes 2506760 | tf_op jit(solution)/shard_map/ppermute | solution.py:1047
  28.0 6.1 %collective-permute-start.3 = (bf16[528,768]{1,0:T(8,128)(2,1)}, bf16[528,768]{1,0:T(8,128)(2,1)}, u32[]{:S(2)}, u32[]{:S(2)}) collective-permute-start(bf16[528,768]{1,0:T(8,128)(2,1)} %collective-permute-done.2.x_ref.refs_5_.xa), channel_id=1, source_target_pairs={{0,1},{1,0},{2,3},{3,2},{4,5},{5,4},{6,7},{7,6},{8,9},{9,8},{10,11... | collective-permute-start | bytes 2433032 | tf_op jit(solution)/shard_map/ppermute | solution.py:1047
  43.4 14.1 %collective-permute-start.5 = (bf16[544,768]{1,0:T(8,128)(2,1)}, bf16[544,768]{1,0:T(8,128)(2,1)}, u32[]{:S(2)}, u32[]{:S(2)}) collective-permute-start(bf16[544,768]{1,0:T(8,128)(2,1)} %collective-permute-done.4.ca), channel_id=1, source_target_pairs={{0,1},{1,0},{2,3},{3,2},{4,5},{5,4},{6,7},{7,6},{8,9},{9,8},{10,11... | collective-permute-start | bytes 2506760 | tf_op jit(solution)/shard_map/ppermute | solution.py:1047
  77.9 39.9 %collective-permute-start.8 = (bf16[2,512,768]{2,1,0:T(8,128)(2,1)}, bf16[2,512,768]{2,1,0:T(8,128)(2,1)}, u32[]{:S(2)}, u32[]{:S(2)}) collective-permute-start(bf16[2,512,768]{2,1,0:T(8,128)(2,1)} %get-tuple-element.133), channel_id=1, source_target_pairs={{0,1},{1,0},{2,3},{3,2},{4,5},{5,4},{6,7},{7,6},{8,9},{9,8},{10,11... | collective-permute-start | bytes 4718600 | tf_op jit(solution)/shard_map/ppermute | solution.py:1047
  78.5 35.6 %collective-permute-start.6 = (bf16[384,768]{1,0:T(8,128)(2,1)}, bf16[384,768]{1,0:T(8,128)(2,1)}, u32[]{:S(2)}, u32[]{:S(2)}) collective-permute-start(bf16[384,768]{1,0:T(8,128)(2,1)} %get-tuple-element.126), channel_id=1, source_target_pairs={{0,4},{4,0},{8,12},{12,8},{16,20},{20,16},{24,28},{28,24},{1,5},{5... | collective-permute-start | bytes 1769480 | tf_op jit(solution)/shard_map/ppermute | solution.py:1047
  80.0 35.9 %collective-permute-start.7 = (bf16[768,512]{1,0:T(8,128)(2,1)}, bf16[768,512]{1,0:T(8,128)(2,1)}, u32[]{:S(2)}, u32[]{:S(2)}) collective-permute-start(bf16[768,512]{1,0:T(8,128)(2,1)} %get-tuple-element.129), channel_id=1, source_target_pairs={{0,8},{4,12},{8,0},{12,4},{16,24},{20,28},{24,16},{28,20},{1,9},{5... | collective-permute-start | bytes 2359304 | tf_op jit(solution)/shard_map/ppermute | solution.py:1047
  113.0 4.9 %copy-start.1 = (bf16[2,512,768]{2,1,0:T(8,128)(2,1)S(1)}, bf16[2,512,768]{2,1,0:T(8,128)(2,1)}, u32[]{:S(2)}) copy-start(bf16[2,512,768]{2,1,0:T(8,128)(2,1)} %get-tuple-element.132.even) | copy-start | bytes 4718596
  113.0 20.1 %collective-permute-start.9 = (bf16[400,576]{1,0:T(8,128)(2,1)}, bf16[400,576]{1,0:T(8,128)(2,1)}, u32[]{:S(2)}, u32[]{:S(2)}) collective-permute-start(bf16[400,576]{1,0:T(8,128)(2,1)} %get-tuple-element.139), channel_id=1, source_target_pairs={{0,4},{4,0},{8,12},{12,8},{16,20},{20,16},{24,28},{28,24},{1,5},{5... | collective-permute-start | bytes 1382408 | tf_op jit(solution)/shard_map/ppermute | solution.py:1047
  129.1 6.7 %copy-start.2 = (bf16[512,768]{1,0:T(8,128)(2,1)S(1)}, bf16[512,768]{1,0:T(8,128)(2,1)}, u32[]{:S(2)}) copy-start(bf16[512,768]{1,0:T(8,128)(2,1)} %get-tuple-element.140) | copy-start | bytes 2359300
  129.1 6.7 %collective-permute-start.10 = (bf16[512,768]{1,0:T(8,128)(2,1)}, bf16[512,768]{1,0:T(8,128)(2,1)S(1)}, u32[]{:S(2)}, u32[]{:S(2)}) collective-permute-start(bf16[512,768]{1,0:T(8,128)(2,1)} %get-tuple-element.141), channel_id=1, source_target_pairs={{0,1},{1,0},{2,3},{3,2},{4,5},{5,4},{6,7},{7,6},{8,9},{9,8},{10,11... | collective-permute-start | bytes 2359304 | tf_op jit(solution)/shard_map/ppermute | solution.py:1047
  129.2 13.9 %collective-permute-start.12 = (bf16[192,768]{1,0:T(8,128)(2,1)}, bf16[192,768]{1,0:T(8,128)(2,1)S(1)}, u32[]{:S(2)}, u32[]{:S(2)}) collective-permute-start(bf16[192,768]{1,0:T(8,128)(2,1)} %add_convert_fusion.3), channel_id=1, source_target_pairs={{0,8},{4,12},{8,0},{12,4},{16,24},{20,28},{24,16},{28,20},{1,9},{5... | collective-permute-start | bytes 884744 | tf_op jit(solution)/shard_map/ppermute | solution.py:1047
  129.6 11.6 %collective-permute-start.11 = (bf16[384,512]{1,0:T(8,128)(2,1)}, bf16[384,512]{1,0:T(8,128)(2,1)S(1)}, u32[]{:S(2)}, u32[]{:S(2)}) collective-permute-start(bf16[384,512]{1,0:T(8,128)(2,1)} %add_convert_fusion.2), channel_id=1, source_target_pairs={{0,4},{4,0},{8,12},{12,8},{16,20},{20,16},{24,28},{28,24},{1,5},{5... | collective-permute-start | bytes 1179656 | tf_op jit(solution)/shard_map/ppermute | solution.py:1047
  131.5 20.7 %collective-permute-start.14 = (bf16[512,768]{1,0:T(8,128)(2,1)}, bf16[512,768]{1,0:T(8,128)(2,1)}, u32[]{:S(2)}, u32[]{:S(2)}) collective-permute-start(bf16[512,768]{1,0:T(8,128)(2,1)} %fusion.2), channel_id=1, source_target_pairs={{0,2},{1,3},{2,0},{3,1},{4,6},{5,7},{6,4},{7,5},{8,10},{9,11},{10,... | collective-permute-start | bytes 2359304 | tf_op jit(solution)/shard_map/ppermute | solution.py:1047
  135.0 13.3 %collective-permute-start.13 = (bf16[208,576]{1,0:T(8,128)(2,1)S(1)}, bf16[208,576]{1,0:T(8,128)(2,1)S(1)}, u32[]{:S(2)}, u32[]{:S(2)}) collective-permute-start(bf16[208,576]{1,0:T(8,128)(2,1)S(1)} %pad_maximum_fusion), channel_id=1, source_target_pairs={{0,8},{4,12},{8,0},{12,4},{16,24},{20,28},{24,16},{28,20},{1,9},{5... | collective-permute-start | bytes 718856 | tf_op jit(solution)/shard_map/ppermute | solution.py:1047
  135.8 37.8 %collective-permute-start.17 = (bf16[512,768]{1,0:T(8,128)(2,1)}, bf16[512,768]{1,0:T(8,128)(2,1)}, u32[]{:S(2)}, u32[]{:S(2)}) collective-permute-start(bf16[512,768]{1,0:T(8,128)(2,1)} %get-tuple-element.151), channel_id=1, source_target_pairs={{0,1},{1,0},{2,3},{3,2},{4,5},{5,4},{6,7},{7,6},{8,9},{9,8},{10,11... | collective-permute-start | bytes 2359304 | tf_op jit(solution)/shard_map/ppermute | solution.py:1047
  141.2 8.9 %copy-start.4 = (bf16[384,512]{1,0:T(8,128)(2,1)}, bf16[384,512]{1,0:T(8,128)(2,1)S(1)}, u32[]{:S(2)}) copy-start(bf16[384,512]{1,0:T(8,128)(2,1)S(1)} %collective-permute-done.11) | copy-start | bytes 1179652
  143.1 8.2 %copy-start.5 = (bf16[192,768]{1,0:T(8,128)(2,1)}, bf16[192,768]{1,0:T(8,128)(2,1)S(1)}, u32[]{:S(2)}) copy-start(bf16[192,768]{1,0:T(8,128)(2,1)S(1)} %collective-permute-done.12) | copy-start | bytes 884740
  144.9 18.9 %collective-permute-start.15 = (bf16[192,512]{1,0:T(8,128)(2,1)}, bf16[192,512]{1,0:T(8,128)(2,1)}, u32[]{:S(2)}, u32[]{:S(2)}) collective-permute-start(bf16[192,512]{1,0:T(8,128)(2,1)} %add_convert_fusion.6), channel_id=1, source_target_pairs={{0,16},{4,20},{8,24},{12,28},{16,0},{20,4},{24,8},{28,12},{1,17},{... | collective-permute-start | bytes 589832 | tf_op jit(solution)/shard_map/ppermute | solution.py:1047
  146.8 26.9 %collective-permute-start.18 = (bf16[512,768]{1,0:T(8,128)(2,1)}, bf16[512,768]{1,0:T(8,128)(2,1)}, u32[]{:S(2)}, u32[]{:S(2)}) collective-permute-start(bf16[512,768]{1,0:T(8,128)(2,1)} %add_convert_fusion), channel_id=1, source_target_pairs={{0,2},{1,3},{2,0},{3,1},{4,6},{5,7},{6,4},{7,5},{8,10},{9,11},{10,... | collective-permute-start | bytes 2359304 | tf_op jit(solution)/shard_map/ppermute | solution.py:1047
  148.3 1.1 copy-start.3
  150.1 18.7 %collective-permute-start.16 = (bf16[112,576]{1,0:T(8,128)(2,1)}, bf16[112,576]{1,0:T(8,128)(2,1)}, u32[]{:S(2)}, u32[]{:S(2)}) collective-permute-start(bf16[112,576]{1,0:T(8,128)(2,1)} %pad_maximum_fusion.1.refs_4_), channel_id=1, source_target_pairs={{0,16},{4,20},{8,24},{12,28},{16,0},{20,4},{24,8},{28,12},{1,17},{... | collective-permute-start | bytes 387080 | tf_op jit(solution)/shard_map/ppermute | solution.py:1047
  152.3 25.3 %collective-permute-start.19 = (bf16[96,768]{1,0:T(8,128)(2,1)}, bf16[96,768]{1,0:T(8,128)(2,1)}, u32[]{:S(2)}, u32[]{:S(2)}) collective-permute-start(bf16[96,768]{1,0:T(8,128)(2,1)} %add_convert_fusion.7), channel_id=1, source_target_pairs={{0,16},{4,20},{8,24},{12,28},{16,0},{20,4},{24,8},{28,12},{1,17},{... | collective-permute-start | bytes 442376 | tf_op jit(solution)/shard_map/ppermute | solution.py:1047
  165.9 13.6 %collective-permute-start.23 = (bf16[192,512]{1,0:T(8,128)(2,1)}, bf16[192,512]{1,0:T(8,128)(2,1)}, u32[]{:S(2)}, u32[]{:S(2)}) collective-permute-start(bf16[192,512]{1,0:T(8,128)(2,1)} %add_convert_fusion.5), channel_id=1, source_target_pairs={{0,0},{1,8},{2,16},{3,24},{4,1},{5,9},{6,17},{7,25},{8,2},{9,10},{... | collective-permute-start | bytes 589832 | tf_op jit(solution)/shard_map/ppermute | solution.py:1059
  171.5 10.3 %collective-permute-start.22 = (f32[32,192]{1,0:T(8,128)}, f32[32,192]{1,0:T(8,128)}, u32[]{:S(2)}, u32[]{:S(2)}) collective-permute-start(f32[32,192]{1,0:T(8,128)} %get-tuple-element.149.small), channel_id=1, source_target_pairs={{0,3},{1,2},{2,1},{3,0},{4,7},{5,6},{6,5},{7,4},{8,11},{9,10},{10,... | collective-permute-start | bytes 73736 | tf_op jit(solution)/shard_map/ppermute | solution.py:1047
  173.6 8.2 %collective-permute-start.20 = (f32[128,192]{1,0:T(8,128)}, f32[128,192]{1,0:T(8,128)}, u32[]{:S(2)}, u32[]{:S(2)}) collective-permute-start(f32[128,192]{1,0:T(8,128)} %get-tuple-element.155), channel_id=1, source_target_pairs={{0,1},{1,0},{2,3},{3,2},{4,5},{5,4},{6,7},{7,6},{8,9},{9,8},{10,11... | collective-permute-start | bytes 294920 | tf_op jit(solution)/shard_map/ppermute | solution.py:1047
  173.6 8.2 %collective-permute-start.21 = (f32[128,192]{1,0:T(8,128)}, f32[128,192]{1,0:T(8,128)}, u32[]{:S(2)}, u32[]{:S(2)}) collective-permute-start(f32[128,192]{1,0:T(8,128)} %get-tuple-element.156), channel_id=1, source_target_pairs={{0,2},{1,3},{2,0},{3,1},{4,6},{5,7},{6,4},{7,5},{8,10},{9,11},{10,... | collective-permute-start | bytes 294920 | tf_op jit(solution)/shard_map/ppermute | solution.py:1047

commit v8 on v7

--- a/solution.py
+++ b/solution.py
@@ -880,7 +880,7 @@
 
 
 def norm_grad(meta, grad, e_mlp, gain, w, seq):
-    tile = TILE // 2
+    tile = TILE
     per = seq // tile
 
     def slot_tiles(slot, cols):
@@ -929,7 +929,37 @@
     return total
 
 
-def lower_kernel(meta, piece, down_ref, out_ref):
+def sums_kernel(counts, meta, *refs):
+    ins, outs = refs[: sum(counts)], refs[sum(counts) :]
+    for count, out in zip(counts, outs):
+        out[...] = add_up(ins[:count]).astype(BF16)
+        ins = ins[count:]
+
+
+def block_sums(name, meta, steps, *jobs):
+    specs, args, outs, out_specs = [], [], [], []
+    for rows, terms in jobs:
+        size, cols = rows // steps, terms[0][0].shape[1]
+        for array, at in terms:
+            specs.append(pl.BlockSpec((size, cols), lambda i, m, at=at // size: (at + i, 0)))
+            args.append(array)
+        outs.append(jax.ShapeDtypeStruct((rows, cols), BF16))
+        out_specs.append(pl.BlockSpec((size, cols), lambda i, m: (i, 0)))
+    return pl.pallas_call(
+        partial(sums_kernel, [len(terms) for _, terms in jobs]),
+        out_shape=outs,
+        grid_spec=pltpu.PrefetchScalarGridSpec(
+            num_scalar_prefetch=1, grid=(steps,), in_specs=specs, out_specs=out_specs
+        ),
+        compiler_params=params(),
+        cost_estimate=COST,
+        name=name,
+    )(meta, *args)
+
+
+def lower_kernel(meta, piece, *refs):
+    *terms, down_ref, out_ref, up_ref = refs
+    up_ref[...] = add_up(terms)
     cut = down_ref.shape[1]
     down_ref[...] = piece[:, :cut].astype(F32)
     out_ref[...] = piece[:, cut:].astype(F32).T[: out_ref.shape[0]]
@@ -1172,44 +1202,56 @@
     qkv_keep, qkv_send = chunks_of(qkv_keep, qkv_send, rows, 1)
     qkv_got = swap(qkv_send, "rows", 1)
 
-    out_send = add_low(after(out_even, qkv_keep)[1], out_got[1])
-    out_far = swap(out_send, "blk", 2)
     half = D // 2
     if fits(rows):
-        up = [up_keep, up_got]
-        up_send = next_send(up, half)
+        chunk = D // rows
+        meta = after(meta, qkv_keep)
+        up, lower = [up_keep, up_got], [low_keep, low_got]
+        flat = [v.reshape(2 * seq, D) for v in (out_even, out_got)]
+        up_send, low_send, out_send = block_sums(
+            "first_sums",
+            meta,
+            2,
+            (half // 2, [(term, half // 2) for term in up]),
+            (half, [(term, half) for term in lower]),
+            (seq, [(term, seq) for term in flat]),
+        )
         up.append(swap(up_send, "rows", up_masks[1]))
-        lower = [after(low_keep, qkv_keep), low_got]
-        low_send = next_send(lower, D)
         lower.append(swap(low_send, "rows", low_masks[1]))
-        meta = after(meta, up_send, low_send)
+    else:
+        out_send = add_low(out_even[1], out_got[1])
+    out_far = swap(out_send, "blk", 2)
     meta = after(meta, out_send)
     e_own, e_near, e_send, e_last = norm_grad(meta, grad_joined, e_mlp, ln1_gain, w_own, seq)
     e_last = swap(e_last, "blk", 1)
     e_near = swap(e_near, "blk", 1)
     if fits(rows):
-        chunk = D // rows
         joined = [after(qkv_keep, e_own), qkv_got]
         tail = add_low(joined[0][half:], qkv_got[half:])
         qkv_send = jnp.concatenate([next_send(joined, half), tail])
         joined.append(swap(qkv_send, "rows", 2))
-        e_send = after(e_send, qkv_send)
+        meta = after(meta, qkv_send)
+        low_send, up_send = block_sums(
+            "second_sums",
+            meta,
+            1,
+            (width, [(term, width) for term in lower]),
+            (chunk, [(term, chunk) for term in up]),
+        )
+        lower.append(swap(low_send, "rows", low_masks[2]))
+        up.append(swap(up_send, "rows", up_masks[2]))
+        e_send = after(e_send, low_send, out_far)
     e_send = add_low(e_send, e_last)
     e_far = swap(e_send, "blk", 2)
     if fits(rows):
-        lower[0] = after(lower[0], e_send)
-        low_send = next_send(lower, half)
-        lower.append(swap(low_send, "rows", low_masks[2]))
-        up[0] = after(up[0], low_send)
-        up_send = next_send(up, half // 2)
-        up.append(swap(up_send, "rows", up_masks[2]))
-        joined[0] = after(joined[0], up_send)
-        tail = add_low(after(qkv_send, up_send)[half // 2 :], joined[2][half // 2 :])
+        joined[0] = after(joined[0], up_send, e_send)
+        tail = add_low(after(qkv_send, up_send, e_send)[half // 2 :], joined[2][half // 2 :])
         qkv_send = jnp.concatenate([next_send(joined, half // 2), tail])
         joined.append(swap(qkv_send, "rows", 4))
         out_args = (after(tok_own, qkv_send), out_even, out_got, out_far, b_out, b_down)
         result = finish(result_kernel, "result", seq, *out_args)
         meta = after(meta, result)
+        lower[0] = after(lower[0], result)
         piece = sum(term[:width].astype(F32) for term in lower).astype(BF16)
         meta = after(meta, piece)
         piece = spread_rows(piece)
@@ -1228,11 +1270,11 @@
         near, far, diag = swap(near, "blk", 1), swap(far, "blk", 2), swap(small, "blk", 3)
         tok_args = (after(tok_own, small), e_own, e_near, e_far, cot_own)
         grad_tokens = finish(token_kernel, "token_grad", seq, *tok_args)
-        up[0] = after(up[0], grad_tokens)
-        up = sum(term[:chunk].astype(F32) for term in up)
-        ends = [((width, hid // 2), F32), ((width // 2, width), F32)]
-        meta = after(meta, up)
-        down, out_w = simple(lower_kernel, "lower", ends, meta, piece)
+        meta = after(meta, grad_tokens)
+        ends = [((width, hid // 2), F32), ((width // 2, width), F32), ((chunk, hid), F32)]
+        specs = [whole(piece.shape)] + [pl.BlockSpec((chunk, hid), lambda i, m: (0, 0))] * 4
+        down, out_w, up = simple(lower_kernel, "lower", ends, meta, piece, *up, specs=specs)
+        meta = after(meta, down)
         down = down.T
         qkv, gb_qkv, gb_out, gb_up, gb_down, *norms = assemble(
             meta, kept, small, near, far, diag

time: 186 us -> 184 us (0.989)
  other arithmetic: 21.9 us -> 13 us
  waiting for transfers between devices: 18 us -> 23 us
  starting transfers between devices: 23.7 us -> 26.5 us
    convert_element_type x6 -> x2, other arithmetic: 9.75 us -> 2.19 us  [next_send(): sum((term[size // 2:size].astype(F32) for term in terms)).astype(BF16)]
    pallas_call x0 -> x2, Pallas kernels: none -> 6.3 us  [block_sums(): pl.pallas_call(partial(sums_kernel, [len(terms) for _, terms in jobs]), o...]
    ppermute x23, waiting for transfers between devices: 18 us -> 23 us  [swap(): return lax.ppermute(value, axis, [(i, i ^ mask) for i in range(size)])]
    ppermute x23, starting transfers between devices: 20.7 us -> 23.5 us  [swap(): return lax.ppermute(value, axis, [(i, i ^ mask) for i in range(size)])]
    pallas_call x1, Pallas kernels: 23.7 us -> 21 us  [attend_back(): pl.pallas_call(partial(attend_back_kernel, per), out_shape=jax.ShapeDtype...]
    pallas_call x1, Pallas kernels: 9.02 us -> 7.02 us  [norm_grad(): pl.pallas_call(norm_kernel, out_shape=[jax.ShapeDtypeStruct((seq, D), BF1...]
    add x1 -> x0, other arithmetic: 1.91 us -> none  [local(): up = sum((term[:chunk].astype(F32) for term in up))]
    convert_element_type x4 -> x3, other arithmetic: 4.05 us -> 3.95 us  [add_low(): return (left.astype(F32) + right.astype(F32)).astype(BF16)]
  transfers between devices with their start and end apart: 24 -> 24, of which waited for: 5 -> 6; matrix products, arithmetic and copies ran while one was open for 11% -> 6% of each run, Pallas kernels for 52% -> 52%
where the time goes in v8:
time: 184 us
  Pallas kernels  119 us (65%)
  starting transfers between devices  26.5 us (14%)
  waiting for transfers between devices  23 us (12%)
  other arithmetic  13 us (7%)
    pallas_call x2, Pallas kernels, feed_forward(): pl.pallas_call(body, out_shape=outs, grid_spec=pltpu.PrefetchScalarGridSp...  39.4 us
    ppermute x23, starting transfers between devices, swap(): return lax.ppermute(value, axis, [(i, i ^ mask) for i in range(size)])  23.5 us
    ppermute x23, waiting for transfers between devices, swap(): return lax.ppermute(value, axis, [(i, i ^ mask) for i in range(size)])  23 us
    pallas_call x1, Pallas kernels, attend_back(): pl.pallas_call(partial(attend_back_kernel, per), out_shape=jax.ShapeDtype...  21 us
    pallas_call x1, Pallas kernels, attend(): pl.pallas_call(partial(attend_kernel, per), out_shape=[jax.ShapeDtypeStru...  13 us
    pallas_call x2, Pallas kernels, project(): pl.pallas_call(partial(qkv_kernel, slot), out_shape=outs, grid_spec=pltpu...  9.8 us
    pallas_call x1, Pallas kernels, joined_weight(): pl.pallas_call(partial(weight_kernel, rows), out_shape=[jax.ShapeDtypeStr...  8.51 us
    pallas_call x1, Pallas kernels, norm_grad(): pl.pallas_call(norm_kernel, out_shape=[jax.ShapeDtypeStruct((seq, D), BF1...  7.02 us
  transfers between devices with their start and end apart: 24, of which 6 were waited for; matrix products, arithmetic and copies ran while one was open for 6% of the time, Pallas kernels for 52%

profile of v8, /device:TPU:0, one launch (start us, length us, event | category | flops | bytes accessed | tf_op | source)
XLA Modules:
  0.0 184.2 jit_solution(9153037034300238704)
XLA Ops:
  1.4 2.1 %fusion.1.xa.refs_3_.x_ref = bf16[528,768]{1,0:T(8,128)(2,1)} fusion(bf16[1,512]{1,0:T(2,128)(2,1)S(1)} %convert_element_type.70, bf16[512,768]{1,0:T(8,128)(2,1)} %bitcast.16), kind=kLoop, calls=%fused_computation.3 | loop fusion | flops 2433024 | bytes 1598464 | tf_op jit(solution)/shard_map/concatenate | solution.py:1152
  3.9 2.5 %collective-permute-start.2 = (bf16[528,768]{1,0:T(8,128)(2,1)}, bf16[528,768]{1,0:T(8,128)(2,1)}, u32[]{:S(2)}, u32[]{:S(2)}) collective-permute-start(bf16[528,768]{1,0:T(8,128)(2,1)} %fusion.1.xa.refs_3_.x_ref), channel_id=1, source_target_pairs={{0,2},{1,3},{2,0},{3,1},{4,6},{5,7},{6,4},{7,5},{8,10},{9,11},{10,... | collective-permute-start | bytes 2433032 | tf_op jit(solution)/shard_map/ppermute | solution.py:1077
  9.1 18.9 %mlp_first.1 = (bf16[1024,768]{1,0:T(8,128)(2,1)}, bf16[2048,768]{1,0:T(8,128)(2,1)}, bf16[2048,768]{1,0:T(8,128)(2,1)}, bf16[2048,192]{1,0:T(8,128)(2,1)}, f32[...) custom-call(s32[2]{0:T(128)} %pad_add_fusion.meta, ...), custom_call_target="tpu_custom_call" | custom-call | tf_op jit(solution)/shard_map/mlp_first/pallas_call | solution.py:503
  29.5 4.6 %qkv_2.1 = (bf16[2048,192]{1,0:T(8,128)(2,1)}, bf16[2048,192]{1,0:T(8,128)(2,1)}, bf16[2048,192]{1,0:T(8,128)(2,1)}) custom-call(s32[2]{0:T(128)} %pad_add_fusion.meta, s32[1]{0:T(128)S(6)} %copy.50.valid, bf16[528,768]{1,0:T(8,128)(2,1)} %collective-permute-done.2.x_ref.refs_5_.xa, ...), custom_call_target="tpu_custom_call", output_to_operand_aliasing={{0}: (9, {}), {1}: (10, {}), {2}: (11, {})} | custom-call | tf_op jit(solution)/shard_map/qkv_2/pallas_call | solution.py:196
  34.1 5.2 %qkv_3.1 = (bf16[2048,192]{1,0:T(8,128)(2,1)}, bf16[2048,192]{1,0:T(8,128)(2,1)}, bf16[2048,192]{1,0:T(8,128)(2,1)}, s32[8,1,256]{2,1,0:T(1,128)}, s32[8]{0:T(128)}, /*index=5*/s32[8]{0:T(128)}) custom-call(s32[2]{0:T(128)} %pad_add_fusion.meta, s32[1]{0:T(128)S(6)} %copy.50.valid, ...), custom_call_target="tpu_custom_call", output_to_operand_aliasing={{0}: (9, {}), {1}: (10, {}), {2}: (11, {})} | custom-call | tf_op jit(solution)/shard_map/qkv_3/pallas_call | solution.py:196
  39.3 4.1 %collective-permute-done.4.ca = bf16[544,768]{1,0:T(8,128)(2,1)} collective-permute-done((bf16[544,768]{1,0:T(8,128)(2,1)}, bf16[544,768]{1,0:T(8,128)(2,1)}, u32[]{:S(2)}, u32[]{:S(2)}) %collective-permute-start.4) | collective-permute-done | bytes 835616 | tf_op jit(solution)/shard_map/ppermute | solution.py:1077
  43.4 13.0 %attend.1 = (bf16[2048,192]{1,0:T(8,128)(2,1)}, f32[3,8,1,256]{3,2,1,0:T(1,128)}) custom-call(s32[2]{0:T(128)} %pad_add_fusion.meta, s32[8]{0:T(128)} %get-tuple-element.106.lo, s32[8]{0:T(128)} %get-tuple-element.107.hi, bf16[2048,192]{1,0:T(8,128)(2,1)} %get-tuple-element.108.q_ref, bf16[2048,192]{1,0:T(8,128)(2,1)} %get-tuple-element.109.k_ref, ...), custom_call_target="tpu_custom_call" | custom-call | tf_op jit(solution)/shard_map/attend/pallas_call | solution.py:630
  56.4 20.4 %mlp_second.1 = (bf16[2048,768]{1,0:T(8,128)(2,1)}, bf16[2048,768]{1,0:T(8,128)(2,1)}, bf16[2048,192]{1,0:T(8,128)(2,1)}, f32[8,768]{1,0:T(8,128)}, bf16[2,512,7...) custom-call(s32[2]{0:T(128)} %pad_add_fusion.meta, ...), custom_call_target="tpu_custom_call", output_to_operand_aliasing={{0}: (19, {}), {1}: (20, {}), {2}: (21, {})} | custom-call | tf_op jit(solution)/shard_map/mlp_second/pallas_call | solution.py:503
  77.4 1.5 collective-permute-start.7
  78.9 3.0 %collective-permute-start.6 = (bf16[384,768]{1,0:T(8,128)(2,1)}, bf16[384,768]{1,0:T(8,128)(2,1)}, u32[]{:S(2)}, u32[]{:S(2)}) collective-permute-start(bf16[384,768]{1,0:T(8,128)(2,1)} %get-tuple-element.131), channel_id=1, source_target_pairs={{0,4},{4,0},{8,12},{12,8},{16,20},{20,16},{24,28},{28,24},{1,5},{5... | collective-permute-start | bytes 1769480 | tf_op jit(solution)/shard_map/ppermute | solution.py:1077
  81.8 21.0 %attend_back.1.refs_0_.refs_1_.refs_2_.refs_3_ = bf16[2048,576]{1,0:T(8,128)(2,1)} custom-call(s32[2]{0:T(128)} %pad_add_fusion.meta, s32[8]{0:T(128)} %get-tuple-element.106.lo, s32[8]{0:T(128)} %get-tuple-element.107.hi, bf16[2048,192]{1,0:T(8,128)(2,1)} %get-tuple-element.108.q_ref, bf16[2048,192]{1,0:T(8,128)(2,1)} %get-tuple-element.109.k_ref, ...), custom_call_target="tpu_custom_call" | custom-call | tf_op jit(solution)/shard_map/attend_back/pallas_call | solution.py:761
  102.9 8.5 %joined_weight.1 = (bf16[400,576]{1,0:T(8,128)(2,1)}, bf16[400,576]{1,0:T(8,128)(2,1)}, f32[16,576]{1,0:T(8,128)}) custom-call(s32[2]{0:T(128)} %pad_add_fusion.meta, bf16[2048,576]{1,0:T(8,128)(2,1)} %attend_back.1.refs_0_.refs_1_.refs_2_.refs_3_, bf16[2048,768]{1,0:T(8,128)(2,1)} %get-tuple-element.127.refs_1_, f32[768]{0:T(1024)} %refs_8_.1, ...), custom_call_target="tpu_custom_call" | custom-call | tf_op jit(solution)/shard_map/joined_weight/pallas_call | solution.py:858
  111.5 3.6 %first_sums.1 = (bf16[192,768]{1,0:T(8,128)(2,1)}, bf16[384,512]{1,0:T(8,128)(2,1)}, bf16[512,768]{1,0:T(8,128)(2,1)}) custom-call(s32[2]{0:T(128)} %pad_add_fusion.meta, bf16[384,768]{1,0:T(8,128)(2,1)} %get-tuple-element.130.refs_0_.refs_3_, bf16[384,768]{1,0:T(8,128)(2,1)} %collective-permute-done.6.refs_1_.refs_4_, ...), custom_call_target="tpu_custom_call" | custom-call | tf_op jit(solution)/shard_map/first_sums/pallas_call | solution.py:948
  115.1 1.5 collective-permute-start.12
  116.6 7.0 %norm_grad.1 = (bf16[512,768]{1,0:T(8,128)(2,1)}, bf16[512,768]{1,0:T(8,128)(2,1)}, bf16[512,768]{1,0:T(8,128)(2,1)}, bf16[512,768]{1,0:T(8,128)(2,1)}) custom-call(s32[2]{0:T(128)} %pad_add_fusion.meta, bf16[2048,576]{1,0:T(8,128)(2,1)} %attend_back.1.refs_0_.refs_1_.refs_2_.refs_3_, bf16[2048,576]{1,0:T(8,128)(2,1)} %attend_back.1.refs_0_.refs_1_.refs_2_.refs_3_, ...), custom_call_target="tpu_custom_call" | custom-call | tf_op jit(solution)/shard_map/norm_grad/pallas_call | solution.py:889
  123.7 2.7 %collective-permute-start.11 = (bf16[192,768]{1,0:T(8,128)(2,1)}, bf16[192,768]{1,0:T(8,128)(2,1)}, u32[]{:S(2)}, u32[]{:S(2)}) collective-permute-start(bf16[192,768]{1,0:T(8,128)(2,1)} %get-tuple-element.144), channel_id=1, source_target_pairs={{0,8},{4,12},{8,0},{12,4},{16,24},{20,28},{24,16},{28,20},{1,9},{5... | collective-permute-start | bytes 884744 | tf_op jit(solution)/shard_map/ppermute | solution.py:1077
  130.4 4.2 %collective-permute-done.11.refs_5_.refs_2_ = bf16[192,768]{1,0:T(8,128)(2,1)} collective-permute-done((bf16[192,768]{1,0:T(8,128)(2,1)}, bf16[192,768]{1,0:T(8,128)(2,1)}, u32[]{:S(2)}, u32[]{:S(2)}) %collective-permute-start.11) | collective-permute-done | bytes 294944 | tf_op jit(solution)/shard_map/ppermute | solution.py:1077
  134.6 3.3 %collective-permute-done.10.refs_2_ = bf16[384,512]{1,0:T(8,128)(2,1)} collective-permute-done((bf16[384,512]{1,0:T(8,128)(2,1)}, bf16[384,512]{1,0:T(8,128)(2,1)}, u32[]{:S(2)}, u32[]{:S(2)}) %collective-permute-start.10) | collective-permute-done | bytes 393248 | tf_op jit(solution)/shard_map/ppermute | solution.py:1077
  137.9 2.7 %second_sums.1 = (bf16[192,512]{1,0:T(8,128)(2,1)}, bf16[96,768]{1,0:T(8,128)(2,1)}) custom-call(s32[2]{0:T(128)} %pad_add_fusion.meta, bf16[768,512]{1,0:T(8,128)(2,1)} %get-tuple-element.154.refs_2_.refs_0_, bf16[768,512]{1,0:T(8,128)(2,1)} %collective-permute-done.7.refs_3_.refs_1_, bf16[384,512]{1,0:T(8,128)(2,1)} %collective-permute-done.10.refs_2_, ...), custom_call_target="tpu_custom_call" | custom-call | tf_op jit(solution)/shard_map/second_sums/pallas_call | solution.py:948
  140.6 2.7 %collective-permute-start.15 = (bf16[192,512]{1,0:T(8,128)(2,1)}, bf16[192,512]{1,0:T(8,128)(2,1)}, u32[]{:S(2)}, u32[]{:S(2)}) collective-permute-start(bf16[192,512]{1,0:T(8,128)(2,1)} %get-tuple-element.147), channel_id=1, source_target_pairs={{0,16},{4,20},{8,24},{12,28},{16,0},{20,4},{24,8},{28,12},{1,17},{... | collective-permute-start | bytes 589832 | tf_op jit(solution)/shard_map/ppermute | solution.py:1077
  143.3 2.4 %add_convert_fusion = bf16[512,768]{1,0:T(8,128)(2,1)} fusion(bf16[512,768]{1,0:T(8,128)(2,1)} %collective-permute-done.13, bf16[512,768]{1,0:T(8,128)(2,1)} %get-tuple-element.148), kind=kLoop, calls=%fused_computation.2 | loop fusion | flops 1572864 | bytes 2359296 | tf_op jit(solution)/shard_map/convert_element_type | solution.py:1081
  149.0 2.8 %result.1 = bf16[512,768]{1,0:T(8,128)(2,1)} custom-call(bf16[528,768]{1,0:T(8,128)(2,1)} %fusion.1.xa.refs_3_.x_ref, bf16[2,512,768]{2,1,0:T(8,128)(2,1)} %get-tuple-element.134.even, bf16[2,512,768]{2,1,0:T(8,128)(2,1)} %collective-permute-done.8.near, bf16[512,768]{1,0:T(8,128)(2,1)} %collective-permute-done.12.far, f32[768]{0:T(1024)} %b_out.1, f32[768]{0:T(1024)} %b_down.1), custom_call_target="tpu_custom_call" | custom-call | tf_op jit(solution)/shard_map/result/pallas_call | solution.py:1125
  151.8 4.2 %collective-permute-done.15 = bf16[192,512]{1,0:T(8,128)(2,1)} collective-permute-done((bf16[192,512]{1,0:T(8,128)(2,1)}, bf16[192,512]{1,0:T(8,128)(2,1)}, u32[]{:S(2)}, u32[]{:S(2)}) %collective-permute-start.15) | collective-permute-done | bytes 196640 | tf_op jit(solution)/shard_map/ppermute | solution.py:1077
  156.0 2.0 %add_convert_fusion.2 = bf16[192,512]{1,0:T(8,128)(2,1)} fusion(bf16[192,512]{1,0:T(8,128)(2,1)} %collective-permute-done.15, bf16[384,512]{1,0:T(8,128)(2,1)} %collective-permute-done.10.refs_2_, bf16[768,512]{1,0:T(8,128)(2,1)} %collective-permute-done.7.refs_3_.refs_1_, bf16[768,512]{1,0:T(8,128)(2,1)} %get-tuple-element.154.refs_2_.refs_0_), kind=kLoop, calls=%fused_computation.5 | loop fusion | flops 786432 | bytes 983040 | tf_op jit(solution)/shard_map/convert_element_type | solution.py:1255
  158.0 3.0 %collective-permute-start.19 = (bf16[192,512]{1,0:T(8,128)(2,1)}, bf16[192,512]{1,0:T(8,128)(2,1)}, u32[]{:S(2)}, u32[]{:S(2)}) collective-permute-start(bf16[192,512]{1,0:T(8,128)(2,1)} %add_convert_fusion.2), channel_id=1, source_target_pairs={{0,0},{1,8},{2,16},{3,24},{4,1},{5,9},{6,17},{7,25},{8,2},{9,10},{... | collective-permute-start | bytes 589832 | tf_op jit(solution)/shard_map/ppermute | solution.py:1089
  161.0 3.0 %collective-permute-start.20 = (bf16[96,768]{1,0:T(8,128)(2,1)}, bf16[96,768]{1,0:T(8,128)(2,1)}, u32[]{:S(2)}, u32[]{:S(2)}) collective-permute-start(bf16[96,768]{1,0:T(8,128)(2,1)} %get-tuple-element.145), channel_id=1, source_target_pairs={{0,16},{4,20},{8,24},{12,28},{16,0},{20,4},{24,8},{28,12},{1,17},{... | collective-permute-start | bytes 442376 | tf_op jit(solution)/shard_map/ppermute | solution.py:1077
  164.1 2.6 %last_qkv.1 = (f32[96,192]{1,0:T(8,128)}, f32[128,192]{1,0:T(8,128)}, f32[128,192]{1,0:T(8,128)}, f32[32,192]{1,0:T(8,128)}) custom-call(s32[2]{0:T(128)} %pad_add_fusion.meta, bf16[400,576]{1,0:T(8,128)(2,1)} %get-tuple-element.150.refs_0_, bf16[400,576]{1,0:T(8,128)(2,1)} %collective-permute-done.9.refs_1_, ...), custom_call_target="tpu_custom_call" | custom-call | tf_op jit(solution)/shard_map/last_qkv/pallas_call | solution.py:910
  166.7 2.0 %collective-permute-start.22 = (f32[128,192]{1,0:T(8,128)}, f32[128,192]{1,0:T(8,128)}, u32[]{:S(2)}, u32[]{:S(2)}) collective-permute-start(f32[128,192]{1,0:T(8,128)} %get-tuple-element.164), channel_id=1, source_target_pairs={{0,2},{1,3},{2,0},{3,1},{4,6},{5,7},{6,4},{7,5},{8,10},{9,11},{10,... | collective-permute-start | bytes 294920 | tf_op jit(solution)/shard_map/ppermute | solution.py:1077
  168.7 3.5 %token_grad.1 = bf16[512,768]{1,0:T(8,128)(2,1)} custom-call(bf16[528,768]{1,0:T(8,128)(2,1)} %fusion.1.xa.refs_3_.x_ref, bf16[512,768]{1,0:T(8,128)(2,1)} %get-tuple-element.139.even, bf16[512,768]{1,0:T(8,128)(2,1)} %collective-permute-done.17.near, bf16[512,768]{1,0:T(8,128)(2,1)} %collective-permute-done.18.far, bf16[512,768]{1,0:T(8,128)(2,1)} %bitcast.12), custom_call_target="tpu_custom_call" | custom-call | tf_op jit(solution)/shard_map/token_grad/pallas_call | solution.py:1125
  172.1 6.6 %collective-permute-done.20.refs_3_ = bf16[96,768]{1,0:T(8,128)(2,1)} collective-permute-done((bf16[96,768]{1,0:T(8,128)(2,1)}, bf16[96,768]{1,0:T(8,128)(2,1)}, u32[]{:S(2)}, u32[]{:S(2)}) %collective-permute-start.20) | collective-permute-done | bytes 147488 | tf_op jit(solution)/shard_map/ppermute | solution.py:1077
  178.7 2.8 %lower.1 = (f32[192,384]{1,0:T(8,128)}, f32[96,192]{1,0:T(8,128)}, f32[96,768]{1,0:T(8,128)}) custom-call(s32[2]{0:T(128)} %pad_add_fusion.meta, bf16[192,512]{1,0:T(8,128)(2,1)} %collective-permute-done.19.piece, bf16[384,768]{1,0:T(8,128)(2,1)} %get-tuple-element.130.refs_0_.refs_3_, bf16[384,768]{1,0:T(8,128)(2,1)} %collective-permute-done.6.refs_1_.refs_4_, ...), custom_call_target="tpu_custom_call" | custom-call | tf_op jit(solution)/shard_map/lower/pallas_call | solution.py:910
  181.5 2.7 %assemble.1 = (f32[96,576]{1,0:T(8,128)}, f32[2304]{0:T(1024)}, f32[768]{0:T(1024)}, f32[3072]{0:T(1024)}, f32[768]{0:T(1024)}, /*index=5*/f32[768]{0:T(1024)}, f32[768]{0:T(1024)}, f32[768]{0:T(1024)}, f32[768]{0:T(1024)}) custom-call(s32[2]{0:T(128)} %pad_add_fusion.meta, f32[96,192]{1,0:T(8,128)} %get-tuple-element.162.kept, ...), custom_call_target="tpu_custom_call" | custom-call | tf_op jit(solution)/shard_map/assemble/pallas_call | solution.py:1043
  (45 shorter events, 12.7 us)
Async XLA Ops:
  0.6 6.0 %copy-start = (bf16[1,512,768]{2,1,0:T(8,128)(2,1)S(1)}, bf16[1,512,768]{2,1,0:T(8,128)(2,1)}, u32[]{:S(2)}) copy-start(bf16[1,512,768]{2,1,0:T(8,128)(2,1)} %param.33) | copy-start | bytes 2359300
  3.5 5.6 %collective-permute-start = (bf16[528,768]{1,0:T(8,128)(2,1)}, bf16[528,768]{1,0:T(8,128)(2,1)}, u32[]{:S(2)}, u32[]{:S(2)}) collective-permute-start(bf16[528,768]{1,0:T(8,128)(2,1)} %fusion.1.xa.refs_3_.x_ref), channel_id=1, source_target_pairs={{0,1},{1,0},{2,3},{3,2},{4,5},{5,4},{6,7},{7,6},{8,9},{9,8},{10,11... | collective-permute-start | bytes 2433032 | tf_op jit(solution)/shard_map/ppermute | solution.py:1077
  3.9 24.1 %collective-permute-start.2 = (bf16[528,768]{1,0:T(8,128)(2,1)}, bf16[528,768]{1,0:T(8,128)(2,1)}, u32[]{:S(2)}, u32[]{:S(2)}) collective-permute-start(bf16[528,768]{1,0:T(8,128)(2,1)} %fusion.1.xa.refs_3_.x_ref), channel_id=1, source_target_pairs={{0,2},{1,3},{2,0},{3,1},{4,6},{5,7},{6,4},{7,5},{8,10},{9,11},{10,... | collective-permute-start | bytes 2433032 | tf_op jit(solution)/shard_map/ppermute | solution.py:1077
  6.4 2.6 %collective-permute-start.1 = (bf16[512,768]{1,0:T(8,128)(2,1)}, bf16[512,768]{1,0:T(8,128)(2,1)}, u32[]{:S(2)}, u32[]{:S(2)}) collective-permute-start(bf16[512,768]{1,0:T(8,128)(2,1)} %bitcast.9), channel_id=1, source_target_pairs={{0,1},{1,0},{2,3},{3,2},{4,5},{5,4},{6,7},{7,6},{8,9},{9,8},{10,11... | collective-permute-start | bytes 2359304 | tf_op jit(solution)/shard_map/ppermute | solution.py:1077
  7.6 35.8 %collective-permute-start.4 = (bf16[544,768]{1,0:T(8,128)(2,1)}, bf16[544,768]{1,0:T(8,128)(2,1)}, u32[]{:S(2)}, u32[]{:S(2)}) collective-permute-start(bf16[544,768]{1,0:T(8,128)(2,1)} %pad.9), channel_id=1, source_target_pairs={{0,2},{1,3},{2,0},{3,1},{4,6},{5,7},{6,4},{7,5},{8,10},{9,11},{10,... | collective-permute-start | bytes 2506760 | tf_op jit(solution)/shard_map/ppermute | solution.py:1077
  28.0 6.1 %collective-permute-start.3 = (bf16[528,768]{1,0:T(8,128)(2,1)}, bf16[528,768]{1,0:T(8,128)(2,1)}, u32[]{:S(2)}, u32[]{:S(2)}) collective-permute-start(bf16[528,768]{1,0:T(8,128)(2,1)} %collective-permute-done.2.x_ref.refs_5_.xa), channel_id=1, source_target_pairs={{0,1},{1,0},{2,3},{3,2},{4,5},{5,4},{6,7},{7,6},{8,9},{9,8},{10,11... | collective-permute-start | bytes 2433032 | tf_op jit(solution)/shard_map/ppermute | solution.py:1077
  43.4 13.0 %collective-permute-start.5 = (bf16[544,768]{1,0:T(8,128)(2,1)}, bf16[544,768]{1,0:T(8,128)(2,1)}, u32[]{:S(2)}, u32[]{:S(2)}) collective-permute-start(bf16[544,768]{1,0:T(8,128)(2,1)} %collective-permute-done.4.ca), channel_id=1, source_target_pairs={{0,1},{1,0},{2,3},{3,2},{4,5},{5,4},{6,7},{7,6},{8,9},{9,8},{10,11... | collective-permute-start | bytes 2506760 | tf_op jit(solution)/shard_map/ppermute | solution.py:1077
  76.8 34.7 %collective-permute-start.8 = (bf16[2,512,768]{2,1,0:T(8,128)(2,1)}, bf16[2,512,768]{2,1,0:T(8,128)(2,1)}, u32[]{:S(2)}, u32[]{:S(2)}) collective-permute-start(bf16[2,512,768]{2,1,0:T(8,128)(2,1)} %get-tuple-element.135), channel_id=1, source_target_pairs={{0,1},{1,0},{2,3},{3,2},{4,5},{5,4},{6,7},{7,6},{8,9},{9,8},{10,11... | collective-permute-start | bytes 4718600 | tf_op jit(solution)/shard_map/ppermute | solution.py:1077
  77.4 34.1 %collective-permute-start.7 = (bf16[768,512]{1,0:T(8,128)(2,1)}, bf16[768,512]{1,0:T(8,128)(2,1)}, u32[]{:S(2)}, u32[]{:S(2)}) collective-permute-start(bf16[768,512]{1,0:T(8,128)(2,1)} %get-tuple-element.133), channel_id=1, source_target_pairs={{0,8},{4,12},{8,0},{12,4},{16,24},{20,28},{24,16},{28,20},{1,9},{5... | collective-permute-start | bytes 2359304 | tf_op jit(solution)/shard_map/ppermute | solution.py:1077
  78.9 32.6 %collective-permute-start.6 = (bf16[384,768]{1,0:T(8,128)(2,1)}, bf16[384,768]{1,0:T(8,128)(2,1)}, u32[]{:S(2)}, u32[]{:S(2)}) collective-permute-start(bf16[384,768]{1,0:T(8,128)(2,1)} %get-tuple-element.131), channel_id=1, source_target_pairs={{0,4},{4,0},{8,12},{12,8},{16,20},{20,16},{24,28},{28,24},{1,5},{5... | collective-permute-start | bytes 1769480 | tf_op jit(solution)/shard_map/ppermute | solution.py:1077
  111.4 15.0 %collective-permute-start.9 = (bf16[400,576]{1,0:T(8,128)(2,1)}, bf16[400,576]{1,0:T(8,128)(2,1)}, u32[]{:S(2)}, u32[]{:S(2)}) collective-permute-start(bf16[400,576]{1,0:T(8,128)(2,1)} %get-tuple-element.141), channel_id=1, source_target_pairs={{0,4},{4,0},{8,12},{12,8},{16,20},{20,16},{24,28},{28,24},{1,5},{5... | collective-permute-start | bytes 1382408 | tf_op jit(solution)/shard_map/ppermute | solution.py:1077
  115.1 28.2 %collective-permute-start.12 = (bf16[512,768]{1,0:T(8,128)(2,1)}, bf16[512,768]{1,0:T(8,128)(2,1)}, u32[]{:S(2)}, u32[]{:S(2)}) collective-permute-start(bf16[512,768]{1,0:T(8,128)(2,1)} %get-tuple-element.136), channel_id=1, source_target_pairs={{0,2},{1,3},{2,0},{3,1},{4,6},{5,7},{6,4},{7,5},{8,10},{9,11},{10,... | collective-permute-start | bytes 2359304 | tf_op jit(solution)/shard_map/ppermute | solution.py:1077
  123.6 19.7 %collective-permute-start.13 = (bf16[512,768]{1,0:T(8,128)(2,1)}, bf16[512,768]{1,0:T(8,128)(2,1)}, u32[]{:S(2)}, u32[]{:S(2)}) collective-permute-start(bf16[512,768]{1,0:T(8,128)(2,1)} %get-tuple-element.149), channel_id=1, source_target_pairs={{0,1},{1,0},{2,3},{3,2},{4,5},{5,4},{6,7},{7,6},{8,9},{9,8},{10,11... | collective-permute-start | bytes 2359304 | tf_op jit(solution)/shard_map/ppermute | solution.py:1077
  123.7 10.9 %collective-permute-start.11 = (bf16[192,768]{1,0:T(8,128)(2,1)}, bf16[192,768]{1,0:T(8,128)(2,1)}, u32[]{:S(2)}, u32[]{:S(2)}) collective-permute-start(bf16[192,768]{1,0:T(8,128)(2,1)} %get-tuple-element.144), channel_id=1, source_target_pairs={{0,8},{4,12},{8,0},{12,4},{16,24},{20,28},{24,16},{28,20},{1,9},{5... | collective-permute-start | bytes 884744 | tf_op jit(solution)/shard_map/ppermute | solution.py:1077
  126.4 11.5 %collective-permute-start.10 = (bf16[384,512]{1,0:T(8,128)(2,1)}, bf16[384,512]{1,0:T(8,128)(2,1)}, u32[]{:S(2)}, u32[]{:S(2)}) collective-permute-start(bf16[384,512]{1,0:T(8,128)(2,1)} %get-tuple-element.143), channel_id=1, source_target_pairs={{0,4},{4,0},{8,12},{12,8},{16,20},{20,16},{24,28},{28,24},{1,5},{5... | collective-permute-start | bytes 1179656 | tf_op jit(solution)/shard_map/ppermute | solution.py:1077
  129.0 17.2 %collective-permute-start.14 = (bf16[208,576]{1,0:T(8,128)(2,1)}, bf16[208,576]{1,0:T(8,128)(2,1)}, u32[]{:S(2)}, u32[]{:S(2)}) collective-permute-start(bf16[208,576]{1,0:T(8,128)(2,1)} %pad_maximum_fusion), channel_id=1, source_target_pairs={{0,8},{4,12},{8,0},{12,4},{16,24},{20,28},{24,16},{28,20},{1,9},{5... | collective-permute-start | bytes 718856 | tf_op jit(solution)/shard_map/ppermute | solution.py:1077
  134.6 32.1 %collective-permute-start.17 = (bf16[512,768]{1,0:T(8,128)(2,1)}, bf16[512,768]{1,0:T(8,128)(2,1)}, u32[]{:S(2)}, u32[]{:S(2)}) collective-permute-start(bf16[512,768]{1,0:T(8,128)(2,1)} %get-tuple-element.158), channel_id=1, source_target_pairs={{0,1},{1,0},{2,3},{3,2},{4,5},{5,4},{6,7},{7,6},{8,9},{9,8},{10,11... | collective-permute-start | bytes 2359304 | tf_op jit(solution)/shard_map/ppermute | solution.py:1077
  140.6 15.4 %collective-permute-start.15 = (bf16[192,512]{1,0:T(8,128)(2,1)}, bf16[192,512]{1,0:T(8,128)(2,1)}, u32[]{:S(2)}, u32[]{:S(2)}) collective-permute-start(bf16[192,512]{1,0:T(8,128)(2,1)} %get-tuple-element.147), channel_id=1, source_target_pairs={{0,16},{4,20},{8,24},{12,28},{16,0},{20,4},{24,8},{28,12},{1,17},{... | collective-permute-start | bytes 589832 | tf_op jit(solution)/shard_map/ppermute | solution.py:1077
  145.8 22.9 %collective-permute-start.18 = (bf16[512,768]{1,0:T(8,128)(2,1)}, bf16[512,768]{1,0:T(8,128)(2,1)}, u32[]{:S(2)}, u32[]{:S(2)}) collective-permute-start(bf16[512,768]{1,0:T(8,128)(2,1)} %add_convert_fusion), channel_id=1, source_target_pairs={{0,2},{1,3},{2,0},{3,1},{4,6},{5,7},{6,4},{7,5},{8,10},{9,11},{10,... | collective-permute-start | bytes 2359304 | tf_op jit(solution)/shard_map/ppermute | solution.py:1077
  148.7 15.3 %collective-permute-start.16 = (bf16[112,576]{1,0:T(8,128)(2,1)}, bf16[112,576]{1,0:T(8,128)(2,1)}, u32[]{:S(2)}, u32[]{:S(2)}) collective-permute-start(bf16[112,576]{1,0:T(8,128)(2,1)} %pad_maximum_fusion.1.refs_4_), channel_id=1, source_target_pairs={{0,16},{4,20},{8,24},{12,28},{16,0},{20,4},{24,8},{28,12},{1,17},{... | collective-permute-start | bytes 387080 | tf_op jit(solution)/shard_map/ppermute | solution.py:1077
  158.0 20.7 %collective-permute-start.19 = (bf16[192,512]{1,0:T(8,128)(2,1)}, bf16[192,512]{1,0:T(8,128)(2,1)}, u32[]{:S(2)}, u32[]{:S(2)}) collective-permute-start(bf16[192,512]{1,0:T(8,128)(2,1)} %add_convert_fusion.2), channel_id=1, source_target_pairs={{0,0},{1,8},{2,16},{3,24},{4,1},{5,9},{6,17},{7,25},{8,2},{9,10},{... | collective-permute-start | bytes 589832 | tf_op jit(solution)/shard_map/ppermute | solution.py:1089
  161.0 17.7 %collective-permute-start.20 = (bf16[96,768]{1,0:T(8,128)(2,1)}, bf16[96,768]{1,0:T(8,128)(2,1)}, u32[]{:S(2)}, u32[]{:S(2)}) collective-permute-start(bf16[96,768]{1,0:T(8,128)(2,1)} %get-tuple-element.145), channel_id=1, source_target_pairs={{0,16},{4,20},{8,24},{12,28},{16,0},{20,4},{24,8},{28,12},{1,17},{... | collective-permute-start | bytes 442376 | tf_op jit(solution)/shard_map/ppermute | solution.py:1077
  166.7 14.8 %collective-permute-start.21 = (f32[128,192]{1,0:T(8,128)}, f32[128,192]{1,0:T(8,128)}, u32[]{:S(2)}, u32[]{:S(2)}) collective-permute-start(f32[128,192]{1,0:T(8,128)} %get-tuple-element.163), channel_id=1, source_target_pairs={{0,1},{1,0},{2,3},{3,2},{4,5},{5,4},{6,7},{7,6},{8,9},{9,8},{10,11... | collective-permute-start | bytes 294920 | tf_op jit(solution)/shard_map/ppermute | solution.py:1077
  166.7 14.8 %collective-permute-start.22 = (f32[128,192]{1,0:T(8,128)}, f32[128,192]{1,0:T(8,128)}, u32[]{:S(2)}, u32[]{:S(2)}) collective-permute-start(f32[128,192]{1,0:T(8,128)} %get-tuple-element.164), channel_id=1, source_target_pairs={{0,2},{1,3},{2,0},{3,1},{4,6},{5,7},{6,4},{7,5},{8,10},{9,11},{10,... | collective-permute-start | bytes 294920 | tf_op jit(solution)/shard_map/ppermute | solution.py:1077
  168.7 12.8 %collective-permute-start.23 = (f32[32,192]{1,0:T(8,128)}, f32[32,192]{1,0:T(8,128)}, u32[]{:S(2)}, u32[]{:S(2)}) collective-permute-start(f32[32,192]{1,0:T(8,128)} %get-tuple-element.156.small), channel_id=1, source_target_pairs={{0,3},{1,2},{2,1},{3,0},{4,7},{5,6},{6,5},{7,4},{8,11},{9,10},{10,... | collective-permute-start | bytes 73736 | tf_op jit(solution)/shard_map/ppermute | solution.py:1077

commit v9 on v8

--- a/solution.py
+++ b/solution.py
@@ -957,9 +957,7 @@
     )(meta, *args)
 
 
-def lower_kernel(meta, piece, *refs):
-    *terms, down_ref, out_ref, up_ref = refs
-    up_ref[...] = add_up(terms)
+def lower_kernel(meta, piece, down_ref, out_ref):
     cut = down_ref.shape[1]
     down_ref[...] = piece[:, :cut].astype(F32)
     out_ref[...] = piece[:, cut:].astype(F32).T[: out_ref.shape[0]]
@@ -1231,23 +1229,19 @@
         qkv_send = jnp.concatenate([next_send(joined, half), tail])
         joined.append(swap(qkv_send, "rows", 2))
         meta = after(meta, qkv_send)
-        low_send, up_send = block_sums(
-            "second_sums",
-            meta,
-            1,
-            (width, [(term, width) for term in lower]),
-            (chunk, [(term, chunk) for term in up]),
-        )
+        low_send = next_send(lower, half)
         lower.append(swap(low_send, "rows", low_masks[2]))
-        up.append(swap(up_send, "rows", up_masks[2]))
         e_send = after(e_send, low_send, out_far)
     e_send = add_low(e_send, e_last)
     e_far = swap(e_send, "blk", 2)
     if fits(rows):
-        joined[0] = after(joined[0], up_send, e_send)
-        tail = add_low(after(qkv_send, up_send, e_send)[half // 2 :], joined[2][half // 2 :])
+        joined[0] = after(joined[0], e_send)
+        tail = add_low(after(qkv_send, e_send)[half // 2 :], joined[2][half // 2 :])
         qkv_send = jnp.concatenate([next_send(joined, half // 2), tail])
         joined.append(swap(qkv_send, "rows", 4))
+        up[0] = after(up[0], qkv_send)
+        up_send = next_send(up, half // 2)
+        up.append(swap(up_send, "rows", up_masks[2]))
         out_args = (after(tok_own, qkv_send), out_even, out_got, out_far, b_out, b_down)
         result = finish(result_kernel, "result", seq, *out_args)
         meta = after(meta, result)
@@ -1271,14 +1265,15 @@
         tok_args = (after(tok_own, small), e_own, e_near, e_far, cot_own)
         grad_tokens = finish(token_kernel, "token_grad", seq, *tok_args)
         meta = after(meta, grad_tokens)
-        ends = [((width, hid // 2), F32), ((width // 2, width), F32), ((chunk, hid), F32)]
-        specs = [whole(piece.shape)] + [pl.BlockSpec((chunk, hid), lambda i, m: (0, 0))] * 4
-        down, out_w, up = simple(lower_kernel, "lower", ends, meta, piece, *up, specs=specs)
+        ends = [((width, hid // 2), F32), ((width // 2, width), F32)]
+        down, out_w = simple(lower_kernel, "lower", ends, meta, piece)
         meta = after(meta, down)
         down = down.T
         qkv, gb_qkv, gb_out, gb_up, gb_down, *norms = assemble(
             meta, kept, small, near, far, diag
         )
+        up[0] = after(up[0], qkv)
+        up = sum(term[:chunk].astype(F32) for term in up)
     else:
         up = reduce_plain(up_keep, up_got, up_masks[1:])
         weights = reduce_plain(low_keep, low_got, low_masks[1:])

time: 184 us -> 180 us (0.978)
  waiting for transfers between devices: 23 us -> 10.7 us
  starting transfers between devices: 26.5 us -> 34.2 us
  Pallas kernels: 119 us -> 116 us
  other arithmetic: 13 us -> 15.9 us
    ppermute x23, waiting for transfers between devices: 23 us -> 10.7 us  [swap(): return lax.ppermute(value, axis, [(i, i ^ mask) for i in range(size)])]
    ppermute x23, starting transfers between devices: 23.5 us -> 31.2 us  [swap(): return lax.ppermute(value, axis, [(i, i ^ mask) for i in range(size)])]
    convert_element_type x2 -> x4, other arithmetic: 2.19 us -> 5.91 us  [next_send(): sum((term[size // 2:size].astype(F32) for term in terms)).astype(BF16)]
    pallas_call x2 -> x1, Pallas kernels: 6.3 us -> 3.56 us  [block_sums(): pl.pallas_call(partial(sums_kernel, [len(terms) for _, terms in jobs]), o...]
    convert_element_type x3, other arithmetic: 3.95 us -> 1.9 us  [add_low(): return (left.astype(F32) + right.astype(F32)).astype(BF16)]
    add x0 -> x1, other arithmetic: none -> 1.91 us  [local(): up = sum((term[:chunk].astype(F32) for term in up))]
  transfers between devices with their start and end apart: 24 -> 24, of which waited for: 6 -> 3; matrix products, arithmetic and copies ran while one was open for 6% -> 7% of each run, Pallas kernels for 52% -> 53%
where the time goes in v9:
time: 180 us; the launch traced here: 179 us
  Pallas kernels  116 us (64%)
  starting transfers between devices  34.2 us (19%)
  other arithmetic  15.9 us (9%)
  waiting for transfers between devices  10.7 us (6%)
    pallas_call x2, Pallas kernels, feed_forward(): pl.pallas_call(body, out_shape=outs, grid_spec=pltpu.PrefetchScalarGridSp...  39.4 us
    ppermute x23, starting transfers between devices, swap(): return lax.ppermute(value, axis, [(i, i ^ mask) for i in range(size)])  31.2 us
    pallas_call x1, Pallas kernels, attend_back(): pl.pallas_call(partial(attend_back_kernel, per), out_shape=jax.ShapeDtype...  21.1 us
    pallas_call x1, Pallas kernels, attend(): pl.pallas_call(partial(attend_kernel, per), out_shape=[jax.ShapeDtypeStru...  13 us
    ppermute x23, waiting for transfers between devices, swap(): return lax.ppermute(value, axis, [(i, i ^ mask) for i in range(size)])  10.7 us
    pallas_call x2, Pallas kernels, project(): pl.pallas_call(partial(qkv_kernel, slot), out_shape=outs, grid_spec=pltpu...  9.76 us
    pallas_call x1, Pallas kernels, joined_weight(): pl.pallas_call(partial(weight_kernel, rows), out_shape=[jax.ShapeDtypeStr...  8.52 us
    pallas_call x1, Pallas kernels, norm_grad(): pl.pallas_call(norm_kernel, out_shape=[jax.ShapeDtypeStruct((seq, D), BF1...  7.02 us
  transfers between devices with their start and end apart: 24, of which 3 were waited for; matrix products, arithmetic and copies ran while one was open for 7% of the time, Pallas kernels for 53%

profile of v9, /device:TPU:0, one launch (start us, length us, event | category | flops | bytes accessed | tf_op | source)
XLA Modules:
  0.0 179.4 jit_solution(18227980138480248852)
XLA Ops:
  1.4 2.1 %fusion.1.xa.refs_3_.x_ref = bf16[528,768]{1,0:T(8,128)(2,1)} fusion(bf16[1,512]{1,0:T(2,128)(2,1)S(1)} %convert_element_type.106, bf16[512,768]{1,0:T(8,128)(2,1)} %bitcast.16), kind=kLoop, calls=%fused_computation.3 | loop fusion | flops 2433024 | bytes 1598464 | tf_op jit(solution)/shard_map/concatenate | solution.py:1150
  3.9 2.5 %collective-permute-start.2 = (bf16[528,768]{1,0:T(8,128)(2,1)}, bf16[528,768]{1,0:T(8,128)(2,1)}, u32[]{:S(2)}, u32[]{:S(2)}) collective-permute-start(bf16[528,768]{1,0:T(8,128)(2,1)} %fusion.1.xa.refs_3_.x_ref), channel_id=1, source_target_pairs={{0,2},{1,3},{2,0},{3,1},{4,6},{5,7},{6,4},{7,5},{8,10},{9,11},{10,... | collective-permute-start | bytes 2433032 | tf_op jit(solution)/shard_map/ppermute | solution.py:1075
  9.1 18.9 %mlp_first.1 = (bf16[1024,768]{1,0:T(8,128)(2,1)}, bf16[2048,768]{1,0:T(8,128)(2,1)}, bf16[2048,768]{1,0:T(8,128)(2,1)}, bf16[2048,192]{1,0:T(8,128)(2,1)}, f32[...) custom-call(s32[2]{0:T(128)} %pad_add_fusion.meta, ...), custom_call_target="tpu_custom_call" | custom-call | tf_op jit(solution)/shard_map/mlp_first/pallas_call | solution.py:503
  29.5 4.6 %qkv_2.1 = (bf16[2048,192]{1,0:T(8,128)(2,1)}, bf16[2048,192]{1,0:T(8,128)(2,1)}, bf16[2048,192]{1,0:T(8,128)(2,1)}) custom-call(s32[2]{0:T(128)} %pad_add_fusion.meta, s32[1]{0:T(128)S(6)} %copy.50.valid, bf16[528,768]{1,0:T(8,128)(2,1)} %collective-permute-done.2.x_ref.refs_5_.xa, ...), custom_call_target="tpu_custom_call", output_to_operand_aliasing={{0}: (9, {}), {1}: (10, {}), {2}: (11, {})} | custom-call | tf_op jit(solution)/shard_map/qkv_2/pallas_call | solution.py:196
  34.1 5.2 %qkv_3.1 = (bf16[2048,192]{1,0:T(8,128)(2,1)}, bf16[2048,192]{1,0:T(8,128)(2,1)}, bf16[2048,192]{1,0:T(8,128)(2,1)}, s32[8,1,256]{2,1,0:T(1,128)}, s32[8]{0:T(128)}, /*index=5*/s32[8]{0:T(128)}) custom-call(s32[2]{0:T(128)} %pad_add_fusion.meta, s32[1]{0:T(128)S(6)} %copy.50.valid, ...), custom_call_target="tpu_custom_call", output_to_operand_aliasing={{0}: (9, {}), {1}: (10, {}), {2}: (11, {})} | custom-call | tf_op jit(solution)/shard_map/qkv_3/pallas_call | solution.py:196
  39.3 4.1 %collective-permute-done.4.ca = bf16[544,768]{1,0:T(8,128)(2,1)} collective-permute-done((bf16[544,768]{1,0:T(8,128)(2,1)}, bf16[544,768]{1,0:T(8,128)(2,1)}, u32[]{:S(2)}, u32[]{:S(2)}) %collective-permute-start.4) | collective-permute-done | bytes 835616 | tf_op jit(solution)/shard_map/ppermute | solution.py:1075
  43.4 13.0 %attend.1 = (bf16[2048,192]{1,0:T(8,128)(2,1)}, f32[3,8,1,256]{3,2,1,0:T(1,128)}) custom-call(s32[2]{0:T(128)} %pad_add_fusion.meta, s32[8]{0:T(128)} %get-tuple-element.105.lo, s32[8]{0:T(128)} %get-tuple-element.106.hi, bf16[2048,192]{1,0:T(8,128)(2,1)} %get-tuple-element.107.q_ref, bf16[2048,192]{1,0:T(8,128)(2,1)} %get-tuple-element.108.k_ref, ...), custom_call_target="tpu_custom_call" | custom-call | tf_op jit(solution)/shard_map/attend/pallas_call | solution.py:630
  56.4 20.4 %mlp_second.1 = (bf16[2048,768]{1,0:T(8,128)(2,1)}, bf16[2048,768]{1,0:T(8,128)(2,1)}, bf16[2048,192]{1,0:T(8,128)(2,1)}, f32[8,768]{1,0:T(8,128)}, bf16[2,512,7...) custom-call(s32[2]{0:T(128)} %pad_add_fusion.meta, ...), custom_call_target="tpu_custom_call", output_to_operand_aliasing={{0}: (19, {}), {1}: (20, {}), {2}: (21, {})} | custom-call | tf_op jit(solution)/shard_map/mlp_second/pallas_call | solution.py:503
  77.4 2.6 %collective-permute-start.7 = (bf16[768,512]{1,0:T(8,128)(2,1)}, bf16[768,512]{1,0:T(8,128)(2,1)}, u32[]{:S(2)}, u32[]{:S(2)}) collective-permute-start(bf16[768,512]{1,0:T(8,128)(2,1)} %get-tuple-element.132), channel_id=1, source_target_pairs={{0,8},{4,12},{8,0},{12,4},{16,24},{20,28},{24,16},{28,20},{1,9},{5... | collective-permute-start | bytes 2359304 | tf_op jit(solution)/shard_map/ppermute | solution.py:1075
  80.0 1.2 collective-permute-start.6
  81.2 21.1 %attend_back.1.refs_0_.refs_1_.refs_2_.refs_3_ = bf16[2048,576]{1,0:T(8,128)(2,1)} custom-call(s32[2]{0:T(128)} %pad_add_fusion.meta, s32[8]{0:T(128)} %get-tuple-element.105.lo, s32[8]{0:T(128)} %get-tuple-element.106.hi, bf16[2048,192]{1,0:T(8,128)(2,1)} %get-tuple-element.107.q_ref, bf16[2048,192]{1,0:T(8,128)(2,1)} %get-tuple-element.108.k_ref, ...), custom_call_target="tpu_custom_call" | custom-call | tf_op jit(solution)/shard_map/attend_back/pallas_call | solution.py:761
  102.3 8.5 %joined_weight.1 = (bf16[400,576]{1,0:T(8,128)(2,1)}, bf16[400,576]{1,0:T(8,128)(2,1)}, f32[16,576]{1,0:T(8,128)}) custom-call(s32[2]{0:T(128)} %pad_add_fusion.meta, bf16[2048,576]{1,0:T(8,128)(2,1)} %attend_back.1.refs_0_.refs_1_.refs_2_.refs_3_, bf16[2048,768]{1,0:T(8,128)(2,1)} %get-tuple-element.126.refs_1_, f32[768]{0:T(1024)} %refs_8_.1, ...), custom_call_target="tpu_custom_call" | custom-call | tf_op jit(solution)/shard_map/joined_weight/pallas_call | solution.py:858
  110.8 2.8 %collective-permute-start.12 = (bf16[400,576]{1,0:T(8,128)(2,1)}, bf16[400,576]{1,0:T(8,128)(2,1)}, u32[]{:S(2)}, u32[]{:S(2)}) collective-permute-start(bf16[400,576]{1,0:T(8,128)(2,1)} %get-tuple-element.145), channel_id=1, source_target_pairs={{0,4},{4,0},{8,12},{12,8},{16,20},{20,16},{24,28},{28,24},{1,5},{5... | collective-permute-start | bytes 1382408 | tf_op jit(solution)/shard_map/ppermute | solution.py:1075
  113.6 3.6 %first_sums.1 = (bf16[192,768]{1,0:T(8,128)(2,1)}, bf16[384,512]{1,0:T(8,128)(2,1)}, bf16[512,768]{1,0:T(8,128)(2,1)}) custom-call(s32[2]{0:T(128)} %pad_add_fusion.meta, bf16[384,768]{1,0:T(8,128)(2,1)} %get-tuple-element.164.refs_0_, bf16[384,768]{1,0:T(8,128)(2,1)} %collective-permute-done.6.refs_1_, bf16[768,512]{1,0:T(8,128)(2,1)} %get-tuple-element.150.refs_2_, ...), custom_call_target="tpu_custom_call" | custom-call | tf_op jit(solution)/shard_map/first_sums/pallas_call | solution.py:948
  117.2 1.6 collective-permute-start.10
  118.8 7.0 %norm_grad.1 = (bf16[512,768]{1,0:T(8,128)(2,1)}, bf16[512,768]{1,0:T(8,128)(2,1)}, bf16[512,768]{1,0:T(8,128)(2,1)}, bf16[512,768]{1,0:T(8,128)(2,1)}) custom-call(s32[2]{0:T(128)} %pad_add_fusion.meta, bf16[2048,576]{1,0:T(8,128)(2,1)} %attend_back.1.refs_0_.refs_1_.refs_2_.refs_3_, bf16[2048,576]{1,0:T(8,128)(2,1)} %attend_back.1.refs_0_.refs_1_.refs_2_.refs_3_, ...), custom_call_target="tpu_custom_call" | custom-call | tf_op jit(solution)/shard_map/norm_grad/pallas_call | solution.py:889
  126.8 1.1 add_convert_fusion.1
  127.9 1.9 %collective-permute-start.13 = (bf16[208,576]{1,0:T(8,128)(2,1)S(1)}, bf16[208,576]{1,0:T(8,128)(2,1)S(1)}, u32[]{:S(2)}, u32[]{:S(2)}) collective-permute-start(bf16[208,576]{1,0:T(8,128)(2,1)S(1)} %pad_maximum_fusion), channel_id=1, source_target_pairs={{0,8},{4,12},{8,0},{12,4},{16,24},{20,28},{24,16},{28,20},{1,9},{5... | collective-permute-start | bytes 718856 | tf_op jit(solution)/shard_map/ppermute | solution.py:1075
  130.0 6.0 %collective-permute-done.9 = bf16[384,512]{1,0:T(8,128)(2,1)S(1)} collective-permute-done((bf16[384,512]{1,0:T(8,128)(2,1)}, bf16[384,512]{1,0:T(8,128)(2,1)S(1)}, u32[]{:S(2)}, u32[]{:S(2)}) %collective-permute-start.9) | collective-permute-done | bytes 393248 | tf_op jit(solution)/shard_map/ppermute | solution.py:1075
  136.0 1.9 %add_convert_fusion.3 = bf16[192,512]{1,0:T(8,128)(2,1)} fusion(bf16[384,512]{1,0:T(8,128)(2,1)S(1)} %collective-permute-done.9, bf16[768,512]{1,0:T(8,128)(2,1)} %collective-permute-done.7.refs_3_, bf16[768,512]{1,0:T(8,128)(2,1)} %get-tuple-element.150.refs_2_), kind=kLoop, calls=%fused_computation.6 | loop fusion | flops 589824 | bytes 786432 | tf_op jit(solution)/shard_map/convert_element_type | solution.py:1058
  137.9 3.4 %collective-permute-start.14 = (bf16[192,512]{1,0:T(8,128)(2,1)}, bf16[192,512]{1,0:T(8,128)(2,1)}, u32[]{:S(2)}, u32[]{:S(2)}) collective-permute-start(bf16[192,512]{1,0:T(8,128)(2,1)} %add_convert_fusion.3), channel_id=1, source_target_pairs={{0,16},{4,20},{8,24},{12,28},{16,0},{20,4},{24,8},{28,12},{1,17},{... | collective-permute-start | bytes 589832 | tf_op jit(solution)/shard_map/ppermute | solution.py:1075
  144.8 2.8 %result.1 = bf16[512,768]{1,0:T(8,128)(2,1)} custom-call(bf16[528,768]{1,0:T(8,128)(2,1)} %fusion.1.xa.refs_3_.x_ref, bf16[2,512,768]{2,1,0:T(8,128)(2,1)} %get-tuple-element.133.even, bf16[2,512,768]{2,1,0:T(8,128)(2,1)} %collective-permute-done.8.near, bf16[512,768]{1,0:T(8,128)(2,1)} %collective-permute-done.10.far, f32[768]{0:T(1024)} %b_out.1, f32[768]{0:T(1024)} %b_down.1), custom_call_target="tpu_custom_call" | custom-call | tf_op jit(solution)/shard_map/result/pallas_call | solution.py:1123
  147.6 2.0 %add_convert_fusion.2 = bf16[192,512]{1,0:T(8,128)(2,1)} fusion(bf16[192,512]{1,0:T(8,128)(2,1)} %collective-permute-done.14, bf16[384,512]{1,0:T(8,128)(2,1)} %copy-done.3, bf16[768,512]{1,0:T(8,128)(2,1)} %collective-permute-done.7.refs_3_, bf16[768,512]{1,0:T(8,128)(2,1)} %get-tuple-element.150.refs_2_), kind=kLoop, calls=%fused_computation.5 | loop fusion | flops 786432 | bytes 983040 | tf_op jit(solution)/shard_map/convert_element_type | solution.py:1249
  149.6 3.0 %collective-permute-start.18 = (bf16[192,512]{1,0:T(8,128)(2,1)}, bf16[192,512]{1,0:T(8,128)(2,1)}, u32[]{:S(2)}, u32[]{:S(2)}) collective-permute-start(bf16[192,512]{1,0:T(8,128)(2,1)} %add_convert_fusion.2), channel_id=1, source_target_pairs={{0,0},{1,8},{2,16},{3,24},{4,1},{5,9},{6,17},{7,25},{8,2},{9,10},{... | collective-permute-start | bytes 589832 | tf_op jit(solution)/shard_map/ppermute | solution.py:1087
  152.6 1.8 add_convert_fusion.4
  154.4 10.1 %collective-permute-start.23 = (bf16[96,768]{1,0:T(8,128)(2,1)}, bf16[96,768]{1,0:T(8,128)(2,1)}, u32[]{:S(2)}, u32[]{:S(2)}) collective-permute-start(bf16[96,768]{1,0:T(8,128)(2,1)} %add_convert_fusion.4), channel_id=1, source_target_pairs={{0,16},{4,20},{8,24},{12,28},{16,0},{20,4},{24,8},{28,12},{1,17},{... | collective-permute-start | bytes 442376 | tf_op jit(solution)/shard_map/ppermute | solution.py:1075
  164.5 2.6 %last_qkv.1 = (f32[96,192]{1,0:T(8,128)}, f32[128,192]{1,0:T(8,128)}, f32[128,192]{1,0:T(8,128)}, f32[32,192]{1,0:T(8,128)}) custom-call(s32[2]{0:T(128)} %pad_add_fusion.meta, bf16[400,576]{1,0:T(8,128)(2,1)} %get-tuple-element.144.refs_0_, bf16[400,576]{1,0:T(8,128)(2,1)} %collective-permute-done.12.refs_1_, bf16[208,576]{1,0:T(8,128)(2,1)} %copy-done.2, ...), custom_call_target="tpu_custom_call" | custom-call | tf_op jit(solution)/shard_map/last_qkv/pallas_call | solution.py:910
  167.1 1.6 collective-permute-start.20
  169.0 3.4 %token_grad.1 = bf16[512,768]{1,0:T(8,128)(2,1)} custom-call(bf16[528,768]{1,0:T(8,128)(2,1)} %fusion.1.xa.refs_3_.x_ref, bf16[512,768]{1,0:T(8,128)(2,1)} %get-tuple-element.138.even, bf16[512,768]{1,0:T(8,128)(2,1)} %collective-permute-done.16.near, bf16[512,768]{1,0:T(8,128)(2,1)} %collective-permute-done.17.far, bf16[512,768]{1,0:T(8,128)(2,1)} %bitcast.12), custom_call_target="tpu_custom_call" | custom-call | tf_op jit(solution)/shard_map/token_grad/pallas_call | solution.py:1123
  172.4 2.4 %lower.1 = (f32[192,384]{1,0:T(8,128)}, f32[96,192]{1,0:T(8,128)}) custom-call(s32[2]{0:T(128)} %pad_add_fusion.meta, bf16[192,512]{1,0:T(8,128)(2,1)} %collective-permute-done.18.piece), custom_call_target="tpu_custom_call" | custom-call | tf_op jit(solution)/shard_map/lower/pallas_call | solution.py:910
  174.8 2.7 %assemble.1 = (f32[96,576]{1,0:T(8,128)}, f32[2304]{0:T(1024)}, f32[768]{0:T(1024)}, f32[3072]{0:T(1024)}, f32[768]{0:T(1024)}, /*index=5*/f32[768]{0:T(1024)}, f32[768]{0:T(1024)}, f32[768]{0:T(1024)}, f32[768]{0:T(1024)}) custom-call(s32[2]{0:T(128)} %pad_add_fusion.meta, f32[96,192]{1,0:T(8,128)} %get-tuple-element.158.kept, ...), custom_call_target="tpu_custom_call" | custom-call | tf_op jit(solution)/shard_map/assemble/pallas_call | solution.py:1041
  177.5 1.9 %convert_add_fusion = f32[96,768]{1,0:T(8,128)} fusion(bf16[96,768]{1,0:T(8,128)(2,1)} %collective-permute-done.23, bf16[192,768]{1,0:T(8,128)(2,1)} %collective-permute-done.22, bf16[384,768]{1,0:T(8,128)(2,1)} %collective-permute-done.6.refs_1_, bf16[384,768]{1,0:T(8,128)(2,1)} %get-tuple-element.164.refs_0_), kind=kLoop, calls=%fused_computation.7 | loop fusion | flops 516096 | bytes 884736 | tf_op jit(solution)/shard_map/add | solution.py:1276
  (53 shorter events, 10.2 us)
Async XLA Ops:
  0.6 6.0 %copy-start = (bf16[1,512,768]{2,1,0:T(8,128)(2,1)S(1)}, bf16[1,512,768]{2,1,0:T(8,128)(2,1)}, u32[]{:S(2)}) copy-start(bf16[1,512,768]{2,1,0:T(8,128)(2,1)} %param.33) | copy-start | bytes 2359300
  3.5 5.6 %collective-permute-start = (bf16[528,768]{1,0:T(8,128)(2,1)}, bf16[528,768]{1,0:T(8,128)(2,1)}, u32[]{:S(2)}, u32[]{:S(2)}) collective-permute-start(bf16[528,768]{1,0:T(8,128)(2,1)} %fusion.1.xa.refs_3_.x_ref), channel_id=1, source_target_pairs={{0,1},{1,0},{2,3},{3,2},{4,5},{5,4},{6,7},{7,6},{8,9},{9,8},{10,11... | collective-permute-start | bytes 2433032 | tf_op jit(solution)/shard_map/ppermute | solution.py:1075
  3.9 24.1 %collective-permute-start.2 = (bf16[528,768]{1,0:T(8,128)(2,1)}, bf16[528,768]{1,0:T(8,128)(2,1)}, u32[]{:S(2)}, u32[]{:S(2)}) collective-permute-start(bf16[528,768]{1,0:T(8,128)(2,1)} %fusion.1.xa.refs_3_.x_ref), channel_id=1, source_target_pairs={{0,2},{1,3},{2,0},{3,1},{4,6},{5,7},{6,4},{7,5},{8,10},{9,11},{10,... | collective-permute-start | bytes 2433032 | tf_op jit(solution)/shard_map/ppermute | solution.py:1075
  6.4 2.6 %collective-permute-start.1 = (bf16[512,768]{1,0:T(8,128)(2,1)}, bf16[512,768]{1,0:T(8,128)(2,1)}, u32[]{:S(2)}, u32[]{:S(2)}) collective-permute-start(bf16[512,768]{1,0:T(8,128)(2,1)} %bitcast.9), channel_id=1, source_target_pairs={{0,1},{1,0},{2,3},{3,2},{4,5},{5,4},{6,7},{7,6},{8,9},{9,8},{10,11... | collective-permute-start | bytes 2359304 | tf_op jit(solution)/shard_map/ppermute | solution.py:1075
  7.6 35.8 %collective-permute-start.4 = (bf16[544,768]{1,0:T(8,128)(2,1)}, bf16[544,768]{1,0:T(8,128)(2,1)}, u32[]{:S(2)}, u32[]{:S(2)}) collective-permute-start(bf16[544,768]{1,0:T(8,128)(2,1)} %pad.9), channel_id=1, source_target_pairs={{0,2},{1,3},{2,0},{3,1},{4,6},{5,7},{6,4},{7,5},{8,10},{9,11},{10,... | collective-permute-start | bytes 2506760 | tf_op jit(solution)/shard_map/ppermute | solution.py:1075
  28.0 6.1 %collective-permute-start.3 = (bf16[528,768]{1,0:T(8,128)(2,1)}, bf16[528,768]{1,0:T(8,128)(2,1)}, u32[]{:S(2)}, u32[]{:S(2)}) collective-permute-start(bf16[528,768]{1,0:T(8,128)(2,1)} %collective-permute-done.2.x_ref.refs_5_.xa), channel_id=1, source_target_pairs={{0,1},{1,0},{2,3},{3,2},{4,5},{5,4},{6,7},{7,6},{8,9},{9,8},{10,11... | collective-permute-start | bytes 2433032 | tf_op jit(solution)/shard_map/ppermute | solution.py:1075
  43.4 13.0 %collective-permute-start.5 = (bf16[544,768]{1,0:T(8,128)(2,1)}, bf16[544,768]{1,0:T(8,128)(2,1)}, u32[]{:S(2)}, u32[]{:S(2)}) collective-permute-start(bf16[544,768]{1,0:T(8,128)(2,1)} %collective-permute-done.4.ca), channel_id=1, source_target_pairs={{0,1},{1,0},{2,3},{3,2},{4,5},{5,4},{6,7},{7,6},{8,9},{9,8},{10,11... | collective-permute-start | bytes 2506760 | tf_op jit(solution)/shard_map/ppermute | solution.py:1075
  76.8 36.8 %collective-permute-start.8 = (bf16[2,512,768]{2,1,0:T(8,128)(2,1)}, bf16[2,512,768]{2,1,0:T(8,128)(2,1)}, u32[]{:S(2)}, u32[]{:S(2)}) collective-permute-start(bf16[2,512,768]{2,1,0:T(8,128)(2,1)} %get-tuple-element.134), channel_id=1, source_target_pairs={{0,1},{1,0},{2,3},{3,2},{4,5},{5,4},{6,7},{7,6},{8,9},{9,8},{10,11... | collective-permute-start | bytes 4718600 | tf_op jit(solution)/shard_map/ppermute | solution.py:1075
  77.4 36.2 %collective-permute-start.7 = (bf16[768,512]{1,0:T(8,128)(2,1)}, bf16[768,512]{1,0:T(8,128)(2,1)}, u32[]{:S(2)}, u32[]{:S(2)}) collective-permute-start(bf16[768,512]{1,0:T(8,128)(2,1)} %get-tuple-element.132), channel_id=1, source_target_pairs={{0,8},{4,12},{8,0},{12,4},{16,24},{20,28},{24,16},{28,20},{1,9},{5... | collective-permute-start | bytes 2359304 | tf_op jit(solution)/shard_map/ppermute | solution.py:1075
  80.0 33.6 %collective-permute-start.6 = (bf16[384,768]{1,0:T(8,128)(2,1)}, bf16[384,768]{1,0:T(8,128)(2,1)}, u32[]{:S(2)}, u32[]{:S(2)}) collective-permute-start(bf16[384,768]{1,0:T(8,128)(2,1)} %get-tuple-element.130), channel_id=1, source_target_pairs={{0,4},{4,0},{8,12},{12,8},{16,20},{20,16},{24,28},{28,24},{1,5},{5... | collective-permute-start | bytes 1769480 | tf_op jit(solution)/shard_map/ppermute | solution.py:1075
  110.8 15.2 %collective-permute-start.12 = (bf16[400,576]{1,0:T(8,128)(2,1)}, bf16[400,576]{1,0:T(8,128)(2,1)}, u32[]{:S(2)}, u32[]{:S(2)}) collective-permute-start(bf16[400,576]{1,0:T(8,128)(2,1)} %get-tuple-element.145), channel_id=1, source_target_pairs={{0,4},{4,0},{8,12},{12,8},{16,20},{20,16},{24,28},{28,24},{1,5},{5... | collective-permute-start | bytes 1382408 | tf_op jit(solution)/shard_map/ppermute | solution.py:1075
  117.2 20.7 %collective-permute-start.10 = (bf16[512,768]{1,0:T(8,128)(2,1)}, bf16[512,768]{1,0:T(8,128)(2,1)}, u32[]{:S(2)}, u32[]{:S(2)}) collective-permute-start(bf16[512,768]{1,0:T(8,128)(2,1)} %get-tuple-element.135), channel_id=1, source_target_pairs={{0,2},{1,3},{2,0},{3,1},{4,6},{5,7},{6,4},{7,5},{8,10},{9,11},{10,... | collective-permute-start | bytes 2359304 | tf_op jit(solution)/shard_map/ppermute | solution.py:1075
  125.8 15.5 %copy-start.1 = (bf16[512,768]{1,0:T(8,128)(2,1)S(1)}, bf16[512,768]{1,0:T(8,128)(2,1)}, u32[]{:S(2)}) copy-start(bf16[512,768]{1,0:T(8,128)(2,1)} %get-tuple-element.142) | copy-start | bytes 2359300
  125.8 10.2 %collective-permute-start.9 = (bf16[384,512]{1,0:T(8,128)(2,1)}, bf16[384,512]{1,0:T(8,128)(2,1)S(1)}, u32[]{:S(2)}, u32[]{:S(2)}) collective-permute-start(bf16[384,512]{1,0:T(8,128)(2,1)} %get-tuple-element.141), channel_id=1, source_target_pairs={{0,4},{4,0},{8,12},{12,8},{16,20},{20,16},{24,28},{28,24},{1,5},{5... | collective-permute-start | bytes 1179656 | tf_op jit(solution)/shard_map/ppermute | solution.py:1075
  125.9 15.4 %collective-permute-start.11 = (bf16[512,768]{1,0:T(8,128)(2,1)}, bf16[512,768]{1,0:T(8,128)(2,1)S(1)}, u32[]{:S(2)}, u32[]{:S(2)}) collective-permute-start(bf16[512,768]{1,0:T(8,128)(2,1)} %get-tuple-element.143), channel_id=1, source_target_pairs={{0,1},{1,0},{2,3},{3,2},{4,5},{5,4},{6,7},{7,6},{8,9},{9,8},{10,11... | collective-permute-start | bytes 2359304 | tf_op jit(solution)/shard_map/ppermute | solution.py:1075
  127.9 15.0 %collective-permute-start.13 = (bf16[208,576]{1,0:T(8,128)(2,1)S(1)}, bf16[208,576]{1,0:T(8,128)(2,1)S(1)}, u32[]{:S(2)}, u32[]{:S(2)}) collective-permute-start(bf16[208,576]{1,0:T(8,128)(2,1)S(1)} %pad_maximum_fusion), channel_id=1, source_target_pairs={{0,8},{4,12},{8,0},{12,4},{16,24},{20,28},{24,16},{28,20},{1,9},{5... | collective-permute-start | bytes 718856 | tf_op jit(solution)/shard_map/ppermute | solution.py:1075
  129.8 22.8 %collective-permute-start.22 = (bf16[192,768]{1,0:T(8,128)(2,1)}, bf16[192,768]{1,0:T(8,128)(2,1)}, u32[]{:S(2)}, u32[]{:S(2)}) collective-permute-start(bf16[192,768]{1,0:T(8,128)(2,1)} %get-tuple-element.165), channel_id=1, source_target_pairs={{0,8},{4,12},{8,0},{12,4},{16,24},{20,28},{24,16},{28,20},{1,9},{5... | collective-permute-start | bytes 884744 | tf_op jit(solution)/shard_map/ppermute | solution.py:1075
  136.0 5.3 %copy-start.3 = (bf16[384,512]{1,0:T(8,128)(2,1)}, bf16[384,512]{1,0:T(8,128)(2,1)S(1)}, u32[]{:S(2)}) copy-start(bf16[384,512]{1,0:T(8,128)(2,1)S(1)} %collective-permute-done.9) | copy-start | bytes 1179652
  136.0 31.1 %collective-permute-start.16 = (bf16[512,768]{1,0:T(8,128)(2,1)}, bf16[512,768]{1,0:T(8,128)(2,1)}, u32[]{:S(2)}, u32[]{:S(2)}) collective-permute-start(bf16[512,768]{1,0:T(8,128)(2,1)} %get-tuple-element.154), channel_id=1, source_target_pairs={{0,1},{1,0},{2,3},{3,2},{4,5},{5,4},{6,7},{7,6},{8,9},{9,8},{10,11... | collective-permute-start | bytes 2359304 | tf_op jit(solution)/shard_map/ppermute | solution.py:1075
  137.9 9.7 %collective-permute-start.14 = (bf16[192,512]{1,0:T(8,128)(2,1)}, bf16[192,512]{1,0:T(8,128)(2,1)}, u32[]{:S(2)}, u32[]{:S(2)}) collective-permute-start(bf16[192,512]{1,0:T(8,128)(2,1)} %add_convert_fusion.3), channel_id=1, source_target_pairs={{0,16},{4,20},{8,24},{12,28},{16,0},{20,4},{24,8},{28,12},{1,17},{... | collective-permute-start | bytes 589832 | tf_op jit(solution)/shard_map/ppermute | solution.py:1075
  142.4 26.3 %collective-permute-start.17 = (bf16[512,768]{1,0:T(8,128)(2,1)}, bf16[512,768]{1,0:T(8,128)(2,1)}, u32[]{:S(2)}, u32[]{:S(2)}) collective-permute-start(bf16[512,768]{1,0:T(8,128)(2,1)} %add_convert_fusion), channel_id=1, source_target_pairs={{0,2},{1,3},{2,0},{3,1},{4,6},{5,7},{6,4},{7,5},{8,10},{9,11},{10,... | collective-permute-start | bytes 2359304 | tf_op jit(solution)/shard_map/ppermute | solution.py:1075
  143.0 1.1 copy-start.2
  144.8 19.7 %collective-permute-start.15 = (bf16[112,576]{1,0:T(8,128)(2,1)}, bf16[112,576]{1,0:T(8,128)(2,1)}, u32[]{:S(2)}, u32[]{:S(2)}) collective-permute-start(bf16[112,576]{1,0:T(8,128)(2,1)} %pad_maximum_fusion.1.refs_4_), channel_id=1, source_target_pairs={{0,16},{4,20},{8,24},{12,28},{16,0},{20,4},{24,8},{28,12},{1,17},{... | collective-permute-start | bytes 387080 | tf_op jit(solution)/shard_map/ppermute | solution.py:1075
  149.6 22.8 %collective-permute-start.18 = (bf16[192,512]{1,0:T(8,128)(2,1)}, bf16[192,512]{1,0:T(8,128)(2,1)}, u32[]{:S(2)}, u32[]{:S(2)}) collective-permute-start(bf16[192,512]{1,0:T(8,128)(2,1)} %add_convert_fusion.2), channel_id=1, source_target_pairs={{0,0},{1,8},{2,16},{3,24},{4,1},{5,9},{6,17},{7,25},{8,2},{9,10},{... | collective-permute-start | bytes 589832 | tf_op jit(solution)/shard_map/ppermute | solution.py:1087
  154.4 23.1 %collective-permute-start.23 = (bf16[96,768]{1,0:T(8,128)(2,1)}, bf16[96,768]{1,0:T(8,128)(2,1)}, u32[]{:S(2)}, u32[]{:S(2)}) collective-permute-start(bf16[96,768]{1,0:T(8,128)(2,1)} %add_convert_fusion.4), channel_id=1, source_target_pairs={{0,16},{4,20},{8,24},{12,28},{16,0},{20,4},{24,8},{28,12},{1,17},{... | collective-permute-start | bytes 442376 | tf_op jit(solution)/shard_map/ppermute | solution.py:1075
  167.1 7.7 %collective-permute-start.19 = (f32[128,192]{1,0:T(8,128)}, f32[128,192]{1,0:T(8,128)}, u32[]{:S(2)}, u32[]{:S(2)}) collective-permute-start(f32[128,192]{1,0:T(8,128)} %get-tuple-element.159), channel_id=1, source_target_pairs={{0,1},{1,0},{2,3},{3,2},{4,5},{5,4},{6,7},{7,6},{8,9},{9,8},{10,11... | collective-permute-start | bytes 294920 | tf_op jit(solution)/shard_map/ppermute | solution.py:1075
  167.1 7.7 %collective-permute-start.20 = (f32[128,192]{1,0:T(8,128)}, f32[128,192]{1,0:T(8,128)}, u32[]{:S(2)}, u32[]{:S(2)}) collective-permute-start(f32[128,192]{1,0:T(8,128)} %get-tuple-element.160), channel_id=1, source_target_pairs={{0,2},{1,3},{2,0},{3,1},{4,6},{5,7},{6,4},{7,5},{8,10},{9,11},{10,... | collective-permute-start | bytes 294920 | tf_op jit(solution)/shard_map/ppermute | solution.py:1075
  168.7 6.1 %collective-permute-start.21 = (f32[32,192]{1,0:T(8,128)}, f32[32,192]{1,0:T(8,128)}, u32[]{:S(2)}, u32[]{:S(2)}) collective-permute-start(f32[32,192]{1,0:T(8,128)} %get-tuple-element.152.small), channel_id=1, source_target_pairs={{0,3},{1,2},{2,1},{3,0},{4,7},{5,6},{6,5},{7,4},{8,11},{9,10},{10,... | collective-permute-start | bytes 73736 | tf_op jit(solution)/shard_map/ppermute | solution.py:1075

commit v10 on v9

--- a/solution.py
+++ b/solution.py
@@ -140,8 +140,8 @@
     v_ref[...] = joined[:, 384:576].astype(BF16)
 
 
-def find_starts(seq, meta, valid, rows, start_ref, lo_ref, hi_ref):
-    segs = [ref[0:1, 0:seq].astype(F32) for ref in rows]
+def find_starts(seq, meta, valid, pairs, start_ref, lo_ref, hi_ref):
+    segs = [ref[at : at + 1, 0:seq].astype(F32) for ref in pairs for at in range(2)]
     below = [
         sum(jnp.sum((seg < number).astype(F32), axis=1, keepdims=True) for seg in segs)
         for number in (1, 2, 3)
@@ -162,48 +162,33 @@
             hi_ref[block * per + part] = (jnp.max(tile) + (TILE - 1)) // TILE
 
 
-def qkv_kernel(slot, meta, valid, x_ref, gain, shift, low, high, w_ref, b_ref, *refs):
+def qkv_kernel(slot, meta, x_ref, gain, shift, low, high, w_ref, b_ref, *refs):
     per = pl.num_programs(0)
     tile = true_block(meta, slot) * per + pl.program_id(0)
     normed = normalize(x_ref[...].astype(F32))
-    if slot == 3:
-        segs, (*outs, start_ref, lo_ref, hi_ref) = refs[3:7], refs[7:]
-
-        @pl.when(pl.program_id(0) == 0)
-        def _():
-            find_starts(per * TILE, meta, valid, segs, start_ref, lo_ref, hi_ref)
-    else:
-        outs = refs[3:]
-    project_tile(normed, gain, shift, w_ref, b_ref, low, high, tile, *outs)
-
-
-def project(slot, meta, valid, x, gain, shift, low, high, w, b, filled, seq, toks=()):
+    project_tile(normed, gain, shift, w_ref, b_ref, low, high, tile, *refs[3:])
+
+
+def project(slot, meta, x, gain, shift, low, high, w, b, filled, seq):
     width = D // 4
     per = seq // TILE
-    tiles = 4 * per
-    outs = [jax.ShapeDtypeStruct((4 * seq, width), BF16)] * 3
-    out_specs = [pl.BlockSpec((TILE, width), lambda i, m, v: (slot * per + i, 0))] * 3
-    args = [x, gain, shift, low, high, w, b, *filled, *toks]
-    specs = [pl.BlockSpec((TILE, D), lambda i, m, v: (i, 0))]
+    out = jax.ShapeDtypeStruct((4 * seq, width), BF16)
+    out_spec = pl.BlockSpec((TILE, width), lambda i, m: (slot * per + i, 0))
+    args = [x, gain, shift, low, high, w, b, *filled]
+    specs = [pl.BlockSpec((TILE, D), lambda i, m: (i, 0))]
     specs += [whole(a.shape) for a in args[1:7]]
     specs += [pl.BlockSpec(memory_space=pl.ANY)] * 3
-    specs += [pl.BlockSpec((EXTRA, D), lambda i, m, v: (seq // EXTRA, 0)) for _ in toks]
-    if toks:
-        smem = pl.BlockSpec(memory_space=pltpu.SMEM)
-        outs.append(jax.ShapeDtypeStruct((tiles, 1, TILE), jnp.int32))
-        outs += [jax.ShapeDtypeStruct((tiles,), jnp.int32)] * 2
-        out_specs += [whole((tiles, 1, TILE)), smem, smem]
     return pl.pallas_call(
         partial(qkv_kernel, slot),
-        out_shape=outs,
+        out_shape=[out] * 3,
         grid_spec=pltpu.PrefetchScalarGridSpec(
-            num_scalar_prefetch=2, grid=(per,), in_specs=specs, out_specs=out_specs
+            num_scalar_prefetch=1, grid=(per,), in_specs=specs, out_specs=[out_spec] * 3
         ),
-        input_output_aliases={9 + i: i for i in range(3)},
+        input_output_aliases={8 + i: i for i in range(3)},
         compiler_params=params(),
         cost_estimate=COST,
         name=f"qkv_{slot}",
-    )(meta, valid, *args)
+    )(meta, *args)
 
 
 def mask_order(rows, first):
@@ -540,13 +525,17 @@
         to_ref[:, rows] = from_ref[rows, :].astype(F32).T.astype(BF16)
 
 
-def attend_kernel(per, meta, lo, hi, q_ref, k_ref, v_ref, start_ref, o_ref, lse_ref, vt_ref, acc, s_ref):
+def attend_kernel(
+    per, meta, valid, q_ref, k_ref, v_ref, pair_own, pair_far,
+    o_ref, lse_ref, starts_ref, lo, hi, vt_ref, acc, s_ref,
+):
     mask0, mask1 = head_masks()
     tiles = k_ref.shape[0] // TILE
     qi = pl.program_id(0)
 
     @pl.when(qi == 0)
     def _():
+        find_starts(per * TILE, meta, valid, (pair_own, pair_far), starts_ref, lo, hi)
         ones = jnp.where(lax.broadcasted_iota(jnp.int32, (VROWS - HDIM, TILE), 0) == 0, 1.0, 0.0)
 
         @pl.loop(0, tiles)
@@ -561,7 +550,7 @@
     key_iota = lax.broadcasted_iota(jnp.int32, (TILE, TILE), 0)
     query_iota = lax.broadcasted_iota(jnp.int32, (TILE, TILE), 1)
     queries = by_head(mask0, mask1, q_ref[:, 0:128], q_ref[:, 128:192])
-    starts = start_ref[0]
+    starts = starts_ref[jnp.bitwise_xor(qi // per, meta[0]) * per + qi % per]
     acc[...] = jnp.zeros_like(acc)
 
     def key_tile(turn):
@@ -619,31 +608,47 @@
         lse_ref[head, 0] = top + jnp.log2(total)
     o_ref[...] = jnp.concatenate(heads, axis=0).T.astype(BF16)
 
-def attend(meta, lo, hi, query, keys, values, starts, per):
+def attend(meta, valid_len, query, keys, values, seg_pair, cot_far, per):
     total, width = query.shape
     tiles = total // TILE
+
     def slot(i, m):
         return jnp.bitwise_xor(i // per, m[0]) * per + i % per
-    q_spec = pl.BlockSpec((TILE, width), lambda i, m, lo, hi: (slot(i, m), 0))
-    start_spec = pl.BlockSpec((1, 1, TILE), lambda i, m, lo, hi: (slot(i, m), 0, 0))
-    lse_spec = pl.BlockSpec((3, 1, 1, TILE), lambda i, m, lo, hi: (0, slot(i, m), 0, 0))
+
+    q_spec = pl.BlockSpec((TILE, width), lambda i, m, v: (slot(i, m), 0))
+    lse_spec = pl.BlockSpec((3, 1, 1, TILE), lambda i, m, v: (0, slot(i, m), 0, 0))
+    far_spec = pl.BlockSpec((EXTRA, D), lambda i, m, v: (per * TILE // EXTRA, 0))
+    smem = pl.BlockSpec(memory_space=pltpu.SMEM)
     return pl.pallas_call(
         partial(attend_kernel, per),
         out_shape=[
             jax.ShapeDtypeStruct((total, width), BF16),
             jax.ShapeDtypeStruct((3, tiles, 1, TILE), F32),
+            jax.ShapeDtypeStruct((tiles, 1, TILE), jnp.int32),
+            jax.ShapeDtypeStruct((tiles,), jnp.int32),
+            jax.ShapeDtypeStruct((tiles,), jnp.int32),
         ],
         grid_spec=pltpu.PrefetchScalarGridSpec(
-            num_scalar_prefetch=3,
+            num_scalar_prefetch=2,
             grid=(tiles,),
-            in_specs=[q_spec, whole(keys.shape), whole(values.shape), start_spec],
-            out_specs=[q_spec, lse_spec],
-            scratch_shapes=[pltpu.VMEM((3 * VROWS, total), BF16), pltpu.VMEM((3 * VROWS, TILE), F32), pltpu.VMEM((3, TILE, TILE), F32)],
+            in_specs=[
+                q_spec,
+                whole(keys.shape),
+                whole(values.shape),
+                whole(seg_pair.shape),
+                far_spec,
+            ],
+            out_specs=[q_spec, lse_spec, whole((tiles, 1, TILE)), smem, smem],
+            scratch_shapes=[
+                pltpu.VMEM((3 * VROWS, total), BF16),
+                pltpu.VMEM((3 * VROWS, TILE), F32),
+                pltpu.VMEM((3, TILE, TILE), F32),
+            ],
         ),
         compiler_params=params(),
         cost_estimate=COST,
         name="attend",
-    )(meta, lo, hi, query, keys, values, starts)
+    )(meta, valid_len, query, keys, values, seg_pair, cot_far)
 
 
 def attend_back_kernel(
@@ -1146,14 +1151,15 @@
     width = D // 4
     hid = FF // 4
     low, high = angle_parts(4 * seq)
-    seg_row = jnp.pad(seg_ids.astype(BF16), ((0, EXTRA - 1), (0, D - seq)))
-    tok_own = jnp.concatenate([tokens[0], seg_row], axis=0)
-    cot_own = cotangent[0]
+    tok_own, cot_own = tokens[0], cotangent[0]
 
     cot_near = swap(cot_own, "blk", 1)
     tok_far = swap(tok_own, "blk", 2)
     tok_near = swap(tok_own, "blk", 1)
-    cot_long = jnp.pad(cot_own, ((0, 2 * EXTRA), (0, 0)))
+    seg_own = seg_ids.astype(BF16)
+    seg_pair = jnp.concatenate([seg_own, swap(seg_own, "blk", 1)])
+    seg_pair = jnp.pad(seg_pair, ((0, EXTRA - 2), (0, D - seq)))
+    cot_long = jnp.concatenate([cot_own, seg_pair])
     cot_far = swap(cot_long, "blk", 2)
 
     meta = jnp.stack([blk, lax.axis_index("rows")]).astype(jnp.int32)
@@ -1164,23 +1170,22 @@
     )
     meta = after(meta, b_own)
 
-    def more(slot, m, tok, filled, slots=()):
-        args = (ln1_gain, ln1_bias, low, high, w_own, b_own, filled, seq, slots)
-        return project(slot, m, valid_len, tok, *args)
+    def more(slot, m, tok, filled):
+        args = (ln1_gain, ln1_bias, low, high, w_own, b_own, filled, seq)
+        return project(slot, m, tok, *args)
 
     tok_last = swap(after(tok_far, b_own), "blk", 1)
     joined = more(2, meta, tok_far, (query, keys, values))
-    toks = (tok_own, tok_near, tok_far, tok_last)
-    query, keys, values, starts, lo, hi = more(
-        3, after(meta, joined[0]), tok_last, joined, toks
+    query, keys, values = more(3, after(meta, joined[0]), tok_last, joined)
+    cot_last = swap(after(cot_far, query), "blk", 1)
+    cots = (cot_own, cot_near, cot_far, cot_last)
+    attn, lse, starts, lo, hi = attend(
+        meta, valid_len, query, keys, values, seg_pair, cot_far, per
     )
-    cot_last = swap(after(cot_far, lo), "blk", 1)
-    cots = (cot_own, cot_near, cot_far, cot_last)
-    attn, lse = attend(meta, lo, hi, query, keys, values, starts, per)
 
     meta = after(meta, lse)
     e_mlp, normed, grad_vec, mlp_sums, out_even, out_odd, *packets = feed_forward(
-        meta, toks[2:], cots[2:], *mlp_args, before=first, near=cots[:2], attn=attn
+        meta, (tok_far, tok_last), cots[2:], *mlp_args, before=first, near=cots[:2], attn=attn
     )
     up_keep, up_send = chunks_of(*packets[:2], rows, 1)
     low_keep, low_send = low_chunks(*packets[2:], rows)

time: 180 us -> 176 us (0.978); the launches traced: 179 us -> 173 us
  starting transfers between devices: 34.2 us -> 31.9 us
  waiting for transfers between devices: 10.7 us -> 8.72 us
    ppermute x23 -> x24, starting transfers between devices: 31.2 us -> 28.9 us  [swap(): return lax.ppermute(value, axis, [(i, i ^ mask) for i in range(size)])]
    ppermute x23 -> x24, waiting for transfers between devices: 10.7 us -> 8.72 us  [swap(): return lax.ppermute(value, axis, [(i, i ^ mask) for i in range(size)])]
  transfers between devices with their start and end apart: 24 -> 25, of which waited for: 3 -> 4; matrix products, arithmetic and copies ran while one was open for 7% -> 8% of each run, Pallas kernels for 53% -> 55%
where the time goes in v10:
time: 176 us; the launch traced here: 173 us
  Pallas kernels  115 us (65%)
  starting transfers between devices  31.9 us (18%)
  other arithmetic  15.7 us (9%)
  waiting for transfers between devices  8.72 us (5%)
    pallas_call x2, Pallas kernels, feed_forward(): pl.pallas_call(body, out_shape=outs, grid_spec=pltpu.PrefetchScalarGridSp...  39.3 us
    ppermute x24, starting transfers between devices, swap(): return lax.ppermute(value, axis, [(i, i ^ mask) for i in range(size)])  28.9 us
    pallas_call x1, Pallas kernels, attend_back(): pl.pallas_call(partial(attend_back_kernel, per), out_shape=jax.ShapeDtype...  20.4 us
    pallas_call x1, Pallas kernels, attend(): pl.pallas_call(partial(attend_kernel, per), out_shape=[jax.ShapeDtypeStru...  13.2 us
    pallas_call x2, Pallas kernels, project(): pl.pallas_call(partial(qkv_kernel, slot), out_shape=[out] * 3, grid_spec=...  9.09 us
    ppermute x24, waiting for transfers between devices, swap(): return lax.ppermute(value, axis, [(i, i ^ mask) for i in range(size)])  8.72 us
    pallas_call x1, Pallas kernels, joined_weight(): pl.pallas_call(partial(weight_kernel, rows), out_shape=[jax.ShapeDtypeStr...  8.54 us
    pallas_call x1, Pallas kernels, norm_grad(): pl.pallas_call(norm_kernel, out_shape=[jax.ShapeDtypeStruct((seq, D), BF1...  6.98 us
  transfers between devices with their start and end apart: 25, of which 4 were waited for; matrix products, arithmetic and copies ran while one was open for 8% of the time, Pallas kernels for 55%

profile of v10, /device:TPU:0, one launch (start us, length us, event | category | flops | bytes accessed | tf_op | source)
XLA Modules:
  0.0 173.4 jit_solution(8074083922011513875)
XLA Ops:
  1.2 2.9 %collective-permute-start.2 = (bf16[512,768]{1,0:T(8,128)(2,1)}, bf16[512,768]{1,0:T(8,128)(2,1)}, u32[]{:S(2)}, u32[]{:S(2)}) collective-permute-start(bf16[512,768]{1,0:T(8,128)(2,1)} %bitcast.15), channel_id=1, source_target_pairs={{0,2},{1,3},{2,0},{3,1},{4,6},{5,7},{6,4},{7,5},{8,10},{9,11},{10,... | collective-permute-start | bytes 2359304 | tf_op jit(solution)/shard_map/ppermute | solution.py:1080
  4.8 1.2 collective-permute-done.4
  6.6 2.1 %pad_maximum_fusion = bf16[528,768]{1,0:T(8,128)(2,1)} fusion(bf16[16,768]{1,0:T(8,128)(2,1)S(1)} %fusion.5.pair_own, bf16[512,768]{1,0:T(8,128)(2,1)} %bitcast.10), kind=kLoop, calls=%fused_computation.1 | loop fusion | flops 1622016 | bytes 1622016 | tf_op jit(solution)/shard_map/concatenate | solution.py:1162
  10.4 18.9 %mlp_first.1 = (bf16[1024,768]{1,0:T(8,128)(2,1)}, bf16[2048,768]{1,0:T(8,128)(2,1)}, bf16[2048,768]{1,0:T(8,128)(2,1)}, bf16[2048,192]{1,0:T(8,128)(2,1)}, f32[...) custom-call(s32[2]{0:T(128)} %pad_add_fusion.meta, ...), custom_call_target="tpu_custom_call" | custom-call | tf_op jit(solution)/shard_map/mlp_first/pallas_call | solution.py:488
  29.8 4.5 %qkv_2.1 = (bf16[2048,192]{1,0:T(8,128)(2,1)}, bf16[2048,192]{1,0:T(8,128)(2,1)}, bf16[2048,192]{1,0:T(8,128)(2,1)}) custom-call(s32[2]{0:T(128)} %pad_add_fusion.meta, bf16[512,768]{1,0:T(8,128)(2,1)} %collective-permute-done.2.x_ref.xa, f32[768]{0:T(1024)} %refs_8_.1, f32[768]{0:T(1024)} %refs_3_.1, ...), custom_call_target="tpu_custom_call", output_to_operand_aliasing={{0}: (8, {}), {1}: (9, {}), {2}: (10, {})} | custom-call | tf_op jit(solution)/shard_map/qkv_2/pallas_call | solution.py:181
  34.3 4.5 %qkv_3.1 = (bf16[2048,192]{1,0:T(8,128)(2,1)}, bf16[2048,192]{1,0:T(8,128)(2,1)}, bf16[2048,192]{1,0:T(8,128)(2,1)}) custom-call(s32[2]{0:T(128)} %pad_add_fusion.meta, bf16[512,768]{1,0:T(8,128)(2,1)} %collective-permute-done.3.x_ref.xb, f32[768]{0:T(1024)} %refs_8_.1, f32[768]{0:T(1024)} %refs_3_.1, ...), custom_call_target="tpu_custom_call", output_to_operand_aliasing={{0}: (8, {}), {1}: (9, {}), {2}: (10, {})} | custom-call | tf_op jit(solution)/shard_map/qkv_3/pallas_call | solution.py:181
  40.3 13.2 %attend.1 = (bf16[2048,192]{1,0:T(8,128)(2,1)}, f32[3,8,1,256]{3,2,1,0:T(1,128)}, s32[8,1,256]{2,1,0:T(1,128)}, s32[8]{0:T(128)}, s32[8]{0:T(128)}) custom-call(s32[2]{0:T(128)} %pad_add_fusion.meta, s32[1]{0:T(128)S(6)} %copy.50.valid, bf16[2048,192]{1,0:T(8,128)(2,1)} %get-tuple-element.105.q_ref, bf16[2048,192]{1,0:T(8,128)(2,1)} %get-tuple-element.106.k_ref, ...), custom_call_target="tpu_custom_call" | custom-call | tf_op jit(solution)/shard_map/attend/pallas_call | solution.py:622
  53.5 20.4 %mlp_second.1 = (bf16[2048,768]{1,0:T(8,128)(2,1)}, bf16[2048,768]{1,0:T(8,128)(2,1)}, bf16[2048,192]{1,0:T(8,128)(2,1)}, f32[8,768]{1,0:T(8,128)}, bf16[2,512,7...) custom-call(s32[2]{0:T(128)} %pad_add_fusion.meta, ...), custom_call_target="tpu_custom_call", output_to_operand_aliasing={{0}: (19, {}), {1}: (20, {}), {2}: (21, {})} | custom-call | tf_op jit(solution)/shard_map/mlp_second/pallas_call | solution.py:488
  74.4 2.2 %collective-permute-start.8 = (bf16[768,512]{1,0:T(8,128)(2,1)}, bf16[768,512]{1,0:T(8,128)(2,1)}, u32[]{:S(2)}, u32[]{:S(2)}) collective-permute-start(bf16[768,512]{1,0:T(8,128)(2,1)} %get-tuple-element.132), channel_id=1, source_target_pairs={{0,8},{4,12},{8,0},{12,4},{16,24},{20,28},{24,16},{28,20},{1,9},{5... | collective-permute-start | bytes 2359304 | tf_op jit(solution)/shard_map/ppermute | solution.py:1080
  76.6 1.5 collective-permute-start.7
  78.1 20.4 %attend_back.1.refs_0_.refs_1_.refs_2_.refs_3_ = bf16[2048,576]{1,0:T(8,128)(2,1)} custom-call(s32[2]{0:T(128)} %pad_add_fusion.meta, s32[8]{0:T(128)} %get-tuple-element.121.lo, s32[8]{0:T(128)} %get-tuple-element.122.hi, bf16[2048,192]{1,0:T(8,128)(2,1)} %get-tuple-element.105.q_ref, bf16[2048,192]{1,0:T(8,128)(2,1)} %get-tuple-element.106.k_ref, ...), custom_call_target="tpu_custom_call" | custom-call | tf_op jit(solution)/shard_map/attend_back/pallas_call | solution.py:766
  98.5 8.5 %joined_weight.1 = (bf16[400,576]{1,0:T(8,128)(2,1)}, bf16[400,576]{1,0:T(8,128)(2,1)}, f32[16,576]{1,0:T(8,128)}) custom-call(s32[2]{0:T(128)} %pad_add_fusion.meta, bf16[2048,576]{1,0:T(8,128)(2,1)} %attend_back.1.refs_0_.refs_1_.refs_2_.refs_3_, bf16[2048,768]{1,0:T(8,128)(2,1)} %get-tuple-element.126.refs_1_, f32[768]{0:T(1024)} %refs_8_.1, ...), custom_call_target="tpu_custom_call" | custom-call | tf_op jit(solution)/shard_map/joined_weight/pallas_call | solution.py:863
  107.0 1.2 collective-permute-start.13
  108.3 3.6 %first_sums.1 = (bf16[192,768]{1,0:T(8,128)(2,1)}, bf16[384,512]{1,0:T(8,128)(2,1)}, bf16[512,768]{1,0:T(8,128)(2,1)}) custom-call(s32[2]{0:T(128)} %pad_add_fusion.meta, bf16[384,768]{1,0:T(8,128)(2,1)} %get-tuple-element.164.refs_0_, bf16[384,768]{1,0:T(8,128)(2,1)} %collective-permute-done.7.refs_1_, bf16[768,512]{1,0:T(8,128)(2,1)} %get-tuple-element.150.refs_2_, ...), custom_call_target="tpu_custom_call" | custom-call | tf_op jit(solution)/shard_map/first_sums/pallas_call | solution.py:953
  111.8 1.5 collective-permute-start.11
  113.4 7.0 %norm_grad.1 = (bf16[512,768]{1,0:T(8,128)(2,1)}, bf16[512,768]{1,0:T(8,128)(2,1)}, bf16[512,768]{1,0:T(8,128)(2,1)}, bf16[512,768]{1,0:T(8,128)(2,1)}) custom-call(s32[2]{0:T(128)} %pad_add_fusion.meta, bf16[2048,576]{1,0:T(8,128)(2,1)} %attend_back.1.refs_0_.refs_1_.refs_2_.refs_3_, bf16[2048,576]{1,0:T(8,128)(2,1)} %attend_back.1.refs_0_.refs_1_.refs_2_.refs_3_, ...), custom_call_target="tpu_custom_call" | custom-call | tf_op jit(solution)/shard_map/norm_grad/pallas_call | solution.py:894
  125.3 5.3 %collective-permute-done.10 = bf16[384,512]{1,0:T(8,128)(2,1)S(1)} collective-permute-done((bf16[384,512]{1,0:T(8,128)(2,1)}, bf16[384,512]{1,0:T(8,128)(2,1)S(1)}, u32[]{:S(2)}, u32[]{:S(2)}) %collective-permute-start.10) | collective-permute-done | bytes 393248 | tf_op jit(solution)/shard_map/ppermute | solution.py:1080
  130.6 1.9 %add_convert_fusion.3 = bf16[192,512]{1,0:T(8,128)(2,1)} fusion(bf16[384,512]{1,0:T(8,128)(2,1)S(1)} %collective-permute-done.10, bf16[768,512]{1,0:T(8,128)(2,1)} %collective-permute-done.8.refs_3_, bf16[768,512]{1,0:T(8,128)(2,1)} %get-tuple-element.150.refs_2_), kind=kLoop, calls=%fused_computation.4 | loop fusion | flops 589824 | bytes 786432 | tf_op jit(solution)/shard_map/convert_element_type | solution.py:1063
  132.5 3.3 %collective-permute-start.15 = (bf16[192,512]{1,0:T(8,128)(2,1)}, bf16[192,512]{1,0:T(8,128)(2,1)}, u32[]{:S(2)}, u32[]{:S(2)}) collective-permute-start(bf16[192,512]{1,0:T(8,128)(2,1)} %add_convert_fusion.3), channel_id=1, source_target_pairs={{0,16},{4,20},{8,24},{12,28},{16,0},{20,4},{24,8},{28,12},{1,17},{... | collective-permute-start | bytes 589832 | tf_op jit(solution)/shard_map/ppermute | solution.py:1080
  139.3 2.8 %result.1 = bf16[512,768]{1,0:T(8,128)(2,1)} custom-call(bf16[512,768]{1,0:T(8,128)(2,1)} %bitcast.17, bf16[2,512,768]{2,1,0:T(8,128)(2,1)} %get-tuple-element.133.even, bf16[2,512,768]{2,1,0:T(8,128)(2,1)} %collective-permute-done.9.near, bf16[512,768]{1,0:T(8,128)(2,1)} %collective-permute-done.11.far, f32[768]{0:T(1024)} %b_out.1, f32[768]{0:T(1024)} %b_down.1), custom_call_target="tpu_custom_call" | custom-call | tf_op jit(solution)/shard_map/result/pallas_call | solution.py:1128
  142.1 2.0 %add_convert_fusion.2 = bf16[192,512]{1,0:T(8,128)(2,1)} fusion(bf16[192,512]{1,0:T(8,128)(2,1)} %collective-permute-done.15, bf16[384,512]{1,0:T(8,128)(2,1)} %copy-done.2, bf16[768,512]{1,0:T(8,128)(2,1)} %collective-permute-done.8.refs_3_, bf16[768,512]{1,0:T(8,128)(2,1)} %get-tuple-element.150.refs_2_), kind=kLoop, calls=%fused_computation.3 | loop fusion | flops 786432 | bytes 983040 | tf_op jit(solution)/shard_map/convert_element_type | solution.py:1254
  144.1 3.0 %collective-permute-start.19 = (bf16[192,512]{1,0:T(8,128)(2,1)}, bf16[192,512]{1,0:T(8,128)(2,1)}, u32[]{:S(2)}, u32[]{:S(2)}) collective-permute-start(bf16[192,512]{1,0:T(8,128)(2,1)} %add_convert_fusion.2), channel_id=1, source_target_pairs={{0,0},{1,8},{2,16},{3,24},{4,1},{5,9},{6,17},{7,25},{8,2},{9,10},{... | collective-permute-start | bytes 589832 | tf_op jit(solution)/shard_map/ppermute | solution.py:1092
  147.1 1.8 %add_convert_fusion.4 = bf16[96,768]{1,0:T(8,128)(2,1)} fusion(bf16[192,768]{1,0:T(8,128)(2,1)} %collective-permute-done.23, bf16[384,768]{1,0:T(8,128)(2,1)} %collective-permute-done.7.refs_1_, bf16[384,768]{1,0:T(8,128)(2,1)} %get-tuple-element.164.refs_0_), kind=kLoop, calls=%fused_computation.6 | loop fusion | flops 442368 | bytes 589824 | tf_op jit(solution)/shard_map/convert_element_type | solution.py:1063
  148.9 2.0 %collective-permute-start.24 = (bf16[96,768]{1,0:T(8,128)(2,1)}, bf16[96,768]{1,0:T(8,128)(2,1)}, u32[]{:S(2)}, u32[]{:S(2)}) collective-permute-start(bf16[96,768]{1,0:T(8,128)(2,1)} %add_convert_fusion.4), channel_id=1, source_target_pairs={{0,16},{4,20},{8,24},{12,28},{16,0},{20,4},{24,8},{28,12},{1,17},{... | collective-permute-start | bytes 442376 | tf_op jit(solution)/shard_map/ppermute | solution.py:1080
  150.9 1.4 collective-permute-done.16.refs_3_.refs_5_
  152.3 2.6 %last_qkv.1 = (f32[96,192]{1,0:T(8,128)}, f32[128,192]{1,0:T(8,128)}, f32[128,192]{1,0:T(8,128)}, f32[32,192]{1,0:T(8,128)}) custom-call(s32[2]{0:T(128)} %pad_add_fusion.meta, bf16[400,576]{1,0:T(8,128)(2,1)} %get-tuple-element.144.refs_0_, bf16[400,576]{1,0:T(8,128)(2,1)} %collective-permute-done.13.refs_1_, bf16[208,576]{1,0:T(8,128)(2,1)} %copy-done.1, ...), custom_call_target="tpu_custom_call" | custom-call | tf_op jit(solution)/shard_map/last_qkv/pallas_call | solution.py:915
  154.9 4.7 %collective-permute-start.20 = (f32[128,192]{1,0:T(8,128)}, f32[128,192]{1,0:T(8,128)}, u32[]{:S(2)}, u32[]{:S(2)}) collective-permute-start(f32[128,192]{1,0:T(8,128)} %get-tuple-element.159), channel_id=1, source_target_pairs={{0,1},{1,0},{2,3},{3,2},{4,5},{5,4},{6,7},{7,6},{8,9},{9,8},{10,11... | collective-permute-start | bytes 294920 | tf_op jit(solution)/shard_map/ppermute | solution.py:1080
  159.6 3.4 %collective-permute-start.21 = (f32[128,192]{1,0:T(8,128)}, f32[128,192]{1,0:T(8,128)}, u32[]{:S(2)}, u32[]{:S(2)}) collective-permute-start(f32[128,192]{1,0:T(8,128)} %get-tuple-element.160), channel_id=1, source_target_pairs={{0,2},{1,3},{2,0},{3,1},{4,6},{5,7},{6,4},{7,5},{8,10},{9,11},{10,... | collective-permute-start | bytes 294920 | tf_op jit(solution)/shard_map/ppermute | solution.py:1080
  163.0 3.5 %token_grad.1 = bf16[512,768]{1,0:T(8,128)(2,1)} custom-call(bf16[512,768]{1,0:T(8,128)(2,1)} %bitcast.18, bf16[512,768]{1,0:T(8,128)(2,1)} %get-tuple-element.138.even, bf16[512,768]{1,0:T(8,128)(2,1)} %collective-permute-done.17.near, bf16[512,768]{1,0:T(8,128)(2,1)} %collective-permute-done.18.far, bf16[512,768]{1,0:T(8,128)(2,1)} %bitcast.13), custom_call_target="tpu_custom_call" | custom-call | tf_op jit(solution)/shard_map/token_grad/pallas_call | solution.py:1128
  166.4 2.4 %lower.1 = (f32[192,384]{1,0:T(8,128)}, f32[96,192]{1,0:T(8,128)}) custom-call(s32[2]{0:T(128)} %pad_add_fusion.meta, bf16[192,512]{1,0:T(8,128)(2,1)} %collective-permute-done.19.piece), custom_call_target="tpu_custom_call" | custom-call | tf_op jit(solution)/shard_map/lower/pallas_call | solution.py:915
  168.8 2.7 %assemble.1 = (f32[96,576]{1,0:T(8,128)}, f32[2304]{0:T(1024)}, f32[768]{0:T(1024)}, f32[3072]{0:T(1024)}, f32[768]{0:T(1024)}, /*index=5*/f32[768]{0:T(1024)}, f32[768]{0:T(1024)}, f32[768]{0:T(1024)}, f32[768]{0:T(1024)}) custom-call(s32[2]{0:T(128)} %pad_add_fusion.meta, f32[96,192]{1,0:T(8,128)} %get-tuple-element.158.kept, ...), custom_call_target="tpu_custom_call" | custom-call | tf_op jit(solution)/shard_map/assemble/pallas_call | solution.py:1046
  171.5 1.9 %convert_add_fusion = f32[96,768]{1,0:T(8,128)} fusion(bf16[96,768]{1,0:T(8,128)(2,1)} %collective-permute-done.24, bf16[192,768]{1,0:T(8,128)(2,1)} %collective-permute-done.23, bf16[384,768]{1,0:T(8,128)(2,1)} %collective-permute-done.7.refs_1_, bf16[384,768]{1,0:T(8,128)(2,1)} %get-tuple-element.164.refs_0_), kind=kLoop, calls=%fused_computation.5 | loop fusion | flops 516096 | bytes 884736 | tf_op jit(solution)/shard_map/add | solution.py:1281
  (55 shorter events, 13.7 us)
Async XLA Ops:
  0.6 9.7 %collective-permute-start = (bf16[512,768]{1,0:T(8,128)(2,1)}, bf16[512,768]{1,0:T(8,128)(2,1)}, u32[]{:S(2)}, u32[]{:S(2)}) collective-permute-start(bf16[512,768]{1,0:T(8,128)(2,1)} %bitcast.14), channel_id=1, source_target_pairs={{0,1},{1,0},{2,3},{3,2},{4,5},{5,4},{6,7},{7,6},{8,9},{9,8},{10,11... | collective-permute-start | bytes 2359304 | tf_op jit(solution)/shard_map/ppermute | solution.py:1080
  1.2 9.2 %collective-permute-start.1 = (bf16[512,768]{1,0:T(8,128)(2,1)}, bf16[512,768]{1,0:T(8,128)(2,1)}, u32[]{:S(2)}, u32[]{:S(2)}) collective-permute-start(bf16[512,768]{1,0:T(8,128)(2,1)} %bitcast.9), channel_id=1, source_target_pairs={{0,1},{1,0},{2,3},{3,2},{4,5},{5,4},{6,7},{7,6},{8,9},{9,8},{10,11... | collective-permute-start | bytes 2359304 | tf_op jit(solution)/shard_map/ppermute | solution.py:1080
  1.2 28.1 %collective-permute-start.2 = (bf16[512,768]{1,0:T(8,128)(2,1)}, bf16[512,768]{1,0:T(8,128)(2,1)}, u32[]{:S(2)}, u32[]{:S(2)}) collective-permute-start(bf16[512,768]{1,0:T(8,128)(2,1)} %bitcast.15), channel_id=1, source_target_pairs={{0,2},{1,3},{2,0},{3,1},{4,6},{5,7},{6,4},{7,5},{8,10},{9,11},{10,... | collective-permute-start | bytes 2359304 | tf_op jit(solution)/shard_map/ppermute | solution.py:1080
  4.8 1.2 collective-permute-start.4
  6.0 0.6 copy-start.3
  8.7 30.9 %collective-permute-start.5 = (bf16[528,768]{1,0:T(8,128)(2,1)}, bf16[528,768]{1,0:T(8,128)(2,1)}, u32[]{:S(2)}, u32[]{:S(2)}) collective-permute-start(bf16[528,768]{1,0:T(8,128)(2,1)} %pad_maximum_fusion), channel_id=1, source_target_pairs={{0,2},{1,3},{2,0},{3,1},{4,6},{5,7},{6,4},{7,5},{8,10},{9,11},{10,... | collective-permute-start | bytes 2433032 | tf_op jit(solution)/shard_map/ppermute | solution.py:1080
  29.3 5.0 %collective-permute-start.3 = (bf16[512,768]{1,0:T(8,128)(2,1)}, bf16[512,768]{1,0:T(8,128)(2,1)}, u32[]{:S(2)}, u32[]{:S(2)}) collective-permute-start(bf16[512,768]{1,0:T(8,128)(2,1)} %collective-permute-done.2.x_ref.xa), channel_id=1, source_target_pairs={{0,1},{1,0},{2,3},{3,2},{4,5},{5,4},{6,7},{7,6},{8,9},{9,8},{10,11... | collective-permute-start | bytes 2359304 | tf_op jit(solution)/shard_map/ppermute | solution.py:1080
  39.6 13.8 %collective-permute-start.6 = (bf16[528,768]{1,0:T(8,128)(2,1)}, bf16[528,768]{1,0:T(8,128)(2,1)}, u32[]{:S(2)}, u32[]{:S(2)}) collective-permute-start(bf16[528,768]{1,0:T(8,128)(2,1)} %collective-permute-done.5.pair_far.ca), channel_id=1, source_target_pairs={{0,1},{1,0},{2,3},{3,2},{4,5},{5,4},{6,7},{7,6},{8,9},{9,8},{10,11... | collective-permute-start | bytes 2433032 | tf_op jit(solution)/shard_map/ppermute | solution.py:1080
  73.9 34.4 %collective-permute-start.9 = (bf16[2,512,768]{2,1,0:T(8,128)(2,1)}, bf16[2,512,768]{2,1,0:T(8,128)(2,1)}, u32[]{:S(2)}, u32[]{:S(2)}) collective-permute-start(bf16[2,512,768]{2,1,0:T(8,128)(2,1)} %get-tuple-element.134), channel_id=1, source_target_pairs={{0,1},{1,0},{2,3},{3,2},{4,5},{5,4},{6,7},{7,6},{8,9},{9,8},{10,11... | collective-permute-start | bytes 4718600 | tf_op jit(solution)/shard_map/ppermute | solution.py:1080
  74.4 33.8 %collective-permute-start.8 = (bf16[768,512]{1,0:T(8,128)(2,1)}, bf16[768,512]{1,0:T(8,128)(2,1)}, u32[]{:S(2)}, u32[]{:S(2)}) collective-permute-start(bf16[768,512]{1,0:T(8,128)(2,1)} %get-tuple-element.132), channel_id=1, source_target_pairs={{0,8},{4,12},{8,0},{12,4},{16,24},{20,28},{24,16},{28,20},{1,9},{5... | collective-permute-start | bytes 2359304 | tf_op jit(solution)/shard_map/ppermute | solution.py:1080
  76.6 31.7 %collective-permute-start.7 = (bf16[384,768]{1,0:T(8,128)(2,1)}, bf16[384,768]{1,0:T(8,128)(2,1)}, u32[]{:S(2)}, u32[]{:S(2)}) collective-permute-start(bf16[384,768]{1,0:T(8,128)(2,1)} %get-tuple-element.130), channel_id=1, source_target_pairs={{0,4},{4,0},{8,12},{12,8},{16,20},{20,16},{24,28},{28,24},{1,5},{5... | collective-permute-start | bytes 1769480 | tf_op jit(solution)/shard_map/ppermute | solution.py:1080
  107.0 14.2 %collective-permute-start.13 = (bf16[400,576]{1,0:T(8,128)(2,1)}, bf16[400,576]{1,0:T(8,128)(2,1)}, u32[]{:S(2)}, u32[]{:S(2)}) collective-permute-start(bf16[400,576]{1,0:T(8,128)(2,1)} %get-tuple-element.145), channel_id=1, source_target_pairs={{0,4},{4,0},{8,12},{12,8},{16,20},{20,16},{24,28},{28,24},{1,5},{5... | collective-permute-start | bytes 1382408 | tf_op jit(solution)/shard_map/ppermute | solution.py:1080
  111.8 20.7 %collective-permute-start.11 = (bf16[512,768]{1,0:T(8,128)(2,1)}, bf16[512,768]{1,0:T(8,128)(2,1)}, u32[]{:S(2)}, u32[]{:S(2)}) collective-permute-start(bf16[512,768]{1,0:T(8,128)(2,1)} %get-tuple-element.135), channel_id=1, source_target_pairs={{0,2},{1,3},{2,0},{3,1},{4,6},{5,7},{6,4},{7,5},{8,10},{9,11},{10,... | collective-permute-start | bytes 2359304 | tf_op jit(solution)/shard_map/ppermute | solution.py:1080
  120.4 15.5 %copy-start = (bf16[512,768]{1,0:T(8,128)(2,1)S(1)}, bf16[512,768]{1,0:T(8,128)(2,1)}, u32[]{:S(2)}) copy-start(bf16[512,768]{1,0:T(8,128)(2,1)} %get-tuple-element.142) | copy-start | bytes 2359300
  120.4 10.2 %collective-permute-start.10 = (bf16[384,512]{1,0:T(8,128)(2,1)}, bf16[384,512]{1,0:T(8,128)(2,1)S(1)}, u32[]{:S(2)}, u32[]{:S(2)}) collective-permute-start(bf16[384,512]{1,0:T(8,128)(2,1)} %get-tuple-element.141), channel_id=1, source_target_pairs={{0,4},{4,0},{8,12},{12,8},{16,20},{20,16},{24,28},{28,24},{1,5},{5... | collective-permute-start | bytes 1179656 | tf_op jit(solution)/shard_map/ppermute | solution.py:1080
  121.3 14.6 %collective-permute-start.12 = (bf16[512,768]{1,0:T(8,128)(2,1)}, bf16[512,768]{1,0:T(8,128)(2,1)S(1)}, u32[]{:S(2)}, u32[]{:S(2)}) collective-permute-start(bf16[512,768]{1,0:T(8,128)(2,1)} %get-tuple-element.143), channel_id=1, source_target_pairs={{0,1},{1,0},{2,3},{3,2},{4,5},{5,4},{6,7},{7,6},{8,9},{9,8},{10,11... | collective-permute-start | bytes 2359304 | tf_op jit(solution)/shard_map/ppermute | solution.py:1080
  123.2 14.2 %collective-permute-start.14 = (bf16[208,576]{1,0:T(8,128)(2,1)S(1)}, bf16[208,576]{1,0:T(8,128)(2,1)S(1)}, u32[]{:S(2)}, u32[]{:S(2)}) collective-permute-start(bf16[208,576]{1,0:T(8,128)(2,1)S(1)} %pad_maximum_fusion.1), channel_id=1, source_target_pairs={{0,8},{4,12},{8,0},{12,4},{16,24},{20,28},{24,16},{28,20},{1,9},{5... | collective-permute-start | bytes 718856 | tf_op jit(solution)/shard_map/ppermute | solution.py:1080
  124.3 22.8 %collective-permute-start.23 = (bf16[192,768]{1,0:T(8,128)(2,1)}, bf16[192,768]{1,0:T(8,128)(2,1)}, u32[]{:S(2)}, u32[]{:S(2)}) collective-permute-start(bf16[192,768]{1,0:T(8,128)(2,1)} %get-tuple-element.165), channel_id=1, source_target_pairs={{0,8},{4,12},{8,0},{12,4},{16,24},{20,28},{24,16},{28,20},{1,9},{5... | collective-permute-start | bytes 884744 | tf_op jit(solution)/shard_map/ppermute | solution.py:1080
  130.6 5.3 %copy-start.2 = (bf16[384,512]{1,0:T(8,128)(2,1)}, bf16[384,512]{1,0:T(8,128)(2,1)S(1)}, u32[]{:S(2)}) copy-start(bf16[384,512]{1,0:T(8,128)(2,1)S(1)} %collective-permute-done.10) | copy-start | bytes 1179652
  130.6 29.0 %collective-permute-start.17 = (bf16[512,768]{1,0:T(8,128)(2,1)}, bf16[512,768]{1,0:T(8,128)(2,1)}, u32[]{:S(2)}, u32[]{:S(2)}) collective-permute-start(bf16[512,768]{1,0:T(8,128)(2,1)} %get-tuple-element.154), channel_id=1, source_target_pairs={{0,1},{1,0},{2,3},{3,2},{4,5},{5,4},{6,7},{7,6},{8,9},{9,8},{10,11... | collective-permute-start | bytes 2359304 | tf_op jit(solution)/shard_map/ppermute | solution.py:1080
  132.5 9.6 %collective-permute-start.15 = (bf16[192,512]{1,0:T(8,128)(2,1)}, bf16[192,512]{1,0:T(8,128)(2,1)}, u32[]{:S(2)}, u32[]{:S(2)}) collective-permute-start(bf16[192,512]{1,0:T(8,128)(2,1)} %add_convert_fusion.3), channel_id=1, source_target_pairs={{0,16},{4,20},{8,24},{12,28},{16,0},{20,4},{24,8},{28,12},{1,17},{... | collective-permute-start | bytes 589832 | tf_op jit(solution)/shard_map/ppermute | solution.py:1080
  136.9 26.0 %collective-permute-start.18 = (bf16[512,768]{1,0:T(8,128)(2,1)}, bf16[512,768]{1,0:T(8,128)(2,1)}, u32[]{:S(2)}, u32[]{:S(2)}) collective-permute-start(bf16[512,768]{1,0:T(8,128)(2,1)} %add_convert_fusion), channel_id=1, source_target_pairs={{0,2},{1,3},{2,0},{3,1},{4,6},{5,7},{6,4},{7,5},{8,10},{9,11},{10,... | collective-permute-start | bytes 2359304 | tf_op jit(solution)/shard_map/ppermute | solution.py:1080
  137.4 1.1 copy-start.1
  139.2 13.0 %collective-permute-start.16 = (bf16[112,576]{1,0:T(8,128)(2,1)}, bf16[112,576]{1,0:T(8,128)(2,1)}, u32[]{:S(2)}, u32[]{:S(2)}) collective-permute-start(bf16[112,576]{1,0:T(8,128)(2,1)} %pad_maximum_fusion.2.refs_4_), channel_id=1, source_target_pairs={{0,16},{4,20},{8,24},{12,28},{16,0},{20,4},{24,8},{28,12},{1,17},{... | collective-permute-start | bytes 387080 | tf_op jit(solution)/shard_map/ppermute | solution.py:1080
  144.1 22.3 %collective-permute-start.19 = (bf16[192,512]{1,0:T(8,128)(2,1)}, bf16[192,512]{1,0:T(8,128)(2,1)}, u32[]{:S(2)}, u32[]{:S(2)}) collective-permute-start(bf16[192,512]{1,0:T(8,128)(2,1)} %add_convert_fusion.2), channel_id=1, source_target_pairs={{0,0},{1,8},{2,16},{3,24},{4,1},{5,9},{6,17},{7,25},{8,2},{9,10},{... | collective-permute-start | bytes 589832 | tf_op jit(solution)/shard_map/ppermute | solution.py:1092
  148.9 22.6 %collective-permute-start.24 = (bf16[96,768]{1,0:T(8,128)(2,1)}, bf16[96,768]{1,0:T(8,128)(2,1)}, u32[]{:S(2)}, u32[]{:S(2)}) collective-permute-start(bf16[96,768]{1,0:T(8,128)(2,1)} %add_convert_fusion.4), channel_id=1, source_target_pairs={{0,16},{4,20},{8,24},{12,28},{16,0},{20,4},{24,8},{28,12},{1,17},{... | collective-permute-start | bytes 442376 | tf_op jit(solution)/shard_map/ppermute | solution.py:1080
  154.9 13.9 %collective-permute-start.20 = (f32[128,192]{1,0:T(8,128)}, f32[128,192]{1,0:T(8,128)}, u32[]{:S(2)}, u32[]{:S(2)}) collective-permute-start(f32[128,192]{1,0:T(8,128)} %get-tuple-element.159), channel_id=1, source_target_pairs={{0,1},{1,0},{2,3},{3,2},{4,5},{5,4},{6,7},{7,6},{8,9},{9,8},{10,11... | collective-permute-start | bytes 294920 | tf_op jit(solution)/shard_map/ppermute | solution.py:1080
  159.6 9.2 %collective-permute-start.21 = (f32[128,192]{1,0:T(8,128)}, f32[128,192]{1,0:T(8,128)}, u32[]{:S(2)}, u32[]{:S(2)}) collective-permute-start(f32[128,192]{1,0:T(8,128)} %get-tuple-element.160), channel_id=1, source_target_pairs={{0,2},{1,3},{2,0},{3,1},{4,6},{5,7},{6,4},{7,5},{8,10},{9,11},{10,... | collective-permute-start | bytes 294920 | tf_op jit(solution)/shard_map/ppermute | solution.py:1080
  163.0 5.8 %collective-permute-start.22 = (f32[32,192]{1,0:T(8,128)}, f32[32,192]{1,0:T(8,128)}, u32[]{:S(2)}, u32[]{:S(2)}) collective-permute-start(f32[32,192]{1,0:T(8,128)} %get-tuple-element.152.small), channel_id=1, source_target_pairs={{0,3},{1,2},{2,1},{3,0},{4,7},{5,6},{6,5},{7,4},{8,11},{9,10},{10,... | collective-permute-start | bytes 73736 | tf_op jit(solution)/shard_map/ppermute | solution.py:1080

commit v11 on v10

--- a/solution.py
+++ b/solution.py
@@ -1250,7 +1250,7 @@
         out_args = (after(tok_own, qkv_send), out_even, out_got, out_far, b_out, b_down)
         result = finish(result_kernel, "result", seq, *out_args)
         meta = after(meta, result)
-        lower[0] = after(lower[0], result)
+        lower[0] = after(lower[0], result, up_send)
         piece = sum(term[:width].astype(F32) for term in lower).astype(BF16)
         meta = after(meta, piece)
         piece = spread_rows(piece)

time: 176 us -> 176 us (level)
  starting transfers between devices: 31.9 us -> 24.1 us
  waiting for transfers between devices: 8.72 us -> 13.3 us
  Pallas kernels: 115 us -> 119 us
    ppermute x24, starting transfers between devices: 28.9 us -> 21.2 us  [swap(): return lax.ppermute(value, axis, [(i, i ^ mask) for i in range(size)])]
    ppermute x24, waiting for transfers between devices: 8.72 us -> 13.3 us  [swap(): return lax.ppermute(value, axis, [(i, i ^ mask) for i in range(size)])]
    pallas_call x1, Pallas kernels: 20.4 us -> 23.1 us  [attend_back(): pl.pallas_call(partial(attend_back_kernel, per), out_shape=jax.ShapeDtype...]
  transfers between devices with their start and end apart: 25 -> 25, of which waited for: 4 -> 4; matrix products, arithmetic and copies ran while one was open for 8% -> 8% of each run, Pallas kernels for 55% -> 57%
where the time goes in v11:
time: 176 us; the launch traced here: 174 us
  Pallas kernels  119 us (68%)
  starting transfers between devices  24.1 us (14%)
  other arithmetic  15.8 us (9%)
  waiting for transfers between devices  13.3 us (8%)
    pallas_call x2, Pallas kernels, feed_forward(): pl.pallas_call(body, out_shape=outs, grid_spec=pltpu.PrefetchScalarGridSp...  39.3 us
    pallas_call x1, Pallas kernels, attend_back(): pl.pallas_call(partial(attend_back_kernel, per), out_shape=jax.ShapeDtype...  23.1 us
    ppermute x24, starting transfers between devices, swap(): return lax.ppermute(value, axis, [(i, i ^ mask) for i in range(size)])  21.2 us
    pallas_call x1, Pallas kernels, attend(): pl.pallas_call(partial(attend_kernel, per), out_shape=[jax.ShapeDtypeStru...  14.3 us
    ppermute x24, waiting for transfers between devices, swap(): return lax.ppermute(value, axis, [(i, i ^ mask) for i in range(size)])  13.3 us
    pallas_call x2, Pallas kernels, project(): pl.pallas_call(partial(qkv_kernel, slot), out_shape=[out] * 3, grid_spec=...  9.09 us
    pallas_call x1, Pallas kernels, joined_weight(): pl.pallas_call(partial(weight_kernel, rows), out_shape=[jax.ShapeDtypeStr...  8.54 us
    pallas_call x1, Pallas kernels, norm_grad(): pl.pallas_call(norm_kernel, out_shape=[jax.ShapeDtypeStruct((seq, D), BF1...  6.98 us
  transfers between devices with their start and end apart: 25, of which 4 were waited for; matrix products, arithmetic and copies ran while one was open for 8% of the time, Pallas kernels for 57%

profile of v11, /device:TPU:0, one launch (start us, length us, event | category | flops | bytes accessed | tf_op | source)
XLA Modules:
  0.0 174.2 jit_solution(6129809608545107746)
XLA Ops:
  1.2 2.9 %collective-permute-start.2 = (bf16[512,768]{1,0:T(8,128)(2,1)}, bf16[512,768]{1,0:T(8,128)(2,1)}, u32[]{:S(2)}, u32[]{:S(2)}) collective-permute-start(bf16[512,768]{1,0:T(8,128)(2,1)} %bitcast.15), channel_id=1, source_target_pairs={{0,2},{1,3},{2,0},{3,1},{4,6},{5,7},{6,4},{7,5},{8,10},{9,11},{10,... | collective-permute-start | bytes 2359304 | tf_op jit(solution)/shard_map/ppermute | solution.py:1080
  4.8 1.2 collective-permute-done.4
  6.6 2.1 %pad_maximum_fusion = bf16[528,768]{1,0:T(8,128)(2,1)} fusion(bf16[16,768]{1,0:T(8,128)(2,1)S(1)} %fusion.5.pair_own, bf16[512,768]{1,0:T(8,128)(2,1)} %bitcast.10), kind=kLoop, calls=%fused_computation.1 | loop fusion | flops 1622016 | bytes 1622016 | tf_op jit(solution)/shard_map/concatenate | solution.py:1162
  10.4 18.9 %mlp_first.1 = (bf16[1024,768]{1,0:T(8,128)(2,1)}, bf16[2048,768]{1,0:T(8,128)(2,1)}, bf16[2048,768]{1,0:T(8,128)(2,1)}, bf16[2048,192]{1,0:T(8,128)(2,1)}, f32[...) custom-call(s32[2]{0:T(128)} %pad_add_fusion.meta, ...), custom_call_target="tpu_custom_call" | custom-call | tf_op jit(solution)/shard_map/mlp_first/pallas_call | solution.py:488
  29.8 4.5 %qkv_2.1 = (bf16[2048,192]{1,0:T(8,128)(2,1)}, bf16[2048,192]{1,0:T(8,128)(2,1)}, bf16[2048,192]{1,0:T(8,128)(2,1)}) custom-call(s32[2]{0:T(128)} %pad_add_fusion.meta, bf16[512,768]{1,0:T(8,128)(2,1)} %collective-permute-done.2.x_ref.xa, f32[768]{0:T(1024)} %refs_8_.1, f32[768]{0:T(1024)} %refs_3_.1, ...), custom_call_target="tpu_custom_call", output_to_operand_aliasing={{0}: (8, {}), {1}: (9, {}), {2}: (10, {})} | custom-call | tf_op jit(solution)/shard_map/qkv_2/pallas_call | solution.py:181
  34.3 4.5 %qkv_3.1 = (bf16[2048,192]{1,0:T(8,128)(2,1)}, bf16[2048,192]{1,0:T(8,128)(2,1)}, bf16[2048,192]{1,0:T(8,128)(2,1)}) custom-call(s32[2]{0:T(128)} %pad_add_fusion.meta, bf16[512,768]{1,0:T(8,128)(2,1)} %collective-permute-done.3.x_ref.xb, f32[768]{0:T(1024)} %refs_8_.1, f32[768]{0:T(1024)} %refs_3_.1, ...), custom_call_target="tpu_custom_call", output_to_operand_aliasing={{0}: (8, {}), {1}: (9, {}), {2}: (10, {})} | custom-call | tf_op jit(solution)/shard_map/qkv_3/pallas_call | solution.py:181
  40.3 14.3 %attend.1 = (bf16[2048,192]{1,0:T(8,128)(2,1)}, f32[3,8,1,256]{3,2,1,0:T(1,128)}, s32[8,1,256]{2,1,0:T(1,128)}, s32[8]{0:T(128)}, s32[8]{0:T(128)}) custom-call(s32[2]{0:T(128)} %pad_add_fusion.meta, s32[1]{0:T(128)S(6)} %copy.50.valid, bf16[2048,192]{1,0:T(8,128)(2,1)} %get-tuple-element.105.q_ref, bf16[2048,192]{1,0:T(8,128)(2,1)} %get-tuple-element.106.k_ref, ...), custom_call_target="tpu_custom_call" | custom-call | tf_op jit(solution)/shard_map/attend/pallas_call | solution.py:622
  54.6 20.4 %mlp_second.1 = (bf16[2048,768]{1,0:T(8,128)(2,1)}, bf16[2048,768]{1,0:T(8,128)(2,1)}, bf16[2048,192]{1,0:T(8,128)(2,1)}, f32[8,768]{1,0:T(8,128)}, bf16[2,512,7...) custom-call(s32[2]{0:T(128)} %pad_add_fusion.meta, ...), custom_call_target="tpu_custom_call", output_to_operand_aliasing={{0}: (19, {}), {1}: (20, {}), {2}: (21, {})} | custom-call | tf_op jit(solution)/shard_map/mlp_second/pallas_call | solution.py:488
  75.6 2.2 %collective-permute-start.8 = (bf16[768,512]{1,0:T(8,128)(2,1)}, bf16[768,512]{1,0:T(8,128)(2,1)}, u32[]{:S(2)}, u32[]{:S(2)}) collective-permute-start(bf16[768,512]{1,0:T(8,128)(2,1)} %get-tuple-element.132), channel_id=1, source_target_pairs={{0,8},{4,12},{8,0},{12,4},{16,24},{20,28},{24,16},{28,20},{1,9},{5... | collective-permute-start | bytes 2359304 | tf_op jit(solution)/shard_map/ppermute | solution.py:1080
  78.1 23.1 %attend_back.1.refs_0_.refs_1_.refs_2_.refs_3_ = bf16[2048,576]{1,0:T(8,128)(2,1)} custom-call(s32[2]{0:T(128)} %pad_add_fusion.meta, s32[8]{0:T(128)} %get-tuple-element.121.lo, s32[8]{0:T(128)} %get-tuple-element.122.hi, bf16[2048,192]{1,0:T(8,128)(2,1)} %get-tuple-element.105.q_ref, bf16[2048,192]{1,0:T(8,128)(2,1)} %get-tuple-element.106.k_ref, ...), custom_call_target="tpu_custom_call" | custom-call | tf_op jit(solution)/shard_map/attend_back/pallas_call | solution.py:766
  101.2 8.5 %joined_weight.1 = (bf16[400,576]{1,0:T(8,128)(2,1)}, bf16[400,576]{1,0:T(8,128)(2,1)}, f32[16,576]{1,0:T(8,128)}) custom-call(s32[2]{0:T(128)} %pad_add_fusion.meta, bf16[2048,576]{1,0:T(8,128)(2,1)} %attend_back.1.refs_0_.refs_1_.refs_2_.refs_3_, bf16[2048,768]{1,0:T(8,128)(2,1)} %get-tuple-element.126.refs_1_, f32[768]{0:T(1024)} %refs_8_.1, ...), custom_call_target="tpu_custom_call" | custom-call | tf_op jit(solution)/shard_map/joined_weight/pallas_call | solution.py:863
  109.8 2.3 %collective-permute-start.13 = (bf16[400,576]{1,0:T(8,128)(2,1)}, bf16[400,576]{1,0:T(8,128)(2,1)}, u32[]{:S(2)}, u32[]{:S(2)}) collective-permute-start(bf16[400,576]{1,0:T(8,128)(2,1)} %get-tuple-element.145), channel_id=1, source_target_pairs={{0,4},{4,0},{8,12},{12,8},{16,20},{20,16},{24,28},{28,24},{1,5},{5... | collective-permute-start | bytes 1382408 | tf_op jit(solution)/shard_map/ppermute | solution.py:1080
  112.1 3.6 %first_sums.1 = (bf16[192,768]{1,0:T(8,128)(2,1)}, bf16[384,512]{1,0:T(8,128)(2,1)}, bf16[512,768]{1,0:T(8,128)(2,1)}) custom-call(s32[2]{0:T(128)} %pad_add_fusion.meta, bf16[384,768]{1,0:T(8,128)(2,1)} %get-tuple-element.165.refs_0_, bf16[384,768]{1,0:T(8,128)(2,1)} %collective-permute-done.7.refs_1_, bf16[768,512]{1,0:T(8,128)(2,1)} %get-tuple-element.152.refs_2_, ...), custom_call_target="tpu_custom_call" | custom-call | tf_op jit(solution)/shard_map/first_sums/pallas_call | solution.py:953
  115.7 1.5 collective-permute-start.11
  117.2 7.0 %norm_grad.1 = (bf16[512,768]{1,0:T(8,128)(2,1)}, bf16[512,768]{1,0:T(8,128)(2,1)}, bf16[512,768]{1,0:T(8,128)(2,1)}, bf16[512,768]{1,0:T(8,128)(2,1)}) custom-call(s32[2]{0:T(128)} %pad_add_fusion.meta, bf16[2048,576]{1,0:T(8,128)(2,1)} %attend_back.1.refs_0_.refs_1_.refs_2_.refs_3_, bf16[2048,576]{1,0:T(8,128)(2,1)} %attend_back.1.refs_0_.refs_1_.refs_2_.refs_3_, ...), custom_call_target="tpu_custom_call" | custom-call | tf_op jit(solution)/shard_map/norm_grad/pallas_call | solution.py:894
  125.2 1.1 add_convert_fusion.1
  126.3 1.9 %collective-permute-start.14 = (bf16[208,576]{1,0:T(8,128)(2,1)S(1)}, bf16[208,576]{1,0:T(8,128)(2,1)S(1)}, u32[]{:S(2)}, u32[]{:S(2)}) collective-permute-start(bf16[208,576]{1,0:T(8,128)(2,1)S(1)} %pad_maximum_fusion.1), channel_id=1, source_target_pairs={{0,8},{4,12},{8,0},{12,4},{16,24},{20,28},{24,16},{28,20},{1,9},{5... | collective-permute-start | bytes 718856 | tf_op jit(solution)/shard_map/ppermute | solution.py:1080
  128.4 6.0 %collective-permute-done.10 = bf16[384,512]{1,0:T(8,128)(2,1)S(1)} collective-permute-done((bf16[384,512]{1,0:T(8,128)(2,1)}, bf16[384,512]{1,0:T(8,128)(2,1)S(1)}, u32[]{:S(2)}, u32[]{:S(2)}) %collective-permute-start.10) | collective-permute-done | bytes 393248 | tf_op jit(solution)/shard_map/ppermute | solution.py:1080
  134.4 1.9 %add_convert_fusion.3 = bf16[192,512]{1,0:T(8,128)(2,1)} fusion(bf16[384,512]{1,0:T(8,128)(2,1)S(1)} %collective-permute-done.10, bf16[768,512]{1,0:T(8,128)(2,1)} %collective-permute-done.8.refs_3_, bf16[768,512]{1,0:T(8,128)(2,1)} %get-tuple-element.152.refs_2_), kind=kLoop, calls=%fused_computation.4 | loop fusion | flops 589824 | bytes 786432 | tf_op jit(solution)/shard_map/convert_element_type | solution.py:1063
  139.8 2.9 %collective-permute-start.17 = (bf16[112,576]{1,0:T(8,128)(2,1)}, bf16[112,576]{1,0:T(8,128)(2,1)}, u32[]{:S(2)}, u32[]{:S(2)}) collective-permute-start(bf16[112,576]{1,0:T(8,128)(2,1)} %pad_maximum_fusion.2.refs_4_), channel_id=1, source_target_pairs={{0,16},{4,20},{8,24},{12,28},{16,0},{20,4},{24,8},{28,12},{1,17},{... | collective-permute-start | bytes 387080 | tf_op jit(solution)/shard_map/ppermute | solution.py:1080
  142.7 2.8 %result.1 = bf16[512,768]{1,0:T(8,128)(2,1)} custom-call(bf16[512,768]{1,0:T(8,128)(2,1)} %bitcast.17, bf16[2,512,768]{2,1,0:T(8,128)(2,1)} %get-tuple-element.133.even, bf16[2,512,768]{2,1,0:T(8,128)(2,1)} %collective-permute-done.9.near, bf16[512,768]{1,0:T(8,128)(2,1)} %collective-permute-done.11.far, f32[768]{0:T(1024)} %b_out.1, f32[768]{0:T(1024)} %b_down.1), custom_call_target="tpu_custom_call" | custom-call | tf_op jit(solution)/shard_map/result/pallas_call | solution.py:1128
  145.5 1.8 %add_convert_fusion.4 = bf16[96,768]{1,0:T(8,128)(2,1)} fusion(bf16[192,768]{1,0:T(8,128)(2,1)} %collective-permute-done.15, bf16[384,768]{1,0:T(8,128)(2,1)} %collective-permute-done.7.refs_1_, bf16[384,768]{1,0:T(8,128)(2,1)} %get-tuple-element.165.refs_0_), kind=kLoop, calls=%fused_computation.6 | loop fusion | flops 442368 | bytes 589824 | tf_op jit(solution)/shard_map/convert_element_type | solution.py:1063
  147.3 5.4 %collective-permute-done.16 = bf16[192,512]{1,0:T(8,128)(2,1)} collective-permute-done((bf16[192,512]{1,0:T(8,128)(2,1)}, bf16[192,512]{1,0:T(8,128)(2,1)}, u32[]{:S(2)}, u32[]{:S(2)}) %collective-permute-start.16) | collective-permute-done | bytes 196640 | tf_op jit(solution)/shard_map/ppermute | solution.py:1080
  152.6 2.0 %add_convert_fusion.2 = bf16[192,512]{1,0:T(8,128)(2,1)} fusion(bf16[192,512]{1,0:T(8,128)(2,1)} %collective-permute-done.16, bf16[384,512]{1,0:T(8,128)(2,1)} %copy-done.2, bf16[768,512]{1,0:T(8,128)(2,1)} %collective-permute-done.8.refs_3_, bf16[768,512]{1,0:T(8,128)(2,1)} %get-tuple-element.152.refs_2_), kind=kLoop, calls=%fused_computation.3 | loop fusion | flops 786432 | bytes 983040 | tf_op jit(solution)/shard_map/convert_element_type | solution.py:1254
  154.6 3.0 %collective-permute-start.20 = (bf16[192,512]{1,0:T(8,128)(2,1)}, bf16[192,512]{1,0:T(8,128)(2,1)}, u32[]{:S(2)}, u32[]{:S(2)}) collective-permute-start(bf16[192,512]{1,0:T(8,128)(2,1)} %add_convert_fusion.2), channel_id=1, source_target_pairs={{0,0},{1,8},{2,16},{3,24},{4,1},{5,9},{6,17},{7,25},{8,2},{9,10},{... | collective-permute-start | bytes 589832 | tf_op jit(solution)/shard_map/ppermute | solution.py:1092
  157.6 1.7 collective-permute-start.24
  159.3 2.6 %last_qkv.1 = (f32[96,192]{1,0:T(8,128)}, f32[128,192]{1,0:T(8,128)}, f32[128,192]{1,0:T(8,128)}, f32[32,192]{1,0:T(8,128)}) custom-call(s32[2]{0:T(128)} %pad_add_fusion.meta, bf16[400,576]{1,0:T(8,128)(2,1)} %get-tuple-element.144.refs_0_, bf16[400,576]{1,0:T(8,128)(2,1)} %collective-permute-done.13.refs_1_, bf16[208,576]{1,0:T(8,128)(2,1)} %copy-done.1, ...), custom_call_target="tpu_custom_call" | custom-call | tf_op jit(solution)/shard_map/last_qkv/pallas_call | solution.py:915
  162.0 1.8 %collective-permute-start.23 = (f32[32,192]{1,0:T(8,128)}, f32[32,192]{1,0:T(8,128)}, u32[]{:S(2)}, u32[]{:S(2)}) collective-permute-start(f32[32,192]{1,0:T(8,128)} %get-tuple-element.154.small), channel_id=1, source_target_pairs={{0,3},{1,2},{2,1},{3,0},{4,7},{5,6},{6,5},{7,4},{8,11},{9,10},{10,... | collective-permute-start | bytes 73736 | tf_op jit(solution)/shard_map/ppermute | solution.py:1080
  163.8 3.5 %token_grad.1 = bf16[512,768]{1,0:T(8,128)(2,1)} custom-call(bf16[512,768]{1,0:T(8,128)(2,1)} %bitcast.18, bf16[512,768]{1,0:T(8,128)(2,1)} %get-tuple-element.138.even, bf16[512,768]{1,0:T(8,128)(2,1)} %collective-permute-done.18.near, bf16[512,768]{1,0:T(8,128)(2,1)} %collective-permute-done.19.far, bf16[512,768]{1,0:T(8,128)(2,1)} %bitcast.13), custom_call_target="tpu_custom_call" | custom-call | tf_op jit(solution)/shard_map/token_grad/pallas_call | solution.py:1128
  167.3 2.4 %lower.1 = (f32[192,384]{1,0:T(8,128)}, f32[96,192]{1,0:T(8,128)}) custom-call(s32[2]{0:T(128)} %pad_add_fusion.meta, bf16[192,512]{1,0:T(8,128)(2,1)} %collective-permute-done.20.piece), custom_call_target="tpu_custom_call" | custom-call | tf_op jit(solution)/shard_map/lower/pallas_call | solution.py:915
  169.6 2.7 %assemble.1 = (f32[96,576]{1,0:T(8,128)}, f32[2304]{0:T(1024)}, f32[768]{0:T(1024)}, f32[3072]{0:T(1024)}, f32[768]{0:T(1024)}, /*index=5*/f32[768]{0:T(1024)}, f32[768]{0:T(1024)}, f32[768]{0:T(1024)}, f32[768]{0:T(1024)}) custom-call(s32[2]{0:T(128)} %pad_add_fusion.meta, f32[96,192]{1,0:T(8,128)} %get-tuple-element.160.kept, ...), custom_call_target="tpu_custom_call" | custom-call | tf_op jit(solution)/shard_map/assemble/pallas_call | solution.py:1046
  172.3 1.9 %convert_add_fusion = f32[96,768]{1,0:T(8,128)} fusion(bf16[96,768]{1,0:T(8,128)(2,1)} %collective-permute-done.24, bf16[192,768]{1,0:T(8,128)(2,1)} %collective-permute-done.15, bf16[384,768]{1,0:T(8,128)(2,1)} %collective-permute-done.7.refs_1_, bf16[384,768]{1,0:T(8,128)(2,1)} %get-tuple-element.165.refs_0_), kind=kLoop, calls=%fused_computation.5 | loop fusion | flops 516096 | bytes 884736 | tf_op jit(solution)/shard_map/add | solution.py:1281
  (55 shorter events, 10.4 us)
Async XLA Ops:
  0.6 9.7 %collective-permute-start = (bf16[512,768]{1,0:T(8,128)(2,1)}, bf16[512,768]{1,0:T(8,128)(2,1)}, u32[]{:S(2)}, u32[]{:S(2)}) collective-permute-start(bf16[512,768]{1,0:T(8,128)(2,1)} %bitcast.14), channel_id=1, source_target_pairs={{0,1},{1,0},{2,3},{3,2},{4,5},{5,4},{6,7},{7,6},{8,9},{9,8},{10,11... | collective-permute-start | bytes 2359304 | tf_op jit(solution)/shard_map/ppermute | solution.py:1080
  1.2 9.2 %collective-permute-start.1 = (bf16[512,768]{1,0:T(8,128)(2,1)}, bf16[512,768]{1,0:T(8,128)(2,1)}, u32[]{:S(2)}, u32[]{:S(2)}) collective-permute-start(bf16[512,768]{1,0:T(8,128)(2,1)} %bitcast.9), channel_id=1, source_target_pairs={{0,1},{1,0},{2,3},{3,2},{4,5},{5,4},{6,7},{7,6},{8,9},{9,8},{10,11... | collective-permute-start | bytes 2359304 | tf_op jit(solution)/shard_map/ppermute | solution.py:1080
  1.2 28.1 %collective-permute-start.2 = (bf16[512,768]{1,0:T(8,128)(2,1)}, bf16[512,768]{1,0:T(8,128)(2,1)}, u32[]{:S(2)}, u32[]{:S(2)}) collective-permute-start(bf16[512,768]{1,0:T(8,128)(2,1)} %bitcast.15), channel_id=1, source_target_pairs={{0,2},{1,3},{2,0},{3,1},{4,6},{5,7},{6,4},{7,5},{8,10},{9,11},{10,... | collective-permute-start | bytes 2359304 | tf_op jit(solution)/shard_map/ppermute | solution.py:1080
  4.8 1.2 collective-permute-start.4
  6.0 0.6 copy-start.3
  8.7 30.9 %collective-permute-start.5 = (bf16[528,768]{1,0:T(8,128)(2,1)}, bf16[528,768]{1,0:T(8,128)(2,1)}, u32[]{:S(2)}, u32[]{:S(2)}) collective-permute-start(bf16[528,768]{1,0:T(8,128)(2,1)} %pad_maximum_fusion), channel_id=1, source_target_pairs={{0,2},{1,3},{2,0},{3,1},{4,6},{5,7},{6,4},{7,5},{8,10},{9,11},{10,... | collective-permute-start | bytes 2433032 | tf_op jit(solution)/shard_map/ppermute | solution.py:1080
  29.3 5.0 %collective-permute-start.3 = (bf16[512,768]{1,0:T(8,128)(2,1)}, bf16[512,768]{1,0:T(8,128)(2,1)}, u32[]{:S(2)}, u32[]{:S(2)}) collective-permute-start(bf16[512,768]{1,0:T(8,128)(2,1)} %collective-permute-done.2.x_ref.xa), channel_id=1, source_target_pairs={{0,1},{1,0},{2,3},{3,2},{4,5},{5,4},{6,7},{7,6},{8,9},{9,8},{10,11... | collective-permute-start | bytes 2359304 | tf_op jit(solution)/shard_map/ppermute | solution.py:1080
  39.6 15.0 %collective-permute-start.6 = (bf16[528,768]{1,0:T(8,128)(2,1)}, bf16[528,768]{1,0:T(8,128)(2,1)}, u32[]{:S(2)}, u32[]{:S(2)}) collective-permute-start(bf16[528,768]{1,0:T(8,128)(2,1)} %collective-permute-done.5.pair_far.ca), channel_id=1, source_target_pairs={{0,1},{1,0},{2,3},{3,2},{4,5},{5,4},{6,7},{7,6},{8,9},{9,8},{10,11... | collective-permute-start | bytes 2433032 | tf_op jit(solution)/shard_map/ppermute | solution.py:1080
  75.0 37.1 %collective-permute-start.9 = (bf16[2,512,768]{2,1,0:T(8,128)(2,1)}, bf16[2,512,768]{2,1,0:T(8,128)(2,1)}, u32[]{:S(2)}, u32[]{:S(2)}) collective-permute-start(bf16[2,512,768]{2,1,0:T(8,128)(2,1)} %get-tuple-element.134), channel_id=1, source_target_pairs={{0,1},{1,0},{2,3},{3,2},{4,5},{5,4},{6,7},{7,6},{8,9},{9,8},{10,11... | collective-permute-start | bytes 4718600 | tf_op jit(solution)/shard_map/ppermute | solution.py:1080
  75.6 36.5 %collective-permute-start.8 = (bf16[768,512]{1,0:T(8,128)(2,1)}, bf16[768,512]{1,0:T(8,128)(2,1)}, u32[]{:S(2)}, u32[]{:S(2)}) collective-permute-start(bf16[768,512]{1,0:T(8,128)(2,1)} %get-tuple-element.132), channel_id=1, source_target_pairs={{0,8},{4,12},{8,0},{12,4},{16,24},{20,28},{24,16},{28,20},{1,9},{5... | collective-permute-start | bytes 2359304 | tf_op jit(solution)/shard_map/ppermute | solution.py:1080
  77.8 34.3 %collective-permute-start.7 = (bf16[384,768]{1,0:T(8,128)(2,1)}, bf16[384,768]{1,0:T(8,128)(2,1)}, u32[]{:S(2)}, u32[]{:S(2)}) collective-permute-start(bf16[384,768]{1,0:T(8,128)(2,1)} %get-tuple-element.130), channel_id=1, source_target_pairs={{0,4},{4,0},{8,12},{12,8},{16,20},{20,16},{24,28},{28,24},{1,5},{5... | collective-permute-start | bytes 1769480 | tf_op jit(solution)/shard_map/ppermute | solution.py:1080
  109.8 14.6 %collective-permute-start.13 = (bf16[400,576]{1,0:T(8,128)(2,1)}, bf16[400,576]{1,0:T(8,128)(2,1)}, u32[]{:S(2)}, u32[]{:S(2)}) collective-permute-start(bf16[400,576]{1,0:T(8,128)(2,1)} %get-tuple-element.145), channel_id=1, source_target_pairs={{0,4},{4,0},{8,12},{12,8},{16,20},{20,16},{24,28},{28,24},{1,5},{5... | collective-permute-start | bytes 1382408 | tf_op jit(solution)/shard_map/ppermute | solution.py:1080
  115.7 20.7 %collective-permute-start.11 = (bf16[512,768]{1,0:T(8,128)(2,1)}, bf16[512,768]{1,0:T(8,128)(2,1)}, u32[]{:S(2)}, u32[]{:S(2)}) collective-permute-start(bf16[512,768]{1,0:T(8,128)(2,1)} %get-tuple-element.135), channel_id=1, source_target_pairs={{0,2},{1,3},{2,0},{3,1},{4,6},{5,7},{6,4},{7,5},{8,10},{9,11},{10,... | collective-permute-start | bytes 2359304 | tf_op jit(solution)/shard_map/ppermute | solution.py:1080
  124.2 12.2 %copy-start = (bf16[512,768]{1,0:T(8,128)(2,1)S(1)}, bf16[512,768]{1,0:T(8,128)(2,1)}, u32[]{:S(2)}) copy-start(bf16[512,768]{1,0:T(8,128)(2,1)} %get-tuple-element.142) | copy-start | bytes 2359300
  124.2 10.2 %collective-permute-start.10 = (bf16[384,512]{1,0:T(8,128)(2,1)}, bf16[384,512]{1,0:T(8,128)(2,1)S(1)}, u32[]{:S(2)}, u32[]{:S(2)}) collective-permute-start(bf16[384,512]{1,0:T(8,128)(2,1)} %get-tuple-element.141), channel_id=1, source_target_pairs={{0,4},{4,0},{8,12},{12,8},{16,20},{20,16},{24,28},{28,24},{1,5},{5... | collective-permute-start | bytes 1179656 | tf_op jit(solution)/shard_map/ppermute | solution.py:1080
  124.3 12.1 %collective-permute-start.12 = (bf16[512,768]{1,0:T(8,128)(2,1)}, bf16[512,768]{1,0:T(8,128)(2,1)S(1)}, u32[]{:S(2)}, u32[]{:S(2)}) collective-permute-start(bf16[512,768]{1,0:T(8,128)(2,1)} %get-tuple-element.143), channel_id=1, source_target_pairs={{0,1},{1,0},{2,3},{3,2},{4,5},{5,4},{6,7},{7,6},{8,9},{9,8},{10,11... | collective-permute-start | bytes 2359304 | tf_op jit(solution)/shard_map/ppermute | solution.py:1080
  126.3 11.6 %collective-permute-start.14 = (bf16[208,576]{1,0:T(8,128)(2,1)S(1)}, bf16[208,576]{1,0:T(8,128)(2,1)S(1)}, u32[]{:S(2)}, u32[]{:S(2)}) collective-permute-start(bf16[208,576]{1,0:T(8,128)(2,1)S(1)} %pad_maximum_fusion.1), channel_id=1, source_target_pairs={{0,8},{4,12},{8,0},{12,4},{16,24},{20,28},{24,16},{28,20},{1,9},{5... | collective-permute-start | bytes 718856 | tf_op jit(solution)/shard_map/ppermute | solution.py:1080
  128.2 17.3 %collective-permute-start.15 = (bf16[192,768]{1,0:T(8,128)(2,1)}, bf16[192,768]{1,0:T(8,128)(2,1)}, u32[]{:S(2)}, u32[]{:S(2)}) collective-permute-start(bf16[192,768]{1,0:T(8,128)(2,1)} %get-tuple-element.151), channel_id=1, source_target_pairs={{0,8},{4,12},{8,0},{12,4},{16,24},{20,28},{24,16},{28,20},{1,9},{5... | collective-permute-start | bytes 884744 | tf_op jit(solution)/shard_map/ppermute | solution.py:1080
  134.4 1.9 %copy-start.2 = (bf16[384,512]{1,0:T(8,128)(2,1)}, bf16[384,512]{1,0:T(8,128)(2,1)S(1)}, u32[]{:S(2)}) copy-start(bf16[384,512]{1,0:T(8,128)(2,1)S(1)} %collective-permute-done.10) | copy-start | bytes 1179652
  134.4 27.5 %collective-permute-start.18 = (bf16[512,768]{1,0:T(8,128)(2,1)}, bf16[512,768]{1,0:T(8,128)(2,1)}, u32[]{:S(2)}, u32[]{:S(2)}) collective-permute-start(bf16[512,768]{1,0:T(8,128)(2,1)} %get-tuple-element.156), channel_id=1, source_target_pairs={{0,1},{1,0},{2,3},{3,2},{4,5},{5,4},{6,7},{7,6},{8,9},{9,8},{10,11... | collective-permute-start | bytes 2359304 | tf_op jit(solution)/shard_map/ppermute | solution.py:1080
  136.4 16.3 %collective-permute-start.16 = (bf16[192,512]{1,0:T(8,128)(2,1)}, bf16[192,512]{1,0:T(8,128)(2,1)}, u32[]{:S(2)}, u32[]{:S(2)}) collective-permute-start(bf16[192,512]{1,0:T(8,128)(2,1)} %add_convert_fusion.3), channel_id=1, source_target_pairs={{0,16},{4,20},{8,24},{12,28},{16,0},{20,4},{24,8},{28,12},{1,17},{... | collective-permute-start | bytes 589832 | tf_op jit(solution)/shard_map/ppermute | solution.py:1080
  137.4 24.6 %collective-permute-start.19 = (bf16[512,768]{1,0:T(8,128)(2,1)}, bf16[512,768]{1,0:T(8,128)(2,1)}, u32[]{:S(2)}, u32[]{:S(2)}) collective-permute-start(bf16[512,768]{1,0:T(8,128)(2,1)} %add_convert_fusion), channel_id=1, source_target_pairs={{0,2},{1,3},{2,0},{3,1},{4,6},{5,7},{6,4},{7,5},{8,10},{9,11},{10,... | collective-permute-start | bytes 2359304 | tf_op jit(solution)/shard_map/ppermute | solution.py:1080
  137.9 1.1 copy-start.1
  139.8 19.5 %collective-permute-start.17 = (bf16[112,576]{1,0:T(8,128)(2,1)}, bf16[112,576]{1,0:T(8,128)(2,1)}, u32[]{:S(2)}, u32[]{:S(2)}) collective-permute-start(bf16[112,576]{1,0:T(8,128)(2,1)} %pad_maximum_fusion.2.refs_4_), channel_id=1, source_target_pairs={{0,16},{4,20},{8,24},{12,28},{16,0},{20,4},{24,8},{28,12},{1,17},{... | collective-permute-start | bytes 387080 | tf_op jit(solution)/shard_map/ppermute | solution.py:1080
  154.6 12.6 %collective-permute-start.20 = (bf16[192,512]{1,0:T(8,128)(2,1)}, bf16[192,512]{1,0:T(8,128)(2,1)}, u32[]{:S(2)}, u32[]{:S(2)}) collective-permute-start(bf16[192,512]{1,0:T(8,128)(2,1)} %add_convert_fusion.2), channel_id=1, source_target_pairs={{0,0},{1,8},{2,16},{3,24},{4,1},{5,9},{6,17},{7,25},{8,2},{9,10},{... | collective-permute-start | bytes 589832 | tf_op jit(solution)/shard_map/ppermute | solution.py:1092
  157.6 14.7 %collective-permute-start.24 = (bf16[96,768]{1,0:T(8,128)(2,1)}, bf16[96,768]{1,0:T(8,128)(2,1)}, u32[]{:S(2)}, u32[]{:S(2)}) collective-permute-start(bf16[96,768]{1,0:T(8,128)(2,1)} %add_convert_fusion.4), channel_id=1, source_target_pairs={{0,16},{4,20},{8,24},{12,28},{16,0},{20,4},{24,8},{28,12},{1,17},{... | collective-permute-start | bytes 442376 | tf_op jit(solution)/shard_map/ppermute | solution.py:1080
  161.9 7.7 %collective-permute-start.21 = (f32[128,192]{1,0:T(8,128)}, f32[128,192]{1,0:T(8,128)}, u32[]{:S(2)}, u32[]{:S(2)}) collective-permute-start(f32[128,192]{1,0:T(8,128)} %get-tuple-element.161), channel_id=1, source_target_pairs={{0,1},{1,0},{2,3},{3,2},{4,5},{5,4},{6,7},{7,6},{8,9},{9,8},{10,11... | collective-permute-start | bytes 294920 | tf_op jit(solution)/shard_map/ppermute | solution.py:1080
  161.9 7.7 %collective-permute-start.22 = (f32[128,192]{1,0:T(8,128)}, f32[128,192]{1,0:T(8,128)}, u32[]{:S(2)}, u32[]{:S(2)}) collective-permute-start(f32[128,192]{1,0:T(8,128)} %get-tuple-element.162), channel_id=1, source_target_pairs={{0,2},{1,3},{2,0},{3,1},{4,6},{5,7},{6,4},{7,5},{8,10},{9,11},{10,... | collective-permute-start | bytes 294920 | tf_op jit(solution)/shard_map/ppermute | solution.py:1080
  162.0 7.6 %collective-permute-start.23 = (f32[32,192]{1,0:T(8,128)}, f32[32,192]{1,0:T(8,128)}, u32[]{:S(2)}, u32[]{:S(2)}) collective-permute-start(f32[32,192]{1,0:T(8,128)} %get-tuple-element.154.small), channel_id=1, source_target_pairs={{0,3},{1,2},{2,1},{3,0},{4,7},{5,6},{6,5},{7,4},{8,11},{9,10},{10,... | collective-permute-start | bytes 73736 | tf_op jit(solution)/shard_map/ppermute | solution.py:1080

commit v12 on v11

--- a/solution.py
+++ b/solution.py
@@ -1214,7 +1214,7 @@
         up_send, low_send, out_send = block_sums(
             "first_sums",
             meta,
-            2,
+            1,
             (half // 2, [(term, half // 2) for term in up]),
             (half, [(term, half) for term in lower]),
             (seq, [(term, seq) for term in flat]),

time: 176 us -> 177 us (level)
  transfers between devices with their start and end apart: 25 -> 25, of which waited for: 4 -> 5; matrix products, arithmetic and copies ran while one was open for 8% -> 8% of each run, Pallas kernels for 57% -> 57%
where the time goes in v12:
time: 177 us; the launch traced here: 174 us
  Pallas kernels  120 us (68%)
  starting transfers between devices  24.8 us (14%)
  other arithmetic  15.7 us (9%)
  waiting for transfers between devices  11.8 us (7%)
    pallas_call x2, Pallas kernels, feed_forward(): pl.pallas_call(body, out_shape=outs, grid_spec=pltpu.PrefetchScalarGridSp...  39.3 us
    pallas_call x1, Pallas kernels, attend_back(): pl.pallas_call(partial(attend_back_kernel, per), out_shape=jax.ShapeDtype...  23.7 us
    ppermute x24, starting transfers between devices, swap(): return lax.ppermute(value, axis, [(i, i ^ mask) for i in range(size)])  21.8 us
    pallas_call x1, Pallas kernels, attend(): pl.pallas_call(partial(attend_kernel, per), out_shape=[jax.ShapeDtypeStru...  14.7 us
    ppermute x24, waiting for transfers between devices, swap(): return lax.ppermute(value, axis, [(i, i ^ mask) for i in range(size)])  11.8 us
    pallas_call x2, Pallas kernels, project(): pl.pallas_call(partial(qkv_kernel, slot), out_shape=[out] * 3, grid_spec=...  9.09 us
    pallas_call x1, Pallas kernels, joined_weight(): pl.pallas_call(partial(weight_kernel, rows), out_shape=[jax.ShapeDtypeStr...  8.54 us
    pallas_call x1, Pallas kernels, norm_grad(): pl.pallas_call(norm_kernel, out_shape=[jax.ShapeDtypeStruct((seq, D), BF1...  6.98 us
  transfers between devices with their start and end apart: 25, of which 5 were waited for; matrix products, arithmetic and copies ran while one was open for 8% of the time, Pallas kernels for 57%

profile of v12, /device:TPU:0, one launch (start us, length us, event | category | flops | bytes accessed | tf_op | source)
XLA Modules:
  0.0 174.3 jit_solution(13867367188392739247)
XLA Ops:
  1.2 2.9 %collective-permute-start.2 = (bf16[512,768]{1,0:T(8,128)(2,1)}, bf16[512,768]{1,0:T(8,128)(2,1)}, u32[]{:S(2)}, u32[]{:S(2)}) collective-permute-start(bf16[512,768]{1,0:T(8,128)(2,1)} %bitcast.15), channel_id=1, source_target_pairs={{0,2},{1,3},{2,0},{3,1},{4,6},{5,7},{6,4},{7,5},{8,10},{9,11},{10,... | collective-permute-start | bytes 2359304 | tf_op jit(solution)/shard_map/ppermute | solution.py:1080
  4.8 1.2 collective-permute-done.4
  6.6 2.1 %pad_maximum_fusion = bf16[528,768]{1,0:T(8,128)(2,1)} fusion(bf16[16,768]{1,0:T(8,128)(2,1)S(1)} %fusion.5.pair_own, bf16[512,768]{1,0:T(8,128)(2,1)} %bitcast.10), kind=kLoop, calls=%fused_computation.1 | loop fusion | flops 1622016 | bytes 1622016 | tf_op jit(solution)/shard_map/concatenate | solution.py:1162
  10.4 18.9 %mlp_first.1 = (bf16[1024,768]{1,0:T(8,128)(2,1)}, bf16[2048,768]{1,0:T(8,128)(2,1)}, bf16[2048,768]{1,0:T(8,128)(2,1)}, bf16[2048,192]{1,0:T(8,128)(2,1)}, f32[...) custom-call(s32[2]{0:T(128)} %pad_add_fusion.meta, ...), custom_call_target="tpu_custom_call" | custom-call | tf_op jit(solution)/shard_map/mlp_first/pallas_call | solution.py:488
  29.8 4.5 %qkv_2.1 = (bf16[2048,192]{1,0:T(8,128)(2,1)}, bf16[2048,192]{1,0:T(8,128)(2,1)}, bf16[2048,192]{1,0:T(8,128)(2,1)}) custom-call(s32[2]{0:T(128)} %pad_add_fusion.meta, bf16[512,768]{1,0:T(8,128)(2,1)} %collective-permute-done.2.x_ref.xa, f32[768]{0:T(1024)} %refs_8_.1, f32[768]{0:T(1024)} %refs_3_.1, ...), custom_call_target="tpu_custom_call", output_to_operand_aliasing={{0}: (8, {}), {1}: (9, {}), {2}: (10, {})} | custom-call | tf_op jit(solution)/shard_map/qkv_2/pallas_call | solution.py:181
  34.3 4.5 %qkv_3.1 = (bf16[2048,192]{1,0:T(8,128)(2,1)}, bf16[2048,192]{1,0:T(8,128)(2,1)}, bf16[2048,192]{1,0:T(8,128)(2,1)}) custom-call(s32[2]{0:T(128)} %pad_add_fusion.meta, bf16[512,768]{1,0:T(8,128)(2,1)} %collective-permute-done.3.x_ref.xb, f32[768]{0:T(1024)} %refs_8_.1, f32[768]{0:T(1024)} %refs_3_.1, ...), custom_call_target="tpu_custom_call", output_to_operand_aliasing={{0}: (8, {}), {1}: (9, {}), {2}: (10, {})} | custom-call | tf_op jit(solution)/shard_map/qkv_3/pallas_call | solution.py:181
  40.3 14.7 %attend.1 = (bf16[2048,192]{1,0:T(8,128)(2,1)}, f32[3,8,1,256]{3,2,1,0:T(1,128)}, s32[8,1,256]{2,1,0:T(1,128)}, s32[8]{0:T(128)}, s32[8]{0:T(128)}) custom-call(s32[2]{0:T(128)} %pad_add_fusion.meta, s32[1]{0:T(128)S(6)} %copy.50.valid, bf16[2048,192]{1,0:T(8,128)(2,1)} %get-tuple-element.105.q_ref, bf16[2048,192]{1,0:T(8,128)(2,1)} %get-tuple-element.106.k_ref, ...), custom_call_target="tpu_custom_call" | custom-call | tf_op jit(solution)/shard_map/attend/pallas_call | solution.py:622
  55.0 20.4 %mlp_second.1 = (bf16[2048,768]{1,0:T(8,128)(2,1)}, bf16[2048,768]{1,0:T(8,128)(2,1)}, bf16[2048,192]{1,0:T(8,128)(2,1)}, f32[8,768]{1,0:T(8,128)}, bf16[2,512,7...) custom-call(s32[2]{0:T(128)} %pad_add_fusion.meta, ...), custom_call_target="tpu_custom_call", output_to_operand_aliasing={{0}: (19, {}), {1}: (20, {}), {2}: (21, {})} | custom-call | tf_op jit(solution)/shard_map/mlp_second/pallas_call | solution.py:488
  75.9 2.2 %collective-permute-start.7 = (bf16[384,768]{1,0:T(8,128)(2,1)}, bf16[384,768]{1,0:T(8,128)(2,1)}, u32[]{:S(2)}, u32[]{:S(2)}) collective-permute-start(bf16[384,768]{1,0:T(8,128)(2,1)} %get-tuple-element.130), channel_id=1, source_target_pairs={{0,4},{4,0},{8,12},{12,8},{16,20},{20,16},{24,28},{28,24},{1,5},{5... | collective-permute-start | bytes 1769480 | tf_op jit(solution)/shard_map/ppermute | solution.py:1080
  78.1 23.7 %attend_back.1.refs_0_.refs_1_.refs_2_.refs_3_ = bf16[2048,576]{1,0:T(8,128)(2,1)} custom-call(s32[2]{0:T(128)} %pad_add_fusion.meta, s32[8]{0:T(128)} %get-tuple-element.121.lo, s32[8]{0:T(128)} %get-tuple-element.122.hi, bf16[2048,192]{1,0:T(8,128)(2,1)} %get-tuple-element.105.q_ref, bf16[2048,192]{1,0:T(8,128)(2,1)} %get-tuple-element.106.k_ref, ...), custom_call_target="tpu_custom_call" | custom-call | tf_op jit(solution)/shard_map/attend_back/pallas_call | solution.py:766
  101.8 8.5 %joined_weight.1 = (bf16[400,576]{1,0:T(8,128)(2,1)}, bf16[400,576]{1,0:T(8,128)(2,1)}, f32[16,576]{1,0:T(8,128)}) custom-call(s32[2]{0:T(128)} %pad_add_fusion.meta, bf16[2048,576]{1,0:T(8,128)(2,1)} %attend_back.1.refs_0_.refs_1_.refs_2_.refs_3_, bf16[2048,768]{1,0:T(8,128)(2,1)} %get-tuple-element.126.refs_1_, f32[768]{0:T(1024)} %refs_8_.1, ...), custom_call_target="tpu_custom_call" | custom-call | tf_op jit(solution)/shard_map/joined_weight/pallas_call | solution.py:863
  110.4 3.7 %first_sums.1 = (bf16[192,768]{1,0:T(8,128)(2,1)}, bf16[384,512]{1,0:T(8,128)(2,1)}, bf16[512,768]{1,0:T(8,128)(2,1)}) custom-call(s32[2]{0:T(128)} %pad_add_fusion.meta, bf16[384,768]{1,0:T(8,128)(2,1)} %get-tuple-element.165.refs_0_, bf16[384,768]{1,0:T(8,128)(2,1)} %collective-permute-done.7.refs_1_, bf16[768,512]{1,0:T(8,128)(2,1)} %get-tuple-element.152.refs_2_, ...), custom_call_target="tpu_custom_call" | custom-call | tf_op jit(solution)/shard_map/first_sums/pallas_call | solution.py:953
  114.1 1.6 collective-permute-start.11
  115.6 7.0 %norm_grad.1 = (bf16[512,768]{1,0:T(8,128)(2,1)}, bf16[512,768]{1,0:T(8,128)(2,1)}, bf16[512,768]{1,0:T(8,128)(2,1)}, bf16[512,768]{1,0:T(8,128)(2,1)}) custom-call(s32[2]{0:T(128)} %pad_add_fusion.meta, bf16[2048,576]{1,0:T(8,128)(2,1)} %attend_back.1.refs_0_.refs_1_.refs_2_.refs_3_, bf16[2048,576]{1,0:T(8,128)(2,1)} %attend_back.1.refs_0_.refs_1_.refs_2_.refs_3_, ...), custom_call_target="tpu_custom_call" | custom-call | tf_op jit(solution)/shard_map/norm_grad/pallas_call | solution.py:894
  122.6 2.1 %collective-permute-start.10 = (bf16[384,512]{1,0:T(8,128)(2,1)}, bf16[384,512]{1,0:T(8,128)(2,1)S(1)}, u32[]{:S(2)}, u32[]{:S(2)}) collective-permute-start(bf16[384,512]{1,0:T(8,128)(2,1)} %get-tuple-element.141), channel_id=1, source_target_pairs={{0,4},{4,0},{8,12},{12,8},{16,20},{20,16},{24,28},{28,24},{1,5},{5... | collective-permute-start | bytes 1179656 | tf_op jit(solution)/shard_map/ppermute | solution.py:1080
  125.5 1.1 add_convert_fusion.1
  126.7 2.0 %collective-permute-start.15 = (bf16[192,768]{1,0:T(8,128)(2,1)}, bf16[192,768]{1,0:T(8,128)(2,1)}, u32[]{:S(2)}, u32[]{:S(2)}) collective-permute-start(bf16[192,768]{1,0:T(8,128)(2,1)} %get-tuple-element.151), channel_id=1, source_target_pairs={{0,8},{4,12},{8,0},{12,4},{16,24},{20,28},{24,16},{28,20},{1,9},{5... | collective-permute-start | bytes 884744 | tf_op jit(solution)/shard_map/ppermute | solution.py:1080
  128.7 4.4 %collective-permute-done.10 = bf16[384,512]{1,0:T(8,128)(2,1)S(1)} collective-permute-done((bf16[384,512]{1,0:T(8,128)(2,1)}, bf16[384,512]{1,0:T(8,128)(2,1)S(1)}, u32[]{:S(2)}, u32[]{:S(2)}) %collective-permute-start.10) | collective-permute-done | bytes 393248 | tf_op jit(solution)/shard_map/ppermute | solution.py:1080
  133.1 1.9 %add_convert_fusion.3 = bf16[192,512]{1,0:T(8,128)(2,1)} fusion(bf16[384,512]{1,0:T(8,128)(2,1)S(1)} %collective-permute-done.10, bf16[768,512]{1,0:T(8,128)(2,1)} %collective-permute-done.8.refs_3_, bf16[768,512]{1,0:T(8,128)(2,1)} %get-tuple-element.152.refs_2_), kind=kLoop, calls=%fused_computation.4 | loop fusion | flops 589824 | bytes 786432 | tf_op jit(solution)/shard_map/convert_element_type | solution.py:1063
  135.1 2.8 %collective-permute-start.16 = (bf16[192,512]{1,0:T(8,128)(2,1)}, bf16[192,512]{1,0:T(8,128)(2,1)}, u32[]{:S(2)}, u32[]{:S(2)}) collective-permute-start(bf16[192,512]{1,0:T(8,128)(2,1)} %add_convert_fusion.3), channel_id=1, source_target_pairs={{0,16},{4,20},{8,24},{12,28},{16,0},{20,4},{24,8},{28,12},{1,17},{... | collective-permute-start | bytes 589832 | tf_op jit(solution)/shard_map/ppermute | solution.py:1080
  141.4 2.8 %result.1 = bf16[512,768]{1,0:T(8,128)(2,1)} custom-call(bf16[512,768]{1,0:T(8,128)(2,1)} %bitcast.17, bf16[2,512,768]{2,1,0:T(8,128)(2,1)} %get-tuple-element.133.even, bf16[2,512,768]{2,1,0:T(8,128)(2,1)} %collective-permute-done.9.near, bf16[512,768]{1,0:T(8,128)(2,1)} %collective-permute-done.11.far, f32[768]{0:T(1024)} %b_out.1, f32[768]{0:T(1024)} %b_down.1), custom_call_target="tpu_custom_call" | custom-call | tf_op jit(solution)/shard_map/result/pallas_call | solution.py:1128
  145.1 1.8 %add_convert_fusion.4 = bf16[96,768]{1,0:T(8,128)(2,1)} fusion(bf16[192,768]{1,0:T(8,128)(2,1)} %collective-permute-done.15, bf16[384,768]{1,0:T(8,128)(2,1)} %collective-permute-done.7.refs_1_, bf16[384,768]{1,0:T(8,128)(2,1)} %get-tuple-element.165.refs_0_), kind=kLoop, calls=%fused_computation.6 | loop fusion | flops 442368 | bytes 589824 | tf_op jit(solution)/shard_map/convert_element_type | solution.py:1063
  146.9 4.5 %collective-permute-done.16 = bf16[192,512]{1,0:T(8,128)(2,1)} collective-permute-done((bf16[192,512]{1,0:T(8,128)(2,1)}, bf16[192,512]{1,0:T(8,128)(2,1)}, u32[]{:S(2)}, u32[]{:S(2)}) %collective-permute-start.16) | collective-permute-done | bytes 196640 | tf_op jit(solution)/shard_map/ppermute | solution.py:1080
  151.3 2.0 %add_convert_fusion.2 = bf16[192,512]{1,0:T(8,128)(2,1)} fusion(bf16[192,512]{1,0:T(8,128)(2,1)} %collective-permute-done.16, bf16[384,512]{1,0:T(8,128)(2,1)} %copy-done.2, bf16[768,512]{1,0:T(8,128)(2,1)} %collective-permute-done.8.refs_3_, bf16[768,512]{1,0:T(8,128)(2,1)} %get-tuple-element.152.refs_2_), kind=kLoop, calls=%fused_computation.3 | loop fusion | flops 786432 | bytes 983040 | tf_op jit(solution)/shard_map/convert_element_type | solution.py:1254
  153.3 3.0 %collective-permute-start.20 = (bf16[192,512]{1,0:T(8,128)(2,1)}, bf16[192,512]{1,0:T(8,128)(2,1)}, u32[]{:S(2)}, u32[]{:S(2)}) collective-permute-start(bf16[192,512]{1,0:T(8,128)(2,1)} %add_convert_fusion.2), channel_id=1, source_target_pairs={{0,0},{1,8},{2,16},{3,24},{4,1},{5,9},{6,17},{7,25},{8,2},{9,10},{... | collective-permute-start | bytes 589832 | tf_op jit(solution)/shard_map/ppermute | solution.py:1092
  156.3 3.1 %collective-permute-start.24 = (bf16[96,768]{1,0:T(8,128)(2,1)}, bf16[96,768]{1,0:T(8,128)(2,1)}, u32[]{:S(2)}, u32[]{:S(2)}) collective-permute-start(bf16[96,768]{1,0:T(8,128)(2,1)} %add_convert_fusion.4), channel_id=1, source_target_pairs={{0,16},{4,20},{8,24},{12,28},{16,0},{20,4},{24,8},{28,12},{1,17},{... | collective-permute-start | bytes 442376 | tf_op jit(solution)/shard_map/ppermute | solution.py:1080
  159.4 2.6 %last_qkv.1 = (f32[96,192]{1,0:T(8,128)}, f32[128,192]{1,0:T(8,128)}, f32[128,192]{1,0:T(8,128)}, f32[32,192]{1,0:T(8,128)}) custom-call(s32[2]{0:T(128)} %pad_add_fusion.meta, bf16[400,576]{1,0:T(8,128)(2,1)} %get-tuple-element.144.refs_0_, bf16[400,576]{1,0:T(8,128)(2,1)} %collective-permute-done.13.refs_1_, bf16[208,576]{1,0:T(8,128)(2,1)} %copy-done.1, ...), custom_call_target="tpu_custom_call" | custom-call | tf_op jit(solution)/shard_map/last_qkv/pallas_call | solution.py:915
  162.1 1.8 %collective-permute-start.23 = (f32[32,192]{1,0:T(8,128)}, f32[32,192]{1,0:T(8,128)}, u32[]{:S(2)}, u32[]{:S(2)}) collective-permute-start(f32[32,192]{1,0:T(8,128)} %get-tuple-element.154.small), channel_id=1, source_target_pairs={{0,3},{1,2},{2,1},{3,0},{4,7},{5,6},{6,5},{7,4},{8,11},{9,10},{10,... | collective-permute-start | bytes 73736 | tf_op jit(solution)/shard_map/ppermute | solution.py:1080
  163.9 3.5 %token_grad.1 = bf16[512,768]{1,0:T(8,128)(2,1)} custom-call(bf16[512,768]{1,0:T(8,128)(2,1)} %bitcast.18, bf16[512,768]{1,0:T(8,128)(2,1)} %get-tuple-element.138.even, bf16[512,768]{1,0:T(8,128)(2,1)} %collective-permute-done.18.near, bf16[512,768]{1,0:T(8,128)(2,1)} %collective-permute-done.19.far, bf16[512,768]{1,0:T(8,128)(2,1)} %bitcast.13), custom_call_target="tpu_custom_call" | custom-call | tf_op jit(solution)/shard_map/token_grad/pallas_call | solution.py:1128
  167.4 2.4 %lower.1 = (f32[192,384]{1,0:T(8,128)}, f32[96,192]{1,0:T(8,128)}) custom-call(s32[2]{0:T(128)} %pad_add_fusion.meta, bf16[192,512]{1,0:T(8,128)(2,1)} %collective-permute-done.20.piece), custom_call_target="tpu_custom_call" | custom-call | tf_op jit(solution)/shard_map/lower/pallas_call | solution.py:915
  169.7 2.7 %assemble.1 = (f32[96,576]{1,0:T(8,128)}, f32[2304]{0:T(1024)}, f32[768]{0:T(1024)}, f32[3072]{0:T(1024)}, f32[768]{0:T(1024)}, /*index=5*/f32[768]{0:T(1024)}, f32[768]{0:T(1024)}, f32[768]{0:T(1024)}, f32[768]{0:T(1024)}) custom-call(s32[2]{0:T(128)} %pad_add_fusion.meta, f32[96,192]{1,0:T(8,128)} %get-tuple-element.160.kept, ...), custom_call_target="tpu_custom_call" | custom-call | tf_op jit(solution)/shard_map/assemble/pallas_call | solution.py:1046
  172.4 1.9 %convert_add_fusion = f32[96,768]{1,0:T(8,128)} fusion(bf16[96,768]{1,0:T(8,128)(2,1)} %collective-permute-done.24, bf16[192,768]{1,0:T(8,128)(2,1)} %collective-permute-done.15, bf16[384,768]{1,0:T(8,128)(2,1)} %collective-permute-done.7.refs_1_, bf16[384,768]{1,0:T(8,128)(2,1)} %get-tuple-element.165.refs_0_), kind=kLoop, calls=%fused_computation.5 | loop fusion | flops 516096 | bytes 884736 | tf_op jit(solution)/shard_map/add | solution.py:1281
  (55 shorter events, 10.7 us)
Async XLA Ops:
  0.6 9.7 %collective-permute-start = (bf16[512,768]{1,0:T(8,128)(2,1)}, bf16[512,768]{1,0:T(8,128)(2,1)}, u32[]{:S(2)}, u32[]{:S(2)}) collective-permute-start(bf16[512,768]{1,0:T(8,128)(2,1)} %bitcast.14), channel_id=1, source_target_pairs={{0,1},{1,0},{2,3},{3,2},{4,5},{5,4},{6,7},{7,6},{8,9},{9,8},{10,11... | collective-permute-start | bytes 2359304 | tf_op jit(solution)/shard_map/ppermute | solution.py:1080
  1.2 9.2 %collective-permute-start.1 = (bf16[512,768]{1,0:T(8,128)(2,1)}, bf16[512,768]{1,0:T(8,128)(2,1)}, u32[]{:S(2)}, u32[]{:S(2)}) collective-permute-start(bf16[512,768]{1,0:T(8,128)(2,1)} %bitcast.9), channel_id=1, source_target_pairs={{0,1},{1,0},{2,3},{3,2},{4,5},{5,4},{6,7},{7,6},{8,9},{9,8},{10,11... | collective-permute-start | bytes 2359304 | tf_op jit(solution)/shard_map/ppermute | solution.py:1080
  1.2 28.1 %collective-permute-start.2 = (bf16[512,768]{1,0:T(8,128)(2,1)}, bf16[512,768]{1,0:T(8,128)(2,1)}, u32[]{:S(2)}, u32[]{:S(2)}) collective-permute-start(bf16[512,768]{1,0:T(8,128)(2,1)} %bitcast.15), channel_id=1, source_target_pairs={{0,2},{1,3},{2,0},{3,1},{4,6},{5,7},{6,4},{7,5},{8,10},{9,11},{10,... | collective-permute-start | bytes 2359304 | tf_op jit(solution)/shard_map/ppermute | solution.py:1080
  4.8 1.2 collective-permute-start.4
  6.0 0.6 copy-start.3
  8.7 30.9 %collective-permute-start.5 = (bf16[528,768]{1,0:T(8,128)(2,1)}, bf16[528,768]{1,0:T(8,128)(2,1)}, u32[]{:S(2)}, u32[]{:S(2)}) collective-permute-start(bf16[528,768]{1,0:T(8,128)(2,1)} %pad_maximum_fusion), channel_id=1, source_target_pairs={{0,2},{1,3},{2,0},{3,1},{4,6},{5,7},{6,4},{7,5},{8,10},{9,11},{10,... | collective-permute-start | bytes 2433032 | tf_op jit(solution)/shard_map/ppermute | solution.py:1080
  29.3 5.0 %collective-permute-start.3 = (bf16[512,768]{1,0:T(8,128)(2,1)}, bf16[512,768]{1,0:T(8,128)(2,1)}, u32[]{:S(2)}, u32[]{:S(2)}) collective-permute-start(bf16[512,768]{1,0:T(8,128)(2,1)} %collective-permute-done.2.x_ref.xa), channel_id=1, source_target_pairs={{0,1},{1,0},{2,3},{3,2},{4,5},{5,4},{6,7},{7,6},{8,9},{9,8},{10,11... | collective-permute-start | bytes 2359304 | tf_op jit(solution)/shard_map/ppermute | solution.py:1080
  39.6 15.3 %collective-permute-start.6 = (bf16[528,768]{1,0:T(8,128)(2,1)}, bf16[528,768]{1,0:T(8,128)(2,1)}, u32[]{:S(2)}, u32[]{:S(2)}) collective-permute-start(bf16[528,768]{1,0:T(8,128)(2,1)} %collective-permute-done.5.pair_far.ca), channel_id=1, source_target_pairs={{0,1},{1,0},{2,3},{3,2},{4,5},{5,4},{6,7},{7,6},{8,9},{9,8},{10,11... | collective-permute-start | bytes 2433032 | tf_op jit(solution)/shard_map/ppermute | solution.py:1080
  75.4 35.0 %collective-permute-start.9 = (bf16[2,512,768]{2,1,0:T(8,128)(2,1)}, bf16[2,512,768]{2,1,0:T(8,128)(2,1)}, u32[]{:S(2)}, u32[]{:S(2)}) collective-permute-start(bf16[2,512,768]{2,1,0:T(8,128)(2,1)} %get-tuple-element.134), channel_id=1, source_target_pairs={{0,1},{1,0},{2,3},{3,2},{4,5},{5,4},{6,7},{7,6},{8,9},{9,8},{10,11... | collective-permute-start | bytes 4718600 | tf_op jit(solution)/shard_map/ppermute | solution.py:1080
  75.9 34.4 %collective-permute-start.8 = (bf16[768,512]{1,0:T(8,128)(2,1)}, bf16[768,512]{1,0:T(8,128)(2,1)}, u32[]{:S(2)}, u32[]{:S(2)}) collective-permute-start(bf16[768,512]{1,0:T(8,128)(2,1)} %get-tuple-element.132), channel_id=1, source_target_pairs={{0,8},{4,12},{8,0},{12,4},{16,24},{20,28},{24,16},{28,20},{1,9},{5... | collective-permute-start | bytes 2359304 | tf_op jit(solution)/shard_map/ppermute | solution.py:1080
  75.9 34.4 %collective-permute-start.7 = (bf16[384,768]{1,0:T(8,128)(2,1)}, bf16[384,768]{1,0:T(8,128)(2,1)}, u32[]{:S(2)}, u32[]{:S(2)}) collective-permute-start(bf16[384,768]{1,0:T(8,128)(2,1)} %get-tuple-element.130), channel_id=1, source_target_pairs={{0,4},{4,0},{8,12},{12,8},{16,20},{20,16},{24,28},{28,24},{1,5},{5... | collective-permute-start | bytes 1769480 | tf_op jit(solution)/shard_map/ppermute | solution.py:1080
  110.3 14.3 %collective-permute-start.13 = (bf16[400,576]{1,0:T(8,128)(2,1)}, bf16[400,576]{1,0:T(8,128)(2,1)}, u32[]{:S(2)}, u32[]{:S(2)}) collective-permute-start(bf16[400,576]{1,0:T(8,128)(2,1)} %get-tuple-element.145), channel_id=1, source_target_pairs={{0,4},{4,0},{8,12},{12,8},{16,20},{20,16},{24,28},{28,24},{1,5},{5... | collective-permute-start | bytes 1382408 | tf_op jit(solution)/shard_map/ppermute | solution.py:1080
  114.1 21.0 %collective-permute-start.11 = (bf16[512,768]{1,0:T(8,128)(2,1)}, bf16[512,768]{1,0:T(8,128)(2,1)}, u32[]{:S(2)}, u32[]{:S(2)}) collective-permute-start(bf16[512,768]{1,0:T(8,128)(2,1)} %get-tuple-element.135), channel_id=1, source_target_pairs={{0,2},{1,3},{2,0},{3,1},{4,6},{5,7},{6,4},{7,5},{8,10},{9,11},{10,... | collective-permute-start | bytes 2359304 | tf_op jit(solution)/shard_map/ppermute | solution.py:1080
  122.6 15.3 %copy-start = (bf16[512,768]{1,0:T(8,128)(2,1)S(1)}, bf16[512,768]{1,0:T(8,128)(2,1)}, u32[]{:S(2)}) copy-start(bf16[512,768]{1,0:T(8,128)(2,1)} %get-tuple-element.142) | copy-start | bytes 2359300
  122.6 10.5 %collective-permute-start.10 = (bf16[384,512]{1,0:T(8,128)(2,1)}, bf16[384,512]{1,0:T(8,128)(2,1)S(1)}, u32[]{:S(2)}, u32[]{:S(2)}) collective-permute-start(bf16[384,512]{1,0:T(8,128)(2,1)} %get-tuple-element.141), channel_id=1, source_target_pairs={{0,4},{4,0},{8,12},{12,8},{16,20},{20,16},{24,28},{28,24},{1,5},{5... | collective-permute-start | bytes 1179656 | tf_op jit(solution)/shard_map/ppermute | solution.py:1080
  124.7 13.2 %collective-permute-start.12 = (bf16[512,768]{1,0:T(8,128)(2,1)}, bf16[512,768]{1,0:T(8,128)(2,1)S(1)}, u32[]{:S(2)}, u32[]{:S(2)}) collective-permute-start(bf16[512,768]{1,0:T(8,128)(2,1)} %get-tuple-element.143), channel_id=1, source_target_pairs={{0,1},{1,0},{2,3},{3,2},{4,5},{5,4},{6,7},{7,6},{8,9},{9,8},{10,11... | collective-permute-start | bytes 2359304 | tf_op jit(solution)/shard_map/ppermute | solution.py:1080
  126.6 12.8 %collective-permute-start.14 = (bf16[208,576]{1,0:T(8,128)(2,1)S(1)}, bf16[208,576]{1,0:T(8,128)(2,1)S(1)}, u32[]{:S(2)}, u32[]{:S(2)}) collective-permute-start(bf16[208,576]{1,0:T(8,128)(2,1)S(1)} %pad_maximum_fusion.1), channel_id=1, source_target_pairs={{0,8},{4,12},{8,0},{12,4},{16,24},{20,28},{24,16},{28,20},{1,9},{5... | collective-permute-start | bytes 718856 | tf_op jit(solution)/shard_map/ppermute | solution.py:1080
  126.7 18.4 %collective-permute-start.15 = (bf16[192,768]{1,0:T(8,128)(2,1)}, bf16[192,768]{1,0:T(8,128)(2,1)}, u32[]{:S(2)}, u32[]{:S(2)}) collective-permute-start(bf16[192,768]{1,0:T(8,128)(2,1)} %get-tuple-element.151), channel_id=1, source_target_pairs={{0,8},{4,12},{8,0},{12,4},{16,24},{20,28},{24,16},{28,20},{1,9},{5... | collective-permute-start | bytes 884744 | tf_op jit(solution)/shard_map/ppermute | solution.py:1080
  133.1 4.8 %copy-start.2 = (bf16[384,512]{1,0:T(8,128)(2,1)}, bf16[384,512]{1,0:T(8,128)(2,1)S(1)}, u32[]{:S(2)}) copy-start(bf16[384,512]{1,0:T(8,128)(2,1)S(1)} %collective-permute-done.10) | copy-start | bytes 1179652
  133.1 28.9 %collective-permute-start.18 = (bf16[512,768]{1,0:T(8,128)(2,1)}, bf16[512,768]{1,0:T(8,128)(2,1)}, u32[]{:S(2)}, u32[]{:S(2)}) collective-permute-start(bf16[512,768]{1,0:T(8,128)(2,1)} %get-tuple-element.156), channel_id=1, source_target_pairs={{0,1},{1,0},{2,3},{3,2},{4,5},{5,4},{6,7},{7,6},{8,9},{9,8},{10,11... | collective-permute-start | bytes 2359304 | tf_op jit(solution)/shard_map/ppermute | solution.py:1080
  135.1 16.3 %collective-permute-start.16 = (bf16[192,512]{1,0:T(8,128)(2,1)}, bf16[192,512]{1,0:T(8,128)(2,1)}, u32[]{:S(2)}, u32[]{:S(2)}) collective-permute-start(bf16[192,512]{1,0:T(8,128)(2,1)} %add_convert_fusion.3), channel_id=1, source_target_pairs={{0,16},{4,20},{8,24},{12,28},{16,0},{20,4},{24,8},{28,12},{1,17},{... | collective-permute-start | bytes 589832 | tf_op jit(solution)/shard_map/ppermute | solution.py:1080
  139.0 23.2 %collective-permute-start.19 = (bf16[512,768]{1,0:T(8,128)(2,1)}, bf16[512,768]{1,0:T(8,128)(2,1)}, u32[]{:S(2)}, u32[]{:S(2)}) collective-permute-start(bf16[512,768]{1,0:T(8,128)(2,1)} %add_convert_fusion), channel_id=1, source_target_pairs={{0,2},{1,3},{2,0},{3,1},{4,6},{5,7},{6,4},{7,5},{8,10},{9,11},{10,... | collective-permute-start | bytes 2359304 | tf_op jit(solution)/shard_map/ppermute | solution.py:1080
  139.5 1.1 copy-start.1
  141.3 18.1 %collective-permute-start.17 = (bf16[112,576]{1,0:T(8,128)(2,1)}, bf16[112,576]{1,0:T(8,128)(2,1)}, u32[]{:S(2)}, u32[]{:S(2)}) collective-permute-start(bf16[112,576]{1,0:T(8,128)(2,1)} %pad_maximum_fusion.2.refs_4_), channel_id=1, source_target_pairs={{0,16},{4,20},{8,24},{12,28},{16,0},{20,4},{24,8},{28,12},{1,17},{... | collective-permute-start | bytes 387080 | tf_op jit(solution)/shard_map/ppermute | solution.py:1080
  153.3 14.0 %collective-permute-start.20 = (bf16[192,512]{1,0:T(8,128)(2,1)}, bf16[192,512]{1,0:T(8,128)(2,1)}, u32[]{:S(2)}, u32[]{:S(2)}) collective-permute-start(bf16[192,512]{1,0:T(8,128)(2,1)} %add_convert_fusion.2), channel_id=1, source_target_pairs={{0,0},{1,8},{2,16},{3,24},{4,1},{5,9},{6,17},{7,25},{8,2},{9,10},{... | collective-permute-start | bytes 589832 | tf_op jit(solution)/shard_map/ppermute | solution.py:1092
  156.3 16.1 %collective-permute-start.24 = (bf16[96,768]{1,0:T(8,128)(2,1)}, bf16[96,768]{1,0:T(8,128)(2,1)}, u32[]{:S(2)}, u32[]{:S(2)}) collective-permute-start(bf16[96,768]{1,0:T(8,128)(2,1)} %add_convert_fusion.4), channel_id=1, source_target_pairs={{0,16},{4,20},{8,24},{12,28},{16,0},{20,4},{24,8},{28,12},{1,17},{... | collective-permute-start | bytes 442376 | tf_op jit(solution)/shard_map/ppermute | solution.py:1080
  162.0 7.7 %collective-permute-start.21 = (f32[128,192]{1,0:T(8,128)}, f32[128,192]{1,0:T(8,128)}, u32[]{:S(2)}, u32[]{:S(2)}) collective-permute-start(f32[128,192]{1,0:T(8,128)} %get-tuple-element.161), channel_id=1, source_target_pairs={{0,1},{1,0},{2,3},{3,2},{4,5},{5,4},{6,7},{7,6},{8,9},{9,8},{10,11... | collective-permute-start | bytes 294920 | tf_op jit(solution)/shard_map/ppermute | solution.py:1080
  162.0 7.7 %collective-permute-start.22 = (f32[128,192]{1,0:T(8,128)}, f32[128,192]{1,0:T(8,128)}, u32[]{:S(2)}, u32[]{:S(2)}) collective-permute-start(f32[128,192]{1,0:T(8,128)} %get-tuple-element.162), channel_id=1, source_target_pairs={{0,2},{1,3},{2,0},{3,1},{4,6},{5,7},{6,4},{7,5},{8,10},{9,11},{10,... | collective-permute-start | bytes 294920 | tf_op jit(solution)/shard_map/ppermute | solution.py:1080
  162.1 7.6 %collective-permute-start.23 = (f32[32,192]{1,0:T(8,128)}, f32[32,192]{1,0:T(8,128)}, u32[]{:S(2)}, u32[]{:S(2)}) collective-permute-start(f32[32,192]{1,0:T(8,128)} %get-tuple-element.154.small), channel_id=1, source_target_pairs={{0,3},{1,2},{2,1},{3,0},{4,7},{5,6},{6,5},{7,4},{8,11},{9,10},{10,... | collective-permute-start | bytes 73736 | tf_op jit(solution)/shard_map/ppermute | solution.py:1080

commit v13 on v12

--- a/solution.py
+++ b/solution.py
@@ -857,7 +857,7 @@
 
 def joined_weight(meta, grad, normed, gain, shift, w, mlp_sums, rows):
     total, width = grad.shape
-    tile = 2 * TILE
+    tile = 4 * TILE
     chunks = chunk_shapes(width, rows, SMALL)
     args = [gain, shift, w, mlp_sums]
     return pl.pallas_call(

time: 177 us -> 176 us (level)
  Pallas kernels: 120 us -> 116 us
  waiting for transfers between devices: 11.8 us -> 14.3 us
    pallas_call x1, Pallas kernels: 23.7 us -> 21.1 us  [attend_back(): pl.pallas_call(partial(attend_back_kernel, per), out_shape=jax.ShapeDtype...]
    ppermute x24, waiting for transfers between devices: 11.8 us -> 14.3 us  [swap(): return lax.ppermute(value, axis, [(i, i ^ mask) for i in range(size)])]
  transfers between devices with their start and end apart: 25 -> 25, of which waited for: 5 -> 5; matrix products, arithmetic and copies ran while one was open for 8% -> 8% of each run, Pallas kernels for 57% -> 55%
where the time goes in v13:
time: 176 us; the launch traced here: 173 us
  Pallas kernels  116 us (66%)
  starting transfers between devices  25.8 us (15%)
  other arithmetic  15.8 us (9%)
  waiting for transfers between devices  14.3 us (8%)
    pallas_call x2, Pallas kernels, feed_forward(): pl.pallas_call(body, out_shape=outs, grid_spec=pltpu.PrefetchScalarGridSp...  39.3 us
    ppermute x24, starting transfers between devices, swap(): return lax.ppermute(value, axis, [(i, i ^ mask) for i in range(size)])  22.8 us
    pallas_call x1, Pallas kernels, attend_back(): pl.pallas_call(partial(attend_back_kernel, per), out_shape=jax.ShapeDtype...  21.1 us
    ppermute x24, waiting for transfers between devices, swap(): return lax.ppermute(value, axis, [(i, i ^ mask) for i in range(size)])  14.3 us
    pallas_call x1, Pallas kernels, attend(): pl.pallas_call(partial(attend_kernel, per), out_shape=[jax.ShapeDtypeStru...  13.5 us
    pallas_call x2, Pallas kernels, project(): pl.pallas_call(partial(qkv_kernel, slot), out_shape=[out] * 3, grid_spec=...  9.09 us
    pallas_call x1, Pallas kernels, joined_weight(): pl.pallas_call(partial(weight_kernel, rows), out_shape=[jax.ShapeDtypeStr...  7.91 us
    pallas_call x1, Pallas kernels, norm_grad(): pl.pallas_call(norm_kernel, out_shape=[jax.ShapeDtypeStruct((seq, D), BF1...  6.98 us
  transfers between devices with their start and end apart: 25, of which 5 were waited for; matrix products, arithmetic and copies ran while one was open for 8% of the time, Pallas kernels for 55%

profile of v13, /device:TPU:0, one launch (start us, length us, event | category | flops | bytes accessed | tf_op | source)
XLA Modules:
  0.0 173.5 jit_solution(7460423678160826490)
XLA Ops:
  1.2 2.9 %collective-permute-start.2 = (bf16[512,768]{1,0:T(8,128)(2,1)}, bf16[512,768]{1,0:T(8,128)(2,1)}, u32[]{:S(2)}, u32[]{:S(2)}) collective-permute-start(bf16[512,768]{1,0:T(8,128)(2,1)} %bitcast.15), channel_id=1, source_target_pairs={{0,2},{1,3},{2,0},{3,1},{4,6},{5,7},{6,4},{7,5},{8,10},{9,11},{10,... | collective-permute-start | bytes 2359304 | tf_op jit(solution)/shard_map/ppermute | solution.py:1080
  4.8 1.2 collective-permute-done.4
  6.6 2.1 %pad_maximum_fusion = bf16[528,768]{1,0:T(8,128)(2,1)} fusion(bf16[16,768]{1,0:T(8,128)(2,1)S(1)} %fusion.5.pair_own, bf16[512,768]{1,0:T(8,128)(2,1)} %bitcast.10), kind=kLoop, calls=%fused_computation.1 | loop fusion | flops 1622016 | bytes 1622016 | tf_op jit(solution)/shard_map/concatenate | solution.py:1162
  10.4 18.9 %mlp_first.1 = (bf16[1024,768]{1,0:T(8,128)(2,1)}, bf16[2048,768]{1,0:T(8,128)(2,1)}, bf16[2048,768]{1,0:T(8,128)(2,1)}, bf16[2048,192]{1,0:T(8,128)(2,1)}, f32[...) custom-call(s32[2]{0:T(128)} %pad_add_fusion.meta, ...), custom_call_target="tpu_custom_call" | custom-call | tf_op jit(solution)/shard_map/mlp_first/pallas_call | solution.py:488
  29.8 4.5 %qkv_2.1 = (bf16[2048,192]{1,0:T(8,128)(2,1)}, bf16[2048,192]{1,0:T(8,128)(2,1)}, bf16[2048,192]{1,0:T(8,128)(2,1)}) custom-call(s32[2]{0:T(128)} %pad_add_fusion.meta, bf16[512,768]{1,0:T(8,128)(2,1)} %collective-permute-done.2.x_ref.xa, f32[768]{0:T(1024)} %refs_8_.1, f32[768]{0:T(1024)} %refs_3_.1, ...), custom_call_target="tpu_custom_call", output_to_operand_aliasing={{0}: (8, {}), {1}: (9, {}), {2}: (10, {})} | custom-call | tf_op jit(solution)/shard_map/qkv_2/pallas_call | solution.py:181
  34.3 4.5 %qkv_3.1 = (bf16[2048,192]{1,0:T(8,128)(2,1)}, bf16[2048,192]{1,0:T(8,128)(2,1)}, bf16[2048,192]{1,0:T(8,128)(2,1)}) custom-call(s32[2]{0:T(128)} %pad_add_fusion.meta, bf16[512,768]{1,0:T(8,128)(2,1)} %collective-permute-done.3.x_ref.xb, f32[768]{0:T(1024)} %refs_8_.1, f32[768]{0:T(1024)} %refs_3_.1, ...), custom_call_target="tpu_custom_call", output_to_operand_aliasing={{0}: (8, {}), {1}: (9, {}), {2}: (10, {})} | custom-call | tf_op jit(solution)/shard_map/qkv_3/pallas_call | solution.py:181
  40.3 13.5 %attend.1 = (bf16[2048,192]{1,0:T(8,128)(2,1)}, f32[3,8,1,256]{3,2,1,0:T(1,128)}, s32[8,1,256]{2,1,0:T(1,128)}, s32[8]{0:T(128)}, s32[8]{0:T(128)}) custom-call(s32[2]{0:T(128)} %pad_add_fusion.meta, s32[1]{0:T(128)S(6)} %copy.50.valid, bf16[2048,192]{1,0:T(8,128)(2,1)} %get-tuple-element.105.q_ref, bf16[2048,192]{1,0:T(8,128)(2,1)} %get-tuple-element.106.k_ref, ...), custom_call_target="tpu_custom_call" | custom-call | tf_op jit(solution)/shard_map/attend/pallas_call | solution.py:622
  53.8 20.4 %mlp_second.1 = (bf16[2048,768]{1,0:T(8,128)(2,1)}, bf16[2048,768]{1,0:T(8,128)(2,1)}, bf16[2048,192]{1,0:T(8,128)(2,1)}, f32[8,768]{1,0:T(8,128)}, bf16[2,512,7...) custom-call(s32[2]{0:T(128)} %pad_add_fusion.meta, ...), custom_call_target="tpu_custom_call", output_to_operand_aliasing={{0}: (19, {}), {1}: (20, {}), {2}: (21, {})} | custom-call | tf_op jit(solution)/shard_map/mlp_second/pallas_call | solution.py:488
  74.8 1.8 %collective-permute-start.8 = (bf16[768,512]{1,0:T(8,128)(2,1)}, bf16[768,512]{1,0:T(8,128)(2,1)}, u32[]{:S(2)}, u32[]{:S(2)}) collective-permute-start(bf16[768,512]{1,0:T(8,128)(2,1)} %get-tuple-element.132), channel_id=1, source_target_pairs={{0,8},{4,12},{8,0},{12,4},{16,24},{20,28},{24,16},{28,20},{1,9},{5... | collective-permute-start | bytes 2359304 | tf_op jit(solution)/shard_map/ppermute | solution.py:1080
  76.6 1.5 collective-permute-start.7
  78.1 21.1 %attend_back.1.refs_0_.refs_1_.refs_2_.refs_3_ = bf16[2048,576]{1,0:T(8,128)(2,1)} custom-call(s32[2]{0:T(128)} %pad_add_fusion.meta, s32[8]{0:T(128)} %get-tuple-element.121.lo, s32[8]{0:T(128)} %get-tuple-element.122.hi, bf16[2048,192]{1,0:T(8,128)(2,1)} %get-tuple-element.105.q_ref, bf16[2048,192]{1,0:T(8,128)(2,1)} %get-tuple-element.106.k_ref, ...), custom_call_target="tpu_custom_call" | custom-call | tf_op jit(solution)/shard_map/attend_back/pallas_call | solution.py:766
  99.2 7.9 %joined_weight.1 = (bf16[400,576]{1,0:T(8,128)(2,1)}, bf16[400,576]{1,0:T(8,128)(2,1)}, f32[16,576]{1,0:T(8,128)}) custom-call(s32[2]{0:T(128)} %pad_add_fusion.meta, bf16[2048,576]{1,0:T(8,128)(2,1)} %attend_back.1.refs_0_.refs_1_.refs_2_.refs_3_, bf16[2048,768]{1,0:T(8,128)(2,1)} %get-tuple-element.126.refs_1_, f32[768]{0:T(1024)} %refs_8_.1, ...), custom_call_target="tpu_custom_call" | custom-call | tf_op jit(solution)/shard_map/joined_weight/pallas_call | solution.py:863
  107.1 3.2 %collective-permute-start.13 = (bf16[400,576]{1,0:T(8,128)(2,1)}, bf16[400,576]{1,0:T(8,128)(2,1)}, u32[]{:S(2)}, u32[]{:S(2)}) collective-permute-start(bf16[400,576]{1,0:T(8,128)(2,1)} %get-tuple-element.145), channel_id=1, source_target_pairs={{0,4},{4,0},{8,12},{12,8},{16,20},{20,16},{24,28},{28,24},{1,5},{5... | collective-permute-start | bytes 1382408 | tf_op jit(solution)/shard_map/ppermute | solution.py:1080
  110.3 3.7 %first_sums.1 = (bf16[192,768]{1,0:T(8,128)(2,1)}, bf16[384,512]{1,0:T(8,128)(2,1)}, bf16[512,768]{1,0:T(8,128)(2,1)}) custom-call(s32[2]{0:T(128)} %pad_add_fusion.meta, bf16[384,768]{1,0:T(8,128)(2,1)} %get-tuple-element.165.refs_0_, bf16[384,768]{1,0:T(8,128)(2,1)} %collective-permute-done.7.refs_1_, bf16[768,512]{1,0:T(8,128)(2,1)} %get-tuple-element.152.refs_2_, ...), custom_call_target="tpu_custom_call" | custom-call | tf_op jit(solution)/shard_map/first_sums/pallas_call | solution.py:953
  114.0 1.5 collective-permute-start.11
  115.5 7.0 %norm_grad.1 = (bf16[512,768]{1,0:T(8,128)(2,1)}, bf16[512,768]{1,0:T(8,128)(2,1)}, bf16[512,768]{1,0:T(8,128)(2,1)}, bf16[512,768]{1,0:T(8,128)(2,1)}) custom-call(s32[2]{0:T(128)} %pad_add_fusion.meta, bf16[2048,576]{1,0:T(8,128)(2,1)} %attend_back.1.refs_0_.refs_1_.refs_2_.refs_3_, bf16[2048,576]{1,0:T(8,128)(2,1)} %attend_back.1.refs_0_.refs_1_.refs_2_.refs_3_, ...), custom_call_target="tpu_custom_call" | custom-call | tf_op jit(solution)/shard_map/norm_grad/pallas_call | solution.py:894
  125.0 1.7 collective-permute-start.15
  126.7 6.0 %collective-permute-done.10 = bf16[384,512]{1,0:T(8,128)(2,1)S(1)} collective-permute-done((bf16[384,512]{1,0:T(8,128)(2,1)}, bf16[384,512]{1,0:T(8,128)(2,1)S(1)}, u32[]{:S(2)}, u32[]{:S(2)}) %collective-permute-start.10) | collective-permute-done | bytes 393248 | tf_op jit(solution)/shard_map/ppermute | solution.py:1080
  132.7 1.9 %add_convert_fusion.3 = bf16[192,512]{1,0:T(8,128)(2,1)} fusion(bf16[384,512]{1,0:T(8,128)(2,1)S(1)} %collective-permute-done.10, bf16[768,512]{1,0:T(8,128)(2,1)} %collective-permute-done.8.refs_3_, bf16[768,512]{1,0:T(8,128)(2,1)} %get-tuple-element.152.refs_2_), kind=kLoop, calls=%fused_computation.4 | loop fusion | flops 589824 | bytes 786432 | tf_op jit(solution)/shard_map/convert_element_type | solution.py:1063
  138.0 2.9 %collective-permute-start.17 = (bf16[112,576]{1,0:T(8,128)(2,1)}, bf16[112,576]{1,0:T(8,128)(2,1)}, u32[]{:S(2)}, u32[]{:S(2)}) collective-permute-start(bf16[112,576]{1,0:T(8,128)(2,1)} %pad_maximum_fusion.2.refs_4_), channel_id=1, source_target_pairs={{0,16},{4,20},{8,24},{12,28},{16,0},{20,4},{24,8},{28,12},{1,17},{... | collective-permute-start | bytes 387080 | tf_op jit(solution)/shard_map/ppermute | solution.py:1080
  141.0 2.8 %result.1 = bf16[512,768]{1,0:T(8,128)(2,1)} custom-call(bf16[512,768]{1,0:T(8,128)(2,1)} %bitcast.17, bf16[2,512,768]{2,1,0:T(8,128)(2,1)} %get-tuple-element.133.even, bf16[2,512,768]{2,1,0:T(8,128)(2,1)} %collective-permute-done.9.near, bf16[512,768]{1,0:T(8,128)(2,1)} %collective-permute-done.11.far, f32[768]{0:T(1024)} %b_out.1, f32[768]{0:T(1024)} %b_down.1), custom_call_target="tpu_custom_call" | custom-call | tf_op jit(solution)/shard_map/result/pallas_call | solution.py:1128
  143.8 1.8 %add_convert_fusion.4 = bf16[96,768]{1,0:T(8,128)(2,1)} fusion(bf16[192,768]{1,0:T(8,128)(2,1)} %collective-permute-done.15, bf16[384,768]{1,0:T(8,128)(2,1)} %collective-permute-done.7.refs_1_, bf16[384,768]{1,0:T(8,128)(2,1)} %get-tuple-element.165.refs_0_), kind=kLoop, calls=%fused_computation.6 | loop fusion | flops 442368 | bytes 589824 | tf_op jit(solution)/shard_map/convert_element_type | solution.py:1063
  145.6 5.4 %collective-permute-done.16 = bf16[192,512]{1,0:T(8,128)(2,1)} collective-permute-done((bf16[192,512]{1,0:T(8,128)(2,1)}, bf16[192,512]{1,0:T(8,128)(2,1)}, u32[]{:S(2)}, u32[]{:S(2)}) %collective-permute-start.16) | collective-permute-done | bytes 196640 | tf_op jit(solution)/shard_map/ppermute | solution.py:1080
  150.9 2.0 %add_convert_fusion.2 = bf16[192,512]{1,0:T(8,128)(2,1)} fusion(bf16[192,512]{1,0:T(8,128)(2,1)} %collective-permute-done.16, bf16[384,512]{1,0:T(8,128)(2,1)} %copy-done.2, bf16[768,512]{1,0:T(8,128)(2,1)} %collective-permute-done.8.refs_3_, bf16[768,512]{1,0:T(8,128)(2,1)} %get-tuple-element.152.refs_2_), kind=kLoop, calls=%fused_computation.3 | loop fusion | flops 786432 | bytes 983040 | tf_op jit(solution)/shard_map/convert_element_type | solution.py:1254
  152.9 3.0 %collective-permute-start.20 = (bf16[192,512]{1,0:T(8,128)(2,1)}, bf16[192,512]{1,0:T(8,128)(2,1)}, u32[]{:S(2)}, u32[]{:S(2)}) collective-permute-start(bf16[192,512]{1,0:T(8,128)(2,1)} %add_convert_fusion.2), channel_id=1, source_target_pairs={{0,0},{1,8},{2,16},{3,24},{4,1},{5,9},{6,17},{7,25},{8,2},{9,10},{... | collective-permute-start | bytes 589832 | tf_op jit(solution)/shard_map/ppermute | solution.py:1092
  155.9 1.7 collective-permute-start.24
  157.6 2.6 %last_qkv.1 = (f32[96,192]{1,0:T(8,128)}, f32[128,192]{1,0:T(8,128)}, f32[128,192]{1,0:T(8,128)}, f32[32,192]{1,0:T(8,128)}) custom-call(s32[2]{0:T(128)} %pad_add_fusion.meta, bf16[400,576]{1,0:T(8,128)(2,1)} %get-tuple-element.144.refs_0_, bf16[400,576]{1,0:T(8,128)(2,1)} %collective-permute-done.13.refs_1_, bf16[208,576]{1,0:T(8,128)(2,1)} %copy-done.1, ...), custom_call_target="tpu_custom_call" | custom-call | tf_op jit(solution)/shard_map/last_qkv/pallas_call | solution.py:915
  160.2 1.3 collective-permute-start.22
  162.1 3.5 %token_grad.1 = bf16[512,768]{1,0:T(8,128)(2,1)} custom-call(bf16[512,768]{1,0:T(8,128)(2,1)} %bitcast.18, bf16[512,768]{1,0:T(8,128)(2,1)} %get-tuple-element.138.even, bf16[512,768]{1,0:T(8,128)(2,1)} %collective-permute-done.18.near, bf16[512,768]{1,0:T(8,128)(2,1)} %collective-permute-done.19.far, bf16[512,768]{1,0:T(8,128)(2,1)} %bitcast.13), custom_call_target="tpu_custom_call" | custom-call | tf_op jit(solution)/shard_map/token_grad/pallas_call | solution.py:1128
  165.6 2.4 %lower.1 = (f32[192,384]{1,0:T(8,128)}, f32[96,192]{1,0:T(8,128)}) custom-call(s32[2]{0:T(128)} %pad_add_fusion.meta, bf16[192,512]{1,0:T(8,128)(2,1)} %collective-permute-done.20.piece), custom_call_target="tpu_custom_call" | custom-call | tf_op jit(solution)/shard_map/lower/pallas_call | solution.py:915
  167.9 2.7 %assemble.1 = (f32[96,576]{1,0:T(8,128)}, f32[2304]{0:T(1024)}, f32[768]{0:T(1024)}, f32[3072]{0:T(1024)}, f32[768]{0:T(1024)}, /*index=5*/f32[768]{0:T(1024)}, f32[768]{0:T(1024)}, f32[768]{0:T(1024)}, f32[768]{0:T(1024)}) custom-call(s32[2]{0:T(128)} %pad_add_fusion.meta, f32[96,192]{1,0:T(8,128)} %get-tuple-element.160.kept, ...), custom_call_target="tpu_custom_call" | custom-call | tf_op jit(solution)/shard_map/assemble/pallas_call | solution.py:1046
  171.6 1.9 %convert_add_fusion = f32[96,768]{1,0:T(8,128)} fusion(bf16[96,768]{1,0:T(8,128)(2,1)} %collective-permute-done.24, bf16[192,768]{1,0:T(8,128)(2,1)} %collective-permute-done.15, bf16[384,768]{1,0:T(8,128)(2,1)} %collective-permute-done.7.refs_1_, bf16[384,768]{1,0:T(8,128)(2,1)} %get-tuple-element.165.refs_0_), kind=kLoop, calls=%fused_computation.5 | loop fusion | flops 516096 | bytes 884736 | tf_op jit(solution)/shard_map/add | solution.py:1281
  (55 shorter events, 12.8 us)
Async XLA Ops:
  0.6 9.7 %collective-permute-start = (bf16[512,768]{1,0:T(8,128)(2,1)}, bf16[512,768]{1,0:T(8,128)(2,1)}, u32[]{:S(2)}, u32[]{:S(2)}) collective-permute-start(bf16[512,768]{1,0:T(8,128)(2,1)} %bitcast.14), channel_id=1, source_target_pairs={{0,1},{1,0},{2,3},{3,2},{4,5},{5,4},{6,7},{7,6},{8,9},{9,8},{10,11... | collective-permute-start | bytes 2359304 | tf_op jit(solution)/shard_map/ppermute | solution.py:1080
  1.2 9.2 %collective-permute-start.1 = (bf16[512,768]{1,0:T(8,128)(2,1)}, bf16[512,768]{1,0:T(8,128)(2,1)}, u32[]{:S(2)}, u32[]{:S(2)}) collective-permute-start(bf16[512,768]{1,0:T(8,128)(2,1)} %bitcast.9), channel_id=1, source_target_pairs={{0,1},{1,0},{2,3},{3,2},{4,5},{5,4},{6,7},{7,6},{8,9},{9,8},{10,11... | collective-permute-start | bytes 2359304 | tf_op jit(solution)/shard_map/ppermute | solution.py:1080
  1.2 28.1 %collective-permute-start.2 = (bf16[512,768]{1,0:T(8,128)(2,1)}, bf16[512,768]{1,0:T(8,128)(2,1)}, u32[]{:S(2)}, u32[]{:S(2)}) collective-permute-start(bf16[512,768]{1,0:T(8,128)(2,1)} %bitcast.15), channel_id=1, source_target_pairs={{0,2},{1,3},{2,0},{3,1},{4,6},{5,7},{6,4},{7,5},{8,10},{9,11},{10,... | collective-permute-start | bytes 2359304 | tf_op jit(solution)/shard_map/ppermute | solution.py:1080
  4.8 1.2 collective-permute-start.4
  6.0 0.6 copy-start.3
  8.7 30.9 %collective-permute-start.5 = (bf16[528,768]{1,0:T(8,128)(2,1)}, bf16[528,768]{1,0:T(8,128)(2,1)}, u32[]{:S(2)}, u32[]{:S(2)}) collective-permute-start(bf16[528,768]{1,0:T(8,128)(2,1)} %pad_maximum_fusion), channel_id=1, source_target_pairs={{0,2},{1,3},{2,0},{3,1},{4,6},{5,7},{6,4},{7,5},{8,10},{9,11},{10,... | collective-permute-start | bytes 2433032 | tf_op jit(solution)/shard_map/ppermute | solution.py:1080
  29.3 5.0 %collective-permute-start.3 = (bf16[512,768]{1,0:T(8,128)(2,1)}, bf16[512,768]{1,0:T(8,128)(2,1)}, u32[]{:S(2)}, u32[]{:S(2)}) collective-permute-start(bf16[512,768]{1,0:T(8,128)(2,1)} %collective-permute-done.2.x_ref.xa), channel_id=1, source_target_pairs={{0,1},{1,0},{2,3},{3,2},{4,5},{5,4},{6,7},{7,6},{8,9},{9,8},{10,11... | collective-permute-start | bytes 2359304 | tf_op jit(solution)/shard_map/ppermute | solution.py:1080
  39.6 14.2 %collective-permute-start.6 = (bf16[528,768]{1,0:T(8,128)(2,1)}, bf16[528,768]{1,0:T(8,128)(2,1)}, u32[]{:S(2)}, u32[]{:S(2)}) collective-permute-start(bf16[528,768]{1,0:T(8,128)(2,1)} %collective-permute-done.5.pair_far.ca), channel_id=1, source_target_pairs={{0,1},{1,0},{2,3},{3,2},{4,5},{5,4},{6,7},{7,6},{8,9},{9,8},{10,11... | collective-permute-start | bytes 2433032 | tf_op jit(solution)/shard_map/ppermute | solution.py:1080
  74.2 36.1 %collective-permute-start.9 = (bf16[2,512,768]{2,1,0:T(8,128)(2,1)}, bf16[2,512,768]{2,1,0:T(8,128)(2,1)}, u32[]{:S(2)}, u32[]{:S(2)}) collective-permute-start(bf16[2,512,768]{2,1,0:T(8,128)(2,1)} %get-tuple-element.134), channel_id=1, source_target_pairs={{0,1},{1,0},{2,3},{3,2},{4,5},{5,4},{6,7},{7,6},{8,9},{9,8},{10,11... | collective-permute-start | bytes 4718600 | tf_op jit(solution)/shard_map/ppermute | solution.py:1080
  74.8 35.5 %collective-permute-start.8 = (bf16[768,512]{1,0:T(8,128)(2,1)}, bf16[768,512]{1,0:T(8,128)(2,1)}, u32[]{:S(2)}, u32[]{:S(2)}) collective-permute-start(bf16[768,512]{1,0:T(8,128)(2,1)} %get-tuple-element.132), channel_id=1, source_target_pairs={{0,8},{4,12},{8,0},{12,4},{16,24},{20,28},{24,16},{28,20},{1,9},{5... | collective-permute-start | bytes 2359304 | tf_op jit(solution)/shard_map/ppermute | solution.py:1080
  76.6 33.7 %collective-permute-start.7 = (bf16[384,768]{1,0:T(8,128)(2,1)}, bf16[384,768]{1,0:T(8,128)(2,1)}, u32[]{:S(2)}, u32[]{:S(2)}) collective-permute-start(bf16[384,768]{1,0:T(8,128)(2,1)} %get-tuple-element.130), channel_id=1, source_target_pairs={{0,4},{4,0},{8,12},{12,8},{16,20},{20,16},{24,28},{28,24},{1,5},{5... | collective-permute-start | bytes 1769480 | tf_op jit(solution)/shard_map/ppermute | solution.py:1080
  107.1 15.5 %collective-permute-start.13 = (bf16[400,576]{1,0:T(8,128)(2,1)}, bf16[400,576]{1,0:T(8,128)(2,1)}, u32[]{:S(2)}, u32[]{:S(2)}) collective-permute-start(bf16[400,576]{1,0:T(8,128)(2,1)} %get-tuple-element.145), channel_id=1, source_target_pairs={{0,4},{4,0},{8,12},{12,8},{16,20},{20,16},{24,28},{28,24},{1,5},{5... | collective-permute-start | bytes 1382408 | tf_op jit(solution)/shard_map/ppermute | solution.py:1080
  114.0 20.7 %collective-permute-start.11 = (bf16[512,768]{1,0:T(8,128)(2,1)}, bf16[512,768]{1,0:T(8,128)(2,1)}, u32[]{:S(2)}, u32[]{:S(2)}) collective-permute-start(bf16[512,768]{1,0:T(8,128)(2,1)} %get-tuple-element.135), channel_id=1, source_target_pairs={{0,2},{1,3},{2,0},{3,1},{4,6},{5,7},{6,4},{7,5},{8,10},{9,11},{10,... | collective-permute-start | bytes 2359304 | tf_op jit(solution)/shard_map/ppermute | solution.py:1080
  122.5 12.2 %copy-start = (bf16[512,768]{1,0:T(8,128)(2,1)S(1)}, bf16[512,768]{1,0:T(8,128)(2,1)}, u32[]{:S(2)}) copy-start(bf16[512,768]{1,0:T(8,128)(2,1)} %get-tuple-element.142) | copy-start | bytes 2359300
  122.5 10.2 %collective-permute-start.10 = (bf16[384,512]{1,0:T(8,128)(2,1)}, bf16[384,512]{1,0:T(8,128)(2,1)S(1)}, u32[]{:S(2)}, u32[]{:S(2)}) collective-permute-start(bf16[384,512]{1,0:T(8,128)(2,1)} %get-tuple-element.141), channel_id=1, source_target_pairs={{0,4},{4,0},{8,12},{12,8},{16,20},{20,16},{24,28},{28,24},{1,5},{5... | collective-permute-start | bytes 1179656 | tf_op jit(solution)/shard_map/ppermute | solution.py:1080
  122.6 12.1 %collective-permute-start.12 = (bf16[512,768]{1,0:T(8,128)(2,1)}, bf16[512,768]{1,0:T(8,128)(2,1)S(1)}, u32[]{:S(2)}, u32[]{:S(2)}) collective-permute-start(bf16[512,768]{1,0:T(8,128)(2,1)} %get-tuple-element.143), channel_id=1, source_target_pairs={{0,1},{1,0},{2,3},{3,2},{4,5},{5,4},{6,7},{7,6},{8,9},{9,8},{10,11... | collective-permute-start | bytes 2359304 | tf_op jit(solution)/shard_map/ppermute | solution.py:1080
  124.7 11.6 %collective-permute-start.14 = (bf16[208,576]{1,0:T(8,128)(2,1)S(1)}, bf16[208,576]{1,0:T(8,128)(2,1)S(1)}, u32[]{:S(2)}, u32[]{:S(2)}) collective-permute-start(bf16[208,576]{1,0:T(8,128)(2,1)S(1)} %pad_maximum_fusion.1), channel_id=1, source_target_pairs={{0,8},{4,12},{8,0},{12,4},{16,24},{20,28},{24,16},{28,20},{1,9},{5... | collective-permute-start | bytes 718856 | tf_op jit(solution)/shard_map/ppermute | solution.py:1080
  125.0 18.8 %collective-permute-start.15 = (bf16[192,768]{1,0:T(8,128)(2,1)}, bf16[192,768]{1,0:T(8,128)(2,1)}, u32[]{:S(2)}, u32[]{:S(2)}) collective-permute-start(bf16[192,768]{1,0:T(8,128)(2,1)} %get-tuple-element.151), channel_id=1, source_target_pairs={{0,8},{4,12},{8,0},{12,4},{16,24},{20,28},{24,16},{28,20},{1,9},{5... | collective-permute-start | bytes 884744 | tf_op jit(solution)/shard_map/ppermute | solution.py:1080
  132.7 1.9 %copy-start.2 = (bf16[384,512]{1,0:T(8,128)(2,1)}, bf16[384,512]{1,0:T(8,128)(2,1)S(1)}, u32[]{:S(2)}) copy-start(bf16[384,512]{1,0:T(8,128)(2,1)S(1)} %collective-permute-done.10) | copy-start | bytes 1179652
  132.7 27.5 %collective-permute-start.18 = (bf16[512,768]{1,0:T(8,128)(2,1)}, bf16[512,768]{1,0:T(8,128)(2,1)}, u32[]{:S(2)}, u32[]{:S(2)}) collective-permute-start(bf16[512,768]{1,0:T(8,128)(2,1)} %get-tuple-element.156), channel_id=1, source_target_pairs={{0,1},{1,0},{2,3},{3,2},{4,5},{5,4},{6,7},{7,6},{8,9},{9,8},{10,11... | collective-permute-start | bytes 2359304 | tf_op jit(solution)/shard_map/ppermute | solution.py:1080
  134.7 16.3 %collective-permute-start.16 = (bf16[192,512]{1,0:T(8,128)(2,1)}, bf16[192,512]{1,0:T(8,128)(2,1)}, u32[]{:S(2)}, u32[]{:S(2)}) collective-permute-start(bf16[192,512]{1,0:T(8,128)(2,1)} %add_convert_fusion.3), channel_id=1, source_target_pairs={{0,16},{4,20},{8,24},{12,28},{16,0},{20,4},{24,8},{28,12},{1,17},{... | collective-permute-start | bytes 589832 | tf_op jit(solution)/shard_map/ppermute | solution.py:1080
  135.7 25.8 %collective-permute-start.19 = (bf16[512,768]{1,0:T(8,128)(2,1)}, bf16[512,768]{1,0:T(8,128)(2,1)}, u32[]{:S(2)}, u32[]{:S(2)}) collective-permute-start(bf16[512,768]{1,0:T(8,128)(2,1)} %add_convert_fusion), channel_id=1, source_target_pairs={{0,2},{1,3},{2,0},{3,1},{4,6},{5,7},{6,4},{7,5},{8,10},{9,11},{10,... | collective-permute-start | bytes 2359304 | tf_op jit(solution)/shard_map/ppermute | solution.py:1080
  136.2 1.1 copy-start.1
  138.0 19.5 %collective-permute-start.17 = (bf16[112,576]{1,0:T(8,128)(2,1)}, bf16[112,576]{1,0:T(8,128)(2,1)}, u32[]{:S(2)}, u32[]{:S(2)}) collective-permute-start(bf16[112,576]{1,0:T(8,128)(2,1)} %pad_maximum_fusion.2.refs_4_), channel_id=1, source_target_pairs={{0,16},{4,20},{8,24},{12,28},{16,0},{20,4},{24,8},{28,12},{1,17},{... | collective-permute-start | bytes 387080 | tf_op jit(solution)/shard_map/ppermute | solution.py:1080
  152.9 12.6 %collective-permute-start.20 = (bf16[192,512]{1,0:T(8,128)(2,1)}, bf16[192,512]{1,0:T(8,128)(2,1)}, u32[]{:S(2)}, u32[]{:S(2)}) collective-permute-start(bf16[192,512]{1,0:T(8,128)(2,1)} %add_convert_fusion.2), channel_id=1, source_target_pairs={{0,0},{1,8},{2,16},{3,24},{4,1},{5,9},{6,17},{7,25},{8,2},{9,10},{... | collective-permute-start | bytes 589832 | tf_op jit(solution)/shard_map/ppermute | solution.py:1092
  155.9 15.7 %collective-permute-start.24 = (bf16[96,768]{1,0:T(8,128)(2,1)}, bf16[96,768]{1,0:T(8,128)(2,1)}, u32[]{:S(2)}, u32[]{:S(2)}) collective-permute-start(bf16[96,768]{1,0:T(8,128)(2,1)} %add_convert_fusion.4), channel_id=1, source_target_pairs={{0,16},{4,20},{8,24},{12,28},{16,0},{20,4},{24,8},{28,12},{1,17},{... | collective-permute-start | bytes 442376 | tf_op jit(solution)/shard_map/ppermute | solution.py:1080
  160.2 7.7 %collective-permute-start.21 = (f32[128,192]{1,0:T(8,128)}, f32[128,192]{1,0:T(8,128)}, u32[]{:S(2)}, u32[]{:S(2)}) collective-permute-start(f32[128,192]{1,0:T(8,128)} %get-tuple-element.161), channel_id=1, source_target_pairs={{0,1},{1,0},{2,3},{3,2},{4,5},{5,4},{6,7},{7,6},{8,9},{9,8},{10,11... | collective-permute-start | bytes 294920 | tf_op jit(solution)/shard_map/ppermute | solution.py:1080
  160.2 7.7 %collective-permute-start.22 = (f32[128,192]{1,0:T(8,128)}, f32[128,192]{1,0:T(8,128)}, u32[]{:S(2)}, u32[]{:S(2)}) collective-permute-start(f32[128,192]{1,0:T(8,128)} %get-tuple-element.162), channel_id=1, source_target_pairs={{0,2},{1,3},{2,0},{3,1},{4,6},{5,7},{6,4},{7,5},{8,10},{9,11},{10,... | collective-permute-start | bytes 294920 | tf_op jit(solution)/shard_map/ppermute | solution.py:1080
  161.5 6.4 %collective-permute-start.23 = (f32[32,192]{1,0:T(8,128)}, f32[32,192]{1,0:T(8,128)}, u32[]{:S(2)}, u32[]{:S(2)}) collective-permute-start(f32[32,192]{1,0:T(8,128)} %get-tuple-element.154.small), channel_id=1, source_target_pairs={{0,3},{1,2},{2,1},{3,0},{4,7},{5,6},{6,5},{7,4},{8,11},{9,10},{10,... | collective-permute-start | bytes 73736 | tf_op jit(solution)/shard_map/ppermute | solution.py:1080
